TPU v7x, 32 devices: a whole 2x2x4 slice. The times are simulated.
32 devices in a mesh: batch: 8 (over z, y), tensor: 4 (over x, core).
Axes of the slice: x: 2, y: 2, z: 4, core: 2. Of those that a mesh axis runs over, the one named last changes fastest.
Arguments:
- tokens: bfloat16 [12288, 768], P('batch'), may hold values from -6 to 6
- lengths: int32 [8], P('batch'), may hold values from 1024 to 1536, as said below
- w_query: bfloat16 [768, 768], P('batch', 'tensor'), may hold values from -0.4375 to 0.4375
- w_key: bfloat16 [768, 768], P('batch', 'tensor'), may hold values from -0.21875 to 0.21875
- w_value: bfloat16 [768, 768], P('batch', 'tensor'), may hold values from -0.21875 to 0.21875
- w_out: bfloat16 [768, 768], P('tensor', 'batch'), may hold values from -0.875 to 0.875
- w_up: bfloat16 [768, 3072], P('batch', 'tensor'), may hold values from -0.21875 to 0.21875
- w_down: bfloat16 [3072, 768], P('tensor', 'batch'), may hold values from -0.109375 to 0.109375
- norm_gain: bfloat16 [2, 768], P(None, 'batch'), may hold values from 0.099609375 to 1.8984375
- norm_shift: bfloat16 [2, 768], P(None, 'batch'), may hold values from -3 to 3
- out_grad: bfloat16 [12288, 768], P('batch'), may hold values from -6 to 6
Outputs:
- layer_out: bfloat16 [12288, 768], P('batch')
- grad_input: bfloat16 [12288, 768], P('batch')
- grad_query: float32 [768, 768], P('batch', 'tensor')
- grad_key: float32 [768, 768], P('batch', 'tensor')
- grad_value: float32 [768, 768], P('batch', 'tensor')
- grad_out: float32 [768, 768], P('tensor', 'batch')
- grad_up: float32 [768, 3072], P('batch', 'tensor')
- grad_down: float32 [3072, 768], P('tensor', 'batch')
- grad_gain: float32 [2, 768], P(None, 'batch')
- grad_shift: float32 [2, 768], P(None, 'batch')
Inputs may be any that keep to these rules, and one draw needn't show every extreme that they name: `lengths`: each sequence's valid tokens; some sequence fills all 1536 slots.
All inputs are finite; a program needn't handle non-finite values.
Results may differ from a plain program's by a relative error of at most 0.017.
Values may be sent and summed in bfloat16 or wider, within the bound.
No kernel may reach another device: no remote copies, remote signals or barrier semaphores. Data moves between devices by JAX's collectives and lax.ppermute only.
A program may use at most 192 MiB of HBM per device.

v0:
```python
import jax
import jax.numpy as jnp
from jax import lax
from jax.sharding import PartitionSpec as P

HD = 64


epsilon = 1e-05


def cut_along(value, dim, length):
    shape = value.shape
    parts = value.reshape(*shape[:dim], length, shape[dim] // length, *shape[dim + 1 :])
    return jnp.moveaxis(parts, dim, 0)


def summed_on_arrival(value, axis, dim):
    length = lax.axis_size(axis)
    parts = lax.all_to_all(cut_along(value, dim, length), axis, 0, 0, tiled=True)
    return jnp.sum(parts.astype(jnp.float32), axis=0)


def normalize_keep(values, gain_row, shift_row):
    middle = jnp.mean(values, axis=-1, keepdims=True)
    centred = values - middle
    spread = jnp.mean(centred * centred, axis=-1, keepdims=True)
    inverse = lax.rsqrt(spread + epsilon)
    scaled = centred * inverse
    return (scaled * gain_row + shift_row, scaled, inverse)


def normalize_back(grad_normed, scaled, inverse, gain_row):
    grad_scaled = grad_normed * gain_row
    mean_grad = jnp.mean(grad_scaled, axis=-1, keepdims=True)
    mean_cross = jnp.mean(grad_scaled * scaled, axis=-1, keepdims=True)
    grad_values = inverse * (grad_scaled - mean_grad - scaled * mean_cross)
    return (grad_values, jnp.sum(grad_normed * scaled, axis=0), jnp.sum(grad_normed, axis=0))


def multiply(left_mat, right_mat):
    return jnp.dot(left_mat, right_mat, preferred_element_type=jnp.float32)


def inner_rows(left_mat, right_mat):
    return lax.dot_general(
        left_mat, right_mat, (((0,), (0,)), ((), ())), preferred_element_type=jnp.float32
    )


def outer_cols(left_mat, right_mat):
    return lax.dot_general(
        left_mat, right_mat, (((1,), (1,)), ((), ())), preferred_element_type=jnp.float32
    )


def gelu_tanh(values):
    return jax.nn.gelu(values, approximate=True)


def score_block(queries_blk, keys_part, row_pos, key_pos, length, scaling):
    raw_scores = jnp.einsum(
        "qhd,khd->hqk", queries_blk, keys_part, preferred_element_type=jnp.float32
    )
    scores = raw_scores * scaling
    allowed = (key_pos[None, :] <= row_pos[:, None]) & (key_pos[None, :] < length)
    magnitude = jnp.where(allowed[None], jnp.abs(scores), -1e30)
    return (scores, magnitude)


def attend_forward(queries, key_rows, value_rows, length, block_rows, scaling):
    seq_rows = queries.shape[0]
    position = jnp.arange(seq_rows, dtype=jnp.int32)
    outputs = []
    log_sums = []
    for number in range(seq_rows // block_rows):
        begin_row = number * block_rows
        end_row = begin_row + block_rows
        scores, magnitude = score_block(
            queries[begin_row:end_row],
            key_rows[:end_row],
            position[begin_row:end_row],
            position[:end_row],
            length,
            scaling,
        )
        row_max = jnp.max(magnitude, axis=-1, keepdims=True)
        exponent = jnp.exp(magnitude - row_max)
        row_sum = jnp.sum(exponent, axis=-1, keepdims=True)
        weights = (jnp.sign(scores) * (exponent / row_sum)).astype(jnp.bfloat16)
        outputs.append(
            jnp.einsum(
                "hqk,khd->qhd", weights, value_rows[:end_row], preferred_element_type=jnp.float32
            )
        )
        log_sums.append(row_max + jnp.log(row_sum))
    return (jnp.concatenate(outputs, axis=0), jnp.concatenate(log_sums, axis=1))


def attend_back(queries, key_rows, value_rows, grad_mixed, log_sums, length, block_rows, scaling):
    seq_rows = queries.shape[0]
    position = jnp.arange(seq_rows, dtype=jnp.int32)
    grad_queries = []
    grad_keys = jnp.zeros(key_rows.shape, jnp.float32)
    grad_values = jnp.zeros(value_rows.shape, jnp.float32)
    for number in range(seq_rows // block_rows):
        begin_row = number * block_rows
        end_row = begin_row + block_rows
        scores, magnitude = score_block(
            queries[begin_row:end_row],
            key_rows[:end_row],
            position[begin_row:end_row],
            position[:end_row],
            length,
            scaling,
        )
        probability = jnp.exp(magnitude - log_sums[:, begin_row:end_row])
        signs = jnp.sign(scores)
        weights = signs * probability
        grad_blk = grad_mixed[begin_row:end_row]
        grad_weights = jnp.einsum(
            "qhd,khd->hqk", grad_blk, value_rows[:end_row], preferred_element_type=jnp.float32
        )
        delta_row = jnp.sum(weights * grad_weights, axis=-1, keepdims=True)
        grad_raw = (signs * probability * (signs * grad_weights - delta_row) * scaling).astype(
            jnp.bfloat16
        )
        grad_queries.append(
            jnp.einsum(
                "hqk,khd->qhd", grad_raw, key_rows[:end_row], preferred_element_type=jnp.float32
            )
        )
        grad_keys = grad_keys.at[:end_row].add(
            jnp.einsum(
                "hqk,qhd->khd",
                grad_raw,
                queries[begin_row:end_row],
                preferred_element_type=jnp.float32,
            )
        )
        grad_values = grad_values.at[:end_row].add(
            jnp.einsum(
                "hqk,qhd->khd",
                weights.astype(jnp.bfloat16),
                grad_blk,
                preferred_element_type=jnp.float32,
            )
        )
    return (jnp.concatenate(grad_queries, axis=0), grad_keys, grad_values)


def per_device(
    tokens, lengths, w_query, w_key, w_value, w_out, w_up, w_down, norm_gain, norm_shift, out_grad
):
    seq_rows = tokens.shape[0]
    seq_count = lengths.shape[0]
    seq_len = seq_rows // seq_count
    position = jnp.arange(seq_rows, dtype=jnp.int32)
    slot_length = jnp.repeat(lengths, seq_len)
    is_valid = (position % seq_len < slot_length).astype(jnp.float32)[:, None]
    block_rows = min(512, seq_len)
    scaling = float(HD) ** (-0.5)
    gathered = (
        lax.all_gather(w_query, "batch", axis=0, tiled=True),
        lax.all_gather(w_key, "batch", axis=0, tiled=True),
        lax.all_gather(w_value, "batch", axis=0, tiled=True),
        lax.all_gather(w_out, "batch", axis=1, tiled=True),
        lax.all_gather(w_up, "batch", axis=0, tiled=True),
        lax.all_gather(w_down, "batch", axis=1, tiled=True),
        lax.all_gather(norm_gain, "batch", axis=1, tiled=True),
        lax.all_gather(norm_shift, "batch", axis=1, tiled=True),
    )
    full_query, full_key, full_value, full_out, full_up, full_down, gain_full, shift_full = gathered
    gain_rows = gain_full.astype(jnp.float32)
    shift_rows = shift_full.astype(jnp.float32)
    head_count = full_query.shape[1] // HD

    def per_sequence(values):
        return values.reshape(seq_count, seq_len, head_count, HD)

    inputs = tokens.astype(jnp.float32)
    normed, scaled_one, inverse_one = normalize_keep(inputs, gain_rows[0], shift_rows[0])
    normed_low = normed.astype(jnp.bfloat16)
    queries = (
        multiply(normed_low, full_query).astype(jnp.bfloat16).reshape(seq_rows, head_count, HD)
    )
    key_rows = multiply(normed_low, full_key).astype(jnp.bfloat16).reshape(seq_rows, head_count, HD)
    value_rows = (
        multiply(normed_low, full_value).astype(jnp.bfloat16).reshape(seq_rows, head_count, HD)
    )

    def forward_one(items):
        return attend_forward(items[0], items[1], items[2], items[3], block_rows, scaling)

    mixed_heads, log_sums = lax.map(
        forward_one,
        (per_sequence(queries), per_sequence(key_rows), per_sequence(value_rows), lengths),
    )
    mixed_low = mixed_heads.reshape(seq_rows, head_count * HD).astype(jnp.bfloat16)
    attn_partial = multiply(mixed_low, full_out)
    hidden = inputs + lax.psum(attn_partial, "tensor")
    normed_two, scaled_two, inverse_two = normalize_keep(hidden, gain_rows[1], shift_rows[1])
    normed_two_low = normed_two.astype(jnp.bfloat16)
    up_proj = multiply(normed_two_low, full_up)
    active_full, gelu_pull = jax.vjp(gelu_tanh, up_proj)
    active = active_full.astype(jnp.bfloat16)
    down_partial = multiply(active, full_down)
    branch = lax.psum(down_partial.astype(jnp.bfloat16), "tensor").astype(jnp.float32)
    out_rows = ((hidden + branch) * is_valid).astype(jnp.bfloat16)
    grad_rows = out_grad * is_valid.astype(jnp.bfloat16)
    grad_down = inner_rows(active, grad_rows)
    grad_active = outer_cols(grad_rows, full_down)
    grad_upper = gelu_pull(grad_active)[0].astype(jnp.bfloat16)
    grad_up = inner_rows(normed_two_low, grad_upper)
    mid_partial = outer_cols(grad_upper, full_up)
    grad_normed_two = lax.psum(mid_partial, "tensor")
    grad_from_two, gain_two, shift_two = normalize_back(
        grad_normed_two, scaled_two, inverse_two, gain_rows[1]
    )
    grad_hidden = grad_rows.astype(jnp.float32) + grad_from_two
    grad_attn = grad_hidden.astype(jnp.bfloat16)
    grad_out = inner_rows(mixed_low, grad_attn)
    grad_mixed = (
        outer_cols(grad_attn, full_out).astype(jnp.bfloat16).reshape(seq_rows, head_count, HD)
    )

    def backward_one(items):
        return attend_back(
            items[0], items[1], items[2], items[3], items[4], items[5], block_rows, scaling
        )

    grad_queries, grad_keys, grad_values = lax.map(
        backward_one,
        (
            per_sequence(queries),
            per_sequence(key_rows),
            per_sequence(value_rows),
            per_sequence(grad_mixed),
            log_sums,
            lengths,
        ),
    )
    queries_low = grad_queries.astype(jnp.bfloat16).reshape(seq_rows, head_count * HD)
    keys_low = grad_keys.astype(jnp.bfloat16).reshape(seq_rows, head_count * HD)
    values_low = grad_values.astype(jnp.bfloat16).reshape(seq_rows, head_count * HD)
    grad_query = inner_rows(normed_low, queries_low)
    grad_key = inner_rows(normed_low, keys_low)
    grad_value = inner_rows(normed_low, values_low)
    partial_in = (
        outer_cols(queries_low, full_query)
        + outer_cols(keys_low, full_key)
        + outer_cols(values_low, full_value)
    )
    grad_normed = lax.psum(partial_in.astype(jnp.bfloat16), "tensor").astype(jnp.float32)
    grad_from_one, gain_one, shift_one = normalize_back(
        grad_normed, scaled_one, inverse_one, gain_rows[0]
    )
    grad_input = (grad_hidden + grad_from_one).astype(jnp.bfloat16)
    gain_pair = jnp.stack([gain_one, gain_two])
    shift_pair = jnp.stack([shift_one, shift_two])
    everything = (
        summed_on_arrival(grad_query.astype(jnp.bfloat16), "batch", 0),
        summed_on_arrival(grad_key.astype(jnp.bfloat16), "batch", 0),
        summed_on_arrival(grad_value.astype(jnp.bfloat16), "batch", 0),
        summed_on_arrival(grad_out.astype(jnp.bfloat16), "batch", 1),
        summed_on_arrival(grad_up.astype(jnp.bfloat16), "batch", 0),
        summed_on_arrival(grad_down.astype(jnp.bfloat16), "batch", 1),
        summed_on_arrival(gain_pair.astype(jnp.bfloat16), "batch", 1),
        summed_on_arrival(shift_pair.astype(jnp.bfloat16), "batch", 1),
    )
    (
        shard_query,
        shard_key,
        shard_value,
        shard_out,
        shard_up,
        shard_down,
        shard_gain,
        shard_shift,
    ) = everything
    return (
        out_rows,
        grad_input,
        shard_query,
        shard_key,
        shard_value,
        shard_out,
        shard_up,
        shard_down,
        shard_gain,
        shard_shift,
    )


def solution(mesh):
    in_specs = (
        P("batch", None),
        P("batch"),
        P("batch", "tensor"),
        P("batch", "tensor"),
        P("batch", "tensor"),
        P("tensor", "batch"),
        P("batch", "tensor"),
        P("tensor", "batch"),
        P(None, "batch"),
        P(None, "batch"),
        P("batch", None),
    )
    out_specs = (
        P("batch", None),
        P("batch", None),
        P("batch", "tensor"),
        P("batch", "tensor"),
        P("batch", "tensor"),
        P("tensor", "batch"),
        P("batch", "tensor"),
        P("tensor", "batch"),
        P(None, "batch"),
        P(None, "batch"),
    )
    return jax.shard_map(
        per_device, mesh=mesh, in_specs=in_specs, out_specs=out_specs, check_vma=False
    )
```

profile of v0, /device:TPU:0, one launch (start us, length us, event | category | flops | bytes accessed | tf_op | source)
XLA Modules:
  0.0 747.1 jit_solution(5650384383720290563)
XLA Ops:
  9.3 22.3 %all-gather = bf16[8,96,2]{1,2,0:T(2,128)(2,1)S(1)} all-gather(bf16[1,96,2]{1,2,0:T(2,128)(2,1)} %bitcast.189), channel_id=1, replica_groups=mesh['batch'=8,'tensor'=4] {'batch'}, dimensions={0}, use_global_device_ids=true | all-gather | bytes 3456 | tf_op jit(solution)/shard_map/all_gather | solution.py:170
  32.3 16.4 %all-gather.1 = bf16[8,96,2]{1,2,0:T(2,128)(2,1)S(1)} all-gather(bf16[1,96,2]{1,2,0:T(2,128)(2,1)} %bitcast.190), channel_id=1, replica_groups=mesh['batch'=8,'tensor'=4] {'batch'}, dimensions={0}, use_global_device_ids=true | all-gather | bytes 3456 | tf_op jit(solution)/shard_map/all_gather | solution.py:171
  54.0 31.0 %all_gather.28 = bf16[768,192]{1,0:T(8,128)(2,1)S(1)} all-gather(bf16[96,192]{1,0:T(8,128)(2,1)S(1)} %copy-done.50), channel_id=1, replica_groups=mesh['batch'=8,'tensor'=4] {'batch'}, dimensions={0}, use_global_device_ids=true | all-gather | bytes 331776 | tf_op jit(solution)/shard_map/all_gather | solution.py:165
  88.7 31.2 %all_gather.26 = bf16[768,192]{1,0:T(8,128)(2,1)S(1)} all-gather(bf16[96,192]{1,0:T(8,128)(2,1)S(1)} %copy-done.51), channel_id=1, replica_groups=mesh['batch'=8,'tensor'=4] {'batch'}, dimensions={0}, use_global_device_ids=true | all-gather | bytes 331776 | tf_op jit(solution)/shard_map/all_gather | solution.py:166
  125.1 31.3 %all_gather.29 = bf16[192,768]{0,1:T(8,128)(2,1)S(1)} all-gather(bf16[192,96]{0,1:T(8,128)(2,1)} %copy.70), channel_id=1, replica_groups=mesh['batch'=8,'tensor'=4] {'batch'}, dimensions={1}, use_global_device_ids=true | all-gather | bytes 331776 | tf_op jit(solution)/shard_map/all_gather | solution.py:167
  156.4 31.2 %all_gather.27 = bf16[768,192]{1,0:T(8,128)(2,1)S(1)} all-gather(bf16[96,192]{1,0:T(8,128)(2,1)} %param.29), channel_id=1, replica_groups=mesh['batch'=8,'tensor'=4] {'batch'}, dimensions={0}, use_global_device_ids=true | all-gather | bytes 331776 | tf_op jit(solution)/shard_map/all_gather | solution.py:164
  199.6 4.2 fusion.151
  206.4 3.2 fusion.4
  210.1 6.4 fusion.150
  222.0 90.3 %all-reduce.7.cloned.1.call-done = f32[1536,768]{1,0:T(8,128)} async-done(((f32[1536,768]{1,0:T(8,128)}), f32[1536,768]{1,0:T(8,128)}) %all-reduce.7.cloned.1.call-update) | async-done | bytes 4718608 | tf_op jit(solution)/shard_map/psum | solution.py:201
  319.8 6.2 fusion.203
  325.9 7.1 fusion.31
  334.5 4.2 fusion.204
  341.3 6.8 fusion.107
  348.2 5.6 all-to-all-start.5
  353.8 5.6 convolution_convert_fusion.5
  359.4 6.8 convolution_convert_fusion
  366.2 66.7 %all-reduce.9.cloned.1.call-done = f32[1536,768]{1,0:T(8,128)} async-done(((f32[1536,768]{1,0:T(8,128)}), f32[1536,768]{1,0:T(8,128)}) %all-reduce.9.cloned.1.call-update) | async-done | bytes 4718608 | tf_op jit(solution)/shard_map/psum | solution.py:216
  433.0 5.6 multiply_reduce_fusion.2
  438.8 4.4 multiply_add_fusion
  450.7 9.7 %fusion.128 = f32[512,3,64]{0,2,1:T(8,128)} fusion(bf16[512,3,64]{0,2,1:T(8,128)(2,1)} %bitcast.178, f32[3,512,512]{1,2,0:T(8,128)} %fusion.205, f32[3,512,512]{1,2,0:T(8,128)} %copy-done.18, f32[3,512]{1,0:T(4,128)S(1)} %copy-done.61, pred[512,512]{0,1:T(8,128)(4,1)} %copy-done.28), kind=kOutput, calls=%fused_computation.130 | convolution fusion | flops 114821120 | bytes 7149568 | tf_op jit(solution)/shard_map/while/body/eval_jaxpr/hqk,qhd->khd/dot_general | solution.py:134
  460.4 4.8 fusion.206
  465.2 5.1 fusion.207
  470.3 20.3 %fusion.145 = bf16[3,64,512]{2,1,0:T(8,128)(2,1)} fusion(bf16[1024,3,64]{0,2,1:T(8,128)(2,1)} %bitcast.171, f32[3,512,1024]{2,1,0:T(8,128)} %fusion.206, f32[3,512,1024]{2,1,0:T(8,128)} %copy-done.7, f32[3,512]{1,0:T(4,128)} %log_add_fusion.1, pred[512,1024]{1,0:T(8,128)(4,1)} %copy-done.23), kind=kOutput, calls=%fused_computation.139 | convolution fusion | flops 229739008 | bytes 13703168 | tf_op jit(solution)/shard_map/while/body/eval_jaxpr/hqk,khd->qhd/dot_general | solution.py:129
  493.9 9.8 %fusion.141 = bf16[3,64,512]{2,1,0:T(8,128)(2,1)} fusion(bf16[512,3,64]{0,2,1:T(8,128)(2,1)} %bitcast.179, f32[3,512,512]{1,2,0:T(8,128)} %fusion.205, f32[3,512,512]{1,2,0:T(8,128)} %copy-done.18, f32[3,512]{1,0:T(4,128)S(1)} %copy-done.61, pred[512,512]{0,1:T(8,128)(4,1)} %copy-done.28), kind=kOutput, calls=%fused_computation.137 | convolution fusion | flops 114919424 | bytes 6952960 | tf_op jit(solution)/shard_map/while/body/eval_jaxpr/hqk,khd->qhd/dot_general | solution.py:129
  503.7 26.5 %fusion.138 = bf16[3,64,512]{2,1,0:T(8,128)(2,1)} fusion(bf16[1536,3,64]{0,2,1:T(8,128)(2,1)S(1)} %bitcast.154, f32[3,512,1536]{2,1,0:T(8,128)} %fusion.207, f32[3,512,1536]{2,1,0:T(8,128)} %copy-done.6, f32[3,512]{1,0:T(4,128)S(1)} %copy-done.62, pred[512,1536]{1,0:T(8,128)(4,1)} %copy-done.16), kind=kOutput, calls=%fused_computation.136 | convolution fusion | flops 344558592 | bytes 20453376 | tf_op jit(solution)/shard_map/while/body/eval_jaxpr/hqk,khd->qhd/dot_general | solution.py:129
  530.3 20.4 %fusion.119 = f32[1536,3,64]{0,2,1:T(8,128)} fusion(f32[1536,3,64]{0,2,1:T(8,128)} %scatter-add.14, bf16[512,3,64]{0,2,1:T(8,128)(2,1)} %bitcast.176, f32[3,512,1024]{2,1,0:T(8,128)} %fusion.206, f32[3,512,1024]{2,1,0:T(8,128)} %copy-done.7, f32[3,512]{1,0:T(4,128)S(1)} %copy-done.63, pred[512,1024]{1,0:T(8,128)(4,1)} %copy-done.23), kind=kOutput, calls=%fused_computation.123 | convolution fusion | flops 229837312 | bytes 28000256 | tf_op jit(solution)/shard_map/while/body/eval_jaxpr/hqk,qhd->khd/dot_general | solution.py:134
  550.7 28.0 %fusion.76 = bf16[1536,3,64]{0,2,1:T(8,128)(2,1)} fusion(f32[1536,3,64]{0,2,1:T(8,128)} %fusion.119, bf16[512,3,64]{0,2,1:T(8,128)(2,1)S(1)} %bitcast.174, f32[3,512,1536]{2,1,0:T(8,128)} %fusion.207, f32[3,512,1536]{2,1,0:T(8,128)} %copy-done.6, f32[3,512]{1,0:T(4,128)S(1)} %copy-done.62, pred[512,1536]{1,0:T(8,128)(4,1)} %copy-done.16), kind=kOutput, calls=%fused_computation.94 | convolution fusion | flops 345050112 | bytes 21633024 | tf_op jit(solution)/shard_map/while/body/eval_jaxpr/hqk,qhd->khd/dot_general | solution.py:134
  578.7 4.1 fusion.208
  582.8 7.9 %fusion.125 = f32[1536,3,64]{0,2,1:T(8,128)} fusion(f32[1536,3,64]{0,2,1:T(8,128)} %scatter-add.16, bf16[512,3,64]{0,2,1:T(8,128)(2,1)S(1)} %bitcast.166, f32[3,512]{1,0:T(4,128)S(1)} %copy-done.63, pred[512,1024]{1,0:T(8,128)(4,1)S(1)} %copy-done.24, f32[3,512,1024]{2,1,0:T(8,128)} %copy-done.7), kind=kOutput, calls=%fused_computation.125 | convolution fusion | flops 212533248 | bytes 8591360 | tf_op jit(solution)/shard_map/while/body/eval_jaxpr/hqk,qhd->khd/dot_general | solution.py:142
  590.7 5.5 all-to-all-start.4
  598.6 8.8 %fusion.73 = bf16[1536,3,64]{0,2,1:T(8,128)(2,1)S(1)} fusion(f32[1536,3,64]{0,2,1:T(8,128)} %fusion.125, bf16[512,3,64]{0,2,1:T(8,128)(2,1)S(1)} %bitcast.160, f32[3,512]{1,0:T(4,128)S(1)} %copy-done.62, f32[3,512,1536]{2,1,0:T(8,128)} %copy-done.6, pred[512,1536]{1,0:T(8,128)(4,1)S(1)} %copy-done.17), kind=kOutput, calls=%fused_computation.93 | convolution fusion | flops 319094784 | bytes 12195840 | tf_op jit(solution)/shard_map/while/body/eval_jaxpr/hqk,qhd->khd/dot_general | solution.py:142
  616.9 7.9 %all-to-all-done.4 = bf16[8,96,768]{2,1,0:T(8,128)(2,1)} async-done(((bf16[8,96,768]{2,1,0:T(8,128)(2,1)}), bf16[8,96,768]{2,1,0:T(8,128)(2,1)}, u32[]{:S(2)}, u32[]{:S(2)}) %all-to-all-start.4) | async-done | bytes 1179680 | tf_op jit(solution)/shard_map/all_to_all | solution.py:20
  624.7 3.6 all-to-all-start.2
  628.3 3.4 convolution_convert_fusion.8
  635.7 4.5 all-to-all-done.2
  640.2 4.1 all-to-all-start
  644.9 3.2 convolution_convert_fusion.7
  652.1 3.7 all-to-all-done
  655.8 4.1 all-to-all-start.1
  662.0 3.9 convolution_convert_fusion.9
  670.6 3.7 all-to-all-start.3
  686.1 19.5 %all-reduce.11.cloned.1.call-done = (bf16[1536,768]{1,0:T(8,128)(2,1)}, bf16[1536,768]{1,0:T(8,128)(2,1)}) async-done(((bf16[1536,768]{1,0:T(8,128)(2,1)}, bf16[1536,768]{1,0:T(8,128)(2,1)}), (bf16[1536,768]{1,0:T(8,128)(2,1)}, bf16[1536,768]{1,0:T(8,128)(2,1)})) %all-reduce.11.cloned.1.call-update) | async-done | bytes 4718608 | tf_op jit(solution)/shard_map/psum | solution.py:208
  705.6 3.8 fusion.24
  712.1 5.5 all-to-all-start.7
  717.8 5.2 multiply_convert_fusion.4
  726.8 6.0 all-to-all-start.6
  733.3 5.9 all-to-all-done.6
  (251 shorter events, 104.8 us)
Async XLA Ops:
  8.0 77.0 %copy-start.1 = (bf16[1536,768]{1,0:T(8,128)(2,1)S(1)}, bf16[1536,768]{1,0:T(8,128)(2,1)}, u32[]{:S(2)}) copy-start(bf16[1536,768]{1,0:T(8,128)(2,1)} %param.27) | copy-start | bytes 7077892
  8.0 45.9 %copy-start.50 = (bf16[96,192]{1,0:T(8,128)(2,1)S(1)}, bf16[96,192]{1,0:T(8,128)(2,1)}, u32[]{:S(2)}) copy-start(bf16[96,192]{1,0:T(8,128)(2,1)} %param.30) | copy-start | bytes 110596
  8.0 304.3 %all-reduce.7.cloned.1.call-start = ((), (), s32[]{:S(2)}) async-start(), calls=%async_computation.8 | async-start | bytes 9437184 | tf_op jit(solution)/shard_map/psum | solution.py:201
  32.3 53.9 %copy-start.46 = (f32[768]{0:T(1024)}, f32[768]{0:T(1024)S(1)}, u32[]{:S(2)}) copy-start(f32[768]{0:T(1024)S(1)} %get-tuple-element.217) | copy-start | bytes 9220
  51.4 35.7 %copy-start.37 = (f32[1536]{0:T(1024)}, f32[1536]{0:T(1024)S(1)}, u32[]{:S(2)}) copy-start(f32[1536]{0:T(1024)S(1)} %broadcast_multiply_fusion.5) | copy-start | bytes 18436
  53.9 31.0 %copy-start.44 = (f32[1536]{0:T(1024)}, f32[1536]{0:T(1024)S(1)}, u32[]{:S(2)}) copy-start(f32[1536]{0:T(1024)S(1)} %add_rsqrt_fusion.1) | copy-start | bytes 18436
  86.2 36.1 %copy-start.3 = (bf16[1536,768]{1,0:T(8,128)(2,1)}, bf16[1536,768]{1,0:T(8,128)(2,1)S(1)}, u32[]{:S(2)}) copy-start(bf16[1536,768]{1,0:T(8,128)(2,1)S(1)} %fusion.17) | copy-start | bytes 7077892
  87.1 116.7 %copy-start.21 = (bf16[1536,192]{0,1:T(8,128)(2,1)}, bf16[1536,192]{0,1:T(8,128)(2,1)S(1)}, u32[]{:S(2)}) copy-start(bf16[1536,192]{0,1:T(8,128)(2,1)S(1)} %convolution_convert_fusion.2) | copy-start | bytes 1769476
  125.1 66.2 %copy-start.43 = (bf16[512,192]{0,1:T(8,128)(2,1)S(1)}, bf16[512,192]{0,1:T(8,128)(2,1)}, u32[]{:S(2)}) copy-start(bf16[512,192]{0,1:T(8,128)(2,1)} %slice.337) | copy-start | bytes 589828
  156.4 60.2 %copy-start.14 = (bf16[192,768]{0,1:T(8,128)(2,1)}, bf16[192,768]{0,1:T(8,128)(2,1)S(1)}, u32[]{:S(2)}) copy-start(bf16[192,768]{0,1:T(8,128)(2,1)S(1)} %all_gather.29) | copy-start | bytes 884740
  190.4 13.5 %copy-start.39 = (bf16[512,192]{0,1:T(8,128)(2,1)}, bf16[512,192]{0,1:T(8,128)(2,1)S(1)}, u32[]{:S(2)}) copy-start(bf16[512,192]{0,1:T(8,128)(2,1)S(1)} %get-tuple-element.228) | copy-start | bytes 589828
  191.2 18.4 %copy-start.16 = (pred[512,1536]{1,0:T(8,128)(4,1)}, pred[512,1536]{1,0:T(8,128)(4,1)S(1)}, u32[]{:S(2)}) copy-start(pred[512,1536]{1,0:T(8,128)(4,1)S(1)} %fusion.50) | copy-start | bytes 2359300
  197.4 6.4 copy-start.7
  197.4 6.4 copy-start.52
  209.6 6.9 copy-start.55
  219.6 100.2 %all-gather.5.cloned.1.call-start = ((), (), s32[]{:S(2)}) async-start(), calls=%async_computation.9 | async-start | bytes 1327104 | tf_op jit(solution)/shard_map/all_gather | solution.py:168
  220.1 105.8 %all-gather.7.cloned.1.call-start = ((), (), s32[]{:S(2)}) async-start(), calls=%async_computation.10 | async-start | bytes 1327104 | tf_op jit(solution)/shard_map/all_gather | solution.py:169
  220.7 212.2 %all-reduce.9.cloned.1.call-start = ((), (), s32[]{:S(2)}) async-start(), calls=%async_computation.11 | async-start | bytes 9437184 | tf_op jit(solution)/shard_map/psum | solution.py:216
  325.9 8.5 %copy-start.66 = (bf16[768,768]{1,0:T(8,128)(2,1)S(1)}, bf16[768,768]{1,0:T(8,128)(2,1)}, u32[]{:S(2)}) copy-start(bf16[768,768]{1,0:T(8,128)(2,1)} %all-gather.5.cloned.1.call-done) | copy-start | bytes 3538948
  348.2 242.5 %all-to-all-start.5 = ((bf16[8,768,96]{1,2,0:T(8,128)(2,1)}), bf16[8,768,96]{1,2,0:T(8,128)(2,1)}, u32[]{:S(2)}, u32[]{:S(2)}) async-start(bf16[8,768,96]{1,2,0:T(8,128)(2,1)} %bitcast.158), calls=%async_computation.5 | async-start | bytes 2359296 | tf_op jit(solution)/shard_map/all_to_all | solution.py:20
  353.8 5.6 copy-start.65
  432.9 5.6 copy-start.5
  432.9 5.9 copy-start.20
  432.9 5.9 copy-start.49
  433.0 5.9 copy-start.58
  470.3 22.5 %copy-start.36 = (f32[512,3,64]{0,2,1:T(8,128)S(1)}, f32[512,3,64]{0,2,1:T(8,128)}, u32[]{:S(2)}) copy-start(f32[512,3,64]{0,2,1:T(8,128)} %fusion.128) | copy-start | bytes 1179652
  493.9 9.8 %copy-start.22 = (bf16[1536,192]{0,1:T(8,128)(2,1)S(1)}, bf16[1536,192]{0,1:T(8,128)(2,1)}, u32[]{:S(2)}) copy-start(bf16[1536,192]{0,1:T(8,128)(2,1)} %copy-done.21) | copy-start | bytes 1769476
  493.9 9.8 %copy-start.62 = (f32[3,512]{1,0:T(4,128)S(1)}, f32[3,512]{1,0:T(4,128)}, u32[]{:S(2)}) copy-start(f32[3,512]{1,0:T(4,128)} %log_add_fusion) | copy-start | bytes 18436
  503.7 26.6 %copy-start.63 = (f32[3,512]{1,0:T(4,128)S(1)}, f32[3,512]{1,0:T(4,128)}, u32[]{:S(2)}) copy-start(f32[3,512]{1,0:T(4,128)} %log_add_fusion.1) | copy-start | bytes 18436
  530.3 20.4 %copy-start.40 = (bf16[512,192]{0,1:T(8,128)(2,1)S(1)}, bf16[512,192]{0,1:T(8,128)(2,1)}, u32[]{:S(2)}) copy-start(bf16[512,192]{0,1:T(8,128)(2,1)} %copy-done.39) | copy-start | bytes 589828
  550.7 28.0 %copy-start.13 = (bf16[768,192]{1,0:T(8,128)(2,1)S(1)}, bf16[768,192]{1,0:T(8,128)(2,1)}, u32[]{:S(2)}) copy-start(bf16[768,192]{1,0:T(8,128)(2,1)} %copy-done.12) | copy-start | bytes 884740
  582.8 13.6 %copy-start.11 = (bf16[768,192]{1,0:T(8,128)(2,1)S(1)}, bf16[768,192]{1,0:T(8,128)(2,1)}, u32[]{:S(2)}) copy-start(bf16[768,192]{1,0:T(8,128)(2,1)} %copy-done.10) | copy-start | bytes 884740
  590.7 34.0 %all-to-all-start.4 = ((bf16[8,96,768]{2,1,0:T(8,128)(2,1)}), bf16[8,96,768]{2,1,0:T(8,128)(2,1)}, u32[]{:S(2)}, u32[]{:S(2)}) async-start(bf16[8,96,768]{2,1,0:T(8,128)(2,1)} %bitcast.157), calls=%async_computation.4 | async-start | bytes 2359296 | tf_op jit(solution)/shard_map/all_to_all | solution.py:20
  596.2 109.3 %all-reduce.11.cloned.1.call-start = ((), (), s32[]{:S(2)}) async-start(), calls=%async_computation.12 | async-start | bytes 9437184 | tf_op jit(solution)/shard_map/psum | solution.py:208
  596.5 11.8 %slice-start.2 = ((s8[4718592]{0:T(1024)(128)(4,1)}), s8[4194304]{0:T(1024)(128)(4,1)S(1)}, s32[]{:S(2)}) async-start(s8[4718592]{0:T(1024)(128)(4,1)} %bitcast.147), calls=%async_computation.15 | async-start | bytes 8388608
  598.6 9.6 %slice-start.3 = ((s8[4718592]{0:T(1024)(128)(4,1)}), s8[524288]{0:T(1024)(128)(4,1)S(1)}, s32[]{:S(2)}) async-start(s8[4718592]{0:T(1024)(128)(4,1)} %bitcast.147), calls=%async_computation.16 | async-start | bytes 1048576
  598.6 9.6 %copy-start.9 = (bf16[768,192]{1,0:T(8,128)(2,1)S(1)}, bf16[768,192]{1,0:T(8,128)(2,1)}, u32[]{:S(2)}) copy-start(bf16[768,192]{1,0:T(8,128)(2,1)} %copy-done.8) | copy-start | bytes 884740
  624.7 15.5 %all-to-all-start.2 = ((bf16[8,96,192]{1,2,0:T(8,128)(2,1)}), bf16[8,96,192]{1,2,0:T(8,128)(2,1)S(1)}, u32[]{:S(2)}, u32[]{:S(2)}) async-start(bf16[8,96,192]{1,2,0:T(8,128)(2,1)} %copy.78), calls=%async_computation.2 | async-start | bytes 786432 | tf_op jit(solution)/shard_map/all_to_all | solution.py:20
  640.2 15.6 %all-to-all-start = ((bf16[8,96,192]{1,2,0:T(8,128)(2,1)}), bf16[8,96,192]{1,2,0:T(8,128)(2,1)}, u32[]{:S(2)}, u32[]{:S(2)}) async-start(bf16[8,96,192]{1,2,0:T(8,128)(2,1)} %copy.74), calls=%async_computation | async-start | bytes 786432 | tf_op jit(solution)/shard_map/all_to_all | solution.py:20
  655.8 14.9 %all-to-all-start.1 = ((bf16[8,96,192]{1,2,0:T(8,128)(2,1)}), bf16[8,96,192]{1,2,0:T(8,128)(2,1)}, u32[]{:S(2)}, u32[]{:S(2)}) async-start(bf16[8,96,192]{1,2,0:T(8,128)(2,1)} %copy.76), calls=%async_computation.1 | async-start | bytes 786432 | tf_op jit(solution)/shard_map/all_to_all | solution.py:20
  662.0 43.5 %copy-start.38 = (f32[1536]{0:T(1024)S(1)}, f32[1536]{0:T(1024)}, u32[]{:S(2)}) copy-start(f32[1536]{0:T(1024)} %copy-done.37) | copy-start | bytes 18436
  662.0 43.6 %copy-start.45 = (f32[1536]{0:T(1024)S(1)}, f32[1536]{0:T(1024)}, u32[]{:S(2)}) copy-start(f32[1536]{0:T(1024)} %copy-done.44) | copy-start | bytes 18436
  665.9 39.6 %copy-start.47 = (f32[768]{0:T(1024)S(1)}, f32[768]{0:T(1024)}, u32[]{:S(2)}) copy-start(f32[768]{0:T(1024)} %copy-done.46) | copy-start | bytes 9220
  670.6 14.8 %all-to-all-start.3 = ((bf16[8,192,96]{2,1,0:T(8,128)(2,1)}), bf16[8,192,96]{2,1,0:T(8,128)(2,1)S(1)}, u32[]{:S(2)}, u32[]{:S(2)}) async-start(bf16[8,192,96]{2,1,0:T(8,128)(2,1)} %bitcast.139), calls=%async_computation.3 | async-start | bytes 786432 | tf_op jit(solution)/shard_map/all_to_all | solution.py:20
  678.1 39.6 %copy-start.56 = (f32[1536]{0:T(1024)S(1)}, f32[1536]{0:T(1024)}, u32[]{:S(2)}) copy-start(f32[1536]{0:T(1024)} %fusion.154) | copy-start | bytes 18436
  705.6 17.4 %slice-start = ((s8[4718592]{0:T(1024)(128)(4,1)}), s8[524288]{0:T(1024)(128)(4,1)S(1)}, s32[]{:S(2)}) async-start(s8[4718592]{0:T(1024)(128)(4,1)} %bitcast.145), calls=%async_computation.13 | async-start | bytes 1048576
  712.1 14.6 %all-to-all-start.7 = ((bf16[8,2,96]{2,1,0:T(2,128)(2,1)}), bf16[8,2,96]{2,1,0:T(2,128)(2,1)S(1)}, u32[]{:S(2)}, u32[]{:S(2)}) async-start(bf16[8,2,96]{2,1,0:T(2,128)(2,1)} %copy.82), calls=%async_computation.7 | async-start | bytes 8192 | tf_op jit(solution)/shard_map/all_to_all | solution.py:20
  726.8 12.5 %all-to-all-start.6 = ((bf16[8,2,96]{2,1,0:T(2,128)(2,1)}), bf16[8,2,96]{2,1,0:T(2,128)(2,1)S(1)}, u32[]{:S(2)}, u32[]{:S(2)}) async-start(bf16[8,2,96]{2,1,0:T(2,128)(2,1)} %copy.81), calls=%async_computation.6 | async-start | bytes 8192 | tf_op jit(solution)/shard_map/all_to_all | solution.py:20
  (37 other events, 120.4 us)
Sparse Core Ops, SparseCore 0:
  219.7 92.5 all-reduce.6
  338.8 94.1 all-reduce.8
  610.7 94.8 all-reduce.10
Sparse Core Ops, SparseCore 1:
  222.2 39.9 all-gather.4
  264.2 40.0 all-gather.6
where the time goes:
time: 757 us; the launch traced here: 747 us
  matrix products  231 us (31%)
  waiting for transfers between devices  205 us (27%)
  blocking collectives  163 us (22%)
  other arithmetic  57.9 us (8%)
  starting transfers between devices  38.5 us (5%)
  local copies, waits for them, and re-layouts  34.2 us (5%)
  between operations  17 us (2%)
    psum x1, waiting for transfers between devices, per_device(): hidden = inputs + lax.psum(attn_partial, 'tensor')  90.3 us
    psum x1, waiting for transfers between devices, per_device(): grad_normed_two = lax.psum(mid_partial, 'tensor')  66.7 us
    dot_general x3, matrix products, attend_back(): jnp.einsum('hqk,qhd->khd', grad_raw, queries[begin_row:end_row], preferre...  58.1 us
    dot_general x3, matrix products, attend_back(): jnp.einsum('hqk,khd->qhd', grad_raw, key_rows[:end_row], preferred_elemen...  56.6 us
    all_to_all x8, starting transfers between devices, summed_on_arrival(): lax.all_to_all(cut_along(value, dim, length), axis, 0, 0, tiled=True)  38.1 us
    all_gather x1, blocking collectives, per_device(): lax.all_gather(w_out, 'batch', axis=1, tiled=True)  31.3 us
    all_gather x1, blocking collectives, per_device(): lax.all_gather(w_value, 'batch', axis=0, tiled=True)  31.2 us
    all_gather x1, blocking collectives, per_device(): lax.all_gather(w_query, 'batch', axis=0, tiled=True)  31.2 us
  transfers between devices with their start and end apart: 13, of which 9 were waited for; matrix products, arithmetic and copies ran while one was open for 34% of the time, Pallas kernels for 0%

commit v1 on v0

v1 whole, which is shorter than its diff:
```python
import functools

import jax
import jax.numpy as jnp
from jax import lax
from jax.experimental import pallas as pl
from jax.experimental.pallas import tpu as pltpu
from jax.sharding import PartitionSpec as P

HD = 64
EPSILON = 1e-05
LOG2E = 1.4426950408889634
HUGE = 3e38
FAR = -1e30
LOW = jnp.bfloat16
WIDE = jnp.float32
LANES = 128


def multiply(left, right):
    return lax.dot_general(left, right, (((1,), (0,)), ((), ())), preferred_element_type=WIDE)


def outer_cols(left, right):
    return lax.dot_general(left, right, (((1,), (1,)), ((), ())), preferred_element_type=WIDE)


def inner_rows(left, right):
    return lax.dot_general(left, right, (((0,), (0,)), ((), ())), preferred_element_type=WIDE)


def whole():
    return pl.BlockSpec(memory_space=pltpu.VMEM)


def scalars():
    return pl.BlockSpec(memory_space=pltpu.SMEM)


def struct(shape, dtype):
    return jax.ShapeDtypeStruct(shape, dtype)


def swap(value, axis, bits):
    size = lax.axis_size(axis)
    return lax.ppermute(value, axis, [(i, i ^ bits) for i in range(size)])


def gather_batch(shard):
    size = lax.axis_size("batch")
    if size != 8:
        return lax.all_gather(shard, "batch", axis=0, tiled=True)
    rows = shard.shape[0]
    me = lax.axis_index("batch")
    pieces = {0: shard}
    for bits in (2, 4, 6):
        pieces[bits] = swap(shard, "batch", bits)
    for bits in (0, 2, 4, 6):
        pieces[bits + 1] = swap(pieces[bits], "batch", 1)
    full = jnp.zeros((size * rows, shard.shape[1]), shard.dtype)
    for bits, piece in pieces.items():
        full = lax.dynamic_update_slice(full, piece, ((me ^ bits) * rows, 0))
    return full


def scatter_batch(value):
    size = lax.axis_size("batch")
    parts = value.reshape(size, value.shape[0] // size, value.shape[1])
    parts = lax.all_to_all(parts, "batch", 0, 0, tiled=True)
    return jnp.sum(parts.astype(WIDE), axis=0)


def gather_tensor(piece):
    across = swap(piece, "tensor", 2)
    beside = swap(piece, "tensor", 1)
    both = swap(across, "tensor", 1)
    return piece, across, beside, both


def pair_sum(keep, send):
    mine = (keep.astype(WIDE) + swap(send, "tensor", 1).astype(WIDE)).astype(LOW)
    return mine, swap(mine, "tensor", 2)


def standardize(values):
    middle = jnp.mean(values, axis=-1, keepdims=True)
    centred = values - middle
    spread = jnp.mean(centred * centred, axis=-1, keepdims=True)
    inverse = lax.rsqrt(spread + EPSILON)
    return centred * inverse, inverse


def standardize_back(grad, scaled, inverse, gain):
    grad = grad * gain
    mean_grad = jnp.mean(grad, axis=-1, keepdims=True)
    mean_cross = jnp.mean(grad * scaled, axis=-1, keepdims=True)
    return inverse * (grad - mean_grad - scaled * mean_cross)


def project_kernel(tokens_ref, weights_ref, normed_ref, queries_ref, keys_ref, values_ref, rows_ref, *, width):
    first = (3 * width) // LANES * LANES
    offset = 3 * width - first

    @pl.when(pl.program_id(0) == 0)
    def _():
        columns = weights_ref[:, first : first + LANES].astype(WIDE)
        rows_ref[...] = jnp.transpose(columns)[offset : offset + 8, :]

    scaled, _ = standardize(tokens_ref[...].astype(WIDE))
    normed = (scaled * rows_ref[0:1, :] + rows_ref[2:3, :]).astype(LOW)
    normed_ref[...] = normed
    projected = multiply(normed, weights_ref[:, : 3 * width]).astype(LOW)
    queries_ref[...] = projected[:, :width]
    keys_ref[...] = projected[:, width : 2 * width]
    values_ref[...] = projected[:, 2 * width :]


def project(tokens, weights, width, block):
    count, depth = tokens.shape
    return pl.pallas_call(
        functools.partial(project_kernel, width=width),
        grid=(count // block,),
        in_specs=[pl.BlockSpec((block, depth), lambda i: (i, 0)), whole()],
        out_specs=(
            pl.BlockSpec((block, depth), lambda i: (i, 0)),
            pl.BlockSpec((block, width), lambda i: (i, 0)),
            pl.BlockSpec((block, width), lambda i: (i, 0)),
            pl.BlockSpec((block, width), lambda i: (i, 0)),
            pl.BlockSpec((8, depth), lambda i: (0, 0)),
        ),
        out_shape=(
            struct((count, depth), LOW),
            struct((count, width), LOW),
            struct((count, width), LOW),
            struct((count, width), LOW),
            struct((8, depth), WIDE),
        ),
        compiler_params=pltpu.CompilerParams(vmem_limit_bytes=24 << 20),
        name="project",
    )(tokens, weights)


def sign_of(scores):
    return jnp.minimum(jnp.maximum(scores * HUGE, -1.0), 1.0)


def attend_kernel(length_ref, q_ref, k_ref, v_ref, mixed_ref, sums_ref, *, begin, rows, block, heads, sure):
    length = length_ref[0]
    factor = LOG2E * HD**-0.5
    for i in range(rows // block):
        row0 = begin + i * block
        outs = []
        sums = []
        for h in range(heads):
            cols = slice(h * HD, (h + 1) * HD)
            q = q_ref[i * block : (i + 1) * block, cols]
            row = lax.broadcasted_iota(jnp.int32, (block, 1), 0) + row0
            key = lax.broadcasted_iota(jnp.int32, (block, block), 1) + row0
            near = outer_cols(q, k_ref[row0 : row0 + block, cols])
            near_size = jnp.where(key <= jnp.minimum(row, length - 1), jnp.abs(near) * factor, FAR)
            top = jnp.max(near_size, axis=1, keepdims=True)
            if row0 > 0:
                past = outer_cols(q, k_ref[:row0, cols])
                past_size = jnp.abs(past) * factor
                if row0 > sure:
                    past_key = lax.broadcasted_iota(jnp.int32, (block, row0), 1)
                    past_size = jnp.where(past_key < length, past_size, FAR)
                top = jnp.maximum(top, jnp.max(past_size, axis=1, keepdims=True))
                past_prob = jnp.exp2(past_size - top)
            near_prob = jnp.exp2(near_size - top)
            total = jnp.sum(near_prob, axis=1, keepdims=True)
            mixed = multiply((near_prob * sign_of(near)).astype(LOW), v_ref[row0 : row0 + block, cols])
            if row0 > 0:
                total = total + jnp.sum(past_prob, axis=1, keepdims=True)
                mixed = mixed + multiply((past_prob * sign_of(past)).astype(LOW), v_ref[:row0, cols])
            outs.append((mixed / total).astype(LOW))
            sums.append(top + jnp.log2(total))
        mixed_ref[i * block : (i + 1) * block, :] = jnp.concatenate(outs, axis=1)
        blank = jnp.zeros((block, LANES - heads), WIDE)
        sums_ref[i] = jnp.transpose(jnp.concatenate(sums + [blank], axis=1))[:8, :]


def attend(queries, keys, values, lengths, begin, rows, block, sure):
    width = keys.shape[1]
    heads = width // HD
    return pl.pallas_call(
        functools.partial(attend_kernel, begin=begin, rows=rows, block=block, heads=heads, sure=sure),
        in_specs=[scalars(), whole(), whole(), whole()],
        out_specs=(whole(), whole()),
        out_shape=(struct((rows, width), LOW), struct((rows // block, 8, block), WIDE)),
        compiler_params=pltpu.CompilerParams(vmem_limit_bytes=32 << 20),
        name="attend_forward",
    )(lengths, queries, keys, values)


def attend_back_kernel(
    length_ref, q_ref, k_ref, v_ref, g_ref, mixed_ref, sums_ref, dq_ref, dk_ref, dv_ref, delta, dq_turned, *, rows, block, heads, sure
):
    length = length_ref[0]
    scaling = HD**-0.5
    factor = LOG2E * scaling
    blocks = rows // block
    for i in range(blocks):
        part = slice(i * block, (i + 1) * block)
        both = g_ref[part, :].astype(WIDE) * mixed_ref[part, :].astype(WIDE)
        cols = [jnp.sum(both[:, h * HD : (h + 1) * HD], axis=1, keepdims=True) for h in range(heads)]
        blank = jnp.zeros((block, LANES - heads), WIDE)
        delta[i] = jnp.transpose(jnp.concatenate(cols + [blank], axis=1))[:8, :]
    dq_turned[...] = jnp.zeros_like(dq_turned)
    for j in range(blocks):
        key0 = j * block

        def body(i, carry, near):
            row0 = i * block if near else pl.multiple_of(i * block, block)
            dks, dvs = [], []
            for h in range(heads):
                cols = slice(h * HD, (h + 1) * HD)
                q = q_ref[pl.ds(row0, block), cols]
                g = g_ref[pl.ds(row0, block), cols]
                k = k_ref[key0 : key0 + block, cols]
                v = v_ref[key0 : key0 + block, cols]
                scores = outer_cols(k, q)
                grad_weights = outer_cols(v, g)
                size = jnp.abs(scores) * factor - sums_ref[i, h : h + 1, :]
                key = lax.broadcasted_iota(jnp.int32, (block, block), 0) + key0
                if near:
                    row = lax.broadcasted_iota(jnp.int32, (1, block), 1) + row0
                    size = jnp.where(key <= jnp.minimum(row, length - 1), size, FAR)
                elif key0 + block > sure:
                    size = jnp.where(key < length, size, FAR)
                sign = sign_of(scores)
                weights = jnp.exp2(size) * sign
                raw = (weights * (sign * grad_weights - delta[i, h : h + 1, :])).astype(LOW)
                dvs.append(carry[1][h] + multiply(weights.astype(LOW), g))
                dks.append(carry[0][h] + multiply(raw, q))
                dq_turned[cols, pl.ds(row0, block)] += inner_rows(k, raw)
            return tuple(dks), tuple(dvs)

        blank = tuple(jnp.zeros((block, HD), WIDE) for _ in range(heads))
        carry = body(j, (blank, blank), True)
        if j + 1 < blocks:
            carry = lax.fori_loop(j + 1, blocks, lambda i, kept: body(i, kept, False), carry)
        dks, dvs = carry
        part = slice(key0, key0 + block)
        dk_ref[part, :] = jnp.concatenate([dk * scaling for dk in dks], axis=1).astype(LOW)
        dv_ref[part, :] = jnp.concatenate(dvs, axis=1).astype(LOW)
    for i in range(blocks):
        part = slice(i * block, (i + 1) * block)
        dq_ref[part, :] = (jnp.transpose(dq_turned[:, part]) * scaling).astype(LOW)


def attend_back(queries, keys, values, grad_mixed, mixed, sums, lengths, block, sure):
    rows, width = keys.shape
    heads = width // HD
    return pl.pallas_call(
        functools.partial(attend_back_kernel, rows=rows, block=block, heads=heads, sure=sure),
        in_specs=[scalars()] + [whole()] * 6,
        out_specs=(whole(),) * 3,
        out_shape=(struct((rows, width), LOW),) * 3,
        scratch_shapes=[pltpu.VMEM((rows // block, 8, block), WIDE), pltpu.VMEM((width, rows), WIDE)],
        compiler_params=pltpu.CompilerParams(vmem_limit_bytes=32 << 20),
        name="attend_backward",
    )(lengths, queries, keys, values, grad_mixed, mixed, sums)


def gelu_pair(up):
    root = 0.7978845608028654
    square = up * up
    bent = jnp.tanh(root * up * (1.0 + 0.044715 * square))
    half = 0.5 * (1.0 + bent)
    slope = half + 0.5 * up * (1.0 - bent * bent) * (root * (1.0 + 3 * 0.044715 * square))
    return up * half, slope


def feed_kernel(
    scalar_ref, tokens_ref, grad_ref, m0, m1, m2, m3, o0, o1, o2, o3, up_ref, down_ref, rows_ref,
    keep_ref, send_ref, hidden_ref, normed_ref, active_ref, upper_ref, sums_ref, mixed_ref, *, block, blocks,
):
    i = pl.program_id(0)
    half = blocks // 2
    core = scalar_ref[0]
    row0 = lax.rem(i + (1 - core) * half, blocks) * block
    row = lax.broadcasted_iota(jnp.int32, (block, 1), 0) + row0
    @pl.when(scalar_ref[2] == 0)
    def _():
        across = outer_cols(m0[...], o0[...]) + outer_cols(m1[...], o1[...])
        mixed_ref[...] = across + outer_cols(m2[...], o2[...]) + outer_cols(m3[...], o3[...])

    @pl.when(scalar_ref[2] != 0)
    def _():
        across = outer_cols(m1[...], o1[...]) + outer_cols(m0[...], o0[...])
        mixed_ref[...] = across + outer_cols(m3[...], o3[...]) + outer_cols(m2[...], o2[...])

    hidden = tokens_ref[...].astype(WIDE) + mixed_ref[...]
    scaled, _ = standardize(hidden)
    normed = (scaled * rows_ref[1:2, :] + rows_ref[3:4, :]).astype(LOW)
    normed_ref[...] = normed
    grad = jnp.where(row < scalar_ref[1], grad_ref[...].astype(WIDE), 0.0).astype(LOW)
    active, slope = gelu_pair(multiply(normed, up_ref[...]))
    active_ref[...] = active.astype(LOW)
    upper = (multiply(grad, down_ref[...]) * slope).astype(LOW)
    upper_ref[...] = upper
    back = outer_cols(upper, up_ref[...])

    @pl.when(i == 0)
    def _():
        sums_ref[...] = jnp.zeros_like(sums_ref)

    sums_ref[0:1, :] += jnp.sum(back * scaled, axis=0, keepdims=True)
    sums_ref[1:2, :] += jnp.sum(back, axis=0, keepdims=True)

    @pl.when(i < half)
    def _():
        send_ref[...] = back.astype(LOW)

    @pl.when(i >= half)
    def _():
        keep_ref[...] = back.astype(LOW)
        hidden_ref[...] = hidden


def feed(pair, tokens, out_grad, mixed, outs, up, down, rows, block):
    count, depth = tokens.shape
    hidden_units = up.shape[1]
    width = mixed[0].shape[1]
    blocks = count // block
    half = blocks // 2

    def turned(i, scalar_ref):
        return (lax.rem(i + (1 - scalar_ref[0]) * half, blocks), 0)

    def fixed(i, scalar_ref):
        return (0, 0)

    def row_block(columns):
        return pl.BlockSpec((block, columns), turned)

    def kept(i, scalar_ref):
        return (jnp.maximum(i - half, 0), 0)

    def sent(i, scalar_ref):
        return (jnp.minimum(i, half - 1), 0)

    return pl.pallas_call(
        functools.partial(feed_kernel, block=block, blocks=blocks),
        grid_spec=pltpu.PrefetchScalarGridSpec(
            num_scalar_prefetch=1,
            grid=(blocks,),
            in_specs=[row_block(depth), row_block(depth)]
            + [row_block(width)] * 4
            + [whole()] * 7,
            out_specs=(
                pl.BlockSpec((block, depth), kept),
                pl.BlockSpec((block, depth), sent),
                pl.BlockSpec((block, depth), kept),
                row_block(depth),
                row_block(hidden_units),
                row_block(hidden_units),
                pl.BlockSpec((8, depth), fixed),
            ),
            scratch_shapes=[pltpu.VMEM((block, depth), WIDE)],
        ),
        out_shape=(
            struct((count // 2, depth), LOW),
            struct((count // 2, depth), LOW),
            struct((count // 2, depth), WIDE),
            struct((count, depth), LOW),
            struct((count, hidden_units), LOW),
            struct((count, hidden_units), LOW),
            struct((8, depth), WIDE),
        ),
        compiler_params=pltpu.CompilerParams(vmem_limit_bytes=40 << 20),
        name="feed_forward",
    )(pair, tokens, out_grad, *mixed, *outs, up, down, rows)


def second_back_kernel(scalar_ref, mine_ref, other_ref, hidden_ref, grad_ref, rows_ref, wide_ref, low_ref, *, block, blocks):
    row0 = (pl.program_id(0) + scalar_ref[0] * blocks) * block
    row = lax.broadcasted_iota(jnp.int32, (block, 1), 0) + row0
    grad_normed = mine_ref[...].astype(WIDE) + other_ref[...].astype(WIDE)
    scaled, inverse = standardize(hidden_ref[...])
    grad = jnp.where(row < scalar_ref[1], grad_ref[...].astype(WIDE), 0.0)
    grad = grad + standardize_back(grad_normed, scaled, inverse, rows_ref[1:2, :])
    wide_ref[...] = grad
    low_ref[...] = grad.astype(LOW)


def second_back(pair, mine, other, hidden, out_grad, rows, block):
    count, depth = hidden.shape
    blocks = count // block

    def own(i, scalar_ref):
        return (i, 0)

    def placed(i, scalar_ref):
        return (i + scalar_ref[0] * blocks, 0)

    return pl.pallas_call(
        functools.partial(second_back_kernel, block=block, blocks=blocks),
        grid_spec=pltpu.PrefetchScalarGridSpec(
            num_scalar_prefetch=1,
            grid=(blocks,),
            in_specs=[pl.BlockSpec((block, depth), own)] * 3 + [pl.BlockSpec((block, depth), placed), whole()],
            out_specs=(pl.BlockSpec((block, depth), own),) * 2,
        ),
        out_shape=(struct((count, depth), WIDE), struct((count, depth), LOW)),
        compiler_params=pltpu.CompilerParams(vmem_limit_bytes=24 << 20),
        name="second_norm_backward",
    )(pair, mine, other, hidden, out_grad, rows)


def inward_kernel(scalar_ref, dq_ref, dk_ref, dv_ref, tokens_ref, weights_ref, keep_ref, send_ref, sums_ref, *, blocks, width):
    i = pl.program_id(0)
    half = blocks // 2
    back = outer_cols(dq_ref[...], weights_ref[:, :width])
    back = back + outer_cols(dk_ref[...], weights_ref[:, width : 2 * width])
    back = back + outer_cols(dv_ref[...], weights_ref[:, 2 * width : 3 * width])
    scaled, _ = standardize(tokens_ref[...].astype(WIDE))

    @pl.when(i == 0)
    def _():
        sums_ref[...] = jnp.zeros_like(sums_ref)

    sums_ref[0:1, :] += jnp.sum(back * scaled, axis=0, keepdims=True)
    sums_ref[1:2, :] += jnp.sum(back, axis=0, keepdims=True)

    @pl.when(i < half)
    def _():
        send_ref[...] = back.astype(LOW)

    @pl.when(i >= half)
    def _():
        keep_ref[...] = back.astype(LOW)


def inward(pair, dq, dk, dv, tokens, weights, block):
    count, depth = tokens.shape
    width = dq.shape[1]
    blocks = count // block
    half = blocks // 2

    def turned(i, scalar_ref):
        return (lax.rem(i + (1 - scalar_ref[0]) * half, blocks), 0)

    def kept(i, scalar_ref):
        return (jnp.maximum(i - half, 0), 0)

    def sent(i, scalar_ref):
        return (jnp.minimum(i, half - 1), 0)

    return pl.pallas_call(
        functools.partial(inward_kernel, blocks=blocks, width=width),
        grid_spec=pltpu.PrefetchScalarGridSpec(
            num_scalar_prefetch=1,
            grid=(blocks,),
            in_specs=[pl.BlockSpec((block, width), turned)] * 3 + [pl.BlockSpec((block, depth), turned), whole()],
            out_specs=(
                pl.BlockSpec((block, depth), kept),
                pl.BlockSpec((block, depth), sent),
                pl.BlockSpec((8, depth), lambda i, scalar_ref: (0, 0)),
            ),
        ),
        out_shape=(
            struct((count // 2, depth), LOW),
            struct((count // 2, depth), LOW),
            struct((8, depth), WIDE),
        ),
        compiler_params=pltpu.CompilerParams(vmem_limit_bytes=24 << 20),
        name="grad_normed",
    )(pair, dq, dk, dv, tokens, weights)


def first_back_kernel(scalar_ref, mine_ref, other_ref, tokens_ref, grad_ref, rows_ref, own_ref, full_ref):
    grad_normed = mine_ref[...].astype(WIDE) + other_ref[...].astype(WIDE)
    scaled, inverse = standardize(tokens_ref[...].astype(WIDE))
    grad = grad_ref[...] + standardize_back(grad_normed, scaled, inverse, rows_ref[0:1, :])
    low = grad.astype(LOW)
    own_ref[...] = low
    full_ref[...] = low


def first_back(pair, mine, other, tokens, grad_hidden, rows, block):
    count, depth = grad_hidden.shape
    blocks = count // block

    def own(i, scalar_ref):
        return (i, 0)

    def placed(i, scalar_ref):
        return (i + scalar_ref[0] * blocks, 0)

    return pl.pallas_call(
        first_back_kernel,
        grid_spec=pltpu.PrefetchScalarGridSpec(
            num_scalar_prefetch=1,
            grid=(blocks,),
            in_specs=[
                pl.BlockSpec((block, depth), own),
                pl.BlockSpec((block, depth), own),
                pl.BlockSpec((block, depth), placed),
                pl.BlockSpec((block, depth), own),
                whole(),
            ],
            out_specs=(pl.BlockSpec((block, depth), own), pl.BlockSpec((block, depth), placed)),
        ),
        out_shape=(struct((count, depth), LOW), struct((2 * count, depth), LOW)),
        compiler_params=pltpu.CompilerParams(vmem_limit_bytes=24 << 20),
        name="first_norm_backward",
    )(pair, mine, other, tokens, grad_hidden, rows)


def per_device(tokens, lengths, w_query, w_key, w_value, w_out, w_up, w_down, norm_gain, norm_shift, out_grad):
    count, depth = tokens.shape
    if lengths.shape[0] != 1 or lax.axis_size("tensor") != 4:
        raise ValueError("unsupported mesh")
    width = w_query.shape[1]
    core = lax.axis_index("tensor") & 1
    half = count // 2
    pair = jnp.stack([core.astype(jnp.int32), lengths[0], (lax.axis_index("tensor") >> 1).astype(jnp.int32)])
    block = 256
    sure = 2 * count // 3

    blank = jnp.zeros((w_query.shape[0], -(3 * width + 4) % LANES), LOW)
    early = jnp.concatenate([w_query, w_key, w_value, norm_gain.T, norm_shift.T, blank], axis=1)
    early = gather_batch(early)
    w_out_turned = gather_batch(w_out.T)
    late = gather_batch(jnp.concatenate([w_up, w_down.T], axis=1))
    full_up = late[:, : w_up.shape[1]]
    full_down = late[:, w_up.shape[1] :]
    outs = gather_tensor(w_out_turned)

    normed, queries, keys, values, rows = project(tokens, early, width, block)
    mixed, sums = attend(queries, keys, values, lengths, 0, count, block, sure)
    pieces = gather_tensor(mixed)
    keep, send, hidden, normed_two, active, upper, sums_two = feed(
        pair, tokens, out_grad, pieces, outs, full_up, full_down, rows, block
    )
    mine, other = pair_sum(keep, send)
    is_valid = (jnp.arange(count, dtype=jnp.int32) < lengths[0])[:, None]
    grad_rows = jnp.where(is_valid, out_grad, jnp.zeros_like(out_grad))
    branch = outer_cols(active, full_down).astype(LOW)
    shard_up = scatter_batch(inner_rows(normed_two, upper).astype(LOW))
    shard_down = scatter_batch(inner_rows(grad_rows, active).astype(LOW)).T

    grad_hidden, grad_attn = second_back(pair, mine, other, hidden, out_grad, rows, block)
    beside = swap(grad_attn, "tensor", 1)
    grad_attn = jnp.where(
        core == 0, jnp.concatenate([grad_attn, beside]), jnp.concatenate([beside, grad_attn])
    )
    grad_mixed = multiply(grad_attn, w_out_turned).astype(LOW)
    shard_out = scatter_batch(inner_rows(grad_attn, mixed).astype(LOW)).T
    dq, dk, dv = attend_back(queries, keys, values, grad_mixed, mixed, sums, lengths, block, sure)

    branch_keep = lax.dynamic_slice(branch, (core * half, 0), (half, depth))
    branch_send = lax.dynamic_slice(branch, ((1 - core) * half, 0), (half, depth))
    branch_mine, branch_other = pair_sum(branch_keep, branch_send)
    own_valid = lax.dynamic_slice(is_valid, (core * half, 0), (half, 1))
    own_out = hidden + (branch_mine.astype(WIDE) + branch_other.astype(WIDE))
    own_out = jnp.where(own_valid, own_out, 0.0).astype(LOW)
    other_out = swap(own_out, "tensor", 1)
    layer_out = jnp.where(
        core == 0, jnp.concatenate([own_out, other_out]), jnp.concatenate([other_out, own_out])
    )

    keep, send, sums_one = inward(pair, dq, dk, dv, tokens, early, block)
    mine, other = pair_sum(keep, send)
    own_grad, grad_input = first_back(pair, mine, other, tokens, grad_hidden, rows, block)
    grad_input = lax.dynamic_update_slice(grad_input, swap(own_grad, "tensor", 1), ((1 - core) * half, 0))

    turned = jnp.stack([sums_one[0], sums_two[0], sums_one[1], sums_two[1]]).T
    grads = inner_rows(normed, jnp.concatenate([dq, dk, dv], axis=1))
    blank = jnp.zeros((depth, early.shape[1] - 3 * width - 4), WIDE)
    grads = scatter_batch(jnp.concatenate([grads, turned, blank], axis=1).astype(LOW))
    small = grads[:, 3 * width : 3 * width + 4]
    small = small + swap(small, "tensor", 2)
    small = (small + swap(small, "tensor", 1)).T
    return (
        layer_out,
        grad_input,
        grads[:, :width],
        grads[:, width : 2 * width],
        grads[:, 2 * width : 3 * width],
        shard_out,
        shard_up,
        shard_down,
        small[:2],
        small[2:],
    )


def solution(mesh):
    tall = P("batch", "tensor")
    wide = P("tensor", "batch")
    rows = P("batch", None)
    pair = P(None, "batch")
    return jax.shard_map(
        per_device,
        mesh=mesh,
        in_specs=(rows, P("batch"), tall, tall, tall, wide, tall, wide, pair, pair, rows),
        out_specs=(rows, rows, tall, tall, tall, wide, tall, wide, pair, pair),
        check_vma=False,
    )
```

time: 757 us -> 333 us (0.44)
  matrix products: 231 us -> 24.2 us
  blocking collectives: 163 us -> 0 us
  waiting for transfers between devices: 205 us -> 84 us
  Pallas kernels: 0 us -> 69.8 us
  other arithmetic: 57.9 us -> 24.6 us
  local copies, waits for them, and re-layouts: 34.2 us -> 63.5 us
  starting transfers between devices: 38.5 us -> 60 us
  between operations: 17 us -> 1.97 us
    dot_general x36 -> x6, matrix products: 231 us -> 24.2 us  [the longest x4 15.9 us: inner_rows(): lax.dot_general(left, right, (((0,), (0,)), ((), ())), preferred_element_...]
    psum x3 -> x0, waiting for transfers between devices: 177 us -> none  [the longest x1 90.3 us: per_device(): hidden = inputs + lax.psum(attn_partial, 'tensor')]
    all_gather x6 -> x0, blocking collectives: 163 us -> none  [the longest x1 31.3 us: per_device(): lax.all_gather(w_out, 'batch', axis=1, tiled=True)]
    ppermute x0 -> x38, waiting for transfers between devices: none -> 76.2 us  [swap(): return lax.ppermute(value, axis, [(i, i ^ bits) for i in range(size)])]
    pallas_call x0 -> x7, Pallas kernels: none -> 69.8 us  [the longest x1 20.8 us: attend_back(): pl.pallas_call(functools.partial(attend_back_kernel, rows=rows, block=blo...]
    ppermute x0 -> x38, starting transfers between devices: none -> 39.5 us  [swap(): return lax.ppermute(value, axis, [(i, i ^ bits) for i in range(size)])]
    reduce_sum x18 -> x4, other arithmetic: 34.2 us -> 7.41 us  [scatter_batch(): return jnp.sum(parts.astype(WIDE), axis=0)]
    all_to_all x8 -> x4, waiting for transfers between devices: 27.2 us -> 7.83 us  [scatter_batch(): parts = lax.all_to_all(parts, 'batch', 0, 0, tiled=True)]
  transfers between devices with their start and end apart: 13 -> 42, of which waited for: 9 -> 18; matrix products, arithmetic and copies ran while one was open for 34% -> 27% of each run, Pallas kernels for 0% -> 16%
where the time goes in v1:
time: 333 us; the launch traced here: 328 us
  waiting for transfers between devices  84 us (25%)
  Pallas kernels  69.8 us (21%)
  local copies, waits for them, and re-layouts  63.5 us (19%)
  starting transfers between devices  60 us (18%)
  other arithmetic  24.6 us (7%)
  matrix products  24.2 us (7%)
    ppermute x38, waiting for transfers between devices, swap(): return lax.ppermute(value, axis, [(i, i ^ bits) for i in range(size)])  76.2 us
    ppermute x38, starting transfers between devices, swap(): return lax.ppermute(value, axis, [(i, i ^ bits) for i in range(size)])  39.5 us
    unnamed x95, local copies, waits for them, and re-layouts  22.8 us
    pallas_call x1, Pallas kernels, attend_back(): pl.pallas_call(functools.partial(attend_back_kernel, rows=rows, block=blo...  20.8 us
    all_to_all x4, starting transfers between devices, scatter_batch(): parts = lax.all_to_all(parts, 'batch', 0, 0, tiled=True)  20.6 us
    pallas_call x1, Pallas kernels, feed(): pl.pallas_call(functools.partial(feed_kernel, block=block, blocks=blocks)...  17.3 us
    dot_general x4, matrix products, inner_rows(): lax.dot_general(left, right, (((0,), (0,)), ((), ())), preferred_element_...  15.9 us
    dynamic_update_slice x23, local copies, waits for them, and re-layouts, gather_batch(): full = lax.dynamic_update_slice(full, piece, ((me ^ bits) * rows, 0))  15.8 us
  transfers between devices with their start and end apart: 42, of which 18 were waited for; matrix products, arithmetic and copies ran while one was open for 27% of the time, Pallas kernels for 16%

profile of v1, /device:TPU:0, one launch (start us, length us, event | category | flops | bytes accessed | tf_op | source)
XLA Modules:
  0.0 328.1 jit_solution(12176815439865402477)
XLA Ops:
  3.2 3.0 collective-permute-start.20
  6.2 2.6 collective-permute-start.21
  13.7 15.9 %collective-permute-done.10 = bf16[96,192]{1,0:T(8,128)(2,1)} collective-permute-done((bf16[96,192]{1,0:T(8,128)(2,1)S(1)}, bf16[96,192]{1,0:T(8,128)(2,1)}, u32[]{:S(2)}, u32[]{:S(2)}) %collective-permute-start.10) | collective-permute-done | bytes 36896 | tf_op jit(solution)/shard_map/ppermute | solution.py:46
  29.6 3.0 collective-permute-start.11
  34.1 2.8 collective-permute-done.11
  36.9 2.7 collective-permute-start.12
  40.2 2.6 collective-permute-done.12
  44.9 2.0 collective-permute-done.13
  49.0 2.2 collective-permute-done.14
  53.3 1.9 collective-permute-done.15
  60.0 3.1 collective-permute-start.2
  64.0 3.8 %collective-permute-done.1 = bf16[96,640]{1,0:T(8,128)(2,1)S(1)} collective-permute-done((bf16[96,640]{1,0:T(8,128)(2,1)S(1)}, bf16[96,640]{1,0:T(8,128)(2,1)S(1)}, u32[]{:S(2)}, u32[]{:S(2)}) %collective-permute-start.1) | collective-permute-done | bytes 122912 | tf_op jit(solution)/shard_map/ppermute | solution.py:46
  69.9 4.1 %collective-permute-done.3 = bf16[96,640]{1,0:T(8,128)(2,1)S(1)} collective-permute-done((bf16[96,640]{1,0:T(8,128)(2,1)S(1)}, bf16[96,640]{1,0:T(8,128)(2,1)S(1)}, u32[]{:S(2)}, u32[]{:S(2)}) %collective-permute-start.3) | collective-permute-done | bytes 122912 | tf_op jit(solution)/shard_map/ppermute | solution.py:46
  77.0 2.0 collective-permute-done.5
  82.1 4.5 %project.1 = (bf16[1536,768]{1,0:T(8,128)(2,1)S(1)}, bf16[1536,192]{1,0:T(8,128)(2,1)S(1)}, bf16[1536,192]{1,0:T(8,128)(2,1)S(1)}, bf16[1536,192]{1,0:T(8,128)(2,1)S(1)}, f32[8,768]{1,0:T(8,128)S(1)}) custom-call(bf16[1536,768]{1,0:T(8,128)(2,1)S(1)} %copy-done, bf16[768,640]{1,0:T(8,128)(2,1)S(1)} %constant_dynamic-update-slice_fusion.17.weights_ref), custom_call_target="tpu_custom_call" | custom-call | tf_op jit(solution)/shard_map/project/pallas_call | solution.py:120
  88.0 11.0 %attend_forward.1 = (bf16[1536,192]{1,0:T(8,128)(2,1)S(1)}, f32[6,8,256]{2,1,0:T(8,128)S(1)}) custom-call(s32[1]{0:T(128)} %copy.91.length_ref, bf16[1536,192]{1,0:T(8,128)(2,1)S(1)} %get-tuple-element.34.q_ref, bf16[1536,192]{1,0:T(8,128)(2,1)S(1)} %get-tuple-element.35.k_ref, bf16[1536,192]{1,0:T(8,128)(2,1)S(1)} %get-tuple-element.36.v_ref), custom_call_target="tpu_custom_call" | custom-call | tf_op jit(solution)/shard_map/attend_forward/pallas_call | solution.py:186
  109.7 4.6 %collective-permute-done.24 = bf16[96,1536]{1,0:T(8,128)(2,1)S(1)} collective-permute-done((bf16[96,1536]{1,0:T(8,128)(2,1)}, bf16[96,1536]{1,0:T(8,128)(2,1)S(1)}, u32[]{:S(2)}, u32[]{:S(2)}) %collective-permute-start.24) | collective-permute-done | bytes 294944 | tf_op jit(solution)/shard_map/ppermute | solution.py:46
  116.3 4.3 %collective-permute-done.25 = bf16[96,1536]{1,0:T(8,128)(2,1)S(1)} collective-permute-done((bf16[96,1536]{1,0:T(8,128)(2,1)}, bf16[96,1536]{1,0:T(8,128)(2,1)S(1)}, u32[]{:S(2)}, u32[]{:S(2)}) %collective-permute-start.25) | collective-permute-done | bytes 294944 | tf_op jit(solution)/shard_map/ppermute | solution.py:46
  121.9 4.4 %collective-permute-done.26 = bf16[96,1536]{1,0:T(8,128)(2,1)S(1)} collective-permute-done((bf16[96,1536]{1,0:T(8,128)(2,1)}, bf16[96,1536]{1,0:T(8,128)(2,1)S(1)}, u32[]{:S(2)}, u32[]{:S(2)}) %collective-permute-start.26) | collective-permute-done | bytes 294944 | tf_op jit(solution)/shard_map/ppermute | solution.py:46
  127.0 3.4 %fusion.21 = (bf16[768,768]{1,0:T(8,128)(2,1)}, bf16[768,768]{1,0:T(8,128)(2,1)}) fusion(bf16[768,1536]{1,0:T(8,128)(2,1)} %constant_dynamic-update-slice_fusion.1), kind=kLoop, calls=%fused_computation.64 | loop fusion | bytes 4718592 | tf_op jit(solution)/shard_map/slice | solution.py:529
  130.4 2.2 copy.56.m1
  132.6 2.2 copy.57.m2
  134.8 2.2 copy.58.m3
  147.6 17.3 %feed_forward.1 = (bf16[768,768]{1,0:T(8,128)(2,1)S(1)}, bf16[768,768]{1,0:T(8,128)(2,1)}, f32[768,768]{1,0:T(8,128)S(1)}, bf16[1536,768]{1,0:T(8,128)(2,1)S(1)}...) custom-call(s32[3]{0:T(128)S(1)} %pad_add_fusion.scalar_ref, ...), custom_call_target="tpu_custom_call" | custom-call | tf_op jit(solution)/shard_map/feed_forward/pallas_call | solution.py:344
  166.0 5.6 %convolution_convert_fusion.2 = bf16[768,768]{1,0:T(8,128)(2,1)} fusion(bf16[1536,768]{1,0:T(8,128)(2,1)S(1)} %get-tuple-element.56, bf16[1536,768]{1,0:T(8,128)(2,1)} %get-tuple-element.57), kind=kOutput, calls=%fused_computation.21 | convolution fusion | flops 1812529152 | bytes 5898240 | tf_op jit(solution)/shard_map/dot_general | solution.py:29
  171.5 4.3 %all-to-all-start.2 = ((bf16[8,96,768]{2,1,0:T(8,128)(2,1)}), bf16[8,96,768]{2,1,0:T(8,128)(2,1)}, u32[]{:S(2)}, u32[]{:S(2)}) async-start(bf16[8,96,768]{2,1,0:T(8,128)(2,1)} %bitcast.30), calls=%async_computation.2 | async-start | bytes 2359296 | tf_op jit(solution)/shard_map/all_to_all | solution.py:69
  175.8 2.9 add_convert_fusion.1.mine_ref
  180.2 4.0 %convolution_convert_fusion = bf16[1536,768]{1,0:T(8,128)(2,1)S(1)} fusion(bf16[1536,768]{1,0:T(8,128)(2,1)} %get-tuple-element.40, bf16[768,1536]{1,0:T(8,128)(2,1)} %constant_dynamic-update-slice_fusion.1), kind=kOutput, calls=%fused_computation | convolution fusion | flops 1813118976 | bytes 5898240 | tf_op jit(solution)/shard_map/dot_general | solution.py:25
  185.4 21.2 %collective-permute-done.31.other_ref = bf16[768,768]{1,0:T(8,128)(2,1)} collective-permute-done((bf16[768,768]{1,0:T(8,128)(2,1)}, bf16[768,768]{1,0:T(8,128)(2,1)}, u32[]{:S(2)}, u32[]{:S(2)}) %collective-permute-start.31) | collective-permute-done | bytes 1179680 | tf_op jit(solution)/shard_map/ppermute | solution.py:46
  206.6 5.0 %second_norm_backward.1 = (f32[768,768]{1,0:T(8,128)S(1)}, bf16[768,768]{1,0:T(8,128)(2,1)}) custom-call(s32[3]{0:T(128)S(1)} %pad_add_fusion.scalar_ref, bf16[768,768]{1,0:T(8,128)(2,1)} %add_convert_fusion.1.mine_ref, bf16[768,768]{1,0:T(8,128)(2,1)} %collective-permute-done.31.other_ref, f32[768,768]{1,0:T(8,128)S(1)} %get-tuple-element.39.hidden_ref, ...), custom_call_target="tpu_custom_call" | custom-call | tf_op jit(solution)/shard_map/second_norm_backward/pallas_call | solution.py:398
  213.1 3.3 fusion.9
  216.4 6.2 %all-to-all-start.3 = ((bf16[8,96,768]{2,1,0:T(8,128)(2,1)}), bf16[8,96,768]{2,1,0:T(8,128)(2,1)}, u32[]{:S(2)}, u32[]{:S(2)}) async-start(bf16[8,96,768]{2,1,0:T(8,128)(2,1)} %bitcast.29), calls=%async_computation.3 | async-start | bytes 2359296 | tf_op jit(solution)/shard_map/all_to_all | solution.py:69
  222.7 2.6 add_convert_fusion.2
  226.8 4.3 %convolution_convert_fusion.1 = bf16[1536,192]{0,1:T(8,128)(2,1)} fusion(bf16[768,192]{1,0:T(8,128)(2,1)} %constant_dynamic-update-slice_fusion.9.o0, bf16[768,768]{1,0:T(8,128)(2,1)} %collective-permute-done.32, bf16[768,768]{1,0:T(8,128)(2,1)} %get-tuple-element.43, pred[]{:T(512)S(6)} %eq.4), kind=kOutput, calls=%fused_computation.1 | convolution fusion | flops 463896576 | bytes 3244033 | tf_op jit(solution)/shard_map/dot_general | solution.py:21
  231.1 2.4 copy.59.g_ref
  239.1 20.8 %attend_backward.1 = (bf16[1536,192]{1,0:T(8,128)(2,1)S(1)}, bf16[1536,192]{1,0:T(8,128)(2,1)S(1)}, bf16[1536,192]{1,0:T(8,128)(2,1)S(1)}) custom-call(s32[1]{0:T(128)} %copy.91.length_ref, bf16[1536,192]{1,0:T(8,128)(2,1)S(1)} %copy-done.11, bf16[1536,192]{1,0:T(8,128)(2,1)S(1)} %copy-done.13, bf16[1536,192]{1,0:T(8,128)(2,1)S(1)} %copy-done.15, ...), custom_call_target="tpu_custom_call" | custom-call | tf_op jit(solution)/shard_map/attend_backward/pallas_call | solution.py:255
  259.9 6.3 %grad_normed.1 = (bf16[768,768]{1,0:T(8,128)(2,1)S(1)}, bf16[768,768]{1,0:T(8,128)(2,1)}, f32[8,768]{1,0:T(8,128)S(1)}) custom-call(s32[3]{0:T(128)S(1)} %pad_add_fusion.scalar_ref, bf16[1536,192]{1,0:T(8,128)(2,1)S(1)} %get-tuple-element.45.dq_ref, bf16[1536,192]{1,0:T(8,128)(2,1)S(1)} %get-tuple-element.46.dk_ref, ...), custom_call_target="tpu_custom_call" | custom-call | tf_op jit(solution)/shard_map/grad_normed/pallas_call | solution.py:451
  266.3 3.0 fusion.12
  272.3 6.0 %all-to-all-start = ((bf16[8,96,640]{2,1,0:T(8,128)(2,1)}), bf16[8,96,640]{2,1,0:T(8,128)(2,1)}, u32[]{:S(2)}, u32[]{:S(2)}) async-start(bf16[8,96,640]{2,1,0:T(8,128)(2,1)} %maximum_maximum_fusion), calls=%async_computation | async-start | bytes 1966080 | tf_op jit(solution)/shard_map/all_to_all | solution.py:69
  279.0 3.9 %select_convert_fusion = bf16[768,768]{1,0:T(8,128)(2,1)} fusion(f32[768,768]{1,0:T(8,128)} %copy-done.2, bf16[768,768]{1,0:T(8,128)(2,1)} %collective-permute-done.28, bf16[768,768]{1,0:T(8,128)(2,1)} %add_convert_fusion.2, pred[768]{0:T(1024)(128)(4,1)S(1)} %dynamic-slice.3), kind=kLoop, calls=%fused_computation.10 | loop fusion | flops 3538944 | bytes 5899008 | tf_op jit(solution)/shard_map/convert_element_type | solution.py:559
  285.4 2.2 convert_reduce_fusion.1
  287.6 4.0 %convolution_convert_fusion.3 = bf16[768,192]{0,1:T(8,128)(2,1)} fusion(bf16[1536,192]{1,0:T(8,128)(2,1)S(1)} %copy-done.7, bf16[768,768]{1,0:T(8,128)(2,1)} %collective-permute-done.32, bf16[768,768]{1,0:T(8,128)(2,1)} %get-tuple-element.43, pred[]{:T(512)S(6)} %eq.4), kind=kOutput, calls=%fused_computation.23 | convolution fusion | flops 463749120 | bytes 3244033 | tf_op jit(solution)/shard_map/dot_general | solution.py:29
  291.6 2.2 reshape.41
  295.6 7.8 %all-to-all-done = bf16[8,96,640]{2,1,0:T(8,128)(2,1)} async-done(((bf16[8,96,640]{2,1,0:T(8,128)(2,1)}), bf16[8,96,640]{2,1,0:T(8,128)(2,1)}, u32[]{:S(2)}, u32[]{:S(2)}) %all-to-all-start) | async-done | bytes 983072 | tf_op jit(solution)/shard_map/all_to_all | solution.py:69
  303.4 4.1 %all-to-all-start.1 = ((bf16[8,96,192]{1,2,0:T(8,128)(2,1)}), bf16[8,96,192]{1,2,0:T(8,128)(2,1)}, u32[]{:S(2)}, u32[]{:S(2)}) async-start(bf16[8,96,192]{1,2,0:T(8,128)(2,1)} %copy.62), calls=%async_computation.1 | async-start | bytes 786432 | tf_op jit(solution)/shard_map/all_to_all | solution.py:69
  307.5 2.2 convert_reduce_fusion
  309.7 3.9 %maximum_select_fusion = bf16[1536,768]{1,0:T(8,128)(2,1)} fusion(bf16[768,768]{1,0:T(8,128)(2,1)} %collective-permute-done.29, bf16[768,768]{1,0:T(8,128)(2,1)} %select_convert_fusion, pred[]{:T(512)S(6)} %eq.4), kind=kLoop, calls=%fused_computation.2 | loop fusion | flops 10616832 | bytes 4718593 | tf_op jit(solution)/shard_map/jit(_where)/select_n | solution.py:561
  313.6 4.9 %first_norm_backward.1 = (bf16[768,768]{1,0:T(8,128)(2,1)}, bf16[1536,768]{1,0:T(8,128)(2,1)}) custom-call(s32[3]{0:T(128)S(1)} %pad_add_fusion.scalar_ref, bf16[768,768]{1,0:T(8,128)(2,1)S(1)} %add_convert_fusion.mine_ref, bf16[768,768]{1,0:T(8,128)(2,1)} %collective-permute-done.34.other_ref, bf16[1536,768]{1,0:T(8,128)(2,1)S(1)} %copy-done.1, ...), custom_call_target="tpu_custom_call" | custom-call | tf_op jit(solution)/shard_map/first_norm_backward/pallas_call | solution.py:492
  (209 shorter events, 85.4 us)
Async XLA Ops:
  3.2 97.1 %collective-permute-start.20 = (bf16[96,1536]{1,0:T(8,128)(2,1)}, bf16[96,1536]{1,0:T(8,128)(2,1)}, u32[]{:S(2)}, u32[]{:S(2)}) collective-permute-start(bf16[96,1536]{1,0:T(8,128)(2,1)} %get-tuple-element.100), channel_id=1, source_target_pairs={{0,8},{4,12},{8,0},{12,4},{16,24},{20,28},{24,16},{28,20},{1,9},{5... | collective-permute-start | bytes 884744 | tf_op jit(solution)/shard_map/ppermute | solution.py:46
  6.2 95.9 %collective-permute-start.21 = (bf16[96,1536]{1,0:T(8,128)(2,1)}, bf16[96,1536]{1,0:T(8,128)(2,1)}, u32[]{:S(2)}, u32[]{:S(2)}) collective-permute-start(bf16[96,1536]{1,0:T(8,128)(2,1)} %get-tuple-element.100), channel_id=1, source_target_pairs={{0,16},{4,20},{8,24},{12,28},{16,0},{20,4},{24,8},{28,12},{1,17},{... | collective-permute-start | bytes 884744 | tf_op jit(solution)/shard_map/ppermute | solution.py:46
  8.8 95.5 %collective-permute-start.22 = (bf16[96,1536]{1,0:T(8,128)(2,1)}, bf16[96,1536]{1,0:T(8,128)(2,1)}, u32[]{:S(2)}, u32[]{:S(2)}) collective-permute-start(bf16[96,1536]{1,0:T(8,128)(2,1)} %get-tuple-element.100), channel_id=1, source_target_pairs={{0,24},{4,28},{8,16},{12,20},{16,8},{20,12},{24,0},{28,4},{1,25},{... | collective-permute-start | bytes 884744 | tf_op jit(solution)/shard_map/ppermute | solution.py:46
  8.9 73.2 %copy-start = (bf16[1536,768]{1,0:T(8,128)(2,1)S(1)}, bf16[1536,768]{1,0:T(8,128)(2,1)}, u32[]{:S(2)}) copy-start(bf16[1536,768]{1,0:T(8,128)(2,1)} %tokens_ref.7) | copy-start | bytes 7077892
  9.2 50.8 %collective-permute-start = (bf16[96,640]{1,0:T(8,128)(2,1)S(1)}, bf16[96,640]{1,0:T(8,128)(2,1)}, u32[]{:S(2)}, u32[]{:S(2)}) collective-permute-start(bf16[96,640]{1,0:T(8,128)(2,1)S(1)} %concatenate.30), channel_id=1, source_target_pairs={{0,8},{4,12},{8,0},{12,4},{16,24},{20,28},{24,16},{28,20},{1,9},{5... | collective-permute-start | bytes 368648 | tf_op jit(solution)/shard_map/ppermute | solution.py:46
  10.3 19.4 %collective-permute-start.10 = (bf16[96,192]{1,0:T(8,128)(2,1)S(1)}, bf16[96,192]{1,0:T(8,128)(2,1)}, u32[]{:S(2)}, u32[]{:S(2)}) collective-permute-start(bf16[96,192]{1,0:T(8,128)(2,1)S(1)} %bitcast.33), channel_id=1, source_target_pairs={{0,8},{4,12},{8,0},{12,4},{16,24},{20,28},{24,16},{28,20},{1,9},{5... | collective-permute-start | bytes 110600 | tf_op jit(solution)/shard_map/ppermute | solution.py:46
  29.6 7.3 %collective-permute-start.11 = (bf16[96,192]{1,0:T(8,128)(2,1)S(1)}, bf16[96,192]{1,0:T(8,128)(2,1)S(1)}, u32[]{:S(2)}, u32[]{:S(2)}) collective-permute-start(bf16[96,192]{1,0:T(8,128)(2,1)S(1)} %bitcast.34), channel_id=1, source_target_pairs={{0,16},{4,20},{8,24},{12,28},{16,0},{20,4},{24,8},{28,12},{1,17},{... | collective-permute-start | bytes 110600 | tf_op jit(solution)/shard_map/ppermute | solution.py:46
  36.9 5.9 %collective-permute-start.12 = (bf16[96,192]{1,0:T(8,128)(2,1)S(1)}, bf16[96,192]{1,0:T(8,128)(2,1)S(1)}, u32[]{:S(2)}, u32[]{:S(2)}) collective-permute-start(bf16[96,192]{1,0:T(8,128)(2,1)S(1)} %bitcast.35), channel_id=1, source_target_pairs={{0,24},{4,28},{8,16},{12,20},{16,8},{20,12},{24,0},{28,4},{1,25},{... | collective-permute-start | bytes 110600 | tf_op jit(solution)/shard_map/ppermute | solution.py:46
  42.8 4.1 %collective-permute-start.13 = (bf16[96,192]{1,0:T(8,128)(2,1)S(1)}, bf16[96,192]{1,0:T(8,128)(2,1)S(1)}, u32[]{:S(2)}, u32[]{:S(2)}) collective-permute-start(bf16[96,192]{1,0:T(8,128)(2,1)S(1)} %bitcast.36), channel_id=1, source_target_pairs={{0,4},{4,0},{8,12},{12,8},{16,20},{20,16},{24,28},{28,24},{1,5},{5... | collective-permute-start | bytes 110600 | tf_op jit(solution)/shard_map/ppermute | solution.py:46
  46.9 4.3 %collective-permute-start.14 = (bf16[96,192]{1,0:T(8,128)(2,1)}, bf16[96,192]{1,0:T(8,128)(2,1)S(1)}, u32[]{:S(2)}, u32[]{:S(2)}) collective-permute-start(bf16[96,192]{1,0:T(8,128)(2,1)} %collective-permute-done.10), channel_id=1, source_target_pairs={{0,4},{4,0},{8,12},{12,8},{16,20},{20,16},{24,28},{28,24},{1,5},{5... | collective-permute-start | bytes 110600 | tf_op jit(solution)/shard_map/ppermute | solution.py:46
  51.2 4.1 %collective-permute-start.15 = (bf16[96,192]{1,0:T(8,128)(2,1)S(1)}, bf16[96,192]{1,0:T(8,128)(2,1)S(1)}, u32[]{:S(2)}, u32[]{:S(2)}) collective-permute-start(bf16[96,192]{1,0:T(8,128)(2,1)S(1)} %collective-permute-done.11), channel_id=1, source_target_pairs={{0,4},{4,0},{8,12},{12,8},{16,20},{20,16},{24,28},{28,24},{1,5},{5... | collective-permute-start | bytes 110600 | tf_op jit(solution)/shard_map/ppermute | solution.py:46
  55.3 4.1 %collective-permute-start.16 = (bf16[96,192]{1,0:T(8,128)(2,1)S(1)}, bf16[96,192]{1,0:T(8,128)(2,1)S(1)}, u32[]{:S(2)}, u32[]{:S(2)}) collective-permute-start(bf16[96,192]{1,0:T(8,128)(2,1)S(1)} %collective-permute-done.12), channel_id=1, source_target_pairs={{0,4},{4,0},{8,12},{12,8},{16,20},{20,16},{24,28},{28,24},{1,5},{5... | collective-permute-start | bytes 110600 | tf_op jit(solution)/shard_map/ppermute | solution.py:46
  59.4 8.4 %collective-permute-start.1 = (bf16[96,640]{1,0:T(8,128)(2,1)S(1)}, bf16[96,640]{1,0:T(8,128)(2,1)S(1)}, u32[]{:S(2)}, u32[]{:S(2)}) collective-permute-start(bf16[96,640]{1,0:T(8,128)(2,1)S(1)} %concatenate.30), channel_id=1, source_target_pairs={{0,16},{4,20},{8,24},{12,28},{16,0},{20,4},{24,8},{28,12},{1,17},{... | collective-permute-start | bytes 368648 | tf_op jit(solution)/shard_map/ppermute | solution.py:46
  60.0 9.3 %collective-permute-start.2 = (bf16[96,640]{1,0:T(8,128)(2,1)S(1)}, bf16[96,640]{1,0:T(8,128)(2,1)S(1)}, u32[]{:S(2)}, u32[]{:S(2)}) collective-permute-start(bf16[96,640]{1,0:T(8,128)(2,1)S(1)} %concatenate.30), channel_id=1, source_target_pairs={{0,24},{4,28},{8,16},{12,20},{16,8},{20,12},{24,0},{28,4},{1,25},{... | collective-permute-start | bytes 368648 | tf_op jit(solution)/shard_map/ppermute | solution.py:46
  67.8 6.3 %collective-permute-start.3 = (bf16[96,640]{1,0:T(8,128)(2,1)S(1)}, bf16[96,640]{1,0:T(8,128)(2,1)S(1)}, u32[]{:S(2)}, u32[]{:S(2)}) collective-permute-start(bf16[96,640]{1,0:T(8,128)(2,1)S(1)} %concatenate.30), channel_id=1, source_target_pairs={{0,4},{4,0},{8,12},{12,8},{16,20},{20,16},{24,28},{28,24},{1,5},{5... | collective-permute-start | bytes 368648 | tf_op jit(solution)/shard_map/ppermute | solution.py:46
  69.3 6.3 %collective-permute-start.4 = (bf16[96,640]{1,0:T(8,128)(2,1)}, bf16[96,640]{1,0:T(8,128)(2,1)S(1)}, u32[]{:S(2)}, u32[]{:S(2)}) collective-permute-start(bf16[96,640]{1,0:T(8,128)(2,1)} %collective-permute-done), channel_id=1, source_target_pairs={{0,4},{4,0},{8,12},{12,8},{16,20},{20,16},{24,28},{28,24},{1,5},{5... | collective-permute-start | bytes 368648 | tf_op jit(solution)/shard_map/ppermute | solution.py:46
  74.1 4.9 %collective-permute-start.5 = (bf16[96,640]{1,0:T(8,128)(2,1)S(1)}, bf16[96,640]{1,0:T(8,128)(2,1)S(1)}, u32[]{:S(2)}, u32[]{:S(2)}) collective-permute-start(bf16[96,640]{1,0:T(8,128)(2,1)S(1)} %collective-permute-done.1), channel_id=1, source_target_pairs={{0,4},{4,0},{8,12},{12,8},{16,20},{20,16},{24,28},{28,24},{1,5},{5... | collective-permute-start | bytes 368648 | tf_op jit(solution)/shard_map/ppermute | solution.py:46
  75.6 4.9 %collective-permute-start.6 = (bf16[96,640]{1,0:T(8,128)(2,1)S(1)}, bf16[96,640]{1,0:T(8,128)(2,1)S(1)}, u32[]{:S(2)}, u32[]{:S(2)}) collective-permute-start(bf16[96,640]{1,0:T(8,128)(2,1)S(1)} %collective-permute-done.2), channel_id=1, source_target_pairs={{0,4},{4,0},{8,12},{12,8},{16,20},{20,16},{24,28},{28,24},{1,5},{5... | collective-permute-start | bytes 368648 | tf_op jit(solution)/shard_map/ppermute | solution.py:46
  78.9 28.3 %collective-permute-start.23 = (bf16[96,1536]{1,0:T(8,128)(2,1)}, bf16[96,1536]{1,0:T(8,128)(2,1)}, u32[]{:S(2)}, u32[]{:S(2)}) collective-permute-start(bf16[96,1536]{1,0:T(8,128)(2,1)} %get-tuple-element.100), channel_id=1, source_target_pairs={{0,4},{4,0},{8,12},{12,8},{16,20},{20,16},{24,28},{28,24},{1,5},{5... | collective-permute-start | bytes 884744 | tf_op jit(solution)/shard_map/ppermute | solution.py:46
  80.6 35.8 %collective-permute-start.17 = (bf16[768,192]{1,0:T(8,128)(2,1)}, bf16[768,192]{1,0:T(8,128)(2,1)}, u32[]{:S(2)}, u32[]{:S(2)}) collective-permute-start(bf16[768,192]{1,0:T(8,128)(2,1)} %constant_dynamic-update-slice_fusion.9.o0), channel_id=1, source_target_pairs={{0,2},{1,3},{2,0},{3,1},{4,6},{5,7},{6,4},{7,5},{8,10},{9,11},{10,... | collective-permute-start | bytes 884744 | tf_op jit(solution)/shard_map/ppermute | solution.py:46
  88.0 118.6 %copy-start.29 = (f32[8,768]{1,0:T(8,128)}, f32[8,768]{1,0:T(8,128)S(1)}, u32[]{:S(2)}) copy-start(f32[8,768]{1,0:T(8,128)S(1)} %get-tuple-element.38.rows_ref) | copy-start | bytes 73732
  100.2 36.8 %collective-permute-start.18 = (bf16[768,192]{1,0:T(8,128)(2,1)}, bf16[768,192]{1,0:T(8,128)(2,1)S(1)}, u32[]{:S(2)}, u32[]{:S(2)}) collective-permute-start(bf16[768,192]{1,0:T(8,128)(2,1)} %constant_dynamic-update-slice_fusion.9.o0), channel_id=1, source_target_pairs={{0,1},{1,0},{2,3},{3,2},{4,5},{5,4},{6,7},{7,6},{8,9},{9,8},{10,11... | collective-permute-start | bytes 884744 | tf_op jit(solution)/shard_map/ppermute | solution.py:46
  102.0 18.6 %collective-permute-start.7 = (bf16[1536,192]{0,1:T(8,128)(2,1)S(1)}, bf16[1536,192]{0,1:T(8,128)(2,1)}, u32[]{:S(2)}, u32[]{:S(2)}) collective-permute-start(bf16[1536,192]{0,1:T(8,128)(2,1)S(1)} %copy.53), channel_id=1, source_target_pairs={{0,2},{1,3},{2,0},{3,1},{4,6},{5,7},{6,4},{7,5},{8,10},{9,11},{10,... | collective-permute-start | bytes 1769480 | tf_op jit(solution)/shard_map/ppermute | solution.py:46
  104.3 10.1 %collective-permute-start.24 = (bf16[96,1536]{1,0:T(8,128)(2,1)}, bf16[96,1536]{1,0:T(8,128)(2,1)S(1)}, u32[]{:S(2)}, u32[]{:S(2)}) collective-permute-start(bf16[96,1536]{1,0:T(8,128)(2,1)} %collective-permute-done.20), channel_id=1, source_target_pairs={{0,4},{4,0},{8,12},{12,8},{16,20},{20,16},{24,28},{28,24},{1,5},{5... | collective-permute-start | bytes 884744 | tf_op jit(solution)/shard_map/ppermute | solution.py:46
  107.2 13.4 %collective-permute-start.25 = (bf16[96,1536]{1,0:T(8,128)(2,1)}, bf16[96,1536]{1,0:T(8,128)(2,1)S(1)}, u32[]{:S(2)}, u32[]{:S(2)}) collective-permute-start(bf16[96,1536]{1,0:T(8,128)(2,1)} %collective-permute-done.21), channel_id=1, source_target_pairs={{0,4},{4,0},{8,12},{12,8},{16,20},{20,16},{24,28},{28,24},{1,5},{5... | collective-permute-start | bytes 884744 | tf_op jit(solution)/shard_map/ppermute | solution.py:46
  114.3 11.9 %collective-permute-start.26 = (bf16[96,1536]{1,0:T(8,128)(2,1)}, bf16[96,1536]{1,0:T(8,128)(2,1)S(1)}, u32[]{:S(2)}, u32[]{:S(2)}) collective-permute-start(bf16[96,1536]{1,0:T(8,128)(2,1)} %collective-permute-done.22), channel_id=1, source_target_pairs={{0,4},{4,0},{8,12},{12,8},{16,20},{20,16},{24,28},{28,24},{1,5},{5... | collective-permute-start | bytes 884744 | tf_op jit(solution)/shard_map/ppermute | solution.py:46
  116.3 16.2 %collective-permute-start.8 = (bf16[1536,192]{0,1:T(8,128)(2,1)S(1)}, bf16[1536,192]{0,1:T(8,128)(2,1)}, u32[]{:S(2)}, u32[]{:S(2)}) collective-permute-start(bf16[1536,192]{0,1:T(8,128)(2,1)S(1)} %copy.53), channel_id=1, source_target_pairs={{0,1},{1,0},{2,3},{3,2},{4,5},{5,4},{6,7},{7,6},{8,9},{9,8},{10,11... | collective-permute-start | bytes 1769480 | tf_op jit(solution)/shard_map/ppermute | solution.py:46
  120.6 17.2 %collective-permute-start.19 = (bf16[768,192]{1,0:T(8,128)(2,1)}, bf16[768,192]{1,0:T(8,128)(2,1)S(1)}, u32[]{:S(2)}, u32[]{:S(2)}) collective-permute-start(bf16[768,192]{1,0:T(8,128)(2,1)} %collective-permute-done.17.o1), channel_id=1, source_target_pairs={{0,1},{1,0},{2,3},{3,2},{4,5},{5,4},{6,7},{7,6},{8,9},{9,8},{10,11... | collective-permute-start | bytes 884744 | tf_op jit(solution)/shard_map/ppermute | solution.py:46
  120.6 14.2 %collective-permute-start.9 = (bf16[1536,192]{0,1:T(8,128)(2,1)}, bf16[1536,192]{0,1:T(8,128)(2,1)}, u32[]{:S(2)}, u32[]{:S(2)}) collective-permute-start(bf16[1536,192]{0,1:T(8,128)(2,1)} %collective-permute-done.7), channel_id=1, source_target_pairs={{0,1},{1,0},{2,3},{3,2},{4,5},{5,4},{6,7},{7,6},{8,9},{9,8},{10,11... | collective-permute-start | bytes 1769480 | tf_op jit(solution)/shard_map/ppermute | solution.py:46
  166.0 40.6 %copy-start.2 = (f32[768,768]{1,0:T(8,128)}, f32[768,768]{1,0:T(8,128)S(1)}, u32[]{:S(2)}) copy-start(f32[768,768]{1,0:T(8,128)S(1)} %get-tuple-element.39.hidden_ref) | copy-start | bytes 7077892
  166.0 9.8 %collective-permute-start.30 = (bf16[768,768]{1,0:T(8,128)(2,1)}, bf16[768,768]{1,0:T(8,128)(2,1)}, u32[]{:S(2)}, u32[]{:S(2)}) collective-permute-start(bf16[768,768]{1,0:T(8,128)(2,1)} %get-tuple-element.42), channel_id=1, source_target_pairs={{0,1},{1,0},{2,3},{3,2},{4,5},{5,4},{6,7},{7,6},{8,9},{9,8},{10,11... | collective-permute-start | bytes 3538952 | tf_op jit(solution)/shard_map/ppermute | solution.py:46
  171.5 44.8 %all-to-all-start.2 = ((bf16[8,96,768]{2,1,0:T(8,128)(2,1)}), bf16[8,96,768]{2,1,0:T(8,128)(2,1)}, u32[]{:S(2)}, u32[]{:S(2)}) async-start(bf16[8,96,768]{2,1,0:T(8,128)(2,1)} %bitcast.30), calls=%async_computation.2 | async-start | bytes 2359296 | tf_op jit(solution)/shard_map/all_to_all | solution.py:69
  178.7 27.8 %collective-permute-start.31 = (bf16[768,768]{1,0:T(8,128)(2,1)}, bf16[768,768]{1,0:T(8,128)(2,1)}, u32[]{:S(2)}, u32[]{:S(2)}) collective-permute-start(bf16[768,768]{1,0:T(8,128)(2,1)} %add_convert_fusion.1.mine_ref), channel_id=1, source_target_pairs={{0,2},{1,3},{2,0},{3,1},{4,6},{5,7},{6,4},{7,5},{8,10},{9,11},{10,... | collective-permute-start | bytes 3538952 | tf_op jit(solution)/shard_map/ppermute | solution.py:46
  184.2 22.3 %copy-start.33 = (bf16[1536,768]{1,0:T(8,128)(2,1)}, bf16[1536,768]{1,0:T(8,128)(2,1)S(1)}, u32[]{:S(2)}) copy-start(bf16[1536,768]{1,0:T(8,128)(2,1)S(1)} %convolution_convert_fusion) | copy-start | bytes 7077892
  184.2 22.3 %copy-start.3 = (bf16[1536,768]{1,0:T(8,128)(2,1)S(1)}, bf16[1536,768]{1,0:T(8,128)(2,1)}, u32[]{:S(2)}) copy-start(bf16[1536,768]{1,0:T(8,128)(2,1)} %grad_ref.3) | copy-start | bytes 7077892
  185.4 37.3 %collective-permute-start.27 = (bf16[768,768]{1,0:T(8,128)(2,1)}, bf16[768,768]{1,0:T(8,128)(2,1)}, u32[]{:S(2)}, u32[]{:S(2)}) collective-permute-start(bf16[768,768]{1,0:T(8,128)(2,1)} %constant_dynamic-slice_fusion), channel_id=1, source_target_pairs={{0,1},{1,0},{2,3},{3,2},{4,5},{5,4},{6,7},{7,6},{8,9},{9,8},{10,11... | collective-permute-start | bytes 3538952 | tf_op jit(solution)/shard_map/ppermute | solution.py:46
  213.1 13.7 %collective-permute-start.32 = (bf16[768,768]{1,0:T(8,128)(2,1)}, bf16[768,768]{1,0:T(8,128)(2,1)}, u32[]{:S(2)}, u32[]{:S(2)}) collective-permute-start(bf16[768,768]{1,0:T(8,128)(2,1)} %get-tuple-element.43), channel_id=1, source_target_pairs={{0,1},{1,0},{2,3},{3,2},{4,5},{5,4},{6,7},{7,6},{8,9},{9,8},{10,11... | collective-permute-start | bytes 3538952 | tf_op jit(solution)/shard_map/ppermute | solution.py:46
  216.4 55.9 %all-to-all-start.3 = ((bf16[8,96,768]{2,1,0:T(8,128)(2,1)}), bf16[8,96,768]{2,1,0:T(8,128)(2,1)}, u32[]{:S(2)}, u32[]{:S(2)}) async-start(bf16[8,96,768]{2,1,0:T(8,128)(2,1)} %bitcast.29), calls=%async_computation.3 | async-start | bytes 2359296 | tf_op jit(solution)/shard_map/all_to_all | solution.py:69
  225.3 53.7 %collective-permute-start.28 = (bf16[768,768]{1,0:T(8,128)(2,1)}, bf16[768,768]{1,0:T(8,128)(2,1)}, u32[]{:S(2)}, u32[]{:S(2)}) collective-permute-start(bf16[768,768]{1,0:T(8,128)(2,1)} %add_convert_fusion.2), channel_id=1, source_target_pairs={{0,2},{1,3},{2,0},{3,1},{4,6},{5,7},{6,4},{7,5},{8,10},{9,11},{10,... | collective-permute-start | bytes 3538952 | tf_op jit(solution)/shard_map/ppermute | solution.py:46
  231.1 28.8 %copy-start.1 = (bf16[1536,768]{1,0:T(8,128)(2,1)S(1)}, bf16[1536,768]{1,0:T(8,128)(2,1)}, u32[]{:S(2)}) copy-start(bf16[1536,768]{1,0:T(8,128)(2,1)} %tokens_ref.7) | copy-start | bytes 7077892
  266.3 16.9 %collective-permute-start.33 = (bf16[768,768]{1,0:T(8,128)(2,1)}, bf16[768,768]{1,0:T(8,128)(2,1)}, u32[]{:S(2)}, u32[]{:S(2)}) collective-permute-start(bf16[768,768]{1,0:T(8,128)(2,1)} %get-tuple-element.49), channel_id=1, source_target_pairs={{0,1},{1,0},{2,3},{3,2},{4,5},{5,4},{6,7},{7,6},{8,9},{9,8},{10,11... | collective-permute-start | bytes 3538952 | tf_op jit(solution)/shard_map/ppermute | solution.py:46
  272.3 31.1 %all-to-all-start = ((bf16[8,96,640]{2,1,0:T(8,128)(2,1)}), bf16[8,96,640]{2,1,0:T(8,128)(2,1)}, u32[]{:S(2)}, u32[]{:S(2)}) async-start(bf16[8,96,640]{2,1,0:T(8,128)(2,1)} %maximum_maximum_fusion), calls=%async_computation | async-start | bytes 1966080 | tf_op jit(solution)/shard_map/all_to_all | solution.py:69
  282.9 26.8 %collective-permute-start.29 = (bf16[768,768]{1,0:T(8,128)(2,1)}, bf16[768,768]{1,0:T(8,128)(2,1)}, u32[]{:S(2)}, u32[]{:S(2)}) collective-permute-start(bf16[768,768]{1,0:T(8,128)(2,1)} %select_convert_fusion), channel_id=1, source_target_pairs={{0,1},{1,0},{2,3},{3,2},{4,5},{5,4},{6,7},{7,6},{8,9},{9,8},{10,11... | collective-permute-start | bytes 3538952 | tf_op jit(solution)/shard_map/ppermute | solution.py:46
  284.8 28.8 %collective-permute-start.34 = (bf16[768,768]{1,0:T(8,128)(2,1)S(1)}, bf16[768,768]{1,0:T(8,128)(2,1)}, u32[]{:S(2)}, u32[]{:S(2)}) collective-permute-start(bf16[768,768]{1,0:T(8,128)(2,1)S(1)} %add_convert_fusion.mine_ref), channel_id=1, source_target_pairs={{0,2},{1,3},{2,0},{3,1},{4,6},{5,7},{6,4},{7,5},{8,10},{9,11},{10,... | collective-permute-start | bytes 3538952 | tf_op jit(solution)/shard_map/ppermute | solution.py:46
  303.4 17.1 %all-to-all-start.1 = ((bf16[8,96,192]{1,2,0:T(8,128)(2,1)}), bf16[8,96,192]{1,2,0:T(8,128)(2,1)}, u32[]{:S(2)}, u32[]{:S(2)}) async-start(bf16[8,96,192]{1,2,0:T(8,128)(2,1)} %copy.62), calls=%async_computation.1 | async-start | bytes 786432 | tf_op jit(solution)/shard_map/all_to_all | solution.py:69
  318.5 8.3 %collective-permute-start.35 = (bf16[768,768]{1,0:T(8,128)(2,1)}, bf16[768,768]{1,0:T(8,128)(2,1)S(1)}, u32[]{:S(2)}, u32[]{:S(2)}) collective-permute-start(bf16[768,768]{1,0:T(8,128)(2,1)} %get-tuple-element.52), channel_id=1, source_target_pairs={{0,1},{1,0},{2,3},{3,2},{4,5},{5,4},{6,7},{7,6},{8,9},{9,8},{10,11... | collective-permute-start | bytes 3538952 | tf_op jit(solution)/shard_map/ppermute | solution.py:46
  319.9 4.2 %collective-permute-start.36 = (f32[96,4]{1,0:T(8,128)S(1)}, f32[96,4]{1,0:T(8,128)S(1)}, u32[]{:S(2)}, u32[]{:S(2)}) collective-permute-start(f32[96,4]{1,0:T(8,128)S(1)} %slice.61), channel_id=1, source_target_pairs={{0,2},{1,3},{2,0},{3,1},{4,6},{5,7},{6,4},{7,5},{8,10},{9,11},{10,... | collective-permute-start | bytes 4616 | tf_op jit(solution)/shard_map/ppermute | solution.py:46
  324.1 1.3 collective-permute-start.37
  (39 other events, 161.1 us)

commit v2 on v1

v2 whole, which is shorter than its diff:
```python
import functools

import jax
import jax.numpy as jnp
from jax import lax
from jax.experimental import pallas as pl
from jax.experimental.pallas import tpu as pltpu
from jax.sharding import PartitionSpec as P

HD = 64
EPSILON = 1e-05
LOG2E = 1.4426950408889634
HUGE = 3e38
FAR = -1e30
LOW = jnp.bfloat16
WIDE = jnp.float32
LANES = 128
BLOCK = 256


def multiply(left, right):
    return lax.dot_general(left, right, (((1,), (0,)), ((), ())), preferred_element_type=WIDE)


def outer_cols(left, right):
    return lax.dot_general(left, right, (((1,), (1,)), ((), ())), preferred_element_type=WIDE)


def inner_rows(left, right):
    return lax.dot_general(left, right, (((0,), (0,)), ((), ())), preferred_element_type=WIDE)


def whole():
    return pl.BlockSpec(memory_space=pltpu.VMEM)


def scalars():
    return pl.BlockSpec(memory_space=pltpu.SMEM)


def struct(shape, dtype):
    return jax.ShapeDtypeStruct(shape, dtype)


def held(shape, dtype):
    return pltpu.VMEM(shape, dtype)


def stored_far(shape, dtype):
    return pltpu.HBM(shape, dtype)


def params(mebibytes):
    return pltpu.CompilerParams(vmem_limit_bytes=mebibytes << 20)


def cost(microseconds):
    return pl.CostEstimate(flops=int(microseconds * 1.1e9), bytes_accessed=0, transcendentals=0)


def after(value, *others):
    return lax.optimization_barrier((value, *others))[0]


def swap(value, axis, bits):
    size = lax.axis_size(axis)
    return lax.ppermute(value, axis, [(i, i ^ bits) for i in range(size)])


def gather_far(shard):
    return [swap(shard, "batch", bits) for bits in (2, 4, 6)]


def pair_sum(keep, send):
    mine = (keep.astype(WIDE) + swap(send, "tensor", 1).astype(WIDE)).astype(LOW)
    return mine, swap(mine, "tensor", 2)


def standardize(values):
    middle = jnp.mean(values, axis=-1, keepdims=True)
    centred = values - middle
    spread = jnp.mean(centred * centred, axis=-1, keepdims=True)
    inverse = lax.rsqrt(spread + EPSILON)
    return centred * inverse, inverse


def standardize_back(grad, scaled, inverse, gain):
    grad = grad * gain
    mean_grad = jnp.mean(grad, axis=-1, keepdims=True)
    mean_cross = jnp.mean(grad * scaled, axis=-1, keepdims=True)
    return inverse * (grad - mean_grad - scaled * mean_cross)


def collect(index, pieces, scratch):
    count = pieces[0].shape[0]
    for bits, piece in enumerate(pieces):
        at = pl.multiple_of((index ^ bits) * count, 32) if len(pieces) > 1 else 0
        scratch[pl.ds(at, count), :] = piece[...]


def project_kernel(scalar_ref, *refs, parts, width):
    pieces, refs = refs[:parts], refs[parts:]
    tokens_ref, normed_ref, projected_ref, rows_ref, weights_ref, outs_ref = refs

    @pl.when(pl.program_id(0) == 0)
    def _():
        collect(scalar_ref[3], pieces, weights_ref)
        rows_ref[...] = jnp.transpose(weights_ref[:, 4 * width : 4 * width + LANES].astype(WIDE))[:8, :]
        outs_ref[...] = jnp.transpose(weights_ref[:, 3 * width : 4 * width])

    scaled, _ = standardize(tokens_ref[...].astype(WIDE))
    normed = (scaled * rows_ref[0:1, :] + rows_ref[2:3, :]).astype(LOW)
    normed_ref[...] = normed
    projected_ref[...] = multiply(normed, weights_ref[:, : 3 * width]).astype(LOW)


def project(scalar, tokens, pieces, width):
    count, depth = tokens.shape
    total = pieces[0].shape[1]
    return pl.pallas_call(
        functools.partial(project_kernel, parts=len(pieces), width=width),
        grid=(count // BLOCK,),
        in_specs=[scalars()]
        + [whole()] * len(pieces)
        + [pl.BlockSpec((BLOCK, depth), lambda i: (i, 0))],
        out_specs=(
            pl.BlockSpec((BLOCK, depth), lambda i: (i, 0)),
            pl.BlockSpec((BLOCK, 3 * width), lambda i: (i, 0)),
            pl.BlockSpec((8, depth), lambda i: (0, 0)),
            pl.BlockSpec((depth, total), lambda i: (0, 0)),
            pl.BlockSpec((width, depth), lambda i: (0, 0)),
        ),
        out_shape=(
            stored_far((count, depth), LOW),
            struct((count, 3 * width), LOW),
            struct((8, depth), WIDE),
            struct((depth, total), LOW),
            struct((width, depth), LOW),
        ),
        compiler_params=params(14),
        cost_estimate=cost(4),
        name="project",
    )(scalar, *pieces, pltpu.with_memory_space_constraint(tokens, pltpu.HBM))


def assemble_kernel(scalar_ref, *refs, parts, units):
    pieces, (up_ref, down_ref) = refs[:parts], refs[parts:]
    count = pieces[0].shape[0]
    for bits, piece in enumerate(pieces):
        at = pl.multiple_of((scalar_ref[3] ^ bits) * count, 32) if parts > 1 else 0
        up_ref[pl.ds(at, count), :] = piece[:, :units]
        down_ref[pl.ds(at, count), :] = piece[:, units:]


def assemble(scalar, pieces, units):
    depth = sum(piece.shape[0] for piece in pieces)
    return pl.pallas_call(
        functools.partial(assemble_kernel, parts=len(pieces), units=units),
        in_specs=[scalars()] + [whole()] * len(pieces),
        out_specs=(whole(),) * 2,
        out_shape=(struct((depth, units), LOW), struct((depth, units), LOW)),
        compiler_params=params(10),
        cost_estimate=cost(1),
        name="assemble",
    )(scalar, *pieces)


def sign_of(scores):
    scores = scores.astype(LOW) * LOW(HUGE)
    return jnp.minimum(jnp.maximum(scores, LOW(-1)), LOW(1))


def attend_kernel(scalar_ref, projected_ref, mixed_ref, sums_ref, *, places, heads, sure):
    length = scalar_ref[1]
    factor = LOG2E * HD**-0.5
    width = heads * HD
    for i, place in enumerate(places):
        row0 = place * BLOCK
        here = slice(row0, row0 + BLOCK)
        row = lax.broadcasted_iota(jnp.int32, (BLOCK, 1), 0) + row0
        key = lax.broadcasted_iota(jnp.int32, (BLOCK, BLOCK), 1) + row0
        allowed = key <= jnp.minimum(row, length - 1)
        def each(function):
            return jnp.concatenate([function(h) for h in range(heads)], axis=0)

        def column(kind, h):
            return slice(kind * width + h * HD, kind * width + (h + 1) * HD)

        def split(value, h):
            return value[h * BLOCK : (h + 1) * BLOCK]

        near = each(lambda h: outer_cols(projected_ref[here, column(0, h)], projected_ref[here, column(1, h)]))
        near_size = jnp.where(jnp.concatenate([allowed] * heads, axis=0), jnp.abs(near) * factor, FAR)
        top = jnp.max(near_size, axis=1, keepdims=True)
        if row0 > 0:
            past = each(lambda h: outer_cols(projected_ref[here, column(0, h)], projected_ref[:row0, column(1, h)]))
            past_size = jnp.abs(past) * factor
            if row0 > sure:
                past_key = lax.broadcasted_iota(jnp.int32, (1, row0), 1)
                past_size = jnp.where(past_key < length, past_size, FAR)
            top = jnp.maximum(top, jnp.max(past_size, axis=1, keepdims=True))
            past_prob = jnp.exp2(past_size - top)
            past_signed = past_prob.astype(LOW) * sign_of(past)
        near_prob = jnp.exp2(near_size - top)
        near_signed = near_prob.astype(LOW) * sign_of(near)
        total = jnp.sum(near_prob, axis=1, keepdims=True)
        mixed = each(lambda h: multiply(split(near_signed, h), projected_ref[here, column(2, h)]))
        if row0 > 0:
            total = total + jnp.sum(past_prob, axis=1, keepdims=True)
            mixed = mixed + each(lambda h: multiply(split(past_signed, h), projected_ref[:row0, column(2, h)]))
        mixed = (mixed / total).astype(LOW)
        logs = top + jnp.log2(total)
        outs = [split(mixed, h) for h in range(heads)]
        sums = [split(logs, h) for h in range(heads)]
        part = slice(i * BLOCK, (i + 1) * BLOCK)
        mixed_ref[:, part] = jnp.transpose(jnp.concatenate(outs, axis=1))
        blank = jnp.zeros((BLOCK, LANES - heads), WIDE)
        sums_ref[i] = jnp.transpose(jnp.concatenate(sums + [blank], axis=1))[:8, :]


def attend(scalar, projected, places, sure):
    width = projected.shape[1] // 3
    heads = width // HD
    return pl.pallas_call(
        functools.partial(attend_kernel, places=places, heads=heads, sure=sure),
        in_specs=[scalars(), whole()],
        out_specs=(whole(), whole()),
        out_shape=(struct((width, len(places) * BLOCK), LOW), struct((len(places), 8, BLOCK), WIDE)),
        compiler_params=params(16),
        cost_estimate=cost(sum(places) / 2 + 1),
        name="attend_forward",
    )(scalar, projected)


def attend_back_kernel(scalar_ref, *refs, chunks, rows, heads, sure):
    length = scalar_ref[1]
    core = scalar_ref[0]
    projected_ref, outs_ref, refs = refs[0], refs[1], refs[2:]
    mixed_refs, refs = refs[: len(chunks)], refs[len(chunks) :]
    sums_refs, refs = refs[: len(chunks)], refs[len(chunks) :]
    grad_refs, refs = refs[: 2 * len(chunks)], refs[2 * len(chunks) :]
    grads_ref, outs_grad_ref, whole_ref, grad_mixed, delta, logs, dq_turned = refs
    scaling = HD**-0.5
    factor = LOG2E * scaling
    width = heads * HD
    blocks = rows // BLOCK
    outs_grad = jnp.zeros(outs_ref.shape, WIDE)
    half = blocks // 2
    for number, (begin, size) in enumerate(chunks):
        for side in range(2):
            for k in range(size // BLOCK):
                local = side * size + k * BLOCK
                inside = slice(local, local + BLOCK)
                i = side * half + begin // BLOCK + k
                rows_i = slice(i * BLOCK, (i + 1) * BLOCK)
                mine = grad_refs[2 * number][k * BLOCK : (k + 1) * BLOCK, :]
                other = grad_refs[2 * number + 1][k * BLOCK : (k + 1) * BLOCK, :]

                @pl.when(core == side)
                def _():
                    whole_ref[rows_i, :] = mine

                @pl.when(core != side)
                def _():
                    whole_ref[rows_i, :] = other

                grad = whole_ref[rows_i, :]
                mixed = mixed_refs[number][:, inside]
                outs_grad = outs_grad + multiply(mixed, grad)
                turned = outer_cols(outs_ref[...], grad)
                grad_mixed[rows_i, :] = jnp.transpose(turned).astype(LOW)
                logs[:, rows_i] = sums_refs[number][local // BLOCK]
                both = turned.astype(LOW).astype(WIDE) * mixed.astype(WIDE)
                for h in range(heads):
                    delta[h : h + 1, rows_i] = jnp.sum(both[h * HD : (h + 1) * HD, :], axis=0, keepdims=True)
    outs_grad_ref[...] = jnp.transpose(outs_grad).astype(LOW)
    for j in range(blocks):
        here = slice(j * BLOCK, (j + 1) * BLOCK)
        later = slice((j + 1) * BLOCK, rows)
        dks, dvs = [], []
        for h in range(heads):
            cols = slice(h * HD, (h + 1) * HD)
            k = projected_ref[here, width + h * HD : width + (h + 1) * HD]
            v = projected_ref[here, 2 * width + h * HD : 2 * width + (h + 1) * HD]
            dk = jnp.zeros((BLOCK, HD), WIDE)
            dv = jnp.zeros((BLOCK, HD), WIDE)
            for part in (here, later):
                span = part.stop - part.start
                if span == 0:
                    continue
                q = projected_ref[part, cols]
                g = grad_mixed[part, cols]
                scores = outer_cols(k, q)
                grad_weights = outer_cols(v, g)
                reach = jnp.abs(scores) * factor - logs[h : h + 1, part]
                if part is here:
                    key = lax.broadcasted_iota(jnp.int32, (BLOCK, span), 0) + j * BLOCK
                    row = lax.broadcasted_iota(jnp.int32, (1, span), 1) + j * BLOCK
                    reach = jnp.where(key <= jnp.minimum(row, length - 1), reach, FAR)
                elif (j + 1) * BLOCK > sure:
                    key = lax.broadcasted_iota(jnp.int32, (BLOCK, 1), 0) + j * BLOCK
                    reach = jnp.where(key < length, reach, FAR)
                sign = sign_of(scores)
                weights = jnp.exp2(reach)
                signed = sign.astype(WIDE)
                raw = (weights * (grad_weights - signed * delta[h : h + 1, part])).astype(LOW) * (sign * sign)
                dv = dv + multiply(weights.astype(LOW) * sign, g)
                dk = dk + multiply(raw, q)
                more = inner_rows(k, raw)
                if j == 0:
                    dq_turned[cols, part] = more
                else:
                    dq_turned[cols, part] += more
            dks.append(dk * scaling)
            dvs.append(dv)
        grads_ref[:width, here] = (dq_turned[:, here] * scaling).astype(LOW)
        grads_ref[width : 2 * width, here] = jnp.transpose(jnp.concatenate(dks, axis=1)).astype(LOW)
        grads_ref[2 * width :, here] = jnp.transpose(jnp.concatenate(dvs, axis=1)).astype(LOW)


def attend_back(scalar, projected, outs, mixed, sums, grads, chunks, sure):
    rows = projected.shape[0]
    width = projected.shape[1] // 3
    depth = outs.shape[1]
    heads = width // HD
    return pl.pallas_call(
        functools.partial(attend_back_kernel, chunks=chunks, rows=rows, heads=heads, sure=sure),
        in_specs=[scalars()] + [whole()] * (2 + 4 * len(chunks)),
        out_specs=(whole(),) * 3,
        out_shape=(struct((3 * width, rows), LOW), struct((depth, width), LOW), struct((rows, depth), LOW)),
        scratch_shapes=[
            pltpu.VMEM((rows, width), LOW),
            pltpu.VMEM((8, rows), WIDE),
            pltpu.VMEM((8, rows), WIDE),
            pltpu.VMEM((width, rows), WIDE),
        ],
        compiler_params=params(24),
        cost_estimate=cost(8),
        name="attend_backward",
    )(scalar, projected, outs, *mixed, *sums, *grads)


def gelu_pair(up):
    root = 0.7978845608028654
    square = up * up
    bent = jnp.tanh(up * (root + (root * 0.044715) * square))
    half = 0.5 * bent + 0.5
    slope = half + (0.5 * up) * (1.0 - bent * bent) * (root + (3 * root * 0.044715) * square)
    return up * half, slope


def feed_kernel(scalar_ref, *refs, begin, half, keep, given):
    tokens_ref, grad_ref, m0, m1, m2, m3, o0, o1, o2, o3, up_ref, down_ref, rows_ref = refs[:13]
    results = refs[13 + given : -1]
    back_ref, sums_ref, normed_ref, active_ref, upper_ref = results[:5]
    mixed_ref = refs[-1]
    i = pl.program_id(0)
    place = scalar_ref[0] if keep else 1 - scalar_ref[0]
    row0 = begin + place * half + i * BLOCK
    row = lax.broadcasted_iota(jnp.int32, (BLOCK, 1), 0) + row0

    @pl.when(scalar_ref[2] == 0)
    def _():
        across = inner_rows(m0[...], o0[...]) + inner_rows(m1[...], o1[...])
        mixed_ref[...] = across + inner_rows(m2[...], o2[...]) + inner_rows(m3[...], o3[...])

    @pl.when(scalar_ref[2] != 0)
    def _():
        across = inner_rows(m1[...], o1[...]) + inner_rows(m0[...], o0[...])
        mixed_ref[...] = across + inner_rows(m3[...], o3[...]) + inner_rows(m2[...], o2[...])

    hidden = tokens_ref[...].astype(WIDE) + mixed_ref[...]
    if keep:
        results[5][...] = hidden
    scaled, _ = standardize(hidden)
    normed = (scaled * rows_ref[1:2, :] + rows_ref[3:4, :]).astype(LOW)
    normed_ref[...] = normed
    grad = jnp.where(row < scalar_ref[1], grad_ref[...].astype(WIDE), 0.0).astype(LOW)
    back = jnp.zeros(hidden.shape, WIDE)
    units = up_ref.shape[1]
    for first in range(0, units, BLOCK):
        part = slice(first, first + BLOCK)
        active, slope = gelu_pair(multiply(normed, up_ref[:, part]))
        active_ref[:, part] = active.astype(LOW)
        upper = (multiply(grad, down_ref[:, part]) * slope).astype(LOW)
        upper_ref[:, part] = upper
        back = back + outer_cols(upper, up_ref[:, part])
    back_ref[...] = back.astype(LOW)

    @pl.when(i == 0)
    def _():
        sums_ref[...] = jnp.zeros_like(sums_ref)

    sums_ref[0:1, :] += jnp.sum(back * scaled, axis=0, keepdims=True)
    sums_ref[1:2, :] += jnp.sum(back, axis=0, keepdims=True)


def feed(scalar, tokens, out_grad, mixed, outs, up, down, rows, stored, begin, size, keep):
    count, depth = tokens.shape
    units = up.shape[1]
    width = outs[0].shape[0]
    half = count // 2
    base = begin // BLOCK
    blocks = size // BLOCK

    def side(scalar_ref):
        return scalar_ref[0] if keep else 1 - scalar_ref[0]

    def placed(i, scalar_ref):
        return (base + side(scalar_ref) * (half // BLOCK) + i, 0)

    def inside(i, scalar_ref):
        return (0, side(scalar_ref) * blocks + i)

    def own(i, scalar_ref):
        return (i, 0)

    def kept(i, scalar_ref):
        return (base + i, 0)

    def fixed(i, scalar_ref):
        return (0, 0)

    out_specs = (
        pl.BlockSpec((BLOCK, depth), own),
        pl.BlockSpec((8, depth), fixed),
        pl.BlockSpec((BLOCK, depth), placed),
        pl.BlockSpec((BLOCK, units), placed),
        pl.BlockSpec((BLOCK, units), placed),
        pl.BlockSpec((BLOCK, depth), kept),
    )
    out_shape = (
        struct((size, depth), LOW),
        struct((8, depth), WIDE),
        struct((count, depth), LOW),
        struct((count, units), LOW),
        struct((count, units), LOW),
        struct((half, depth), WIDE),
    )[: 6 if keep else 5]
    stored = stored[: len(out_shape) - 2]
    return pl.pallas_call(
        functools.partial(feed_kernel, begin=begin, half=half, keep=keep, given=len(stored)),
        grid_spec=pltpu.PrefetchScalarGridSpec(
            num_scalar_prefetch=1,
            grid=(blocks,),
            in_specs=[pl.BlockSpec((BLOCK, depth), placed)] * 2
            + [pl.BlockSpec((width, BLOCK), inside)] * 4
            + [whole()] * 7
            + [pl.BlockSpec(memory_space=pl.ANY)] * len(stored),
            out_specs=out_specs[: len(out_shape)],
            scratch_shapes=[pltpu.VMEM((BLOCK, depth), WIDE)],
        ),
        out_shape=out_shape,
        input_output_aliases={14 + k: 2 + k for k in range(len(stored))},
        compiler_params=params(20),
        cost_estimate=cost(size / 100),
        name="feed_forward",
    )(scalar, tokens, out_grad, *mixed, *outs, up, down, rows, *stored)


def weigh_kernel(scalar_ref, normed_ref, upper_ref, active_ref, grad_ref, down_ref, keep_ref, send_ref, grads_ref, up_sum, down_sum, *, blocks):
    i = pl.program_id(0)
    half = blocks // 2
    units = down_ref.shape[1]
    row0 = lax.rem(i + (1 - scalar_ref[0]) * half, blocks) * BLOCK
    row = lax.broadcasted_iota(jnp.int32, (BLOCK, 1), 0) + row0
    branch = outer_cols(active_ref[...], down_ref[...]).astype(LOW)

    @pl.when(i < half)
    def _():
        send_ref[...] = branch

    @pl.when(i >= half)
    def _():
        keep_ref[...] = branch

    grad = jnp.where(row < scalar_ref[1], grad_ref[...].astype(WIDE), 0.0).astype(LOW)

    @pl.when(i == 0)
    def _():
        up_sum[...] = jnp.zeros_like(up_sum)
        down_sum[...] = jnp.zeros_like(down_sum)

    up_sum[...] += inner_rows(normed_ref[...], upper_ref[...])
    down_sum[...] += inner_rows(grad, active_ref[...])

    @pl.when(i == blocks - 1)
    def _():
        grads_ref[:, :units] = up_sum[...].astype(LOW)
        grads_ref[:, units:] = down_sum[...].astype(LOW)


def weigh(scalar, normed, upper, active, out_grad, down):
    count, depth = normed.shape
    units = down.shape[1]
    blocks = count // BLOCK
    half = blocks // 2

    def turned(i, scalar_ref):
        return (lax.rem(i + (1 - scalar_ref[0]) * half, blocks), 0)

    return pl.pallas_call(
        functools.partial(weigh_kernel, blocks=blocks),
        grid_spec=pltpu.PrefetchScalarGridSpec(
            num_scalar_prefetch=1,
            grid=(blocks,),
            in_specs=[pl.BlockSpec((BLOCK, depth), turned)] * 4 + [whole()],
            out_specs=(
                pl.BlockSpec((BLOCK, depth), lambda i, s: (jnp.maximum(i - half, 0), 0)),
                pl.BlockSpec((BLOCK, depth), lambda i, s: (jnp.minimum(i, half - 1), 0)),
                pl.BlockSpec((depth, 2 * units), lambda i, s: (0, 0)),
            ),
            scratch_shapes=[pltpu.VMEM((depth, units), WIDE)] * 2,
        ),
        out_shape=(
            struct((count // 2, depth), LOW),
            struct((count // 2, depth), LOW),
            struct((depth, 2 * units), LOW),
        ),
        compiler_params=params(24),
        cost_estimate=cost(1),
        name="feed_forward_weights",
    )(scalar, normed, upper, active, out_grad, down)


def second_back_kernel(scalar_ref, mine_ref, other_ref, hidden_ref, grad_ref, rows_ref, low_ref, *, begin, half):
    row0 = begin + scalar_ref[0] * half + pl.program_id(0) * BLOCK
    row = lax.broadcasted_iota(jnp.int32, (BLOCK, 1), 0) + row0
    grad_normed = mine_ref[...].astype(WIDE) + other_ref[...].astype(WIDE)
    scaled, inverse = standardize(hidden_ref[...])
    grad = jnp.where(row < scalar_ref[1], grad_ref[...].astype(WIDE), 0.0)
    grad = grad + standardize_back(grad_normed, scaled, inverse, rows_ref[1:2, :])
    low_ref[...] = grad.astype(LOW)


def second_back(scalar, mine, other, hidden, out_grad, rows, begin, size):
    half, depth = hidden.shape
    base = begin // BLOCK

    def own(i, scalar_ref):
        return (i, 0)

    def kept(i, scalar_ref):
        return (base + i, 0)

    def placed(i, scalar_ref):
        return (base + i + scalar_ref[0] * (half // BLOCK), 0)

    return pl.pallas_call(
        functools.partial(second_back_kernel, begin=begin, half=half),
        grid_spec=pltpu.PrefetchScalarGridSpec(
            num_scalar_prefetch=1,
            grid=(size // BLOCK,),
            in_specs=[pl.BlockSpec((BLOCK, depth), own)] * 2
            + [pl.BlockSpec((BLOCK, depth), kept), pl.BlockSpec((BLOCK, depth), placed), whole()],
            out_specs=pl.BlockSpec((BLOCK, depth), own),
        ),
        out_shape=struct((size, depth), LOW),
        compiler_params=params(12),
        cost_estimate=cost(size / 1000),
        name="second_norm_backward",
    )(scalar, mine, other, hidden, out_grad, rows)


def inward_kernel(scalar_ref, grads_ref, tokens_ref, weights_ref, back_ref, sums_ref):
    i = pl.program_id(0)
    width = grads_ref.shape[0]
    back = lax.dot_general(
        grads_ref[...], weights_ref[:, :width], (((0,), (1,)), ((), ())), preferred_element_type=WIDE
    )
    scaled, _ = standardize(tokens_ref[...].astype(WIDE))
    back_ref[...] = back.astype(LOW)

    @pl.when(i == 0)
    def _():
        sums_ref[...] = jnp.zeros_like(sums_ref)

    sums_ref[0:1, :] += jnp.sum(back * scaled, axis=0, keepdims=True)
    sums_ref[1:2, :] += jnp.sum(back, axis=0, keepdims=True)


def inward(scalar, grads, tokens, weights, begin, half, keep):
    depth = tokens.shape[1]
    width = grads.shape[0]
    blocks = half // BLOCK

    def placed(i, scalar_ref):
        place = scalar_ref[0] if keep else 1 - scalar_ref[0]
        return (begin // BLOCK + place * blocks + i, 0)

    def lanes(i, scalar_ref):
        return placed(i, scalar_ref)[::-1]

    return pl.pallas_call(
        inward_kernel,
        grid_spec=pltpu.PrefetchScalarGridSpec(
            num_scalar_prefetch=1,
            grid=(blocks,),
            in_specs=[pl.BlockSpec((width, BLOCK), lanes), pl.BlockSpec((BLOCK, depth), placed), whole()],
            out_specs=(
                pl.BlockSpec((BLOCK, depth), lambda i, s: (i, 0)),
                pl.BlockSpec((8, depth), lambda i, s: (0, 0)),
            ),
        ),
        out_shape=(struct((half, depth), LOW), struct((8, depth), WIDE)),
        compiler_params=params(12),
        cost_estimate=cost(3),
        name="grad_normed",
    )(scalar, grads, tokens, weights)


def project_back_kernel(grads_ref, normed_ref, outs_ref, *refs, width, split):
    sums, out_ref = refs[:-1], refs[-1]
    last = out_ref.shape[1] - outs_ref.shape[1]
    out_ref[:, last:] = outs_ref[...]
    out_ref[:, :width] = jnp.transpose(multiply(grads_ref[...], normed_ref[...])).astype(LOW)
    ones, twos = sums[:split], sums[split:]
    one = sum(ref[...] for ref in ones[1:]) + ones[0][...]
    two = sum(ref[...] for ref in twos[1:]) + twos[0][...]
    rows = jnp.concatenate([one, two, jnp.zeros((LANES - 16, one.shape[1]), WIDE)], axis=0)
    out_ref[:, width:last] = jnp.transpose(rows)[:, : last - width].astype(LOW)


def project_back(grads, normed, outs_grad, ones, twos):
    width = grads.shape[0]
    depth = normed.shape[1]
    sums = list(ones) + list(twos)
    return pl.pallas_call(
        functools.partial(project_back_kernel, width=width, split=len(ones)),
        in_specs=[whole()] * (3 + len(sums)),
        out_specs=whole(),
        out_shape=struct((depth, width + -width % LANES + outs_grad.shape[1]), LOW),
        compiler_params=params(16),
        cost_estimate=cost(3),
        name="projection_weights",
    )(grads, normed, outs_grad, *sums)


def finish_kernel(scalar_ref, mine_ref, other_ref, hidden_ref, own_ref, full_ref, *, begin, half):
    row0 = begin + scalar_ref[0] * half + pl.program_id(0) * BLOCK
    row = lax.broadcasted_iota(jnp.int32, (BLOCK, 1), 0) + row0
    total = hidden_ref[...] + (mine_ref[...].astype(WIDE) + other_ref[...].astype(WIDE))
    low = jnp.where(row < scalar_ref[1], total, 0.0).astype(LOW)
    own_ref[...] = low
    full_ref[...] = low


def first_back_kernel(scalar_ref, mine_ref, other_ref, tokens_ref, grad_ref, rows_ref, own_ref, full_ref):
    grad_normed = mine_ref[...].astype(WIDE) + other_ref[...].astype(WIDE)
    scaled, inverse = standardize(tokens_ref[...].astype(WIDE))
    grad = grad_ref[...].astype(WIDE) + standardize_back(grad_normed, scaled, inverse, rows_ref[0:1, :])
    low = grad.astype(LOW)
    own_ref[...] = low
    full_ref[...] = low


def place_rows(kernel, scalar, owned, spread, fixed, count, begin, half, name):
    depth = owned[0].shape[1]
    blocks = half // BLOCK

    def own(i, scalar_ref):
        return (i, 0)

    def placed(i, scalar_ref):
        return (begin // BLOCK + i + scalar_ref[0] * blocks, 0)

    return pl.pallas_call(
        kernel,
        grid_spec=pltpu.PrefetchScalarGridSpec(
            num_scalar_prefetch=1,
            grid=(blocks,),
            in_specs=[pl.BlockSpec((BLOCK, depth), own)] * 2
            + [pl.BlockSpec((BLOCK, depth), placed)] * len(spread)
            + [pl.BlockSpec((BLOCK, depth), own)] * (len(owned) - 2)
            + [whole()] * len(fixed),
            out_specs=(pl.BlockSpec((BLOCK, depth), own), pl.BlockSpec((BLOCK, depth), placed)),
        ),
        out_shape=(struct((half, depth), LOW), struct((count, depth), LOW)),
        compiler_params=params(12),
        cost_estimate=cost(3),
        name=name,
    )(scalar, *owned[:2], *spread, *owned[2:], *fixed)


def total_kernel(parts_ref, *outs, bounds, flips):
    total = parts_ref[0].astype(WIDE)
    for k in range(1, parts_ref.shape[0]):
        total = total + parts_ref[k].astype(WIDE)
    for out, (first, last), flip in zip(outs, bounds, flips):
        piece = total[:, first:last]
        out[...] = jnp.transpose(piece) if flip else piece


def total_parts(parts, bounds, flips):
    rows = parts.shape[1]
    shapes = []
    for (first, last), flip in zip(bounds, flips):
        shape = (last - first, rows) if flip else (rows, last - first)
        shapes.append(struct(shape, WIDE))
    return pl.pallas_call(
        functools.partial(total_kernel, bounds=bounds, flips=flips),
        in_specs=[whole()],
        out_specs=(whole(),) * len(shapes),
        out_shape=tuple(shapes),
        compiler_params=params(8),
        cost_estimate=cost(1),
        name="total",
    )(parts)


def exchange_batch(value):
    size = lax.axis_size("batch")
    parts = value.reshape(size, value.shape[0] // size, value.shape[1])
    return lax.all_to_all(parts, "batch", 0, 0, tiled=True)


def per_device(tokens, lengths, w_query, w_key, w_value, w_out, w_up, w_down, norm_gain, norm_shift, out_grad):
    count, depth = tokens.shape
    batch = lax.axis_size("batch")
    if lengths.shape[0] != 1 or lax.axis_size("tensor") != 4:
        raise ValueError("unsupported mesh")
    width = w_query.shape[1]
    units = w_up.shape[1]
    tensor = lax.axis_index("tensor").astype(jnp.int32)
    core = tensor & 1
    scalar = jnp.stack([core, lengths[0], tensor >> 1, lax.axis_index("batch").astype(jnp.int32)])
    sure = 2 * count // 3
    half = count // 2
    first = half // 3 * 2
    chunks = ((0, first), (first, half - first))

    blank = jnp.zeros((w_query.shape[0], -(4 * width + 4) % LANES), LOW)
    early = jnp.concatenate([w_query, w_key, w_value, w_out.T, norm_gain.T, norm_shift.T, blank], axis=1)
    late = jnp.concatenate([w_up, w_down.T], axis=1)
    if batch == 8:
        far = gather_far(early)
        early = [early, swap(early, "batch", 1)]
        for piece in far:
            early += [piece, swap(piece, "batch", 1)]
        late = after(late, *far)
        near = swap(late, "batch", 2)
        middle = swap(late, "batch", 4)
        far = swap(middle, "batch", 2)
        late = [late, swap(late, "batch", 1)]
        for piece in (near, middle, far):
            late += [piece, swap(piece, "batch", 1)]
    else:
        early = [lax.all_gather(early, "batch", axis=0, tiled=True)]
        late = [lax.all_gather(late, "batch", axis=0, tiled=True)]

    normed, projected, rows, weights, own_outs = project(scalar, tokens, early, width)
    across = swap(own_outs, "tensor", 2)
    outs = (own_outs, across, swap(own_outs, "tensor", 1), swap(across, "tensor", 1))
    mixed, sums, pieces = [], [], []
    for begin, size in chunks:
        local = tuple(range(begin // BLOCK, (begin + size) // BLOCK))
        part, logs = attend(scalar, projected, local + tuple(k + half // BLOCK for k in local), sure)
        projected = after(projected, part)
        mixed.append(part)
        sums.append(logs)
        across = swap(part, "tensor", 2)
        pieces.append((part, across, swap(part, "tensor", 1), swap(across, "tensor", 1)))
    late = lax.optimization_barrier((*late, *pieces[-1]))[: len(late)]
    full_up, full_down = assemble(scalar, late, units)

    stored = []
    twos, halves = [], []
    for (begin, size), piece in zip(chunks, pieces):
        ends = []
        rows = after(rows, *(mine for mine, _ in halves))
        for keep in (False, True):
            back, two, *fresh = feed(
                scalar, tokens, out_grad, piece, outs, full_up, full_down, rows, stored, begin, size, keep
            )
            stored = fresh + stored[len(fresh) :]
            twos.append(two)
            ends.append(back)
        mine = (ends[1].astype(WIDE) + swap(ends[0], "tensor", 1).astype(WIDE)).astype(LOW)
        halves.append((mine, swap(mine, "tensor", 2)))
    normed_two, active, upper, hidden = stored
    normed_two = after(normed_two, *(mine for mine, _ in halves))
    branch_keep, branch_send, feed_grads = weigh(scalar, normed_two, upper, active, out_grad, full_down)
    feed_parts = exchange_batch(feed_grads)

    beside = swap(branch_send, "tensor", 1)
    grads = []
    for (begin, size), (mine, other) in zip(chunks, halves):
        mine = after(mine, feed_grads)
        low = second_back(scalar, mine, other, hidden, out_grad, rows, begin, size)
        grads += [low, swap(low, "tensor", 1)]
    branch_mine = (branch_keep.astype(WIDE) + beside.astype(WIDE)).astype(LOW)
    branch_mine = after(branch_mine, *grads)
    branch_other = swap(branch_mine, "tensor", 2)
    projected = after(projected, branch_mine)
    attend_grads, outs_grad, grad_attn = attend_back(
        scalar, projected, own_outs, mixed, sums, grads, chunks, sure
    )

    own_out, layer_out = place_rows(
        functools.partial(finish_kernel, begin=0, half=half),
        scalar,
        (branch_mine, branch_other, hidden),
        (),
        (),
        count,
        0,
        half,
        "layer_out",
    )
    there = (1 - core) * half
    layer_out = lax.dynamic_update_slice(layer_out, swap(own_out, "tensor", 1), (there, 0))

    ends, ones = [], []
    attend_grads = after(attend_grads, branch_other)
    for keep in (False, True):
        back, one = inward(scalar, attend_grads, tokens, weights, 0, half, keep)
        ends.append(back)
        ones.append(one)
    back = pair_sum(ends[1], ends[0])
    project_parts = exchange_batch(after(project_back(attend_grads, normed, outs_grad, ones, twos), feed_parts))
    own_grad, grad_input = place_rows(
        first_back_kernel, scalar, back, (tokens, grad_attn), (rows,), count, 0, half, "first_norm_backward"
    )
    grad_input = lax.dynamic_update_slice(grad_input, swap(own_grad, "tensor", 1), (there, 0))

    shard_up, shard_down = total_parts(feed_parts, ((0, units), (units, 2 * units)), (False, True))
    last = 3 * width
    final = project_parts.shape[2]
    shard_query, shard_key, shard_value, small, shard_out = total_parts(
        project_parts,
        ((0, width), (width, 2 * width), (2 * width, last), (last, final - width), (final - width, final)),
        (False, False, False, True, True),
    )
    small = small[:16]
    small = small + swap(small, "tensor", 2)
    small = small + swap(small, "tensor", 1)
    shard_gain = jnp.stack([small[0], small[8]])
    shard_shift = jnp.stack([small[1], small[9]])
    return (
        layer_out,
        grad_input,
        shard_query,
        shard_key,
        shard_value,
        shard_out,
        shard_up,
        shard_down,
        shard_gain,
        shard_shift,
    )


def solution(mesh):
    tall = P("batch", "tensor")
    wide = P("tensor", "batch")
    rows = P("batch", None)
    pair = P(None, "batch")
    return jax.shard_map(
        per_device,
        mesh=mesh,
        in_specs=(rows, P("batch"), tall, tall, tall, wide, tall, wide, pair, pair, rows),
        out_specs=(rows, rows, tall, tall, tall, wide, tall, wide, pair, pair),
        check_vma=False,
    )
```

time: 333 us -> 236 us (0.71)
  local copies, waits for them, and re-layouts: 63.5 us -> 16.8 us
  Pallas kernels: 69.8 us -> 102 us
  matrix products: 24.2 us -> 0 us
  other arithmetic: 24.6 us -> 4.99 us
  waiting for transfers between devices: 84 us -> 64.6 us
  starting transfers between devices: 60 us -> 41 us
    pallas_call x7 -> x19, Pallas kernels: 69.8 us -> 102 us  [the longest x4 29 us: feed(): pl.pallas_call(functools.partial(feed_kernel, begin=begin, half=half, kee...]
    ppermute x38 -> x37, waiting for transfers between devices: 76.2 us -> 50 us  [swap(): return lax.ppermute(value, axis, [(i, i ^ bits) for i in range(size)])]
    dot_general x6 -> x0, matrix products: 24.2 us -> none  [the longest x4 15.9 us: inner_rows(): lax.dot_general(left, right, (((0,), (0,)), ((), ())), preferred_element_...]
    dynamic_update_slice x24 -> x2, local copies, waits for them, and re-layouts: 16.9 us -> 3.46 us  [the longest x1 2.37 us: per_device(): lax.dynamic_update_slice(layer_out, swap(own_out, 'tensor', 1), (there, 0))]
    all_to_all x4 -> x2, starting transfers between devices: 20.6 us -> 8.79 us  [exchange_batch(): return lax.all_to_all(parts, 'batch', 0, 0, tiled=True)]
    unnamed x95 -> x86, local copies, waits for them, and re-layouts: 22.8 us -> 12.4 us
    reduce_sum x4 -> x0, other arithmetic: 7.41 us -> none  [scatter_batch(): return jnp.sum(parts.astype(WIDE), axis=0)]
    ppermute x38 -> x37, starting transfers between devices: 39.5 us -> 32.3 us  [swap(): return lax.ppermute(value, axis, [(i, i ^ bits) for i in range(size)])]
  transfers between devices with their start and end apart: 42 -> 39, of which waited for: 18 -> 14; matrix products, arithmetic and copies ran while one was open for 27% -> 4% of each run, Pallas kernels for 16% -> 35%
where the time goes in v2:
time: 236 us; the launch traced here: 232 us
  Pallas kernels  102 us (43%)
  waiting for transfers between devices  64.6 us (27%)
  starting transfers between devices  41 us (17%)
  local copies, waits for them, and re-layouts  16.8 us (7%)
  other arithmetic  4.99 us (2%)
    ppermute x37, waiting for transfers between devices, swap(): return lax.ppermute(value, axis, [(i, i ^ bits) for i in range(size)])  50 us
    ppermute x37, starting transfers between devices, swap(): return lax.ppermute(value, axis, [(i, i ^ bits) for i in range(size)])  32.3 us
    pallas_call x4, Pallas kernels, feed(): pl.pallas_call(functools.partial(feed_kernel, begin=begin, half=half, kee...  29 us
    pallas_call x1, Pallas kernels, attend_back(): pl.pallas_call(functools.partial(attend_back_kernel, chunks=chunks, rows=...  18.1 us
    all_to_all x2, waiting for transfers between devices, exchange_batch(): return lax.all_to_all(parts, 'batch', 0, 0, tiled=True)  14.6 us
    unnamed x86, local copies, waits for them, and re-layouts  12.4 us
    pallas_call x1, Pallas kernels, weigh(): pl.pallas_call(functools.partial(weigh_kernel, blocks=blocks), grid_spec=...  11.8 us
    pallas_call x2, Pallas kernels, attend(): pl.pallas_call(functools.partial(attend_kernel, places=places, heads=head...  10.9 us
  transfers between devices with their start and end apart: 39, of which 14 were waited for; matrix products, arithmetic and copies ran while one was open for 4% of the time, Pallas kernels for 35%

profile of v2, /device:TPU:0, one launch (start us, length us, event | category | flops | bytes accessed | tf_op | source)
XLA Modules:
  0.0 231.6 jit_solution(5743169838776275862)
XLA Ops:
  4.1 5.1 %collective-permute-start.5 = (bf16[96,896]{1,0:T(8,128)(2,1)S(1)}, bf16[96,896]{1,0:T(8,128)(2,1)S(1)}, u32[]{:S(2)}, u32[]{:S(2)}) collective-permute-start(bf16[96,896]{1,0:T(8,128)(2,1)S(1)} %concatenate.6.refs_0_), channel_id=1, source_target_pairs={{0,24},{4,28},{8,16},{12,20},{16,8},{20,12},{24,0},{28,4},{1,25},{... | collective-permute-start | bytes 516104 | tf_op jit(solution)/shard_map/ppermute | solution.py:67
  9.9 1.7 collective-permute-start
  11.5 3.0 %collective-permute-done.5.refs_6_ = bf16[96,896]{1,0:T(8,128)(2,1)S(1)} collective-permute-done((bf16[96,896]{1,0:T(8,128)(2,1)S(1)}, bf16[96,896]{1,0:T(8,128)(2,1)S(1)}, u32[]{:S(2)}, u32[]{:S(2)}) %collective-permute-start.5) | collective-permute-done | bytes 172064 | tf_op jit(solution)/shard_map/ppermute | solution.py:67
  14.5 1.7 collective-permute-start.6
  16.2 7.6 %collective-permute-done.3.refs_4_ = bf16[96,896]{1,0:T(8,128)(2,1)S(1)} collective-permute-done((bf16[96,896]{1,0:T(8,128)(2,1)S(1)}, bf16[96,896]{1,0:T(8,128)(2,1)S(1)}, u32[]{:S(2)}, u32[]{:S(2)}) %collective-permute-start.3) | collective-permute-done | bytes 172064 | tf_op jit(solution)/shard_map/ppermute | solution.py:67
  23.8 1.5 collective-permute-start.4
  28.1 2.5 %collective-permute-start.14 = (bf16[96,1536]{1,0:T(8,128)(2,1)S(1)}, bf16[96,1536]{1,0:T(8,128)(2,1)S(1)}, u32[]{:S(2)}, u32[]{:S(2)}) collective-permute-start(bf16[96,1536]{1,0:T(8,128)(2,1)S(1)} %pad_maximum_fusion.refs_0_), channel_id=1, source_target_pairs={{0,8},{4,12},{8,0},{12,4},{16,24},{20,28},{24,16},{28,20},{1,9},{5... | collective-permute-start | bytes 884744 | tf_op jit(solution)/shard_map/ppermute | solution.py:67
  30.6 1.5 collective-permute-start.13
  32.1 2.6 %collective-permute-done.2.refs_3_ = bf16[96,896]{1,0:T(8,128)(2,1)S(1)} collective-permute-done((bf16[96,896]{1,0:T(8,128)(2,1)S(1)}, bf16[96,896]{1,0:T(8,128)(2,1)S(1)}, u32[]{:S(2)}, u32[]{:S(2)}) %collective-permute-start.2) | collective-permute-done | bytes 172064 | tf_op jit(solution)/shard_map/ppermute | solution.py:67
  34.7 6.8 %project.1 = (bf16[1536,768]{1,0:T(8,128)(2,1)}, bf16[1536,576]{1,0:T(8,128)(2,1)S(1)}, f32[8,768]{1,0:T(8,128)S(1)}, bf16[768,896]{1,0:T(8,128)(2,1)S(1)}, bf16[192,768]{1,0:T(8,128)(2,1)S(1)}) custom-call(s32[4]{0:T(128)S(1)} %pad_add_fusion.scalar_ref, bf16[96,896]{1,0:T(8,128)(2,1)S(1)} %concatenate.6.refs_0_, ...), custom_call_target="tpu_custom_call" | custom-call | flops 4400000000 | tf_op jit(solution)/shard_map/project/pallas_call | solution.py:120
  41.6 1.6 collective-permute-start.10
  43.1 6.3 %attend_forward.2 = (bf16[192,1024]{1,0:T(8,128)(2,1)S(1)}, f32[4,8,256]{2,1,0:T(8,128)S(1)}) custom-call(s32[4]{0:T(128)S(1)} %pad_add_fusion.scalar_ref, bf16[1536,576]{1,0:T(8,128)(2,1)S(1)} %get-tuple-element.129.projected_ref.refs_0_), custom_call_target="tpu_custom_call" | custom-call | flops 5500000256 | tf_op jit(solution)/shard_map/attend_forward/pallas_call | solution.py:224
  49.5 4.6 %attend_forward.3 = (bf16[192,512]{1,0:T(8,128)(2,1)S(1)}, f32[2,8,256]{2,1,0:T(8,128)S(1)}) custom-call(s32[4]{0:T(128)S(1)} %pad_add_fusion.scalar_ref, bf16[1536,576]{1,0:T(8,128)(2,1)S(1)} %get-tuple-element.129.projected_ref.refs_0_), custom_call_target="tpu_custom_call" | custom-call | flops 4950000128 | tf_op jit(solution)/shard_map/attend_forward/pallas_call | solution.py:224
  54.8 1.5 collective-permute-start.20
  56.3 1.5 collective-permute-start.18
  57.9 1.5 collective-permute-start.17
  59.4 2.6 %collective-permute-done.7.refs_3_ = bf16[192,512]{1,0:T(8,128)(2,1)S(1)} collective-permute-done((bf16[192,512]{1,0:T(8,128)(2,1)S(1)}, bf16[192,512]{1,0:T(8,128)(2,1)S(1)}, u32[]{:S(2)}, u32[]{:S(2)}) %collective-permute-start.7) | collective-permute-done | bytes 196640 | tf_op jit(solution)/shard_map/ppermute | solution.py:67
  62.0 1.5 collective-permute-start.15
  63.5 1.6 collective-permute-done.18.refs_6_
  65.1 1.5 collective-permute-start.19
  66.6 3.3 %collective-permute-done.20.refs_3_ = bf16[192,1024]{1,0:T(8,128)(2,1)S(1)} collective-permute-done((bf16[192,1024]{1,0:T(8,128)(2,1)S(1)}, bf16[192,1024]{1,0:T(8,128)(2,1)S(1)}, u32[]{:S(2)}, u32[]{:S(2)}) %collective-permute-start.20) | collective-permute-done | bytes 393248 | tf_op jit(solution)/shard_map/ppermute | solution.py:67
  70.5 3.4 %collective-permute-done.15.refs_3_ = bf16[96,1536]{1,0:T(8,128)(2,1)S(1)} collective-permute-done((bf16[96,1536]{1,0:T(8,128)(2,1)S(1)}, bf16[96,1536]{1,0:T(8,128)(2,1)S(1)}, u32[]{:S(2)}, u32[]{:S(2)}) %collective-permute-start.15) | collective-permute-done | bytes 294944 | tf_op jit(solution)/shard_map/ppermute | solution.py:67
  73.9 5.1 %collective-permute-done.19.refs_7_ = bf16[96,1536]{1,0:T(8,128)(2,1)S(1)} collective-permute-done((bf16[96,1536]{1,0:T(8,128)(2,1)S(1)}, bf16[96,1536]{1,0:T(8,128)(2,1)S(1)}, u32[]{:S(2)}, u32[]{:S(2)}) %collective-permute-start.19) | collective-permute-done | bytes 294944 | tf_op jit(solution)/shard_map/ppermute | solution.py:67
  79.8 17.5 %feed_forward.4 = (bf16[512,768]{1,0:T(8,128)(2,1)S(1)}, f32[8,768]{1,0:T(8,128)S(1)}, bf16[1536,768]{1,0:T(8,128)(2,1)S(1)}, bf16[1536,768]{1,0:T(8,128)(2,1)S(1)}, bf16[1536,768]{1,0:T(8,128)(2,1)S(1)}) custom-call(s32[4]{0:T(128)S(1)} %pad_add_fusion.scalar_ref, bf16[1536,768]{1,0:T(8,128)(2,1)S(1)} %copy-done.4, bf16[1536,768]{1,0:T(8,128)(2,1)S(1)} %copy-done, ...), custom_call_target="tpu_custom_call" | custom-call | flops 5632000000 | tf_op jit(solution)/shard_map/feed_forward/pallas_call | solution.py:441
  97.9 5.7 %feed_forward.5 = (bf16[512,768]{1,0:T(8,128)(2,1)S(1)}, f32[8,768]{1,0:T(8,128)S(1)}, bf16[1536,768]{1,0:T(8,128)(2,1)S(1)}, bf16[1536,768]{1,0:T(8,128)(2,1)S(...) custom-call(s32[4]{0:T(128)S(1)} %pad_add_fusion.scalar_ref, ...), custom_call_target="tpu_custom_call", output_to_operand_aliasing={{2}: (14, {}), {3}: (15, {}), {4}: (16, {})} | custom-call | flops 5632000000 | tf_op jit(solution)/shard_map/feed_forward/pallas_call | solution.py:441
  104.2 2.9 %feed_forward.6 = (bf16[256,768]{1,0:T(8,128)(2,1)S(1)}, f32[8,768]{1,0:T(8,128)S(1)}, bf16[1536,768]{1,0:T(8,128)(2,1)S(1)}, bf16[1536,768]{1,0:T(8,128)(2,1)S(1)}, bf16[1536,768]{1,0:T(8,128)(2,1)S(1)}) custom-call(s32[4]{0:T(128)S(1)} %pad_add_fusion.scalar_ref, ...), custom_call_target="tpu_custom_call", output_to_operand_aliasing={{2}: (14, {}), {3}: (15, {}), {4}: (16, {})} | custom-call | flops 2816000000 | tf_op jit(solution)/shard_map/feed_forward/pallas_call | solution.py:441
  108.3 2.9 %feed_forward.7 = (bf16[256,768]{1,0:T(8,128)(2,1)S(1)}, f32[8,768]{1,0:T(8,128)S(1)}, bf16[1536,768]{1,0:T(8,128)(2,1)S(1)}, bf16[1536,768]{1,0:T(8,128)(2,1)S(...) custom-call(s32[4]{0:T(128)S(1)} %pad_add_fusion.scalar_ref, ...), custom_call_target="tpu_custom_call", output_to_operand_aliasing={{2}: (14, {}), {3}: (15, {}), {4}: (16, {}), {5}: (17, {})} | custom-call | flops 2816000000 | tf_op jit(solution)/shard_map/feed_forward/pallas_call | solution.py:441
  111.9 11.8 %feed_forward_weights.1 = (bf16[768,768]{1,0:T(8,128)(2,1)S(1)}, bf16[768,768]{1,0:T(8,128)(2,1)}, bf16[768,1536]{1,0:T(8,128)(2,1)S(1)}) custom-call(s32[4]{0:T(128)S(1)} %pad_add_fusion.scalar_ref, bf16[1536,768]{1,0:T(8,128)(2,1)S(1)} %get-tuple-element.116.normed_ref, bf16[1536,768]{1,0:T(8,128)(2,1)S(1)} %get-tuple-element.117.upper_ref, ...), custom_call_target="tpu_custom_call" | custom-call | flops 1100000000 | tf_op jit(solution)/shard_map/feed_forward_weights/pallas_call | solution.py:502
  126.2 1.4 collective-permute-start.28
  127.6 4.5 %all-to-all-start = ((bf16[8,96,1536]{2,1,0:T(8,128)(2,1)}), bf16[8,96,1536]{2,1,0:T(8,128)(2,1)}, u32[]{:S(2)}, u32[]{:S(2)}) async-start(bf16[8,96,1536]{2,1,0:T(8,128)(2,1)} %bitcast.9), calls=%async_computation | async-start | bytes 4718592 | tf_op jit(solution)/shard_map/all_to_all | solution.py:714
  132.2 1.7 copy-done.2
  134.5 2.8 %second_norm_backward.2.refs_6_ = bf16[512,768]{1,0:T(8,128)(2,1)S(1)} custom-call(s32[4]{0:T(128)S(1)} %pad_add_fusion.scalar_ref, bf16[512,768]{1,0:T(8,128)(2,1)S(1)} %add_convert_fusion.2.mine_ref, bf16[512,768]{1,0:T(8,128)(2,1)} %collective-permute-done.26.other_ref, f32[768,768]{1,0:T(8,128)S(1)} %copy-done.2, bf16[1536,768]{1,0:T(8,128)(2,1)S(1)} %copy-done, ...), custom_call_target="tpu_custom_call" | custom-call | flops 563200000 | tf_op jit(solution)/shard_map/second_norm_backward/pallas_call | solution.py:549
  137.8 2.1 second_norm_backward.3.refs_8_
  140.2 1.8 add_convert_fusion.1.mine_ref
  143.4 18.1 %attend_backward.1 = (bf16[576,1536]{1,0:T(8,128)(2,1)S(1)}, bf16[768,192]{1,0:T(8,128)(2,1)S(1)}, bf16[1536,768]{1,0:T(8,128)(2,1)S(1)}) custom-call(s32[4]{0:T(128)S(1)} %pad_add_fusion.scalar_ref, bf16[1536,576]{1,0:T(8,128)(2,1)S(1)} %copy-done.32, bf16[192,768]{1,0:T(8,128)(2,1)S(1)} %copy-done.12, bf16[192,1024]{1,0:T(8,128)(2,1)S(1)} %copy-done.21, ...), custom_call_target="tpu_custom_call" | custom-call | flops 8800000000 | tf_op jit(solution)/shard_map/attend_backward/pallas_call | solution.py:326
  161.6 8.9 %collective-permute-done.30.other_ref = bf16[768,768]{1,0:T(8,128)(2,1)S(1)} collective-permute-done((bf16[768,768]{1,0:T(8,128)(2,1)S(1)}, bf16[768,768]{1,0:T(8,128)(2,1)S(1)}, u32[]{:S(2)}, u32[]{:S(2)}) %collective-permute-start.30) | collective-permute-done | bytes 1179680 | tf_op jit(solution)/shard_map/ppermute | solution.py:67
  170.5 2.8 %grad_normed.3 = (bf16[768,768]{1,0:T(8,128)(2,1)S(1)}, f32[8,768]{1,0:T(8,128)S(1)}) custom-call(s32[4]{0:T(128)S(1)} %pad_add_fusion.scalar_ref, bf16[576,1536]{1,0:T(8,128)(2,1)S(1)} %get-tuple-element.133.grads_ref, bf16[1536,768]{1,0:T(8,128)(2,1)S(1)} %copy-done.5, bf16[768,896]{1,0:T(8,128)(2,1)S(1)} %copy-done.30), custom_call_target="tpu_custom_call" | custom-call | flops 3300000000 | tf_op jit(solution)/shard_map/grad_normed/pallas_call | solution.py:594
  173.4 2.8 %grad_normed.2 = (bf16[768,768]{1,0:T(8,128)(2,1)S(1)}, f32[8,768]{1,0:T(8,128)S(1)}) custom-call(s32[4]{0:T(128)S(1)} %pad_add_fusion.scalar_ref, bf16[576,1536]{1,0:T(8,128)(2,1)S(1)} %get-tuple-element.133.grads_ref, bf16[1536,768]{1,0:T(8,128)(2,1)S(1)} %copy-done.5, bf16[768,896]{1,0:T(8,128)(2,1)S(1)} %copy-done.30), custom_call_target="tpu_custom_call" | custom-call | flops 3300000000 | tf_op jit(solution)/shard_map/grad_normed/pallas_call | solution.py:594
  178.8 1.7 projection_weights.1
  181.6 4.9 %all-to-all-done.parts_ref = bf16[8,96,1536]{2,1,0:T(8,128)(2,1)} async-done(((bf16[8,96,1536]{2,1,0:T(8,128)(2,1)}), bf16[8,96,1536]{2,1,0:T(8,128)(2,1)}, u32[]{:S(2)}, u32[]{:S(2)}) %all-to-all-start) | async-done | bytes 2359328 | tf_op jit(solution)/shard_map/all_to_all | solution.py:714
  186.5 4.3 %all-to-all-start.1 = ((bf16[8,96,832]{2,1,0:T(8,128)(2,1)}), bf16[8,96,832]{2,1,0:T(8,128)(2,1)}, u32[]{:S(2)}, u32[]{:S(2)}) async-start(bf16[8,96,832]{2,1,0:T(8,128)(2,1)} %bitcast.10), calls=%async_computation.1 | async-start | bytes 2752512 | tf_op jit(solution)/shard_map/all_to_all | solution.py:714
  192.1 2.7 %layer_out.1 = (bf16[768,768]{1,0:T(8,128)(2,1)}, bf16[1536,768]{1,0:T(8,128)(2,1)}) custom-call(s32[4]{0:T(128)S(1)} %pad_add_fusion.scalar_ref, bf16[768,768]{1,0:T(8,128)(2,1)S(1)} %add_convert_fusion.1.mine_ref, bf16[768,768]{1,0:T(8,128)(2,1)S(1)} %copy-done.19, f32[768,768]{1,0:T(8,128)S(1)} %copy-done.3), custom_call_target="tpu_custom_call" | custom-call | flops 3300000000 | tf_op jit(solution)/shard_map/layer_out/pallas_call | solution.py:667
  194.8 11.5 %collective-permute-done.33.other_ref = bf16[768,768]{1,0:T(8,128)(2,1)} collective-permute-done((bf16[768,768]{1,0:T(8,128)(2,1)}, bf16[768,768]{1,0:T(8,128)(2,1)}, u32[]{:S(2)}, u32[]{:S(2)}) %collective-permute-start.33) | collective-permute-done | bytes 1179680 | tf_op jit(solution)/shard_map/ppermute | solution.py:67
  206.3 4.9 %first_norm_backward.1 = (bf16[768,768]{1,0:T(8,128)(2,1)S(1)}, bf16[1536,768]{1,0:T(8,128)(2,1)}) custom-call(s32[4]{0:T(128)S(1)} %pad_add_fusion.scalar_ref, bf16[768,768]{1,0:T(8,128)(2,1)} %add_convert_fusion.mine_ref, bf16[768,768]{1,0:T(8,128)(2,1)} %collective-permute-done.33.other_ref, bf16[1536,768]{1,0:T(8,128)(2,1)S(1)} %copy-done.6, ...), custom_call_target="tpu_custom_call" | custom-call | flops 3300000000 | tf_op jit(solution)/shard_map/first_norm_backward/pallas_call | solution.py:667
  211.2 2.4 %constant_dynamic-update-slice_fusion.1 = bf16[1536,768]{1,0:T(8,128)(2,1)} fusion(bf16[1536,768]{1,0:T(8,128)(2,1)} %get-tuple-element.126, bf16[768,768]{1,0:T(8,128)(2,1)} %collective-permute-done.31, s32[]{:T(128)S(6)} %select_n.4), kind=kLoop, calls=%fused_computation.9 | loop fusion | bytes 2359300 | tf_op jit(solution)/shard_map/dynamic_update_slice | solution.py:811
  213.5 9.7 %all-to-all-done.1.parts_ref = bf16[8,96,832]{2,1,0:T(8,128)(2,1)} async-done(((bf16[8,96,832]{2,1,0:T(8,128)(2,1)}), bf16[8,96,832]{2,1,0:T(8,128)(2,1)}, u32[]{:S(2)}, u32[]{:S(2)}) %all-to-all-start.1) | async-done | bytes 1277984 | tf_op jit(solution)/shard_map/all_to_all | solution.py:714
  223.2 2.2 total.2
  226.0 2.7 %total.3 = (f32[96,768]{1,0:T(8,128)}, f32[768,96]{1,0:T(8,128)S(1)}) custom-call(bf16[8,96,1536]{2,1,0:T(8,128)(2,1)} %all-to-all-done.parts_ref), custom_call_target="tpu_custom_call" | custom-call | flops 1100000000 | tf_op jit(solution)/shard_map/total/pallas_call | solution.py:700
  (150 shorter events, 24.8 us)
Async XLA Ops:
  4.1 10.4 %collective-permute-start.5 = (bf16[96,896]{1,0:T(8,128)(2,1)S(1)}, bf16[96,896]{1,0:T(8,128)(2,1)S(1)}, u32[]{:S(2)}, u32[]{:S(2)}) collective-permute-start(bf16[96,896]{1,0:T(8,128)(2,1)S(1)} %concatenate.6.refs_0_), channel_id=1, source_target_pairs={{0,24},{4,28},{8,16},{12,20},{16,8},{20,12},{24,0},{28,4},{1,25},{... | collective-permute-start | bytes 516104 | tf_op jit(solution)/shard_map/ppermute | solution.py:67
  9.2 14.6 %collective-permute-start.3 = (bf16[96,896]{1,0:T(8,128)(2,1)S(1)}, bf16[96,896]{1,0:T(8,128)(2,1)S(1)}, u32[]{:S(2)}, u32[]{:S(2)}) collective-permute-start(bf16[96,896]{1,0:T(8,128)(2,1)S(1)} %concatenate.6.refs_0_), channel_id=1, source_target_pairs={{0,16},{4,20},{8,24},{12,28},{16,0},{20,4},{24,8},{28,12},{1,17},{... | collective-permute-start | bytes 516104 | tf_op jit(solution)/shard_map/ppermute | solution.py:67
  9.2 16.1 %collective-permute-start.1 = (bf16[96,896]{1,0:T(8,128)(2,1)S(1)}, bf16[96,896]{1,0:T(8,128)(2,1)S(1)}, u32[]{:S(2)}, u32[]{:S(2)}) collective-permute-start(bf16[96,896]{1,0:T(8,128)(2,1)S(1)} %concatenate.6.refs_0_), channel_id=1, source_target_pairs={{0,8},{4,12},{8,0},{12,4},{16,24},{20,28},{24,16},{28,20},{1,9},{5... | collective-permute-start | bytes 516104 | tf_op jit(solution)/shard_map/ppermute | solution.py:67
  9.9 18.3 %collective-permute-start = (bf16[96,896]{1,0:T(8,128)(2,1)S(1)}, bf16[96,896]{1,0:T(8,128)(2,1)S(1)}, u32[]{:S(2)}, u32[]{:S(2)}) collective-permute-start(bf16[96,896]{1,0:T(8,128)(2,1)S(1)} %concatenate.6.refs_0_), channel_id=1, source_target_pairs={{0,4},{4,0},{8,12},{12,8},{16,20},{20,16},{24,28},{28,24},{1,5},{5... | collective-permute-start | bytes 516104 | tf_op jit(solution)/shard_map/ppermute | solution.py:67
  14.5 16.1 %collective-permute-start.6 = (bf16[96,896]{1,0:T(8,128)(2,1)S(1)}, bf16[96,896]{1,0:T(8,128)(2,1)S(1)}, u32[]{:S(2)}, u32[]{:S(2)}) collective-permute-start(bf16[96,896]{1,0:T(8,128)(2,1)S(1)} %collective-permute-done.5.refs_6_), channel_id=1, source_target_pairs={{0,4},{4,0},{8,12},{12,8},{16,20},{20,16},{24,28},{28,24},{1,5},{5... | collective-permute-start | bytes 516104 | tf_op jit(solution)/shard_map/ppermute | solution.py:67
  23.8 8.3 %collective-permute-start.4 = (bf16[96,896]{1,0:T(8,128)(2,1)S(1)}, bf16[96,896]{1,0:T(8,128)(2,1)S(1)}, u32[]{:S(2)}, u32[]{:S(2)}) collective-permute-start(bf16[96,896]{1,0:T(8,128)(2,1)S(1)} %collective-permute-done.3.refs_4_), channel_id=1, source_target_pairs={{0,4},{4,0},{8,12},{12,8},{16,20},{20,16},{24,28},{28,24},{1,5},{5... | collective-permute-start | bytes 516104 | tf_op jit(solution)/shard_map/ppermute | solution.py:67
  25.3 9.4 %collective-permute-start.2 = (bf16[96,896]{1,0:T(8,128)(2,1)S(1)}, bf16[96,896]{1,0:T(8,128)(2,1)S(1)}, u32[]{:S(2)}, u32[]{:S(2)}) collective-permute-start(bf16[96,896]{1,0:T(8,128)(2,1)S(1)} %collective-permute-done.1.refs_2_), channel_id=1, source_target_pairs={{0,4},{4,0},{8,12},{12,8},{16,20},{20,16},{24,28},{28,24},{1,5},{5... | collective-permute-start | bytes 516104 | tf_op jit(solution)/shard_map/ppermute | solution.py:67
  27.6 26.6 %collective-permute-start.16 = (bf16[96,1536]{1,0:T(8,128)(2,1)S(1)}, bf16[96,1536]{1,0:T(8,128)(2,1)S(1)}, u32[]{:S(2)}, u32[]{:S(2)}) collective-permute-start(bf16[96,1536]{1,0:T(8,128)(2,1)S(1)} %pad_maximum_fusion.refs_0_), channel_id=1, source_target_pairs={{0,16},{4,20},{8,24},{12,28},{16,0},{20,4},{24,8},{28,12},{1,17},{... | collective-permute-start | bytes 884744 | tf_op jit(solution)/shard_map/ppermute | solution.py:67
  28.1 26.7 %collective-permute-start.14 = (bf16[96,1536]{1,0:T(8,128)(2,1)S(1)}, bf16[96,1536]{1,0:T(8,128)(2,1)S(1)}, u32[]{:S(2)}, u32[]{:S(2)}) collective-permute-start(bf16[96,1536]{1,0:T(8,128)(2,1)S(1)} %pad_maximum_fusion.refs_0_), channel_id=1, source_target_pairs={{0,8},{4,12},{8,0},{12,4},{16,24},{20,28},{24,16},{28,20},{1,9},{5... | collective-permute-start | bytes 884744 | tf_op jit(solution)/shard_map/ppermute | solution.py:67
  30.6 25.7 %collective-permute-start.13 = (bf16[96,1536]{1,0:T(8,128)(2,1)S(1)}, bf16[96,1536]{1,0:T(8,128)(2,1)S(1)}, u32[]{:S(2)}, u32[]{:S(2)}) collective-permute-start(bf16[96,1536]{1,0:T(8,128)(2,1)S(1)} %pad_maximum_fusion.refs_0_), channel_id=1, source_target_pairs={{0,4},{4,0},{8,12},{12,8},{16,20},{20,16},{24,28},{28,24},{1,5},{5... | collective-permute-start | bytes 884744 | tf_op jit(solution)/shard_map/ppermute | solution.py:67
  41.6 66.7 %copy-start.11 = (bf16[192,768]{1,0:T(8,128)(2,1)}, bf16[192,768]{1,0:T(8,128)(2,1)S(1)}, u32[]{:S(2)}) copy-start(bf16[192,768]{1,0:T(8,128)(2,1)S(1)} %get-tuple-element.87.refs_6_.refs_1_) | copy-start | bytes 884740
  41.6 66.7 %copy-start.15 = (f32[8,768]{1,0:T(8,128)}, f32[8,768]{1,0:T(8,128)S(1)}, u32[]{:S(2)}) copy-start(f32[8,768]{1,0:T(8,128)S(1)} %get-tuple-element.105.refs_12_.rows_ref) | copy-start | bytes 73732
  41.6 20.4 %collective-permute-start.10 = (bf16[192,768]{1,0:T(8,128)(2,1)S(1)}, bf16[192,768]{1,0:T(8,128)(2,1)S(1)}, u32[]{:S(2)}, u32[]{:S(2)}) collective-permute-start(bf16[192,768]{1,0:T(8,128)(2,1)S(1)} %get-tuple-element.87.refs_6_.refs_1_), channel_id=1, source_target_pairs={{0,2},{1,3},{2,0},{3,1},{4,6},{5,7},{6,4},{7,5},{8,10},{9,11},{10,... | collective-permute-start | bytes 884744 | tf_op jit(solution)/shard_map/ppermute | solution.py:67
  49.5 48.4 %copy-start.20 = (bf16[192,1024]{1,0:T(8,128)(2,1)}, bf16[192,1024]{1,0:T(8,128)(2,1)S(1)}, u32[]{:S(2)}) copy-start(bf16[192,1024]{1,0:T(8,128)(2,1)S(1)} %get-tuple-element.84.refs_2_) | copy-start | bytes 1179652
  49.5 30.3 %copy-start.4 = (bf16[1536,768]{1,0:T(8,128)(2,1)S(1)}, bf16[1536,768]{1,0:T(8,128)(2,1)}, u32[]{:S(2)}) copy-start(bf16[1536,768]{1,0:T(8,128)(2,1)} %tokens_ref.5) | copy-start | bytes 7077892
  54.1 43.2 %copy-start.39 = (f32[2,8,256]{2,1,0:T(8,128)}, f32[2,8,256]{2,1,0:T(8,128)S(1)}, u32[]{:S(2)}) copy-start(f32[2,8,256]{2,1,0:T(8,128)S(1)} %get-tuple-element.131.refs_5_) | copy-start | bytes 49156
  54.1 54.2 %copy-start.13 = (bf16[192,512]{1,0:T(8,128)(2,1)}, bf16[192,512]{1,0:T(8,128)(2,1)S(1)}, u32[]{:S(2)}) copy-start(bf16[192,512]{1,0:T(8,128)(2,1)S(1)} %get-tuple-element.86.refs_2_.refs_3_) | copy-start | bytes 589828
  54.1 25.7 %copy-start = (bf16[1536,768]{1,0:T(8,128)(2,1)S(1)}, bf16[1536,768]{1,0:T(8,128)(2,1)}, u32[]{:S(2)}) copy-start(bf16[1536,768]{1,0:T(8,128)(2,1)} %grad_ref.5) | copy-start | bytes 7077892
  54.1 3.7 %collective-permute-start.8 = (bf16[192,512]{1,0:T(8,128)(2,1)S(1)}, bf16[192,512]{1,0:T(8,128)(2,1)S(1)}, u32[]{:S(2)}, u32[]{:S(2)}) collective-permute-start(bf16[192,512]{1,0:T(8,128)(2,1)S(1)} %get-tuple-element.86.refs_2_.refs_3_), channel_id=1, source_target_pairs={{0,1},{1,0},{2,3},{3,2},{4,5},{5,4},{6,7},{7,6},{8,9},{9,8},{10,11... | collective-permute-start | bytes 589832 | tf_op jit(solution)/shard_map/ppermute | solution.py:67
  54.2 7.8 %collective-permute-start.7 = (bf16[192,512]{1,0:T(8,128)(2,1)S(1)}, bf16[192,512]{1,0:T(8,128)(2,1)S(1)}, u32[]{:S(2)}, u32[]{:S(2)}) collective-permute-start(bf16[192,512]{1,0:T(8,128)(2,1)S(1)} %get-tuple-element.86.refs_2_.refs_3_), channel_id=1, source_target_pairs={{0,2},{1,3},{2,0},{3,1},{4,6},{5,7},{6,4},{7,5},{8,10},{9,11},{10,... | collective-permute-start | bytes 589832 | tf_op jit(solution)/shard_map/ppermute | solution.py:67
  54.8 15.1 %collective-permute-start.20 = (bf16[192,1024]{1,0:T(8,128)(2,1)S(1)}, bf16[192,1024]{1,0:T(8,128)(2,1)S(1)}, u32[]{:S(2)}, u32[]{:S(2)}) collective-permute-start(bf16[192,1024]{1,0:T(8,128)(2,1)S(1)} %get-tuple-element.84.refs_2_), channel_id=1, source_target_pairs={{0,2},{1,3},{2,0},{3,1},{4,6},{5,7},{6,4},{7,5},{8,10},{9,11},{10,... | collective-permute-start | bytes 1179656 | tf_op jit(solution)/shard_map/ppermute | solution.py:67
  56.3 8.8 %collective-permute-start.18 = (bf16[96,1536]{1,0:T(8,128)(2,1)S(1)}, bf16[96,1536]{1,0:T(8,128)(2,1)S(1)}, u32[]{:S(2)}, u32[]{:S(2)}) collective-permute-start(bf16[96,1536]{1,0:T(8,128)(2,1)S(1)} %collective-permute-done.16.refs_4_), channel_id=1, source_target_pairs={{0,8},{4,12},{8,0},{12,4},{16,24},{20,28},{24,16},{28,20},{1,9},{5... | collective-permute-start | bytes 884744 | tf_op jit(solution)/shard_map/ppermute | solution.py:67
  57.9 12.1 %collective-permute-start.17 = (bf16[96,1536]{1,0:T(8,128)(2,1)S(1)}, bf16[96,1536]{1,0:T(8,128)(2,1)S(1)}, u32[]{:S(2)}, u32[]{:S(2)}) collective-permute-start(bf16[96,1536]{1,0:T(8,128)(2,1)S(1)} %collective-permute-done.16.refs_4_), channel_id=1, source_target_pairs={{0,4},{4,0},{8,12},{12,8},{16,20},{20,16},{24,28},{28,24},{1,5},{5... | collective-permute-start | bytes 884744 | tf_op jit(solution)/shard_map/ppermute | solution.py:67
  62.0 4.6 %collective-permute-start.9 = (bf16[192,512]{1,0:T(8,128)(2,1)S(1)}, bf16[192,512]{1,0:T(8,128)(2,1)S(1)}, u32[]{:S(2)}, u32[]{:S(2)}) collective-permute-start(bf16[192,512]{1,0:T(8,128)(2,1)S(1)} %collective-permute-done.7.refs_3_), channel_id=1, source_target_pairs={{0,1},{1,0},{2,3},{3,2},{4,5},{5,4},{6,7},{7,6},{8,9},{9,8},{10,11... | collective-permute-start | bytes 589832 | tf_op jit(solution)/shard_map/ppermute | solution.py:67
  62.0 11.9 %collective-permute-start.15 = (bf16[96,1536]{1,0:T(8,128)(2,1)S(1)}, bf16[96,1536]{1,0:T(8,128)(2,1)S(1)}, u32[]{:S(2)}, u32[]{:S(2)}) collective-permute-start(bf16[96,1536]{1,0:T(8,128)(2,1)S(1)} %collective-permute-done.14.refs_2_), channel_id=1, source_target_pairs={{0,4},{4,0},{8,12},{12,8},{16,20},{20,16},{24,28},{28,24},{1,5},{5... | collective-permute-start | bytes 884744 | tf_op jit(solution)/shard_map/ppermute | solution.py:67
  65.1 13.9 %collective-permute-start.19 = (bf16[96,1536]{1,0:T(8,128)(2,1)S(1)}, bf16[96,1536]{1,0:T(8,128)(2,1)S(1)}, u32[]{:S(2)}, u32[]{:S(2)}) collective-permute-start(bf16[96,1536]{1,0:T(8,128)(2,1)S(1)} %collective-permute-done.18.refs_6_), channel_id=1, source_target_pairs={{0,4},{4,0},{8,12},{12,8},{16,20},{20,16},{24,28},{28,24},{1,5},{5... | collective-permute-start | bytes 884744 | tf_op jit(solution)/shard_map/ppermute | solution.py:67
  66.6 13.1 %collective-permute-start.21 = (bf16[192,1024]{1,0:T(8,128)(2,1)S(1)}, bf16[192,1024]{1,0:T(8,128)(2,1)S(1)}, u32[]{:S(2)}, u32[]{:S(2)}) collective-permute-start(bf16[192,1024]{1,0:T(8,128)(2,1)S(1)} %get-tuple-element.84.refs_2_), channel_id=1, source_target_pairs={{0,1},{1,0},{2,3},{3,2},{4,5},{5,4},{6,7},{7,6},{8,9},{9,8},{10,11... | collective-permute-start | bytes 1179656 | tf_op jit(solution)/shard_map/ppermute | solution.py:67
  70.0 9.8 %collective-permute-start.22 = (bf16[192,1024]{1,0:T(8,128)(2,1)S(1)}, bf16[192,1024]{1,0:T(8,128)(2,1)S(1)}, u32[]{:S(2)}, u32[]{:S(2)}) collective-permute-start(bf16[192,1024]{1,0:T(8,128)(2,1)S(1)} %collective-permute-done.20.refs_3_), channel_id=1, source_target_pairs={{0,1},{1,0},{2,3},{3,2},{4,5},{5,4},{6,7},{7,6},{8,9},{9,8},{10,11... | collective-permute-start | bytes 1179656 | tf_op jit(solution)/shard_map/ppermute | solution.py:67
  70.0 9.8 %collective-permute-start.11 = (bf16[192,768]{1,0:T(8,128)(2,1)S(1)}, bf16[192,768]{1,0:T(8,128)(2,1)S(1)}, u32[]{:S(2)}, u32[]{:S(2)}) collective-permute-start(bf16[192,768]{1,0:T(8,128)(2,1)S(1)} %get-tuple-element.87.refs_6_.refs_1_), channel_id=1, source_target_pairs={{0,1},{1,0},{2,3},{3,2},{4,5},{5,4},{6,7},{7,6},{8,9},{9,8},{10,11... | collective-permute-start | bytes 884744 | tf_op jit(solution)/shard_map/ppermute | solution.py:67
  73.9 5.8 %collective-permute-start.12 = (bf16[192,768]{1,0:T(8,128)(2,1)S(1)}, bf16[192,768]{1,0:T(8,128)(2,1)S(1)}, u32[]{:S(2)}, u32[]{:S(2)}) collective-permute-start(bf16[192,768]{1,0:T(8,128)(2,1)S(1)} %collective-permute-done.10.refs_7_), channel_id=1, source_target_pairs={{0,1},{1,0},{2,3},{3,2},{4,5},{5,4},{6,7},{7,6},{8,9},{9,8},{10,11... | collective-permute-start | bytes 884744 | tf_op jit(solution)/shard_map/ppermute | solution.py:67
  97.9 5.8 %collective-permute-start.23 = (bf16[512,768]{1,0:T(8,128)(2,1)S(1)}, bf16[512,768]{1,0:T(8,128)(2,1)S(1)}, u32[]{:S(2)}, u32[]{:S(2)}) collective-permute-start(bf16[512,768]{1,0:T(8,128)(2,1)S(1)} %get-tuple-element.104), channel_id=1, source_target_pairs={{0,1},{1,0},{2,3},{3,2},{4,5},{5,4},{6,7},{7,6},{8,9},{9,8},{10,11... | collective-permute-start | bytes 2359304 | tf_op jit(solution)/shard_map/ppermute | solution.py:67
  107.1 4.7 %collective-permute-start.24 = (bf16[256,768]{1,0:T(8,128)(2,1)S(1)}, bf16[256,768]{1,0:T(8,128)(2,1)S(1)}, u32[]{:S(2)}, u32[]{:S(2)}) collective-permute-start(bf16[256,768]{1,0:T(8,128)(2,1)S(1)} %get-tuple-element.115), channel_id=1, source_target_pairs={{0,1},{1,0},{2,3},{3,2},{4,5},{5,4},{6,7},{7,6},{8,9},{9,8},{10,11... | collective-permute-start | bytes 1179656 | tf_op jit(solution)/shard_map/ppermute | solution.py:67
  107.7 24.4 %collective-permute-start.26 = (bf16[512,768]{1,0:T(8,128)(2,1)S(1)}, bf16[512,768]{1,0:T(8,128)(2,1)}, u32[]{:S(2)}, u32[]{:S(2)}) collective-permute-start(bf16[512,768]{1,0:T(8,128)(2,1)S(1)} %add_convert_fusion.2.mine_ref), channel_id=1, source_target_pairs={{0,2},{1,3},{2,0},{3,1},{4,6},{5,7},{6,4},{7,5},{8,10},{9,11},{10,... | collective-permute-start | bytes 2359304 | tf_op jit(solution)/shard_map/ppermute | solution.py:67
  126.2 14.0 %collective-permute-start.25 = (bf16[768,768]{1,0:T(8,128)(2,1)}, bf16[768,768]{1,0:T(8,128)(2,1)}, u32[]{:S(2)}, u32[]{:S(2)}) collective-permute-start(bf16[768,768]{1,0:T(8,128)(2,1)} %get-tuple-element.120), channel_id=1, source_target_pairs={{0,1},{1,0},{2,3},{3,2},{4,5},{5,4},{6,7},{7,6},{8,9},{9,8},{10,11... | collective-permute-start | bytes 3538952 | tf_op jit(solution)/shard_map/ppermute | solution.py:67
  126.2 11.6 %collective-permute-start.28 = (bf16[256,768]{1,0:T(8,128)(2,1)S(1)}, bf16[256,768]{1,0:T(8,128)(2,1)}, u32[]{:S(2)}, u32[]{:S(2)}) collective-permute-start(bf16[256,768]{1,0:T(8,128)(2,1)S(1)} %add_convert_fusion.3.mine_ref), channel_id=1, source_target_pairs={{0,2},{1,3},{2,0},{3,1},{4,6},{5,7},{6,4},{7,5},{8,10},{9,11},{10,... | collective-permute-start | bytes 1179656 | tf_op jit(solution)/shard_map/ppermute | solution.py:67
  127.6 58.9 %all-to-all-start = ((bf16[8,96,1536]{2,1,0:T(8,128)(2,1)}), bf16[8,96,1536]{2,1,0:T(8,128)(2,1)}, u32[]{:S(2)}, u32[]{:S(2)}) async-start(bf16[8,96,1536]{2,1,0:T(8,128)(2,1)} %bitcast.9), calls=%async_computation | async-start | bytes 4718592 | tf_op jit(solution)/shard_map/all_to_all | solution.py:714
  137.3 4.6 %collective-permute-start.27 = (bf16[512,768]{1,0:T(8,128)(2,1)S(1)}, bf16[512,768]{1,0:T(8,128)(2,1)S(1)}, u32[]{:S(2)}, u32[]{:S(2)}) collective-permute-start(bf16[512,768]{1,0:T(8,128)(2,1)S(1)} %second_norm_backward.2.refs_6_), channel_id=1, source_target_pairs={{0,1},{1,0},{2,3},{3,2},{4,5},{5,4},{6,7},{7,6},{8,9},{9,8},{10,11... | collective-permute-start | bytes 2359304 | tf_op jit(solution)/shard_map/ppermute | solution.py:67
  140.0 1.9 collective-permute-start.29
  142.0 28.5 %collective-permute-start.30 = (bf16[768,768]{1,0:T(8,128)(2,1)S(1)}, bf16[768,768]{1,0:T(8,128)(2,1)S(1)}, u32[]{:S(2)}, u32[]{:S(2)}) collective-permute-start(bf16[768,768]{1,0:T(8,128)(2,1)S(1)} %add_convert_fusion.1.mine_ref), channel_id=1, source_target_pairs={{0,2},{1,3},{2,0},{3,1},{4,6},{5,7},{6,4},{7,5},{8,10},{9,11},{10,... | collective-permute-start | bytes 3538952 | tf_op jit(solution)/shard_map/ppermute | solution.py:67
  143.4 27.0 %copy-start.5 = (bf16[1536,768]{1,0:T(8,128)(2,1)S(1)}, bf16[1536,768]{1,0:T(8,128)(2,1)}, u32[]{:S(2)}) copy-start(bf16[1536,768]{1,0:T(8,128)(2,1)} %tokens_ref.5) | copy-start | bytes 7077892
  143.4 27.0 %copy-start.30 = (bf16[768,896]{1,0:T(8,128)(2,1)S(1)}, bf16[768,896]{1,0:T(8,128)(2,1)}, u32[]{:S(2)}) copy-start(bf16[768,896]{1,0:T(8,128)(2,1)} %copy-done.29) | copy-start | bytes 4128772
  173.3 3.0 %collective-permute-start.32 = (bf16[768,768]{1,0:T(8,128)(2,1)S(1)}, bf16[768,768]{1,0:T(8,128)(2,1)S(1)}, u32[]{:S(2)}, u32[]{:S(2)}) collective-permute-start(bf16[768,768]{1,0:T(8,128)(2,1)S(1)} %get-tuple-element.136), channel_id=1, source_target_pairs={{0,1},{1,0},{2,3},{3,2},{4,5},{5,4},{6,7},{7,6},{8,9},{9,8},{10,11... | collective-permute-start | bytes 3538952 | tf_op jit(solution)/shard_map/ppermute | solution.py:67
  177.6 28.7 %collective-permute-start.33 = (bf16[768,768]{1,0:T(8,128)(2,1)}, bf16[768,768]{1,0:T(8,128)(2,1)}, u32[]{:S(2)}, u32[]{:S(2)}) collective-permute-start(bf16[768,768]{1,0:T(8,128)(2,1)} %add_convert_fusion.mine_ref), channel_id=1, source_target_pairs={{0,2},{1,3},{2,0},{3,1},{4,6},{5,7},{6,4},{7,5},{8,10},{9,11},{10,... | collective-permute-start | bytes 3538952 | tf_op jit(solution)/shard_map/ppermute | solution.py:67
  186.5 36.7 %all-to-all-start.1 = ((bf16[8,96,832]{2,1,0:T(8,128)(2,1)}), bf16[8,96,832]{2,1,0:T(8,128)(2,1)}, u32[]{:S(2)}, u32[]{:S(2)}) async-start(bf16[8,96,832]{2,1,0:T(8,128)(2,1)} %bitcast.10), calls=%async_computation.1 | async-start | bytes 2752512 | tf_op jit(solution)/shard_map/all_to_all | solution.py:714
  194.8 16.4 %collective-permute-start.31 = (bf16[768,768]{1,0:T(8,128)(2,1)}, bf16[768,768]{1,0:T(8,128)(2,1)}, u32[]{:S(2)}, u32[]{:S(2)}) collective-permute-start(bf16[768,768]{1,0:T(8,128)(2,1)} %get-tuple-element.127), channel_id=1, source_target_pairs={{0,1},{1,0},{2,3},{3,2},{4,5},{5,4},{6,7},{7,6},{8,9},{9,8},{10,11... | collective-permute-start | bytes 3538952 | tf_op jit(solution)/shard_map/ppermute | solution.py:67
  211.1 18.5 %collective-permute-start.34 = (bf16[768,768]{1,0:T(8,128)(2,1)S(1)}, bf16[768,768]{1,0:T(8,128)(2,1)S(1)}, u32[]{:S(2)}, u32[]{:S(2)}) collective-permute-start(bf16[768,768]{1,0:T(8,128)(2,1)S(1)} %get-tuple-element.139), channel_id=1, source_target_pairs={{0,1},{1,0},{2,3},{3,2},{4,5},{5,4},{6,7},{7,6},{8,9},{9,8},{10,11... | collective-permute-start | bytes 3538952 | tf_op jit(solution)/shard_map/ppermute | solution.py:67
  225.5 4.2 %collective-permute-start.35 = (f32[16,96]{1,0:T(8,128)S(1)}, f32[16,96]{1,0:T(8,128)S(1)}, u32[]{:S(2)}, u32[]{:S(2)}) collective-permute-start(f32[16,96]{1,0:T(8,128)S(1)} %slice.15), channel_id=1, source_target_pairs={{0,2},{1,3},{2,0},{3,1},{4,6},{5,7},{6,4},{7,5},{8,10},{9,11},{10,... | collective-permute-start | bytes 18440 | tf_op jit(solution)/shard_map/ppermute | solution.py:67
  229.7 1.2 collective-permute-start.36
  (32 other events, 147.9 us)

commit v3 on v2

--- a/solution.py
+++ b/solution.py
@@ -16,6 +16,7 @@
 WIDE = jnp.float32
 LANES = 128
 BLOCK = 256
+STEP = 384
 
 
 def multiply(left, right):
@@ -50,12 +51,16 @@
     return pltpu.HBM(shape, dtype)
 
 
+def far(value):
+    return pltpu.with_memory_space_constraint(value, pltpu.HBM)
+
+
 def params(mebibytes):
     return pltpu.CompilerParams(vmem_limit_bytes=mebibytes << 20)
 
 
 def cost(microseconds):
-    return pl.CostEstimate(flops=int(microseconds * 1.1e9), bytes_accessed=0, transcendentals=0)
+    return pl.CostEstimate(flops=int(microseconds * 1.1e6), bytes_accessed=0, transcendentals=0)
 
 
 def after(value, *others):
@@ -98,7 +103,7 @@
         scratch[pl.ds(at, count), :] = piece[...]
 
 
-def project_kernel(scalar_ref, *refs, parts, width):
+def project_kernel(scalar_ref, *refs, parts, width, block):
     pieces, refs = refs[:parts], refs[parts:]
     tokens_ref, normed_ref, projected_ref, rows_ref, weights_ref, outs_ref = refs
 
@@ -108,24 +113,27 @@
         rows_ref[...] = jnp.transpose(weights_ref[:, 4 * width : 4 * width + LANES].astype(WIDE))[:8, :]
         outs_ref[...] = jnp.transpose(weights_ref[:, 3 * width : 4 * width])
 
-    scaled, _ = standardize(tokens_ref[...].astype(WIDE))
-    normed = (scaled * rows_ref[0:1, :] + rows_ref[2:3, :]).astype(LOW)
-    normed_ref[...] = normed
-    projected_ref[...] = multiply(normed, weights_ref[:, : 3 * width]).astype(LOW)
+    for k in range(tokens_ref.shape[0] // block):
+        part = slice(k * block, (k + 1) * block)
+        scaled, _ = standardize(tokens_ref[part, :].astype(WIDE))
+        normed = (scaled * rows_ref[0:1, :] + rows_ref[2:3, :]).astype(LOW)
+        normed_ref[part, :] = normed
+        projected_ref[part, :] = multiply(normed, weights_ref[:, : 3 * width]).astype(LOW)
 
 
 def project(scalar, tokens, pieces, width):
     count, depth = tokens.shape
     total = pieces[0].shape[1]
-    return pl.pallas_call(
-        functools.partial(project_kernel, parts=len(pieces), width=width),
-        grid=(count // BLOCK,),
+    step = 768
+    return pl.pallas_call(
+        functools.partial(project_kernel, parts=len(pieces), width=width, block=256),
+        grid=(count // step,),
         in_specs=[scalars()]
         + [whole()] * len(pieces)
-        + [pl.BlockSpec((BLOCK, depth), lambda i: (i, 0))],
+        + [pl.BlockSpec((step, depth), lambda i: (i, 0))],
         out_specs=(
-            pl.BlockSpec((BLOCK, depth), lambda i: (i, 0)),
-            pl.BlockSpec((BLOCK, 3 * width), lambda i: (i, 0)),
+            pl.BlockSpec((step, depth), lambda i: (i, 0)),
+            pl.BlockSpec((step, 3 * width), lambda i: (i, 0)),
             pl.BlockSpec((8, depth), lambda i: (0, 0)),
             pl.BlockSpec((depth, total), lambda i: (0, 0)),
             pl.BlockSpec((width, depth), lambda i: (0, 0)),
@@ -137,7 +145,7 @@
             struct((depth, total), LOW),
             struct((width, depth), LOW),
         ),
-        compiler_params=params(14),
+        compiler_params=params(20),
         cost_estimate=cost(4),
         name="project",
     )(scalar, *pieces, pltpu.with_memory_space_constraint(tokens, pltpu.HBM))
@@ -227,7 +235,7 @@
         out_specs=(whole(), whole()),
         out_shape=(struct((width, len(places) * BLOCK), LOW), struct((len(places), 8, BLOCK), WIDE)),
         compiler_params=params(16),
-        cost_estimate=cost(sum(places) / 2 + 1),
+        cost_estimate=cost(1),
         name="attend_forward",
     )(scalar, projected)
 
@@ -349,15 +357,21 @@
     return up * half, slope
 
 
-def feed_kernel(scalar_ref, *refs, begin, half, keep, given):
-    tokens_ref, grad_ref, m0, m1, m2, m3, o0, o1, o2, o3, up_ref, down_ref, rows_ref = refs[:13]
-    results = refs[13 + given : -1]
+def add_sums(sums_ref, ahead_ref, back, scaled):
+    sums_ref[0:1, :] = ahead_ref[0:1, :] + jnp.sum(back * scaled, axis=0, keepdims=True)
+    sums_ref[1:2, :] = ahead_ref[1:2, :] + jnp.sum(back, axis=0, keepdims=True)
+    sums_ref[2:8, :] = ahead_ref[2:8, :]
+
+
+def feed_kernel(scalar_ref, *refs, begin, size, half, keep, given):
+    tokens_ref, grad_ref, m0, m1, m2, m3, o0, o1, o2, o3, up_ref, down_ref, rows_ref, ahead_ref = refs[:14]
+    results = refs[14 + given : -1]
     back_ref, sums_ref, normed_ref, active_ref, upper_ref = results[:5]
     mixed_ref = refs[-1]
-    i = pl.program_id(0)
     place = scalar_ref[0] if keep else 1 - scalar_ref[0]
-    row0 = begin + place * half + i * BLOCK
-    row = lax.broadcasted_iota(jnp.int32, (BLOCK, 1), 0) + row0
+    row0 = pl.multiple_of(begin + place * half, BLOCK)
+    here = pl.ds(row0, size)
+    row = lax.broadcasted_iota(jnp.int32, (size, 1), 0) + row0
 
     @pl.when(scalar_ref[2] == 0)
     def _():
@@ -374,148 +388,134 @@
         results[5][...] = hidden
     scaled, _ = standardize(hidden)
     normed = (scaled * rows_ref[1:2, :] + rows_ref[3:4, :]).astype(LOW)
-    normed_ref[...] = normed
+    normed_ref[here, :] = normed
     grad = jnp.where(row < scalar_ref[1], grad_ref[...].astype(WIDE), 0.0).astype(LOW)
     back = jnp.zeros(hidden.shape, WIDE)
     units = up_ref.shape[1]
     for first in range(0, units, BLOCK):
         part = slice(first, first + BLOCK)
         active, slope = gelu_pair(multiply(normed, up_ref[:, part]))
-        active_ref[:, part] = active.astype(LOW)
+        active_ref[here, part] = active.astype(LOW)
         upper = (multiply(grad, down_ref[:, part]) * slope).astype(LOW)
-        upper_ref[:, part] = upper
+        upper_ref[here, part] = upper
         back = back + outer_cols(upper, up_ref[:, part])
     back_ref[...] = back.astype(LOW)
-
-    @pl.when(i == 0)
-    def _():
-        sums_ref[...] = jnp.zeros_like(sums_ref)
-
-    sums_ref[0:1, :] += jnp.sum(back * scaled, axis=0, keepdims=True)
-    sums_ref[1:2, :] += jnp.sum(back, axis=0, keepdims=True)
-
-
-def feed(scalar, tokens, out_grad, mixed, outs, up, down, rows, stored, begin, size, keep):
+    add_sums(sums_ref, ahead_ref, back, scaled)
+
+
+def feed(scalar, tokens, out_grad, mixed, outs, up, down, rows, ahead, stored, begin, size, keep):
     count, depth = tokens.shape
     units = up.shape[1]
     width = outs[0].shape[0]
     half = count // 2
-    base = begin // BLOCK
-    blocks = size // BLOCK
 
     def side(scalar_ref):
         return scalar_ref[0] if keep else 1 - scalar_ref[0]
 
     def placed(i, scalar_ref):
-        return (base + side(scalar_ref) * (half // BLOCK) + i, 0)
+        return ((begin + side(scalar_ref) * half) // BLOCK * BLOCK, 0)
 
     def inside(i, scalar_ref):
-        return (0, side(scalar_ref) * blocks + i)
-
-    def own(i, scalar_ref):
-        return (i, 0)
-
-    def kept(i, scalar_ref):
-        return (base + i, 0)
-
-    def fixed(i, scalar_ref):
-        return (0, 0)
-
-    out_specs = (
-        pl.BlockSpec((BLOCK, depth), own),
-        pl.BlockSpec((8, depth), fixed),
-        pl.BlockSpec((BLOCK, depth), placed),
-        pl.BlockSpec((BLOCK, units), placed),
-        pl.BlockSpec((BLOCK, units), placed),
-        pl.BlockSpec((BLOCK, depth), kept),
-    )
+        return (0, side(scalar_ref))
+
+    rows_spec = pl.BlockSpec((pl.Element(size), pl.Element(depth)), placed)
     out_shape = (
         struct((size, depth), LOW),
         struct((8, depth), WIDE),
         struct((count, depth), LOW),
         struct((count, units), LOW),
         struct((count, units), LOW),
-        struct((half, depth), WIDE),
+        stored_far((size, depth), WIDE),
     )[: 6 if keep else 5]
-    stored = stored[: len(out_shape) - 2]
-    return pl.pallas_call(
-        functools.partial(feed_kernel, begin=begin, half=half, keep=keep, given=len(stored)),
+    return pl.pallas_call(
+        functools.partial(feed_kernel, begin=begin, size=size, half=half, keep=keep, given=len(stored)),
         grid_spec=pltpu.PrefetchScalarGridSpec(
             num_scalar_prefetch=1,
-            grid=(blocks,),
-            in_specs=[pl.BlockSpec((BLOCK, depth), placed)] * 2
-            + [pl.BlockSpec((width, BLOCK), inside)] * 4
-            + [whole()] * 7
+            grid=(1,),
+            in_specs=[rows_spec] * 2
+            + [pl.BlockSpec((width, size), inside)] * 4
+            + [whole()] * 8
             + [pl.BlockSpec(memory_space=pl.ANY)] * len(stored),
-            out_specs=out_specs[: len(out_shape)],
-            scratch_shapes=[pltpu.VMEM((BLOCK, depth), WIDE)],
+            out_specs=(whole(),) * len(out_shape),
+            scratch_shapes=[pltpu.VMEM((size, depth), WIDE)],
         ),
         out_shape=out_shape,
-        input_output_aliases={14 + k: 2 + k for k in range(len(stored))},
+        input_output_aliases={15 + k: 2 + k for k in range(len(stored))},
         compiler_params=params(20),
-        cost_estimate=cost(size / 100),
+        cost_estimate=cost(size / 1000),
         name="feed_forward",
-    )(scalar, tokens, out_grad, *mixed, *outs, up, down, rows, *stored)
-
-
-def weigh_kernel(scalar_ref, normed_ref, upper_ref, active_ref, grad_ref, down_ref, keep_ref, send_ref, grads_ref, up_sum, down_sum, *, blocks):
+    )(scalar, tokens, out_grad, *mixed, *outs, up, down, rows, ahead, *stored)
+
+
+def put_shards(index, outs, value, cols):
+    if len(outs) == 1:
+        outs[0][:, cols] = value
+        return
+    mine, other = outs
+    rows = value.shape[0] // 8
+    for place in range(8):
+        piece = value[place * rows : (place + 1) * rows, :]
+
+        @pl.when((index & 1) == place % 2)
+        def _():
+            mine[place // 2, :, cols] = piece
+
+        @pl.when((index & 1) != place % 2)
+        def _():
+            other[place // 2, :, cols] = piece
+
+
+def shard_shapes(batch, depth, cols):
+    if batch != 8:
+        return (stored_far((depth, cols), LOW),)
+    return (struct((4, depth // 8, cols), LOW),) * 2
+
+
+def weigh_kernel(scalar_ref, normed_ref, upper_ref, active_ref, grad_ref, down_ref, keep_ref, send_ref, *refs):
+    outs, (up_sum, down_sum) = refs[:-2], refs[-2:]
     i = pl.program_id(0)
-    half = blocks // 2
     units = down_ref.shape[1]
-    row0 = lax.rem(i + (1 - scalar_ref[0]) * half, blocks) * BLOCK
-    row = lax.broadcasted_iota(jnp.int32, (BLOCK, 1), 0) + row0
-    branch = outer_cols(active_ref[...], down_ref[...]).astype(LOW)
-
-    @pl.when(i < half)
+    half = grad_ref.shape[0]
+    row0 = pl.multiple_of((scalar_ref[0] ^ 1 ^ i) * half, BLOCK)
+    here = pl.ds(row0, half)
+    row = lax.broadcasted_iota(jnp.int32, (half, 1), 0) + row0
+    active = active_ref[here, :]
+    branch = outer_cols(active, down_ref[...]).astype(LOW)
+    grad = jnp.where(row < scalar_ref[1], grad_ref[...].astype(WIDE), 0.0).astype(LOW)
+    up = inner_rows(normed_ref[here, :], upper_ref[here, :])
+    down = inner_rows(grad, active)
+
+    @pl.when(i == 0)
     def _():
         send_ref[...] = branch
-
-    @pl.when(i >= half)
+        up_sum[...] = up
+        down_sum[...] = down
+
+    @pl.when(i == 1)
     def _():
         keep_ref[...] = branch
-
-    grad = jnp.where(row < scalar_ref[1], grad_ref[...].astype(WIDE), 0.0).astype(LOW)
-
-    @pl.when(i == 0)
-    def _():
-        up_sum[...] = jnp.zeros_like(up_sum)
-        down_sum[...] = jnp.zeros_like(down_sum)
-
-    up_sum[...] += inner_rows(normed_ref[...], upper_ref[...])
-    down_sum[...] += inner_rows(grad, active_ref[...])
-
-    @pl.when(i == blocks - 1)
-    def _():
-        grads_ref[:, :units] = up_sum[...].astype(LOW)
-        grads_ref[:, units:] = down_sum[...].astype(LOW)
-
-
-def weigh(scalar, normed, upper, active, out_grad, down):
+        put_shards(scalar_ref[3], outs, (up_sum[...] + up).astype(LOW), slice(0, units))
+        put_shards(scalar_ref[3], outs, (down_sum[...] + down).astype(LOW), slice(units, 2 * units))
+
+
+def weigh(scalar, normed, upper, active, out_grad, down, batch):
     count, depth = normed.shape
     units = down.shape[1]
-    blocks = count // BLOCK
-    half = blocks // 2
-
-    def turned(i, scalar_ref):
-        return (lax.rem(i + (1 - scalar_ref[0]) * half, blocks), 0)
-
-    return pl.pallas_call(
-        functools.partial(weigh_kernel, blocks=blocks),
+    half = count // 2
+    return pl.pallas_call(
+        weigh_kernel,
         grid_spec=pltpu.PrefetchScalarGridSpec(
             num_scalar_prefetch=1,
-            grid=(blocks,),
-            in_specs=[pl.BlockSpec((BLOCK, depth), turned)] * 4 + [whole()],
-            out_specs=(
-                pl.BlockSpec((BLOCK, depth), lambda i, s: (jnp.maximum(i - half, 0), 0)),
-                pl.BlockSpec((BLOCK, depth), lambda i, s: (jnp.minimum(i, half - 1), 0)),
-                pl.BlockSpec((depth, 2 * units), lambda i, s: (0, 0)),
-            ),
+            grid=(2,),
+            in_specs=[whole()] * 3
+            + [pl.BlockSpec((half, depth), lambda i, scalar_ref: (scalar_ref[0] ^ 1 ^ i, 0)), whole()],
+            out_specs=(whole(),) * (2 + len(shard_shapes(batch, depth, 2 * units))),
             scratch_shapes=[pltpu.VMEM((depth, units), WIDE)] * 2,
         ),
         out_shape=(
-            struct((count // 2, depth), LOW),
-            struct((count // 2, depth), LOW),
-            struct((depth, 2 * units), LOW),
+            struct((half, depth), LOW),
+            struct((half, depth), LOW),
+            *shard_shapes(batch, depth, 2 * units),
         ),
         compiler_params=params(24),
         cost_estimate=cost(1),
@@ -523,9 +523,28 @@
     )(scalar, normed, upper, active, out_grad, down)
 
 
+def fold_kernel(scalar_ref, mine_ref, other_ref, *outs):
+    place = scalar_ref[3] >> 1
+    for k, out in enumerate(outs):
+        out[...] = (mine_ref[place ^ k].astype(WIDE) + other_ref[place ^ k].astype(WIDE)).astype(LOW)
+
+
+def fold(scalar, mine, other):
+    count, rows, cols = mine.shape
+    return pl.pallas_call(
+        fold_kernel,
+        in_specs=[scalars(), whole(), whole()],
+        out_specs=(whole(),) * count,
+        out_shape=(struct((rows, cols), LOW),) * count,
+        compiler_params=params(10),
+        cost_estimate=cost(1),
+        name="fold",
+    )(scalar, mine, other)
+
+
 def second_back_kernel(scalar_ref, mine_ref, other_ref, hidden_ref, grad_ref, rows_ref, low_ref, *, begin, half):
-    row0 = begin + scalar_ref[0] * half + pl.program_id(0) * BLOCK
-    row = lax.broadcasted_iota(jnp.int32, (BLOCK, 1), 0) + row0
+    size = low_ref.shape[0]
+    row = lax.broadcasted_iota(jnp.int32, (size, 1), 0) + (begin + scalar_ref[0] * half)
     grad_normed = mine_ref[...].astype(WIDE) + other_ref[...].astype(WIDE)
     scaled, inverse = standardize(hidden_ref[...])
     grad = jnp.where(row < scalar_ref[1], grad_ref[...].astype(WIDE), 0.0)
@@ -533,116 +552,141 @@
     low_ref[...] = grad.astype(LOW)
 
 
-def second_back(scalar, mine, other, hidden, out_grad, rows, begin, size):
-    half, depth = hidden.shape
-    base = begin // BLOCK
-
-    def own(i, scalar_ref):
-        return (i, 0)
-
-    def kept(i, scalar_ref):
-        return (base + i, 0)
-
-    def placed(i, scalar_ref):
-        return (base + i + scalar_ref[0] * (half // BLOCK), 0)
-
+def second_back(scalar, mine, other, hidden, out_grad, rows, begin):
+    size, depth = hidden.shape
+    half = out_grad.shape[0] // 2
+    placed = pl.BlockSpec(
+        (pl.Element(size), pl.Element(depth)), lambda i, scalar_ref: ((begin + scalar_ref[0] * half) // BLOCK * BLOCK, 0)
+    )
     return pl.pallas_call(
         functools.partial(second_back_kernel, begin=begin, half=half),
         grid_spec=pltpu.PrefetchScalarGridSpec(
             num_scalar_prefetch=1,
-            grid=(size // BLOCK,),
-            in_specs=[pl.BlockSpec((BLOCK, depth), own)] * 2
-            + [pl.BlockSpec((BLOCK, depth), kept), pl.BlockSpec((BLOCK, depth), placed), whole()],
-            out_specs=pl.BlockSpec((BLOCK, depth), own),
+            grid=(1,),
+            in_specs=[whole()] * 2 + [pl.BlockSpec((size, depth), lambda i, scalar_ref: (0, 0)), placed, whole()],
+            out_specs=whole(),
         ),
         out_shape=struct((size, depth), LOW),
-        compiler_params=params(12),
+        compiler_params=params(14),
         cost_estimate=cost(size / 1000),
         name="second_norm_backward",
-    )(scalar, mine, other, hidden, out_grad, rows)
-
-
-def inward_kernel(scalar_ref, grads_ref, tokens_ref, weights_ref, back_ref, sums_ref):
-    i = pl.program_id(0)
+    )(scalar, mine, other, far(hidden), far(out_grad), rows)
+
+
+def inward_kernel(scalar_ref, grads_ref, tokens_ref, weights_ref, ahead_ref, back_ref, sums_ref):
     width = grads_ref.shape[0]
     back = lax.dot_general(
         grads_ref[...], weights_ref[:, :width], (((0,), (1,)), ((), ())), preferred_element_type=WIDE
     )
     scaled, _ = standardize(tokens_ref[...].astype(WIDE))
     back_ref[...] = back.astype(LOW)
-
-    @pl.when(i == 0)
-    def _():
-        sums_ref[...] = jnp.zeros_like(sums_ref)
-
-    sums_ref[0:1, :] += jnp.sum(back * scaled, axis=0, keepdims=True)
-    sums_ref[1:2, :] += jnp.sum(back, axis=0, keepdims=True)
-
-
-def inward(scalar, grads, tokens, weights, begin, half, keep):
-    depth = tokens.shape[1]
+    add_sums(sums_ref, ahead_ref, back, scaled)
+
+
+def inward(scalar, grads, tokens, weights, ahead, keep):
+    count, depth = tokens.shape
     width = grads.shape[0]
-    blocks = half // BLOCK
-
-    def placed(i, scalar_ref):
-        place = scalar_ref[0] if keep else 1 - scalar_ref[0]
-        return (begin // BLOCK + place * blocks + i, 0)
-
-    def lanes(i, scalar_ref):
-        return placed(i, scalar_ref)[::-1]
+    half = count // 2
+
+    def side(scalar_ref):
+        return scalar_ref[0] if keep else 1 - scalar_ref[0]
 
     return pl.pallas_call(
         inward_kernel,
         grid_spec=pltpu.PrefetchScalarGridSpec(
             num_scalar_prefetch=1,
+            grid=(1,),
+            in_specs=[
+                pl.BlockSpec((width, half), lambda i, scalar_ref: (0, side(scalar_ref))),
+                pl.BlockSpec((half, depth), lambda i, scalar_ref: (side(scalar_ref), 0)),
+                whole(),
+                whole(),
+            ],
+            out_specs=(whole(), whole()),
+        ),
+        out_shape=(struct((half, depth), LOW), struct((8, depth), WIDE)),
+        compiler_params=params(16),
+        cost_estimate=cost(1),
+        name="grad_normed",
+    )(scalar, grads, tokens, weights, ahead)
+
+
+def project_back_kernel(scalar_ref, grads_ref, normed_ref, outs_ref, one_ref, two_ref, *outs, width):
+    blank = jnp.zeros((LANES - 16, one_ref.shape[1]), WIDE)
+    rows = jnp.concatenate([one_ref[...], two_ref[...], blank], axis=0)
+    rows = jnp.transpose(rows)[:, : -width % LANES].astype(LOW)
+    grads = jnp.transpose(multiply(grads_ref[...], normed_ref[...])).astype(LOW)
+    value = jnp.concatenate([grads, rows, outs_ref[...]], axis=1)
+    put_shards(scalar_ref[3], outs, value, slice(0, value.shape[1]))
+
+
+def project_back(scalar, grads, normed, outs_grad, one, two, batch):
+    width = grads.shape[0]
+    depth = normed.shape[1]
+    shapes = shard_shapes(batch, depth, width + -width % LANES + outs_grad.shape[1])
+    return pl.pallas_call(
+        functools.partial(project_back_kernel, width=width),
+        in_specs=[scalars()] + [whole()] * 5,
+        out_specs=(whole(),) * len(shapes),
+        out_shape=shapes,
+        compiler_params=params(16),
+        cost_estimate=cost(1),
+        name="projection_weights",
+    )(scalar, grads, normed, outs_grad, one, two)
+
+
+def finish_kernel(scalar_ref, mine_ref, other_ref, *refs, sizes, half):
+    hidden_refs, (own_ref, full_ref) = refs[: len(sizes)], refs[len(sizes) :]
+    i = pl.program_id(0)
+    row = lax.broadcasted_iota(jnp.int32, (BLOCK, 1), 0) + (scalar_ref[0] * half + i * BLOCK)
+    branch = mine_ref[...].astype(WIDE) + other_ref[...].astype(WIDE)
+    first = 0
+    for size, hidden_ref in zip(sizes, hidden_refs):
+        last = first + size // BLOCK
+
+        @pl.when((i >= first) & (i < last))
+        def _():
+            low = jnp.where(row < scalar_ref[1], hidden_ref[...] + branch, 0.0).astype(LOW)
+            own_ref[...] = low
+            full_ref[...] = low
+
+        first = last
+
+
+def finish(scalar, mine, other, hiddens, count):
+    half, depth = mine.shape
+    blocks = half // BLOCK
+    sizes = tuple(hidden.shape[0] for hidden in hiddens)
+    specs = []
+    first = 0
+    for size in sizes:
+        last = size // BLOCK - 1
+
+        def chunk(i, scalar_ref, first=first, last=last):
+            return (jnp.clip(i - first, 0, last), 0)
+
+        specs.append(pl.BlockSpec((BLOCK, depth), chunk))
+        first += last + 1
+
+    def own(i, scalar_ref):
+        return (i, 0)
+
+    return pl.pallas_call(
+        functools.partial(finish_kernel, sizes=sizes, half=half),
+        grid_spec=pltpu.PrefetchScalarGridSpec(
+            num_scalar_prefetch=1,
             grid=(blocks,),
-            in_specs=[pl.BlockSpec((width, BLOCK), lanes), pl.BlockSpec((BLOCK, depth), placed), whole()],
+            in_specs=[pl.BlockSpec((BLOCK, depth), own)] * 2 + specs,
             out_specs=(
-                pl.BlockSpec((BLOCK, depth), lambda i, s: (i, 0)),
-                pl.BlockSpec((8, depth), lambda i, s: (0, 0)),
+                pl.BlockSpec((BLOCK, depth), own),
+                pl.BlockSpec((BLOCK, depth), lambda i, scalar_ref: (i + scalar_ref[0] * blocks, 0)),
             ),
         ),
-        out_shape=(struct((half, depth), LOW), struct((8, depth), WIDE)),
+        out_shape=(struct((half, depth), LOW), stored_far((count, depth), LOW)),
         compiler_params=params(12),
-        cost_estimate=cost(3),
-        name="grad_normed",
-    )(scalar, grads, tokens, weights)
-
-
-def project_back_kernel(grads_ref, normed_ref, outs_ref, *refs, width, split):
-    sums, out_ref = refs[:-1], refs[-1]
-    last = out_ref.shape[1] - outs_ref.shape[1]
-    out_ref[:, last:] = outs_ref[...]
-    out_ref[:, :width] = jnp.transpose(multiply(grads_ref[...], normed_ref[...])).astype(LOW)
-    ones, twos = sums[:split], sums[split:]
-    one = sum(ref[...] for ref in ones[1:]) + ones[0][...]
-    two = sum(ref[...] for ref in twos[1:]) + twos[0][...]
-    rows = jnp.concatenate([one, two, jnp.zeros((LANES - 16, one.shape[1]), WIDE)], axis=0)
-    out_ref[:, width:last] = jnp.transpose(rows)[:, : last - width].astype(LOW)
-
-
-def project_back(grads, normed, outs_grad, ones, twos):
-    width = grads.shape[0]
-    depth = normed.shape[1]
-    sums = list(ones) + list(twos)
-    return pl.pallas_call(
-        functools.partial(project_back_kernel, width=width, split=len(ones)),
-        in_specs=[whole()] * (3 + len(sums)),
-        out_specs=whole(),
-        out_shape=struct((depth, width + -width % LANES + outs_grad.shape[1]), LOW),
-        compiler_params=params(16),
-        cost_estimate=cost(3),
-        name="projection_weights",
-    )(grads, normed, outs_grad, *sums)
-
-
-def finish_kernel(scalar_ref, mine_ref, other_ref, hidden_ref, own_ref, full_ref, *, begin, half):
-    row0 = begin + scalar_ref[0] * half + pl.program_id(0) * BLOCK
-    row = lax.broadcasted_iota(jnp.int32, (BLOCK, 1), 0) + row0
-    total = hidden_ref[...] + (mine_ref[...].astype(WIDE) + other_ref[...].astype(WIDE))
-    low = jnp.where(row < scalar_ref[1], total, 0.0).astype(LOW)
-    own_ref[...] = low
-    full_ref[...] = low
+        cost_estimate=cost(1),
+        name="layer_out",
+    )(scalar, mine, other, *(far(hidden) for hidden in hiddens))
 
 
 def first_back_kernel(scalar_ref, mine_ref, other_ref, tokens_ref, grad_ref, rows_ref, own_ref, full_ref):
@@ -656,62 +700,100 @@
 
 def place_rows(kernel, scalar, owned, spread, fixed, count, begin, half, name):
     depth = owned[0].shape[1]
-    blocks = half // BLOCK
+    blocks = half // STEP
 
     def own(i, scalar_ref):
         return (i, 0)
 
     def placed(i, scalar_ref):
-        return (begin // BLOCK + i + scalar_ref[0] * blocks, 0)
+        return (begin // STEP + i + scalar_ref[0] * blocks, 0)
 
     return pl.pallas_call(
         kernel,
         grid_spec=pltpu.PrefetchScalarGridSpec(
             num_scalar_prefetch=1,
             grid=(blocks,),
-            in_specs=[pl.BlockSpec((BLOCK, depth), own)] * 2
-            + [pl.BlockSpec((BLOCK, depth), placed)] * len(spread)
-            + [pl.BlockSpec((BLOCK, depth), own)] * (len(owned) - 2)
+            in_specs=[pl.BlockSpec((STEP, depth), own)] * 2
+            + [pl.BlockSpec((STEP, depth), placed)] * len(spread)
+            + [pl.BlockSpec((STEP, depth), own)] * (len(owned) - 2)
             + [whole()] * len(fixed),
-            out_specs=(pl.BlockSpec((BLOCK, depth), own), pl.BlockSpec((BLOCK, depth), placed)),
+            out_specs=(pl.BlockSpec((STEP, depth), own), pl.BlockSpec((STEP, depth), placed)),
         ),
-        out_shape=(struct((half, depth), LOW), struct((count, depth), LOW)),
+        out_shape=(struct((half, depth), LOW), stored_far((count, depth), LOW)),
         compiler_params=params(12),
         cost_estimate=cost(3),
         name=name,
     )(scalar, *owned[:2], *spread, *owned[2:], *fixed)
 
 
-def total_kernel(parts_ref, *outs, bounds, flips):
-    total = parts_ref[0].astype(WIDE)
-    for k in range(1, parts_ref.shape[0]):
-        total = total + parts_ref[k].astype(WIDE)
+def place_kernel(scalar_ref, *refs, parts):
+    for source, target in zip(refs[:parts], refs[2 * parts :]):
+        target[...] = source[...]
+
+
+def place(scalar, sources, targets):
+    parts = len(sources)
+    rows, depth = sources[0].shape
+    blocks = rows // STEP
+    return pl.pallas_call(
+        functools.partial(place_kernel, parts=parts),
+        grid_spec=pltpu.PrefetchScalarGridSpec(
+            num_scalar_prefetch=1,
+            grid=(blocks,),
+            in_specs=[pl.BlockSpec((STEP, depth), lambda i, scalar_ref: (i, 0))] * parts
+            + [pl.BlockSpec(memory_space=pl.ANY)] * parts,
+            out_specs=(pl.BlockSpec((STEP, depth), lambda i, scalar_ref: (i + (1 - scalar_ref[0]) * blocks, 0)),) * parts,
+        ),
+        out_shape=tuple(stored_far(value.shape, value.dtype) for value in targets),
+        input_output_aliases={1 + parts + k: k for k in range(parts)},
+        compiler_params=params(12),
+        cost_estimate=cost(1),
+        name="place",
+    )(scalar, *sources, *targets)
+
+
+def total_kernel(*refs, parts, bounds, flips):
+    parts_refs, outs = refs[:parts], refs[parts:]
+    if parts == 1:
+        pieces = [parts_refs[0][k] for k in range(parts_refs[0].shape[0])]
+    else:
+        pieces = [ref[...] for ref in parts_refs]
+    total = pieces[0].astype(WIDE)
+    for piece in pieces[1:]:
+        total = total + piece.astype(WIDE)
     for out, (first, last), flip in zip(outs, bounds, flips):
         piece = total[:, first:last]
         out[...] = jnp.transpose(piece) if flip else piece
 
 
 def total_parts(parts, bounds, flips):
-    rows = parts.shape[1]
+    rows = parts[0].shape[-2]
     shapes = []
     for (first, last), flip in zip(bounds, flips):
         shape = (last - first, rows) if flip else (rows, last - first)
         shapes.append(struct(shape, WIDE))
     return pl.pallas_call(
-        functools.partial(total_kernel, bounds=bounds, flips=flips),
-        in_specs=[whole()],
+        functools.partial(total_kernel, parts=len(parts), bounds=bounds, flips=flips),
+        in_specs=[whole()] * len(parts),
         out_specs=(whole(),) * len(shapes),
         out_shape=tuple(shapes),
         compiler_params=params(8),
         cost_estimate=cost(1),
         name="total",
-    )(parts)
-
-
-def exchange_batch(value):
-    size = lax.axis_size("batch")
-    parts = value.reshape(size, value.shape[0] // size, value.shape[1])
-    return lax.all_to_all(parts, "batch", 0, 0, tiled=True)
+    )(*parts)
+
+
+def exchange_far(scalar, shards, ahead=()):
+    if len(shards) == 1:
+        size = lax.axis_size("batch")
+        parts = shards[0].reshape(size, shards[0].shape[0] // size, shards[0].shape[1])
+        return [lax.all_to_all(parts, "batch", 0, 0, tiled=True)]
+    sums = fold(scalar, after(shards[0], *ahead), shards[1])
+    return [sums[0]] + [swap(piece, "batch", 2 * k) for k, piece in enumerate(sums) if k > 0]
+
+
+def exchange_near(shards):
+    return shards if len(shards) == 1 else (shards[0], swap(shards[1], "batch", 1))
 
 
 def per_device(tokens, lengths, w_query, w_key, w_value, w_out, w_up, w_down, norm_gain, norm_shift, out_grad):
@@ -733,17 +815,15 @@
     early = jnp.concatenate([w_query, w_key, w_value, w_out.T, norm_gain.T, norm_shift.T, blank], axis=1)
     late = jnp.concatenate([w_up, w_down.T], axis=1)
     if batch == 8:
-        far = gather_far(early)
+        others = gather_far(early)
         early = [early, swap(early, "batch", 1)]
-        for piece in far:
-            early += [piece, swap(piece, "batch", 1)]
-        late = after(late, *far)
+        early += [others[0], swap(others[0], "batch", 1)]
+        early += [others[1], swap(after(others[1], early[1], early[3]), "batch", 1)]
+        early += [others[2], swap(others[2], "batch", 1)]
+        late = after(late, *others, early[1], early[3], early[5])
         near = swap(late, "batch", 2)
         middle = swap(late, "batch", 4)
-        far = swap(middle, "batch", 2)
-        late = [late, swap(late, "batch", 1)]
-        for piece in (near, middle, far):
-            late += [piece, swap(piece, "batch", 1)]
+        beside = swap(late, "batch", 1)
     else:
         early = [lax.all_gather(early, "batch", axis=0, tiled=True)]
         late = [lax.all_gather(late, "batch", axis=0, tiled=True)]
@@ -752,41 +832,52 @@
     across = swap(own_outs, "tensor", 2)
     outs = (own_outs, across, swap(own_outs, "tensor", 1), swap(across, "tensor", 1))
     mixed, sums, pieces = [], [], []
-    for begin, size in chunks:
+    if batch == 8:
+        late = [late, beside, near, swap(after(near, own_outs), "batch", 1)]
+    for number, (begin, size) in enumerate(chunks):
         local = tuple(range(begin // BLOCK, (begin + size) // BLOCK))
+        if number == 1:
+            projected = after(projected, *late[3:4])
         part, logs = attend(scalar, projected, local + tuple(k + half // BLOCK for k in local), sure)
         projected = after(projected, part)
         mixed.append(part)
         sums.append(logs)
         across = swap(part, "tensor", 2)
         pieces.append((part, across, swap(part, "tensor", 1), swap(across, "tensor", 1)))
-    late = lax.optimization_barrier((*late, *pieces[-1]))[: len(late)]
+        if number == 0 and batch == 8:
+            middle = after(middle, part)
+            late += [middle, swap(middle, "batch", 1)]
+            last = swap(middle, "batch", 2)
+    if batch == 8:
+        last = after(last, part)
+        late += [last, swap(last, "batch", 1)]
+    late = lax.optimization_barrier((*late, *mixed))[: len(late)]
     full_up, full_down = assemble(scalar, late, units)
+    rows = after(rows, pieces[-1][1])
 
     stored = []
-    twos, halves = [], []
+    twos, halves, hiddens = jnp.zeros((8, depth), WIDE), [], []
     for (begin, size), piece in zip(chunks, pieces):
         ends = []
         rows = after(rows, *(mine for mine, _ in halves))
         for keep in (False, True):
-            back, two, *fresh = feed(
-                scalar, tokens, out_grad, piece, outs, full_up, full_down, rows, stored, begin, size, keep
+            back, twos, *stored = feed(
+                scalar, tokens, out_grad, piece, outs, full_up, full_down, rows, twos, stored, begin, size, keep
             )
-            stored = fresh + stored[len(fresh) :]
-            twos.append(two)
             ends.append(back)
+        hiddens.append(stored.pop())
         mine = (ends[1].astype(WIDE) + swap(ends[0], "tensor", 1).astype(WIDE)).astype(LOW)
         halves.append((mine, swap(mine, "tensor", 2)))
-    normed_two, active, upper, hidden = stored
+    normed_two, active, upper = stored
     normed_two = after(normed_two, *(mine for mine, _ in halves))
-    branch_keep, branch_send, feed_grads = weigh(scalar, normed_two, upper, active, out_grad, full_down)
-    feed_parts = exchange_batch(feed_grads)
+    branch_keep, branch_send, *feed_grads = weigh(scalar, normed_two, upper, active, out_grad, full_down, 0)
+    feed_parts = exchange_far(scalar, feed_grads)
 
     beside = swap(branch_send, "tensor", 1)
     grads = []
-    for (begin, size), (mine, other) in zip(chunks, halves):
-        mine = after(mine, feed_grads)
-        low = second_back(scalar, mine, other, hidden, out_grad, rows, begin, size)
+    for (begin, size), (mine, other), hidden in zip(chunks, halves, hiddens):
+        mine = after(mine, *feed_grads)
+        low = second_back(scalar, mine, other, hidden, out_grad, rows, begin)
         grads += [low, swap(low, "tensor", 1)]
     branch_mine = (branch_keep.astype(WIDE) + beside.astype(WIDE)).astype(LOW)
     branch_mine = after(branch_mine, *grads)
@@ -796,41 +887,32 @@
         scalar, projected, own_outs, mixed, sums, grads, chunks, sure
     )
 
-    own_out, layer_out = place_rows(
-        functools.partial(finish_kernel, begin=0, half=half),
-        scalar,
-        (branch_mine, branch_other, hidden),
-        (),
-        (),
-        count,
-        0,
-        half,
-        "layer_out",
-    )
     there = (1 - core) * half
-    layer_out = lax.dynamic_update_slice(layer_out, swap(own_out, "tensor", 1), (there, 0))
-
-    ends, ones = [], []
-    attend_grads = after(attend_grads, branch_other)
+    ends, ones = [], jnp.zeros((8, depth), WIDE)
     for keep in (False, True):
-        back, one = inward(scalar, attend_grads, tokens, weights, 0, half, keep)
+        if keep:
+            attend_grads = after(attend_grads, branch_other)
+        back, ones = inward(scalar, attend_grads, tokens, weights, ones, keep)
         ends.append(back)
-        ones.append(one)
-    back = pair_sum(ends[1], ends[0])
-    project_parts = exchange_batch(after(project_back(attend_grads, normed, outs_grad, ones, twos), feed_parts))
-    own_grad, grad_input = place_rows(
-        first_back_kernel, scalar, back, (tokens, grad_attn), (rows,), count, 0, half, "first_norm_backward"
-    )
-    grad_input = lax.dynamic_update_slice(grad_input, swap(own_grad, "tensor", 1), (there, 0))
-
-    shard_up, shard_down = total_parts(feed_parts, ((0, units), (units, 2 * units)), (False, True))
+    mine = (ends[1].astype(WIDE) + swap(ends[0], "tensor", 1).astype(WIDE)).astype(LOW)
+    other = swap(mine, "tensor", 2)
+    project_grads = project_back(scalar, after(attend_grads, mine), normed, outs_grad, ones, twos, batch)
+    project_parts = exchange_far(scalar, exchange_near(project_grads))
+    own_out, layer_out = finish(scalar, branch_mine, after(branch_other, project_parts[0]), hiddens, count)
+    other_out = swap(own_out, "tensor", 1)
+    shard_up, shard_down = total_parts(feed_parts, ((0, units), (units, 2 * units)), (False, False))
     last = 3 * width
-    final = project_parts.shape[2]
+    final = project_parts[0].shape[-1]
     shard_query, shard_key, shard_value, small, shard_out = total_parts(
         project_parts,
         ((0, width), (width, 2 * width), (2 * width, last), (last, final - width), (final - width, final)),
         (False, False, False, True, True),
     )
+    mine = after(mine, own_out, shard_up, small)
+    own_grad, grad_input = place_rows(
+        first_back_kernel, scalar, (mine, other), (tokens, grad_attn), (rows,), count, 0, half, "first_norm_backward"
+    )
+    layer_out, grad_input = place(scalar, (other_out, swap(own_grad, "tensor", 1)), (layer_out, grad_input))
     small = small[:16]
     small = small + swap(small, "tensor", 2)
     small = small + swap(small, "tensor", 1)
@@ -844,7 +926,7 @@
         shard_value,
         shard_out,
         shard_up,
-        shard_down,
+        shard_down.T,
         shard_gain,
         shard_shift,
     )

time: 236 us -> 212 us (0.90)
  Pallas kernels: 102 us -> 89.7 us
  local copies, waits for them, and re-layouts: 16.8 us -> 5.86 us
  waiting for transfers between devices: 64.6 us -> 54.6 us
  starting transfers between devices: 41 us -> 50.9 us
    all_to_all x2 -> x1, waiting for transfers between devices: 14.6 us -> 0.01 us  [exchange_far(): return [lax.all_to_all(parts, 'batch', 0, 0, tiled=True)]]
    ppermute x37 -> x41, starting transfers between devices: 32.3 us -> 45.8 us  [swap(): return lax.ppermute(value, axis, [(i, i ^ bits) for i in range(size)])]
    pallas_call x8 -> x11, Pallas kernels: 47.4 us -> 38.9 us  [the longest x4 15.8 us: feed(): pl.pallas_call(functools.partial(feed_kernel, begin=begin, size=size, hal...]
    unnamed x86 -> x39, local copies, waits for them, and re-layouts: 12.4 us -> 4.86 us
    ppermute x37 -> x41, waiting for transfers between devices: 50 us -> 54.6 us  [swap(): return lax.ppermute(value, axis, [(i, i ^ bits) for i in range(size)])]
    all_to_all x2 -> x1, starting transfers between devices: 8.79 us -> 5.11 us  [exchange_far(): return [lax.all_to_all(parts, 'batch', 0, 0, tiled=True)]]
    dynamic_update_slice x2 -> x0, local copies, waits for them, and re-layouts: 3.46 us -> none  [the longest x1 2.37 us: per_device(): lax.dynamic_update_slice(layer_out, swap(own_out, 'tensor', 1), (there, 0))]
    pallas_call x2 -> x1, Pallas kernels: 7.53 us -> 4.28 us  [place_rows(): pl.pallas_call(kernel, grid_spec=pltpu.PrefetchScalarGridSpec(num_scalar_...]
  transfers between devices with their start and end apart: 39 -> 42, of which waited for: 14 -> 13; matrix products, arithmetic and copies ran while one was open for 4% -> 3% of each run, Pallas kernels for 35% -> 38%
where the time goes in v3:
time: 212 us; the launch traced here: 209 us
  Pallas kernels  89.7 us (42%)
  waiting for transfers between devices  54.6 us (26%)
  starting transfers between devices  50.9 us (24%)
  other arithmetic  6.28 us (3%)
  local copies, waits for them, and re-layouts  5.86 us (3%)
    ppermute x41, waiting for transfers between devices, swap(): return lax.ppermute(value, axis, [(i, i ^ bits) for i in range(size)])  54.6 us
    ppermute x41, starting transfers between devices, swap(): return lax.ppermute(value, axis, [(i, i ^ bits) for i in range(size)])  45.8 us
    pallas_call x1, Pallas kernels, attend_back(): pl.pallas_call(functools.partial(attend_back_kernel, chunks=chunks, rows=...  18.3 us
    pallas_call x4, Pallas kernels, feed(): pl.pallas_call(functools.partial(feed_kernel, begin=begin, size=size, hal...  15.8 us
    pallas_call x2, Pallas kernels, attend(): pl.pallas_call(functools.partial(attend_kernel, places=places, heads=head...  11.3 us
    pallas_call x1, Pallas kernels, weigh(): pl.pallas_call(weigh_kernel, grid_spec=pltpu.PrefetchScalarGridSpec(num_s...  9.11 us
    pallas_call x2, Pallas kernels, second_back(): pl.pallas_call(functools.partial(second_back_kernel, begin=begin, half=ha...  6.14 us
    pallas_call x1, Pallas kernels, project(): pl.pallas_call(functools.partial(project_kernel, parts=len(pieces), width...  5.62 us
  transfers between devices with their start and end apart: 42, of which 13 were waited for; matrix products, arithmetic and copies ran while one was open for 3% of the time, Pallas kernels for 38%

profile of v3, /device:TPU:0, one launch (start us, length us, event | category | flops | bytes accessed | tf_op | source)
XLA Modules:
  0.0 209.2 jit_solution(17970022123393267553)
XLA Ops:
  4.1 3.1 %collective-permute-start.1 = (bf16[96,896]{1,0:T(8,128)(2,1)S(1)}, bf16[96,896]{1,0:T(8,128)(2,1)S(1)}, u32[]{:S(2)}, u32[]{:S(2)}) collective-permute-start(bf16[96,896]{1,0:T(8,128)(2,1)S(1)} %concatenate.6.refs_0_), channel_id=1, source_target_pairs={{0,8},{4,12},{8,0},{12,4},{16,24},{20,28},{24,16},{28,20},{1,9},{5... | collective-permute-start | bytes 516104 | tf_op jit(solution)/shard_map/ppermute | solution.py:72
  7.2 1.5 collective-permute-start
  8.7 2.6 %collective-permute-start.3 = (bf16[96,896]{1,0:T(8,128)(2,1)S(1)}, bf16[96,896]{1,0:T(8,128)(2,1)S(1)}, u32[]{:S(2)}, u32[]{:S(2)}) collective-permute-start(bf16[96,896]{1,0:T(8,128)(2,1)S(1)} %concatenate.6.refs_0_), channel_id=1, source_target_pairs={{0,16},{4,20},{8,24},{12,28},{16,0},{20,4},{24,8},{28,12},{1,17},{... | collective-permute-start | bytes 516104 | tf_op jit(solution)/shard_map/ppermute | solution.py:72
  11.6 5.0 %collective-permute-start.2 = (bf16[96,896]{1,0:T(8,128)(2,1)S(1)}, bf16[96,896]{1,0:T(8,128)(2,1)S(1)}, u32[]{:S(2)}, u32[]{:S(2)}) collective-permute-start(bf16[96,896]{1,0:T(8,128)(2,1)S(1)} %collective-permute-done.1.refs_2_), channel_id=1, source_target_pairs={{0,4},{4,0},{8,12},{12,8},{16,20},{20,16},{24,28},{28,24},{1,5},{5... | collective-permute-start | bytes 516104 | tf_op jit(solution)/shard_map/ppermute | solution.py:72
  16.6 2.5 %collective-permute-start.5 = (bf16[96,896]{1,0:T(8,128)(2,1)S(1)}, bf16[96,896]{1,0:T(8,128)(2,1)S(1)}, u32[]{:S(2)}, u32[]{:S(2)}) collective-permute-start(bf16[96,896]{1,0:T(8,128)(2,1)S(1)} %concatenate.6.refs_0_), channel_id=1, source_target_pairs={{0,24},{4,28},{8,16},{12,20},{16,8},{20,12},{24,0},{28,4},{1,25},{... | collective-permute-start | bytes 516104 | tf_op jit(solution)/shard_map/ppermute | solution.py:72
  19.1 2.9 %collective-permute-done.3.refs_4_ = bf16[96,896]{1,0:T(8,128)(2,1)S(1)} collective-permute-done((bf16[96,896]{1,0:T(8,128)(2,1)S(1)}, bf16[96,896]{1,0:T(8,128)(2,1)S(1)}, u32[]{:S(2)}, u32[]{:S(2)}) %collective-permute-start.3) | collective-permute-done | bytes 172064 | tf_op jit(solution)/shard_map/ppermute | solution.py:72
  22.4 1.7 pad_maximum_fusion.refs_0_
  24.1 3.3 %collective-permute-done.4.refs_5_ = bf16[96,896]{1,0:T(8,128)(2,1)S(1)} collective-permute-done((bf16[96,896]{1,0:T(8,128)(2,1)S(1)}, bf16[96,896]{1,0:T(8,128)(2,1)S(1)}, u32[]{:S(2)}, u32[]{:S(2)}) %collective-permute-start.4) | collective-permute-done | bytes 172064 | tf_op jit(solution)/shard_map/ppermute | solution.py:72
  27.4 2.0 collective-permute-start.6
  30.1 5.1 %collective-permute-start.16 = (bf16[96,1536]{1,0:T(8,128)(2,1)}, bf16[96,1536]{1,0:T(8,128)(2,1)S(1)}, u32[]{:S(2)}, u32[]{:S(2)}) collective-permute-start(bf16[96,1536]{1,0:T(8,128)(2,1)} %pad_maximum_fusion.refs_0_), channel_id=1, source_target_pairs={{0,16},{4,20},{8,24},{12,28},{16,0},{20,4},{24,8},{28,12},{1,17},{... | collective-permute-start | bytes 884744 | tf_op jit(solution)/shard_map/ppermute | solution.py:72
  35.3 5.6 %project.1 = (bf16[1536,768]{1,0:T(8,128)(2,1)}, bf16[1536,576]{1,0:T(8,128)(2,1)S(1)}, f32[8,768]{1,0:T(8,128)S(1)}, bf16[768,896]{1,0:T(8,128)(2,1)S(1)}, bf16[192,768]{1,0:T(8,128)(2,1)S(1)}) custom-call(s32[4]{0:T(128)S(1)} %pad_add_fusion.scalar_ref, bf16[96,896]{1,0:T(8,128)(2,1)S(1)} %concatenate.6.refs_0_, ...), custom_call_target="tpu_custom_call" | custom-call | flops 4400000 | tf_op jit(solution)/shard_map/project/pallas_call | solution.py:128
  43.0 6.5 %attend_forward.2 = (bf16[192,1024]{1,0:T(8,128)(2,1)S(1)}, f32[4,8,256]{2,1,0:T(8,128)S(1)}) custom-call(s32[4]{0:T(128)S(1)} %pad_add_fusion.scalar_ref, bf16[1536,576]{1,0:T(8,128)(2,1)S(1)} %get-tuple-element.152.projected_ref.refs_0_), custom_call_target="tpu_custom_call" | custom-call | flops 1100000 | tf_op jit(solution)/shard_map/attend_forward/pallas_call | solution.py:232
  49.6 1.5 collective-permute-start.20
  52.8 4.8 %attend_forward.3 = (bf16[192,512]{1,0:T(8,128)(2,1)S(1)}, f32[2,8,256]{2,1,0:T(8,128)S(1)}) custom-call(s32[4]{0:T(128)S(1)} %pad_add_fusion.scalar_ref, bf16[1536,576]{1,0:T(8,128)(2,1)S(1)} %get-tuple-element.152.projected_ref.refs_0_), custom_call_target="tpu_custom_call" | custom-call | flops 1100000 | tf_op jit(solution)/shard_map/attend_forward/pallas_call | solution.py:232
  57.6 1.6 collective-permute-start.9
  60.2 2.6 %collective-permute-done.12.refs_7_ = bf16[192,768]{1,0:T(8,128)(2,1)S(1)} collective-permute-done((bf16[192,768]{1,0:T(8,128)(2,1)S(1)}, bf16[192,768]{1,0:T(8,128)(2,1)S(1)}, u32[]{:S(2)}, u32[]{:S(2)}) %collective-permute-start.12) | collective-permute-done | bytes 294944 | tf_op jit(solution)/shard_map/ppermute | solution.py:72
  62.9 1.5 collective-permute-start.19
  65.0 4.6 %collective-permute-done.19.refs_7_ = bf16[96,1536]{1,0:T(8,128)(2,1)S(1)} collective-permute-done((bf16[96,1536]{1,0:T(8,128)(2,1)S(1)}, bf16[96,1536]{1,0:T(8,128)(2,1)S(1)}, u32[]{:S(2)}, u32[]{:S(2)}) %collective-permute-start.19) | collective-permute-done | bytes 294944 | tf_op jit(solution)/shard_map/ppermute | solution.py:72
  70.9 4.9 %feed_forward.4 = (bf16[512,768]{1,0:T(8,128)(2,1)S(1)}, f32[8,768]{1,0:T(8,128)S(1)}, bf16[1536,768]{1,0:T(8,128)(2,1)S(1)}, bf16[1536,768]{1,0:T(8,128)(2,1)S(1)}, bf16[1536,768]{1,0:T(8,128)(2,1)S(1)}) custom-call(s32[4]{0:T(128)S(1)} %pad_add_fusion.scalar_ref, bf16[1536,768]{1,0:T(8,128)(2,1)S(1)} %copy-done, bf16[1536,768]{1,0:T(8,128)(2,1)S(1)} %copy-done.1, ...), custom_call_target="tpu_custom_call" | custom-call | flops 563200 | tf_op jit(solution)/shard_map/feed_forward/pallas_call | solution.py:430
  76.4 4.7 %feed_forward.5 = (bf16[512,768]{1,0:T(8,128)(2,1)S(1)}, f32[8,768]{1,0:T(8,128)S(1)}, bf16[1536,768]{1,0:T(8,128)(2,1)S(1)}, bf16[1536,768]{1,0:T(8,128)(2,1)S(...) custom-call(s32[4]{0:T(128)S(1)} %pad_add_fusion.scalar_ref, ...), custom_call_target="tpu_custom_call", output_to_operand_aliasing={{2}: (15, {}), {3}: (16, {}), {4}: (17, {})} | custom-call | flops 563200 | tf_op jit(solution)/shard_map/feed_forward/pallas_call | solution.py:430
  82.2 2.9 %feed_forward.6 = (bf16[256,768]{1,0:T(8,128)(2,1)S(1)}, f32[8,768]{1,0:T(8,128)S(1)}, bf16[1536,768]{1,0:T(8,128)(2,1)S(1)}, bf16[1536,768]{1,0:T(8,128)(2,1)S(1)}, bf16[1536,768]{1,0:T(8,128)(2,1)S(1)}) custom-call(s32[4]{0:T(128)S(1)} %pad_add_fusion.scalar_ref, ...), custom_call_target="tpu_custom_call", output_to_operand_aliasing={{2}: (15, {}), {3}: (16, {}), {4}: (17, {})} | custom-call | flops 281600 | tf_op jit(solution)/shard_map/feed_forward/pallas_call | solution.py:430
  85.6 1.5 collective-permute-start.26
  87.1 3.3 %feed_forward.7 = (bf16[256,768]{1,0:T(8,128)(2,1)S(1)}, f32[8,768]{1,0:T(8,128)S(1)}, bf16[1536,768]{1,0:T(8,128)(2,1)S(1)}, bf16[1536,768]{1,0:T(8,128)(2,1)S(...) custom-call(s32[4]{0:T(128)S(1)} %pad_add_fusion.scalar_ref, ...), custom_call_target="tpu_custom_call", output_to_operand_aliasing={{2}: (15, {}), {3}: (16, {}), {4}: (17, {})} | custom-call | flops 281600 | tf_op jit(solution)/shard_map/feed_forward/pallas_call | solution.py:430
  91.3 9.1 %feed_forward_weights.1 = (bf16[768,768]{1,0:T(8,128)(2,1)S(1)}, bf16[768,768]{1,0:T(8,128)(2,1)}, bf16[768,1536]{1,0:T(8,128)(2,1)}) custom-call(s32[4]{0:T(128)S(1)} %pad_add_fusion.scalar_ref, bf16[1536,768]{1,0:T(8,128)(2,1)S(1)} %get-tuple-element.140.normed_ref, bf16[1536,768]{1,0:T(8,128)(2,1)S(1)} %get-tuple-element.141.upper_ref, ...), custom_call_target="tpu_custom_call" | custom-call | flops 1100000 | tf_op jit(solution)/shard_map/feed_forward_weights/pallas_call | solution.py:505
  101.5 5.1 %all-to-all-start = ((bf16[8,96,1536]{2,1,0:T(8,128)(2,1)}), bf16[8,96,1536]{2,1,0:T(8,128)(2,1)}, u32[]{:S(2)}, u32[]{:S(2)}) async-start(bf16[8,96,1536]{2,1,0:T(8,128)(2,1)} %bitcast.9), calls=%async_computation | async-start | bytes 4718592 | tf_op jit(solution)/shard_map/all_to_all | solution.py:790
  106.6 1.3 collective-permute-start.28
  107.9 3.8 %second_norm_backward.2.refs_6_ = bf16[512,768]{1,0:T(8,128)(2,1)S(1)} custom-call(s32[4]{0:T(128)S(1)} %pad_add_fusion.scalar_ref, bf16[512,768]{1,0:T(8,128)(2,1)} %add_convert_fusion.2.mine_ref, bf16[512,768]{1,0:T(8,128)(2,1)} %collective-permute-done.26.other_ref, f32[512,768]{1,0:T(8,128)} %get-tuple-element.147.hidden_ref.refs_0_, ...), custom_call_target="tpu_custom_call" | custom-call | flops 563200 | tf_op jit(solution)/shard_map/second_norm_backward/pallas_call | solution.py:561
  111.7 6.3 %collective-permute-done.28.other_ref = bf16[256,768]{1,0:T(8,128)(2,1)S(1)} collective-permute-done((bf16[256,768]{1,0:T(8,128)(2,1)}, bf16[256,768]{1,0:T(8,128)(2,1)S(1)}, u32[]{:S(2)}, u32[]{:S(2)}) %collective-permute-start.28) | collective-permute-done | bytes 393248 | tf_op jit(solution)/shard_map/ppermute | solution.py:72
  118.0 2.4 %second_norm_backward.3.refs_8_ = bf16[256,768]{1,0:T(8,128)(2,1)S(1)} custom-call(s32[4]{0:T(128)S(1)} %pad_add_fusion.scalar_ref, bf16[256,768]{1,0:T(8,128)(2,1)S(1)} %copy-done.9, bf16[256,768]{1,0:T(8,128)(2,1)S(1)} %collective-permute-done.28.other_ref, f32[256,768]{1,0:T(8,128)} %get-tuple-element.149.hidden_ref.refs_1_, bf16[1536,768]{1,0:T(8,128)(2,1)} %grad_ref.5, ...), custom_call_target="tpu_custom_call" | custom-call | flops 281600 | tf_op jit(solution)/shard_map/second_norm_backward/pallas_call | solution.py:561
  120.5 1.7 add_convert_fusion.1.mine_ref
  122.2 1.4 collective-permute-start.30
  123.6 18.3 %attend_backward.1 = (bf16[576,1536]{1,0:T(8,128)(2,1)S(1)}, bf16[768,192]{1,0:T(8,128)(2,1)S(1)}, bf16[1536,768]{1,0:T(8,128)(2,1)S(1)}) custom-call(s32[4]{0:T(128)S(1)} %pad_add_fusion.scalar_ref, bf16[1536,576]{1,0:T(8,128)(2,1)S(1)} %copy-done.3, bf16[192,768]{1,0:T(8,128)(2,1)S(1)} %get-tuple-element.104.refs_6_.refs_1_, ...), custom_call_target="tpu_custom_call" | custom-call | flops 8800000 | tf_op jit(solution)/shard_map/attend_backward/pallas_call | solution.py:334
  142.0 1.9 grad_normed.2
  144.0 6.5 %collective-permute-done.30.other_ref = bf16[768,768]{1,0:T(8,128)(2,1)S(1)} collective-permute-done((bf16[768,768]{1,0:T(8,128)(2,1)S(1)}, bf16[768,768]{1,0:T(8,128)(2,1)S(1)}, u32[]{:S(2)}, u32[]{:S(2)}) %collective-permute-start.30) | collective-permute-done | bytes 1179680 | tf_op jit(solution)/shard_map/ppermute | solution.py:72
  150.5 1.9 grad_normed.3
  152.8 1.4 collective-permute-start.37
  154.2 2.3 %projection_weights.1 = (bf16[4,96,832]{2,1,0:T(8,128)(2,1)S(1)}, bf16[4,96,832]{2,1,0:T(8,128)(2,1)S(1)}) custom-call(s32[4]{0:T(128)S(1)} %pad_add_fusion.scalar_ref, bf16[576,1536]{1,0:T(8,128)(2,1)S(1)} %get-tuple-element.161.grads_ref, bf16[1536,768]{1,0:T(8,128)(2,1)S(1)} %copy-done.6, bf16[768,192]{1,0:T(8,128)(2,1)S(1)} %get-tuple-element.163.outs_ref, ...), custom_call_target="tpu_custom_call" | custom-call | flops 1100000 | tf_op jit(solution)/shard_map/projection_weights/pallas_call | solution.py:627
  156.5 1.8 collective-permute-start.32
  158.3 15.2 %collective-permute-done.32.other_ref = bf16[4,96,832]{2,1,0:T(8,128)(2,1)S(1)} collective-permute-done((bf16[4,96,832]{2,1,0:T(8,128)(2,1)S(1)}, bf16[4,96,832]{2,1,0:T(8,128)(2,1)S(1)}, u32[]{:S(2)}, u32[]{:S(2)}) %collective-permute-start.32) | collective-permute-done | bytes 639008 | tf_op jit(solution)/shard_map/ppermute | solution.py:72
  174.3 1.8 collective-permute-start.34
  176.1 2.3 %collective-permute-start.35 = (bf16[96,832]{1,0:T(8,128)(2,1)S(1)}, bf16[96,832]{1,0:T(8,128)(2,1)S(1)}, u32[]{:S(2)}, u32[]{:S(2)}) collective-permute-start(bf16[96,832]{1,0:T(8,128)(2,1)S(1)} %get-tuple-element.173), channel_id=1, source_target_pairs={{0,16},{4,20},{8,24},{12,28},{16,0},{20,4},{24,8},{28,12},{1,17},{... | collective-permute-start | bytes 479240 | tf_op jit(solution)/shard_map/ppermute | solution.py:72
  178.7 4.2 %layer_out.1 = (bf16[768,768]{1,0:T(8,128)(2,1)}, bf16[1536,768]{1,0:T(8,128)(2,1)}) custom-call(s32[4]{0:T(128)S(1)} %pad_add_fusion.scalar_ref, bf16[768,768]{1,0:T(8,128)(2,1)S(1)} %add_convert_fusion.1.mine_ref, bf16[768,768]{1,0:T(8,128)(2,1)S(1)} %collective-permute-done.30.other_ref, f32[512,768]{1,0:T(8,128)} %get-tuple-element.147.hidden_ref.refs_0_, ...), custom_call_target="tpu_custom_call" | custom-call | flops 1100000 | tf_op jit(solution)/shard_map/layer_out/pallas_call | solution.py:674
  182.9 8.1 %collective-permute-done.35.refs_2_ = bf16[96,832]{1,0:T(8,128)(2,1)S(1)} collective-permute-done((bf16[96,832]{1,0:T(8,128)(2,1)S(1)}, bf16[96,832]{1,0:T(8,128)(2,1)S(1)}, u32[]{:S(2)}, u32[]{:S(2)}) %collective-permute-start.35) | collective-permute-done | bytes 159776 | tf_op jit(solution)/shard_map/ppermute | solution.py:72
  192.5 2.8 %total.2 = (f32[96,768]{1,0:T(8,128)}, f32[96,768]{1,0:T(8,128)}) custom-call(bf16[8,96,1536]{2,1,0:T(8,128)(2,1)} %all-to-all-done.refs_0_), custom_call_target="tpu_custom_call" | custom-call | flops 1100000 | tf_op jit(solution)/shard_map/total/pallas_call | solution.py:775
  196.1 4.3 %first_norm_backward.1 = (bf16[768,768]{1,0:T(8,128)(2,1)S(1)}, bf16[1536,768]{1,0:T(8,128)(2,1)}) custom-call(s32[4]{0:T(128)S(1)} %pad_add_fusion.scalar_ref, bf16[768,768]{1,0:T(8,128)(2,1)S(1)} %add_convert_fusion.mine_ref, bf16[768,768]{1,0:T(8,128)(2,1)} %collective-permute-done.37.other_ref, bf16[1536,768]{1,0:T(8,128)(2,1)S(1)} %copy-done, ...), custom_call_target="tpu_custom_call" | custom-call | flops 3300000 | tf_op jit(solution)/shard_map/first_norm_backward/pallas_call | solution.py:711
  200.4 1.4 collective-permute-start.39
  201.8 2.3 %collective-permute-done.39 = f32[16,96]{1,0:T(8,128)S(1)} collective-permute-done((f32[16,96]{1,0:T(8,128)S(1)}, f32[16,96]{1,0:T(8,128)S(1)}, u32[]{:S(2)}, u32[]{:S(2)}) %collective-permute-start.39) | collective-permute-done | bytes 6176 | tf_op jit(solution)/shard_map/ppermute | solution.py:72
  205.9 3.1 %place.1 = (bf16[1536,768]{1,0:T(8,128)(2,1)}, bf16[1536,768]{1,0:T(8,128)(2,1)}) custom-call(s32[4]{0:T(128)S(1)} %pad_add_fusion.scalar_ref, bf16[768,768]{1,0:T(8,128)(2,1)} %collective-permute-done.33.refs_0_, bf16[768,768]{1,0:T(8,128)(2,1)S(1)} %collective-permute-done.38.refs_1_, ...), custom_call_target="tpu_custom_call", output_to_operand_aliasing={{0}: (3, {}), {1}: (4, {})} | custom-call | flops 1100000 | tf_op jit(solution)/shard_map/place/pallas_call | solution.py:738
  (110 shorter events, 20.8 us)
Async XLA Ops:
  4.1 7.5 %collective-permute-start.1 = (bf16[96,896]{1,0:T(8,128)(2,1)S(1)}, bf16[96,896]{1,0:T(8,128)(2,1)S(1)}, u32[]{:S(2)}, u32[]{:S(2)}) collective-permute-start(bf16[96,896]{1,0:T(8,128)(2,1)S(1)} %concatenate.6.refs_0_), channel_id=1, source_target_pairs={{0,8},{4,12},{8,0},{12,4},{16,24},{20,28},{24,16},{28,20},{1,9},{5... | collective-permute-start | bytes 516104 | tf_op jit(solution)/shard_map/ppermute | solution.py:72
  7.2 11.9 %collective-permute-start = (bf16[96,896]{1,0:T(8,128)(2,1)S(1)}, bf16[96,896]{1,0:T(8,128)(2,1)S(1)}, u32[]{:S(2)}, u32[]{:S(2)}) collective-permute-start(bf16[96,896]{1,0:T(8,128)(2,1)S(1)} %concatenate.6.refs_0_), channel_id=1, source_target_pairs={{0,4},{4,0},{8,12},{12,8},{16,20},{20,16},{24,28},{28,24},{1,5},{5... | collective-permute-start | bytes 516104 | tf_op jit(solution)/shard_map/ppermute | solution.py:72
  8.7 13.3 %collective-permute-start.3 = (bf16[96,896]{1,0:T(8,128)(2,1)S(1)}, bf16[96,896]{1,0:T(8,128)(2,1)S(1)}, u32[]{:S(2)}, u32[]{:S(2)}) collective-permute-start(bf16[96,896]{1,0:T(8,128)(2,1)S(1)} %concatenate.6.refs_0_), channel_id=1, source_target_pairs={{0,16},{4,20},{8,24},{12,28},{16,0},{20,4},{24,8},{28,12},{1,17},{... | collective-permute-start | bytes 516104 | tf_op jit(solution)/shard_map/ppermute | solution.py:72
  11.6 10.4 %collective-permute-start.2 = (bf16[96,896]{1,0:T(8,128)(2,1)S(1)}, bf16[96,896]{1,0:T(8,128)(2,1)S(1)}, u32[]{:S(2)}, u32[]{:S(2)}) collective-permute-start(bf16[96,896]{1,0:T(8,128)(2,1)S(1)} %collective-permute-done.1.refs_2_), channel_id=1, source_target_pairs={{0,4},{4,0},{8,12},{12,8},{16,20},{20,16},{24,28},{28,24},{1,5},{5... | collective-permute-start | bytes 516104 | tf_op jit(solution)/shard_map/ppermute | solution.py:72
  16.6 7.6 %collective-permute-start.5 = (bf16[96,896]{1,0:T(8,128)(2,1)S(1)}, bf16[96,896]{1,0:T(8,128)(2,1)S(1)}, u32[]{:S(2)}, u32[]{:S(2)}) collective-permute-start(bf16[96,896]{1,0:T(8,128)(2,1)S(1)} %concatenate.6.refs_0_), channel_id=1, source_target_pairs={{0,24},{4,28},{8,16},{12,20},{16,8},{20,12},{24,0},{28,4},{1,25},{... | collective-permute-start | bytes 516104 | tf_op jit(solution)/shard_map/ppermute | solution.py:72
  22.0 5.4 %collective-permute-start.4 = (bf16[96,896]{1,0:T(8,128)(2,1)S(1)}, bf16[96,896]{1,0:T(8,128)(2,1)S(1)}, u32[]{:S(2)}, u32[]{:S(2)}) collective-permute-start(bf16[96,896]{1,0:T(8,128)(2,1)S(1)} %collective-permute-done.3.refs_4_), channel_id=1, source_target_pairs={{0,4},{4,0},{8,12},{12,8},{16,20},{20,16},{24,28},{28,24},{1,5},{5... | collective-permute-start | bytes 516104 | tf_op jit(solution)/shard_map/ppermute | solution.py:72
  27.4 13.5 %collective-permute-start.7 = (bf16[96,1536]{1,0:T(8,128)(2,1)}, bf16[96,1536]{1,0:T(8,128)(2,1)}, u32[]{:S(2)}, u32[]{:S(2)}) collective-permute-start(bf16[96,1536]{1,0:T(8,128)(2,1)} %pad_maximum_fusion.refs_0_), channel_id=1, source_target_pairs={{0,8},{4,12},{8,0},{12,4},{16,24},{20,28},{24,16},{28,20},{1,9},{5... | collective-permute-start | bytes 884744 | tf_op jit(solution)/shard_map/ppermute | solution.py:72
  27.4 7.8 %collective-permute-start.6 = (bf16[96,896]{1,0:T(8,128)(2,1)S(1)}, bf16[96,896]{1,0:T(8,128)(2,1)S(1)}, u32[]{:S(2)}, u32[]{:S(2)}) collective-permute-start(bf16[96,896]{1,0:T(8,128)(2,1)S(1)} %collective-permute-done.5.refs_6_), channel_id=1, source_target_pairs={{0,4},{4,0},{8,12},{12,8},{16,20},{20,16},{24,28},{28,24},{1,5},{5... | collective-permute-start | bytes 516104 | tf_op jit(solution)/shard_map/ppermute | solution.py:72
  30.1 21.0 %collective-permute-start.16 = (bf16[96,1536]{1,0:T(8,128)(2,1)}, bf16[96,1536]{1,0:T(8,128)(2,1)S(1)}, u32[]{:S(2)}, u32[]{:S(2)}) collective-permute-start(bf16[96,1536]{1,0:T(8,128)(2,1)} %pad_maximum_fusion.refs_0_), channel_id=1, source_target_pairs={{0,16},{4,20},{8,24},{12,28},{16,0},{20,4},{24,8},{28,12},{1,17},{... | collective-permute-start | bytes 884744 | tf_op jit(solution)/shard_map/ppermute | solution.py:72
  40.9 16.7 %copy-start.2 = (bf16[1536,576]{1,0:T(8,128)(2,1)}, bf16[1536,576]{1,0:T(8,128)(2,1)S(1)}, u32[]{:S(2)}) copy-start(bf16[1536,576]{1,0:T(8,128)(2,1)S(1)} %get-tuple-element.152.projected_ref.refs_0_) | copy-start | bytes 5308420
  40.9 16.7 %copy-start.4 = (bf16[768,896]{1,0:T(8,128)(2,1)}, bf16[768,896]{1,0:T(8,128)(2,1)S(1)}, u32[]{:S(2)}) copy-start(bf16[768,896]{1,0:T(8,128)(2,1)S(1)} %get-tuple-element.157.weights_ref) | copy-start | bytes 4128772
  40.9 77.1 %copy-start.10 = (f32[8,768]{1,0:T(8,128)}, f32[8,768]{1,0:T(8,128)S(1)}, u32[]{:S(2)}) copy-start(f32[8,768]{1,0:T(8,128)S(1)} %get-tuple-element.128.refs_12_.rows_ref) | copy-start | bytes 73732
  40.9 10.7 %collective-permute-start.8 = (bf16[96,1536]{1,0:T(8,128)(2,1)}, bf16[96,1536]{1,0:T(8,128)(2,1)S(1)}, u32[]{:S(2)}, u32[]{:S(2)}) collective-permute-start(bf16[96,1536]{1,0:T(8,128)(2,1)} %collective-permute-done.7.refs_2_), channel_id=1, source_target_pairs={{0,4},{4,0},{8,12},{12,8},{16,20},{20,16},{24,28},{28,24},{1,5},{5... | collective-permute-start | bytes 884744 | tf_op jit(solution)/shard_map/ppermute | solution.py:72
  42.2 15.5 %collective-permute-start.15 = (bf16[96,1536]{1,0:T(8,128)(2,1)}, bf16[96,1536]{1,0:T(8,128)(2,1)S(1)}, u32[]{:S(2)}, u32[]{:S(2)}) collective-permute-start(bf16[96,1536]{1,0:T(8,128)(2,1)} %pad_maximum_fusion.refs_0_), channel_id=1, source_target_pairs={{0,4},{4,0},{8,12},{12,8},{16,20},{20,16},{24,28},{28,24},{1,5},{5... | collective-permute-start | bytes 884744 | tf_op jit(solution)/shard_map/ppermute | solution.py:72
  43.0 27.8 %copy-start.1 = (bf16[1536,768]{1,0:T(8,128)(2,1)S(1)}, bf16[1536,768]{1,0:T(8,128)(2,1)}, u32[]{:S(2)}) copy-start(bf16[1536,768]{1,0:T(8,128)(2,1)} %grad_ref.5) | copy-start | bytes 7077892
  49.5 21.3 %copy-start = (bf16[1536,768]{1,0:T(8,128)(2,1)S(1)}, bf16[1536,768]{1,0:T(8,128)(2,1)}, u32[]{:S(2)}) copy-start(bf16[1536,768]{1,0:T(8,128)(2,1)} %tokens_ref.5) | copy-start | bytes 7077892
  49.6 10.1 %collective-permute-start.20 = (bf16[192,1024]{1,0:T(8,128)(2,1)S(1)}, bf16[192,1024]{1,0:T(8,128)(2,1)S(1)}, u32[]{:S(2)}, u32[]{:S(2)}) collective-permute-start(bf16[192,1024]{1,0:T(8,128)(2,1)S(1)} %get-tuple-element.101.refs_2_), channel_id=1, source_target_pairs={{0,2},{1,3},{2,0},{3,1},{4,6},{5,7},{6,4},{7,5},{8,10},{9,11},{10,... | collective-permute-start | bytes 1179656 | tf_op jit(solution)/shard_map/ppermute | solution.py:72
  51.1 8.6 %collective-permute-start.18 = (bf16[96,1536]{1,0:T(8,128)(2,1)S(1)}, bf16[96,1536]{1,0:T(8,128)(2,1)S(1)}, u32[]{:S(2)}, u32[]{:S(2)}) collective-permute-start(bf16[96,1536]{1,0:T(8,128)(2,1)S(1)} %collective-permute-done.16.refs_4_), channel_id=1, source_target_pairs={{0,8},{4,12},{8,0},{12,4},{16,24},{20,28},{24,16},{28,20},{1,9},{5... | collective-permute-start | bytes 884744 | tf_op jit(solution)/shard_map/ppermute | solution.py:72
  51.1 11.7 %collective-permute-start.12 = (bf16[192,768]{1,0:T(8,128)(2,1)S(1)}, bf16[192,768]{1,0:T(8,128)(2,1)S(1)}, u32[]{:S(2)}, u32[]{:S(2)}) collective-permute-start(bf16[192,768]{1,0:T(8,128)(2,1)S(1)} %get-tuple-element.104.refs_6_.refs_1_), channel_id=1, source_target_pairs={{0,2},{1,3},{2,0},{3,1},{4,6},{5,7},{6,4},{7,5},{8,10},{9,11},{10,... | collective-permute-start | bytes 884744 | tf_op jit(solution)/shard_map/ppermute | solution.py:72
  51.6 12.7 %collective-permute-start.17 = (bf16[96,1536]{1,0:T(8,128)(2,1)S(1)}, bf16[96,1536]{1,0:T(8,128)(2,1)S(1)}, u32[]{:S(2)}, u32[]{:S(2)}) collective-permute-start(bf16[96,1536]{1,0:T(8,128)(2,1)S(1)} %collective-permute-done.16.refs_4_), channel_id=1, source_target_pairs={{0,4},{4,0},{8,12},{12,8},{16,20},{20,16},{24,28},{28,24},{1,5},{5... | collective-permute-start | bytes 884744 | tf_op jit(solution)/shard_map/ppermute | solution.py:72
  57.6 7.3 %collective-permute-start.9 = (bf16[192,512]{1,0:T(8,128)(2,1)S(1)}, bf16[192,512]{1,0:T(8,128)(2,1)S(1)}, u32[]{:S(2)}, u32[]{:S(2)}) collective-permute-start(bf16[192,512]{1,0:T(8,128)(2,1)S(1)} %get-tuple-element.107.refs_2_.refs_3_), channel_id=1, source_target_pairs={{0,2},{1,3},{2,0},{3,1},{4,6},{5,7},{6,4},{7,5},{8,10},{9,11},{10,... | collective-permute-start | bytes 589832 | tf_op jit(solution)/shard_map/ppermute | solution.py:72
  59.7 11.1 %collective-permute-start.21 = (bf16[192,1024]{1,0:T(8,128)(2,1)S(1)}, bf16[192,1024]{1,0:T(8,128)(2,1)S(1)}, u32[]{:S(2)}, u32[]{:S(2)}) collective-permute-start(bf16[192,1024]{1,0:T(8,128)(2,1)S(1)} %get-tuple-element.101.refs_2_), channel_id=1, source_target_pairs={{0,1},{1,0},{2,3},{3,2},{4,5},{5,4},{6,7},{7,6},{8,9},{9,8},{10,11... | collective-permute-start | bytes 1179656 | tf_op jit(solution)/shard_map/ppermute | solution.py:72
  59.7 11.1 %collective-permute-start.22 = (bf16[192,1024]{1,0:T(8,128)(2,1)S(1)}, bf16[192,1024]{1,0:T(8,128)(2,1)S(1)}, u32[]{:S(2)}, u32[]{:S(2)}) collective-permute-start(bf16[192,1024]{1,0:T(8,128)(2,1)S(1)} %collective-permute-done.20.refs_3_), channel_id=1, source_target_pairs={{0,1},{1,0},{2,3},{3,2},{4,5},{5,4},{6,7},{7,6},{8,9},{9,8},{10,11... | collective-permute-start | bytes 1179656 | tf_op jit(solution)/shard_map/ppermute | solution.py:72
  62.9 6.7 %collective-permute-start.19 = (bf16[96,1536]{1,0:T(8,128)(2,1)S(1)}, bf16[96,1536]{1,0:T(8,128)(2,1)S(1)}, u32[]{:S(2)}, u32[]{:S(2)}) collective-permute-start(bf16[96,1536]{1,0:T(8,128)(2,1)S(1)} %collective-permute-done.18.refs_6_), channel_id=1, source_target_pairs={{0,4},{4,0},{8,12},{12,8},{16,20},{20,16},{24,28},{28,24},{1,5},{5... | collective-permute-start | bytes 884744 | tf_op jit(solution)/shard_map/ppermute | solution.py:72
  64.3 6.5 %collective-permute-start.13 = (bf16[192,768]{1,0:T(8,128)(2,1)S(1)}, bf16[192,768]{1,0:T(8,128)(2,1)S(1)}, u32[]{:S(2)}, u32[]{:S(2)}) collective-permute-start(bf16[192,768]{1,0:T(8,128)(2,1)S(1)} %get-tuple-element.104.refs_6_.refs_1_), channel_id=1, source_target_pairs={{0,1},{1,0},{2,3},{3,2},{4,5},{5,4},{6,7},{7,6},{8,9},{9,8},{10,11... | collective-permute-start | bytes 884744 | tf_op jit(solution)/shard_map/ppermute | solution.py:72
  65.0 5.9 %collective-permute-start.14 = (bf16[192,768]{1,0:T(8,128)(2,1)S(1)}, bf16[192,768]{1,0:T(8,128)(2,1)S(1)}, u32[]{:S(2)}, u32[]{:S(2)}) collective-permute-start(bf16[192,768]{1,0:T(8,128)(2,1)S(1)} %collective-permute-done.12.refs_7_), channel_id=1, source_target_pairs={{0,1},{1,0},{2,3},{3,2},{4,5},{5,4},{6,7},{7,6},{8,9},{9,8},{10,11... | collective-permute-start | bytes 884744 | tf_op jit(solution)/shard_map/ppermute | solution.py:72
  75.7 5.3 %collective-permute-start.23 = (bf16[512,768]{1,0:T(8,128)(2,1)S(1)}, bf16[512,768]{1,0:T(8,128)(2,1)S(1)}, u32[]{:S(2)}, u32[]{:S(2)}) collective-permute-start(bf16[512,768]{1,0:T(8,128)(2,1)S(1)} %get-tuple-element.127), channel_id=1, source_target_pairs={{0,1},{1,0},{2,3},{3,2},{4,5},{5,4},{6,7},{7,6},{8,9},{9,8},{10,11... | collective-permute-start | bytes 2359304 | tf_op jit(solution)/shard_map/ppermute | solution.py:72
  75.8 6.3 %collective-permute-start.10 = (bf16[192,512]{1,0:T(8,128)(2,1)S(1)}, bf16[192,512]{1,0:T(8,128)(2,1)S(1)}, u32[]{:S(2)}, u32[]{:S(2)}) collective-permute-start(bf16[192,512]{1,0:T(8,128)(2,1)S(1)} %get-tuple-element.107.refs_2_.refs_3_), channel_id=1, source_target_pairs={{0,1},{1,0},{2,3},{3,2},{4,5},{5,4},{6,7},{7,6},{8,9},{9,8},{10,11... | collective-permute-start | bytes 589832 | tf_op jit(solution)/shard_map/ppermute | solution.py:72
  76.3 5.8 %collective-permute-start.11 = (bf16[192,512]{1,0:T(8,128)(2,1)S(1)}, bf16[192,512]{1,0:T(8,128)(2,1)S(1)}, u32[]{:S(2)}, u32[]{:S(2)}) collective-permute-start(bf16[192,512]{1,0:T(8,128)(2,1)S(1)} %collective-permute-done.9.refs_3_), channel_id=1, source_target_pairs={{0,1},{1,0},{2,3},{3,2},{4,5},{5,4},{6,7},{7,6},{8,9},{9,8},{10,11... | collective-permute-start | bytes 589832 | tf_op jit(solution)/shard_map/ppermute | solution.py:72
  85.1 5.4 %collective-permute-start.24 = (bf16[256,768]{1,0:T(8,128)(2,1)S(1)}, bf16[256,768]{1,0:T(8,128)(2,1)S(1)}, u32[]{:S(2)}, u32[]{:S(2)}) collective-permute-start(bf16[256,768]{1,0:T(8,128)(2,1)S(1)} %get-tuple-element.139), channel_id=1, source_target_pairs={{0,1},{1,0},{2,3},{3,2},{4,5},{5,4},{6,7},{7,6},{8,9},{9,8},{10,11... | collective-permute-start | bytes 1179656 | tf_op jit(solution)/shard_map/ppermute | solution.py:72
  85.6 22.3 %collective-permute-start.26 = (bf16[512,768]{1,0:T(8,128)(2,1)}, bf16[512,768]{1,0:T(8,128)(2,1)}, u32[]{:S(2)}, u32[]{:S(2)}) collective-permute-start(bf16[512,768]{1,0:T(8,128)(2,1)} %add_convert_fusion.2.mine_ref), channel_id=1, source_target_pairs={{0,2},{1,3},{2,0},{3,1},{4,6},{5,7},{6,4},{7,5},{8,10},{9,11},{10,... | collective-permute-start | bytes 2359304 | tf_op jit(solution)/shard_map/ppermute | solution.py:72
  101.5 19.0 %collective-permute-start.25 = (bf16[768,768]{1,0:T(8,128)(2,1)}, bf16[768,768]{1,0:T(8,128)(2,1)}, u32[]{:S(2)}, u32[]{:S(2)}) collective-permute-start(bf16[768,768]{1,0:T(8,128)(2,1)} %get-tuple-element.144), channel_id=1, source_target_pairs={{0,1},{1,0},{2,3},{3,2},{4,5},{5,4},{6,7},{7,6},{8,9},{9,8},{10,11... | collective-permute-start | bytes 3538952 | tf_op jit(solution)/shard_map/ppermute | solution.py:72
  101.5 91.1 %all-to-all-start = ((bf16[8,96,1536]{2,1,0:T(8,128)(2,1)}), bf16[8,96,1536]{2,1,0:T(8,128)(2,1)}, u32[]{:S(2)}, u32[]{:S(2)}) async-start(bf16[8,96,1536]{2,1,0:T(8,128)(2,1)} %bitcast.9), calls=%async_computation | async-start | bytes 4718592 | tf_op jit(solution)/shard_map/all_to_all | solution.py:790
  106.6 11.5 %collective-permute-start.28 = (bf16[256,768]{1,0:T(8,128)(2,1)}, bf16[256,768]{1,0:T(8,128)(2,1)S(1)}, u32[]{:S(2)}, u32[]{:S(2)}) collective-permute-start(bf16[256,768]{1,0:T(8,128)(2,1)} %add_convert_fusion.3.mine_ref), channel_id=1, source_target_pairs={{0,2},{1,3},{2,0},{3,1},{4,6},{5,7},{6,4},{7,5},{8,10},{9,11},{10,... | collective-permute-start | bytes 1179656 | tf_op jit(solution)/shard_map/ppermute | solution.py:72
  111.7 10.5 %collective-permute-start.27 = (bf16[512,768]{1,0:T(8,128)(2,1)S(1)}, bf16[512,768]{1,0:T(8,128)(2,1)S(1)}, u32[]{:S(2)}, u32[]{:S(2)}) collective-permute-start(bf16[512,768]{1,0:T(8,128)(2,1)S(1)} %second_norm_backward.2.refs_6_), channel_id=1, source_target_pairs={{0,1},{1,0},{2,3},{3,2},{4,5},{5,4},{6,7},{7,6},{8,9},{9,8},{10,11... | collective-permute-start | bytes 2359304 | tf_op jit(solution)/shard_map/ppermute | solution.py:72
  120.4 1.8 collective-permute-start.29
  122.2 28.3 %collective-permute-start.30 = (bf16[768,768]{1,0:T(8,128)(2,1)S(1)}, bf16[768,768]{1,0:T(8,128)(2,1)S(1)}, u32[]{:S(2)}, u32[]{:S(2)}) collective-permute-start(bf16[768,768]{1,0:T(8,128)(2,1)S(1)} %add_convert_fusion.1.mine_ref), channel_id=1, source_target_pairs={{0,2},{1,3},{2,0},{3,1},{4,6},{5,7},{6,4},{7,5},{8,10},{9,11},{10,... | collective-permute-start | bytes 3538952 | tf_op jit(solution)/shard_map/ppermute | solution.py:72
  123.6 18.3 %copy-start.5 = (bf16[768,896]{1,0:T(8,128)(2,1)S(1)}, bf16[768,896]{1,0:T(8,128)(2,1)}, u32[]{:S(2)}) copy-start(bf16[768,896]{1,0:T(8,128)(2,1)} %copy-done.4) | copy-start | bytes 4128772
  143.9 8.6 %collective-permute-start.31 = (bf16[768,768]{1,0:T(8,128)(2,1)S(1)}, bf16[768,768]{1,0:T(8,128)(2,1)S(1)}, u32[]{:S(2)}, u32[]{:S(2)}) collective-permute-start(bf16[768,768]{1,0:T(8,128)(2,1)S(1)} %get-tuple-element.160), channel_id=1, source_target_pairs={{0,1},{1,0},{2,3},{3,2},{4,5},{5,4},{6,7},{7,6},{8,9},{9,8},{10,11... | collective-permute-start | bytes 3538952 | tf_op jit(solution)/shard_map/ppermute | solution.py:72
  152.8 42.6 %collective-permute-start.37 = (bf16[768,768]{1,0:T(8,128)(2,1)S(1)}, bf16[768,768]{1,0:T(8,128)(2,1)}, u32[]{:S(2)}, u32[]{:S(2)}) collective-permute-start(bf16[768,768]{1,0:T(8,128)(2,1)S(1)} %add_convert_fusion.mine_ref), channel_id=1, source_target_pairs={{0,2},{1,3},{2,0},{3,1},{4,6},{5,7},{6,4},{7,5},{8,10},{9,11},{10,... | collective-permute-start | bytes 3538952 | tf_op jit(solution)/shard_map/ppermute | solution.py:72
  156.5 17.0 %collective-permute-start.32 = (bf16[4,96,832]{2,1,0:T(8,128)(2,1)S(1)}, bf16[4,96,832]{2,1,0:T(8,128)(2,1)S(1)}, u32[]{:S(2)}, u32[]{:S(2)}) collective-permute-start(bf16[4,96,832]{2,1,0:T(8,128)(2,1)S(1)} %get-tuple-element.167), channel_id=1, source_target_pairs={{0,4},{4,0},{8,12},{12,8},{16,20},{20,16},{24,28},{28,24},{1,5},{5... | collective-permute-start | bytes 1916936 | tf_op jit(solution)/shard_map/ppermute | solution.py:72
  174.3 8.7 %collective-permute-start.34 = (bf16[96,832]{1,0:T(8,128)(2,1)S(1)}, bf16[96,832]{1,0:T(8,128)(2,1)S(1)}, u32[]{:S(2)}, u32[]{:S(2)}) collective-permute-start(bf16[96,832]{1,0:T(8,128)(2,1)S(1)} %get-tuple-element.172), channel_id=1, source_target_pairs={{0,8},{4,12},{8,0},{12,4},{16,24},{20,28},{24,16},{28,20},{1,9},{5... | collective-permute-start | bytes 479240 | tf_op jit(solution)/shard_map/ppermute | solution.py:72
  176.1 15.0 %collective-permute-start.35 = (bf16[96,832]{1,0:T(8,128)(2,1)S(1)}, bf16[96,832]{1,0:T(8,128)(2,1)S(1)}, u32[]{:S(2)}, u32[]{:S(2)}) collective-permute-start(bf16[96,832]{1,0:T(8,128)(2,1)S(1)} %get-tuple-element.173), channel_id=1, source_target_pairs={{0,16},{4,20},{8,24},{12,28},{16,0},{20,4},{24,8},{28,12},{1,17},{... | collective-permute-start | bytes 479240 | tf_op jit(solution)/shard_map/ppermute | solution.py:72
  178.3 12.7 %collective-permute-start.36 = (bf16[96,832]{1,0:T(8,128)(2,1)S(1)}, bf16[96,832]{1,0:T(8,128)(2,1)S(1)}, u32[]{:S(2)}, u32[]{:S(2)}) collective-permute-start(bf16[96,832]{1,0:T(8,128)(2,1)S(1)} %get-tuple-element.174), channel_id=1, source_target_pairs={{0,24},{4,28},{8,16},{12,20},{16,8},{20,12},{24,0},{28,4},{1,25},{... | collective-permute-start | bytes 479240 | tf_op jit(solution)/shard_map/ppermute | solution.py:72
  182.9 22.9 %collective-permute-start.33 = (bf16[768,768]{1,0:T(8,128)(2,1)}, bf16[768,768]{1,0:T(8,128)(2,1)}, u32[]{:S(2)}, u32[]{:S(2)}) collective-permute-start(bf16[768,768]{1,0:T(8,128)(2,1)} %get-tuple-element.170), channel_id=1, source_target_pairs={{0,1},{1,0},{2,3},{3,2},{4,5},{5,4},{6,7},{7,6},{8,9},{9,8},{10,11... | collective-permute-start | bytes 3538952 | tf_op jit(solution)/shard_map/ppermute | solution.py:72
  200.4 5.5 %collective-permute-start.38 = (bf16[768,768]{1,0:T(8,128)(2,1)S(1)}, bf16[768,768]{1,0:T(8,128)(2,1)S(1)}, u32[]{:S(2)}, u32[]{:S(2)}) collective-permute-start(bf16[768,768]{1,0:T(8,128)(2,1)S(1)} %get-tuple-element.178), channel_id=1, source_target_pairs={{0,1},{1,0},{2,3},{3,2},{4,5},{5,4},{6,7},{7,6},{8,9},{9,8},{10,11... | collective-permute-start | bytes 3538952 | tf_op jit(solution)/shard_map/ppermute | solution.py:72
  200.4 3.7 %collective-permute-start.39 = (f32[16,96]{1,0:T(8,128)S(1)}, f32[16,96]{1,0:T(8,128)S(1)}, u32[]{:S(2)}, u32[]{:S(2)}) collective-permute-start(f32[16,96]{1,0:T(8,128)S(1)} %slice.15), channel_id=1, source_target_pairs={{0,2},{1,3},{2,0},{3,1},{4,6},{5,7},{6,4},{7,5},{8,10},{9,11},{10,... | collective-permute-start | bytes 18440 | tf_op jit(solution)/shard_map/ppermute | solution.py:72
  204.1 1.2 collective-permute-start.40
  (12 other events, 40.7 us)

commit v4 on v3

--- a/solution.py
+++ b/solution.py
@@ -513,8 +513,8 @@
             scratch_shapes=[pltpu.VMEM((depth, units), WIDE)] * 2,
         ),
         out_shape=(
-            struct((half, depth), LOW),
-            struct((half, depth), LOW),
+            stored_far((half, depth), LOW),
+            stored_far((half, depth), LOW),
             *shard_shapes(batch, depth, 2 * units),
         ),
         compiler_params=params(24),
@@ -552,7 +552,7 @@
     low_ref[...] = grad.astype(LOW)
 
 
-def second_back(scalar, mine, other, hidden, out_grad, rows, begin):
+def second_back(scalar, mine, other, hidden, out_grad, rows, begin, guess):
     size, depth = hidden.shape
     half = out_grad.shape[0] // 2
     placed = pl.BlockSpec(
@@ -568,7 +568,7 @@
         ),
         out_shape=struct((size, depth), LOW),
         compiler_params=params(14),
-        cost_estimate=cost(size / 1000),
+        cost_estimate=cost(guess),
         name="second_norm_backward",
     )(scalar, mine, other, far(hidden), far(out_grad), rows)
 
@@ -636,60 +636,38 @@
 
 
 def finish_kernel(scalar_ref, mine_ref, other_ref, *refs, sizes, half):
-    hidden_refs, (own_ref, full_ref) = refs[: len(sizes)], refs[len(sizes) :]
-    i = pl.program_id(0)
-    row = lax.broadcasted_iota(jnp.int32, (BLOCK, 1), 0) + (scalar_ref[0] * half + i * BLOCK)
+    hidden_refs, owns, full_ref = refs[: len(sizes)], refs[len(sizes) : -1], refs[-1]
+    hidden = jnp.concatenate([ref[...] for ref in hidden_refs], axis=0)
+    row = lax.broadcasted_iota(jnp.int32, (half, 1), 0) + scalar_ref[0] * half
     branch = mine_ref[...].astype(WIDE) + other_ref[...].astype(WIDE)
-    first = 0
-    for size, hidden_ref in zip(sizes, hidden_refs):
-        last = first + size // BLOCK
-
-        @pl.when((i >= first) & (i < last))
-        def _():
-            low = jnp.where(row < scalar_ref[1], hidden_ref[...] + branch, 0.0).astype(LOW)
-            own_ref[...] = low
-            full_ref[...] = low
-
-        first = last
+    low = jnp.where(row < scalar_ref[1], hidden + branch, 0.0).astype(LOW)
+    full_ref[...] = low
+    for k, own_ref in enumerate(owns):
+        own_ref[...] = low[k * STEP : (k + 1) * STEP, :]
 
 
 def finish(scalar, mine, other, hiddens, count):
     half, depth = mine.shape
-    blocks = half // BLOCK
     sizes = tuple(hidden.shape[0] for hidden in hiddens)
-    specs = []
-    first = 0
-    for size in sizes:
-        last = size // BLOCK - 1
-
-        def chunk(i, scalar_ref, first=first, last=last):
-            return (jnp.clip(i - first, 0, last), 0)
-
-        specs.append(pl.BlockSpec((BLOCK, depth), chunk))
-        first += last + 1
-
-    def own(i, scalar_ref):
-        return (i, 0)
-
+    parts = half // STEP
     return pl.pallas_call(
         functools.partial(finish_kernel, sizes=sizes, half=half),
         grid_spec=pltpu.PrefetchScalarGridSpec(
             num_scalar_prefetch=1,
-            grid=(blocks,),
-            in_specs=[pl.BlockSpec((BLOCK, depth), own)] * 2 + specs,
-            out_specs=(
-                pl.BlockSpec((BLOCK, depth), own),
-                pl.BlockSpec((BLOCK, depth), lambda i, scalar_ref: (i + scalar_ref[0] * blocks, 0)),
-            ),
+            grid=(1,),
+            in_specs=[whole()] * (2 + len(sizes)),
+            out_specs=(whole(),) * parts
+            + (pl.BlockSpec((half, depth), lambda i, scalar_ref: (scalar_ref[0], 0)),),
         ),
-        out_shape=(struct((half, depth), LOW), stored_far((count, depth), LOW)),
-        compiler_params=params(12),
+        out_shape=(stored_far((STEP, depth), LOW),) * parts + (stored_far((count, depth), LOW),),
+        compiler_params=params(16),
         cost_estimate=cost(1),
         name="layer_out",
     )(scalar, mine, other, *(far(hidden) for hidden in hiddens))
 
 
-def first_back_kernel(scalar_ref, mine_ref, other_ref, tokens_ref, grad_ref, rows_ref, own_ref, full_ref):
+def first_back_kernel(scalar_ref, mine_ref, other_ref, tokens_ref, grad_ref, rows_ref, *refs):
+    own_ref, full_ref = refs[-2:]
     grad_normed = mine_ref[...].astype(WIDE) + other_ref[...].astype(WIDE)
     scaled, inverse = standardize(tokens_ref[...].astype(WIDE))
     grad = grad_ref[...].astype(WIDE) + standardize_back(grad_normed, scaled, inverse, rows_ref[0:1, :])
@@ -698,58 +676,61 @@
     full_ref[...] = low
 
 
-def place_rows(kernel, scalar, owned, spread, fixed, count, begin, half, name):
-    depth = owned[0].shape[1]
-    blocks = half // STEP
-
-    def own(i, scalar_ref):
-        return (i, 0)
+def first_back(scalar, mine, other, tokens, grad, rows, number, stored):
+    size, depth = mine.shape
+    count = tokens.shape[0]
+    blocks = count // 2 // size
 
     def placed(i, scalar_ref):
-        return (begin // STEP + i + scalar_ref[0] * blocks, 0)
-
-    return pl.pallas_call(
-        kernel,
+        return (number + scalar_ref[0] * blocks, 0)
+
+    return pl.pallas_call(
+        first_back_kernel,
         grid_spec=pltpu.PrefetchScalarGridSpec(
             num_scalar_prefetch=1,
-            grid=(blocks,),
-            in_specs=[pl.BlockSpec((STEP, depth), own)] * 2
-            + [pl.BlockSpec((STEP, depth), placed)] * len(spread)
-            + [pl.BlockSpec((STEP, depth), own)] * (len(owned) - 2)
-            + [whole()] * len(fixed),
-            out_specs=(pl.BlockSpec((STEP, depth), own), pl.BlockSpec((STEP, depth), placed)),
+            grid=(1,),
+            in_specs=[whole(), whole()]
+            + [pl.BlockSpec((size, depth), placed)] * 2
+            + [whole()]
+            + [pl.BlockSpec(memory_space=pl.ANY)] * len(stored),
+            out_specs=(whole(), pl.BlockSpec((size, depth), placed)),
         ),
-        out_shape=(struct((half, depth), LOW), stored_far((count, depth), LOW)),
+        out_shape=(stored_far((size, depth), LOW), stored_far((count, depth), LOW)),
+        input_output_aliases={6: 1} if stored else {},
         compiler_params=params(12),
-        cost_estimate=cost(3),
-        name=name,
-    )(scalar, *owned[:2], *spread, *owned[2:], *fixed)
+        cost_estimate=cost(1),
+        name="first_norm_backward",
+    )(scalar, mine, other, tokens, grad, rows, *stored)
 
 
 def place_kernel(scalar_ref, *refs, parts):
-    for source, target in zip(refs[:parts], refs[2 * parts :]):
-        target[...] = source[...]
-
-
-def place(scalar, sources, targets):
-    parts = len(sources)
-    rows, depth = sources[0].shape
-    blocks = rows // STEP
+    first_refs, second_refs = refs[:parts], refs[parts : 2 * parts]
+    for k in range(parts):
+
+        @pl.when(pl.program_id(0) == k)
+        def _():
+            refs[-2][...] = first_refs[k][...]
+            refs[-1][...] = second_refs[k][...]
+
+
+def place(scalar, first, second, targets):
+    parts = len(first)
+    rows, depth = first[0].shape
+    placed = pl.BlockSpec((rows, depth), lambda i, scalar_ref: (i + (1 - scalar_ref[0]) * parts, 0))
     return pl.pallas_call(
         functools.partial(place_kernel, parts=parts),
         grid_spec=pltpu.PrefetchScalarGridSpec(
             num_scalar_prefetch=1,
-            grid=(blocks,),
-            in_specs=[pl.BlockSpec((STEP, depth), lambda i, scalar_ref: (i, 0))] * parts
-            + [pl.BlockSpec(memory_space=pl.ANY)] * parts,
-            out_specs=(pl.BlockSpec((STEP, depth), lambda i, scalar_ref: (i + (1 - scalar_ref[0]) * blocks, 0)),) * parts,
+            grid=(parts,),
+            in_specs=[whole()] * (2 * parts) + [pl.BlockSpec(memory_space=pl.ANY)] * 2,
+            out_specs=(placed, placed),
         ),
         out_shape=tuple(stored_far(value.shape, value.dtype) for value in targets),
-        input_output_aliases={1 + parts + k: k for k in range(parts)},
+        input_output_aliases={1 + 2 * parts: 0, 2 + 2 * parts: 1},
         compiler_params=params(12),
         cost_estimate=cost(1),
         name="place",
-    )(scalar, *sources, *targets)
+    )(scalar, *first, *second, *targets)
 
 
 def total_kernel(*refs, parts, bounds, flips):
@@ -766,7 +747,7 @@
         out[...] = jnp.transpose(piece) if flip else piece
 
 
-def total_parts(parts, bounds, flips):
+def total_parts(parts, bounds, flips, guess):
     rows = parts[0].shape[-2]
     shapes = []
     for (first, last), flip in zip(bounds, flips):
@@ -778,7 +759,7 @@
         out_specs=(whole(),) * len(shapes),
         out_shape=tuple(shapes),
         compiler_params=params(8),
-        cost_estimate=cost(1),
+        cost_estimate=cost(guess),
         name="total",
     )(*parts)
 
@@ -853,20 +834,22 @@
         late += [last, swap(last, "batch", 1)]
     late = lax.optimization_barrier((*late, *mixed))[: len(late)]
     full_up, full_down = assemble(scalar, late, units)
-    rows = after(rows, pieces[-1][1])
-
-    stored = []
+    rows = after(rows, *pieces[-1][1:])
+
+    stored, sends = [], []
     twos, halves, hiddens = jnp.zeros((8, depth), WIDE), [], []
     for (begin, size), piece in zip(chunks, pieces):
-        ends = []
+        back, twos, *stored = feed(
+            scalar, tokens, out_grad, piece, outs, full_up, full_down, rows, twos, stored, begin, size, False
+        )
+        sends.append(back)
+    for (begin, size), piece, send in zip(chunks, pieces, sends):
         rows = after(rows, *(mine for mine, _ in halves))
-        for keep in (False, True):
-            back, twos, *stored = feed(
-                scalar, tokens, out_grad, piece, outs, full_up, full_down, rows, twos, stored, begin, size, keep
-            )
-            ends.append(back)
+        back, twos, *stored = feed(
+            scalar, tokens, out_grad, piece, outs, full_up, full_down, rows, twos, stored, begin, size, True
+        )
         hiddens.append(stored.pop())
-        mine = (ends[1].astype(WIDE) + swap(ends[0], "tensor", 1).astype(WIDE)).astype(LOW)
+        mine = (back.astype(WIDE) + swap(send, "tensor", 1).astype(WIDE)).astype(LOW)
         halves.append((mine, swap(mine, "tensor", 2)))
     normed_two, active, upper = stored
     normed_two = after(normed_two, *(mine for mine, _ in halves))
@@ -877,10 +860,10 @@
     grads = []
     for (begin, size), (mine, other), hidden in zip(chunks, halves, hiddens):
         mine = after(mine, *feed_grads)
-        low = second_back(scalar, mine, other, hidden, out_grad, rows, begin)
+        low = second_back(scalar, mine, other, hidden, out_grad, rows, begin, 40000 if grads else 1)
         grads += [low, swap(low, "tensor", 1)]
     branch_mine = (branch_keep.astype(WIDE) + beside.astype(WIDE)).astype(LOW)
-    branch_mine = after(branch_mine, *grads)
+    branch_mine = after(branch_mine, halves[-1][1])
     branch_other = swap(branch_mine, "tensor", 2)
     projected = after(projected, branch_mine)
     attend_grads, outs_grad, grad_attn = attend_back(
@@ -890,32 +873,44 @@
     there = (1 - core) * half
     ends, ones = [], jnp.zeros((8, depth), WIDE)
     for keep in (False, True):
-        if keep:
-            attend_grads = after(attend_grads, branch_other)
         back, ones = inward(scalar, attend_grads, tokens, weights, ones, keep)
         ends.append(back)
-    mine = (ends[1].astype(WIDE) + swap(ends[0], "tensor", 1).astype(WIDE)).astype(LOW)
-    other = swap(mine, "tensor", 2)
-    project_grads = project_back(scalar, after(attend_grads, mine), normed, outs_grad, ones, twos, batch)
-    project_parts = exchange_far(scalar, exchange_near(project_grads))
-    own_out, layer_out = finish(scalar, branch_mine, after(branch_other, project_parts[0]), hiddens, count)
-    other_out = swap(own_out, "tensor", 1)
-    shard_up, shard_down = total_parts(feed_parts, ((0, units), (units, 2 * units)), (False, False))
+    project_grads = project_back(scalar, attend_grads, normed, outs_grad, ones, twos, batch)
+    keep = after(ends[1], branch_other, *project_grads)
+    beside = swap(ends[0], "tensor", 1)
+    tails = []
+    for begin in range(0, half, STEP):
+        part = slice(begin, begin + STEP)
+        mine = (keep[part].astype(WIDE) + beside[part].astype(WIDE)).astype(LOW)
+        tails.append((mine, swap(mine, "tensor", 2)))
+    *own_out, layer_out = finish(scalar, branch_mine, after(branch_other, tails[-1][0]), hiddens, count)
+    project_parts = exchange_far(scalar, exchange_near(project_grads), own_out)
+    other_out = [swap(own, "tensor", 1) for own in own_out]
+    stored, other_grads = [], []
+    for number, (mine, other) in enumerate(tails):
+        mine = after(mine, *own_out)
+        own_grad, *stored = first_back(scalar, mine, other, tokens, grad_attn, rows, number, stored)
+        other_grads.append(swap(own_grad, "tensor", 1))
+    feed_parts[0] = after(feed_parts[0], own_grad)
+    shard_up, shard_down = total_parts(feed_parts, ((0, units), (units, 2 * units)), (False, False), 1)
     last = 3 * width
     final = project_parts[0].shape[-1]
-    shard_query, shard_key, shard_value, small, shard_out = total_parts(
+    project_parts[0] = after(project_parts[0], shard_up)
+    (small,) = total_parts(project_parts, ((last, final - width),), (True,), 40000)
+    small = small[:16]
+    across = swap(small, "tensor", 2)
+    project_parts[0] = after(project_parts[0], small)
+    shard_query, shard_key, shard_value, shard_out = total_parts(
         project_parts,
-        ((0, width), (width, 2 * width), (2 * width, last), (last, final - width), (final - width, final)),
-        (False, False, False, True, True),
+        ((0, width), (width, 2 * width), (2 * width, last), (final - width, final)),
+        (False, False, False, True),
+        1,
     )
-    mine = after(mine, own_out, shard_up, small)
-    own_grad, grad_input = place_rows(
-        first_back_kernel, scalar, (mine, other), (tokens, grad_attn), (rows,), count, 0, half, "first_norm_backward"
-    )
-    layer_out, grad_input = place(scalar, (other_out, swap(own_grad, "tensor", 1)), (layer_out, grad_input))
-    small = small[:16]
-    small = small + swap(small, "tensor", 2)
-    small = small + swap(small, "tensor", 1)
+    small = small + after(across, shard_query)
+    across = swap(small, "tensor", 1)
+    other_out[0] = after(other_out[0], small)
+    layer_out, grad_input = place(scalar, other_out, other_grads, (layer_out, stored[0]))
+    small = small + after(across, layer_out)
     shard_gain = jnp.stack([small[0], small[8]])
     shard_shift = jnp.stack([small[1], small[9]])
     return (

time: 212 us -> 196 us (0.925)
  waiting for transfers between devices: 54.6 us -> 37 us
  Pallas kernels: 89.7 us -> 93.2 us
    ppermute x41 -> x44, waiting for transfers between devices: 54.6 us -> 37 us  [swap(): return lax.ppermute(value, axis, [(i, i ^ bits) for i in range(size)])]
    pallas_call x2 -> x3, Pallas kernels: 3.68 us -> 5.73 us  [total_parts(): pl.pallas_call(functools.partial(total_kernel, parts=len(parts), bounds=b...]
    unnamed x39 -> x27, local copies, waits for them, and re-layouts: 4.86 us -> 3.45 us
    ppermute x41 -> x44, starting transfers between devices: 45.8 us -> 46.5 us  [swap(): return lax.ppermute(value, axis, [(i, i ^ bits) for i in range(size)])]
    pallas_call x1 -> x2, Pallas kernels: 4.28 us -> 4.89 us  [first_back(): pl.pallas_call(first_back_kernel, grid_spec=pltpu.PrefetchScalarGridSpec(...]
  transfers between devices with their start and end apart: 42 -> 45, of which waited for: 13 -> 11; matrix products, arithmetic and copies ran while one was open for 3% -> 2% of each run, Pallas kernels for 38% -> 46%
where the time goes in v4:
time: 196 us; the launch traced here: 193 us
  Pallas kernels  93.2 us (48%)
  starting transfers between devices  52 us (27%)
  waiting for transfers between devices  37 us (19%)
  local copies, waits for them, and re-layouts  4.45 us (2%)
  other arithmetic  4.23 us (2%)
    ppermute x44, starting transfers between devices, swap(): return lax.ppermute(value, axis, [(i, i ^ bits) for i in range(size)])  46.5 us
    ppermute x44, waiting for transfers between devices, swap(): return lax.ppermute(value, axis, [(i, i ^ bits) for i in range(size)])  37 us
    pallas_call x1, Pallas kernels, attend_back(): pl.pallas_call(functools.partial(attend_back_kernel, chunks=chunks, rows=...  18.3 us
    pallas_call x4, Pallas kernels, feed(): pl.pallas_call(functools.partial(feed_kernel, begin=begin, size=size, hal...  15.8 us
    pallas_call x2, Pallas kernels, attend(): pl.pallas_call(functools.partial(attend_kernel, places=places, heads=head...  11.4 us
    pallas_call x1, Pallas kernels, weigh(): pl.pallas_call(weigh_kernel, grid_spec=pltpu.PrefetchScalarGridSpec(num_s...  9.59 us
    pallas_call x2, Pallas kernels, second_back(): pl.pallas_call(functools.partial(second_back_kernel, begin=begin, half=ha...  6.38 us
    pallas_call x3, Pallas kernels, total_parts(): pl.pallas_call(functools.partial(total_kernel, parts=len(parts), bounds=b...  5.73 us
  transfers between devices with their start and end apart: 45, of which 11 were waited for; matrix products, arithmetic and copies ran while one was open for 2% of the time, Pallas kernels for 46%

profile of v4, /device:TPU:0, one launch (start us, length us, event | category | flops | bytes accessed | tf_op | source)
XLA Modules:
  0.0 192.8 jit_solution(10507516261210032097)
XLA Ops:
  4.1 3.1 %collective-permute-start.1 = (bf16[96,896]{1,0:T(8,128)(2,1)S(1)}, bf16[96,896]{1,0:T(8,128)(2,1)S(1)}, u32[]{:S(2)}, u32[]{:S(2)}) collective-permute-start(bf16[96,896]{1,0:T(8,128)(2,1)S(1)} %concatenate.6.refs_0_), channel_id=1, source_target_pairs={{0,8},{4,12},{8,0},{12,4},{16,24},{20,28},{24,16},{28,20},{1,9},{5... | collective-permute-start | bytes 516104 | tf_op jit(solution)/shard_map/ppermute | solution.py:72
  7.2 2.6 %collective-permute-start.3 = (bf16[96,896]{1,0:T(8,128)(2,1)S(1)}, bf16[96,896]{1,0:T(8,128)(2,1)S(1)}, u32[]{:S(2)}, u32[]{:S(2)}) collective-permute-start(bf16[96,896]{1,0:T(8,128)(2,1)S(1)} %concatenate.6.refs_0_), channel_id=1, source_target_pairs={{0,16},{4,20},{8,24},{12,28},{16,0},{20,4},{24,8},{28,12},{1,17},{... | collective-permute-start | bytes 516104 | tf_op jit(solution)/shard_map/ppermute | solution.py:72
  9.8 1.5 collective-permute-start
  11.3 3.8 %collective-permute-done.1.refs_2_ = bf16[96,896]{1,0:T(8,128)(2,1)S(1)} collective-permute-done((bf16[96,896]{1,0:T(8,128)(2,1)S(1)}, bf16[96,896]{1,0:T(8,128)(2,1)S(1)}, u32[]{:S(2)}, u32[]{:S(2)}) %collective-permute-start.1) | collective-permute-done | bytes 172064 | tf_op jit(solution)/shard_map/ppermute | solution.py:72
  15.1 1.7 collective-permute-start.2
  16.8 2.5 %collective-permute-start.5 = (bf16[96,896]{1,0:T(8,128)(2,1)S(1)}, bf16[96,896]{1,0:T(8,128)(2,1)S(1)}, u32[]{:S(2)}, u32[]{:S(2)}) collective-permute-start(bf16[96,896]{1,0:T(8,128)(2,1)S(1)} %concatenate.6.refs_0_), channel_id=1, source_target_pairs={{0,24},{4,28},{8,16},{12,20},{16,8},{20,12},{24,0},{28,4},{1,25},{... | collective-permute-start | bytes 516104 | tf_op jit(solution)/shard_map/ppermute | solution.py:72
  20.5 1.9 collective-permute-start.4
  24.1 1.8 collective-permute-done.4.refs_5_
  26.0 1.9 collective-permute-start.6
  28.5 2.9 %collective-permute-start.16 = (bf16[96,1536]{1,0:T(8,128)(2,1)S(1)}, bf16[96,1536]{1,0:T(8,128)(2,1)S(1)}, u32[]{:S(2)}, u32[]{:S(2)}) collective-permute-start(bf16[96,1536]{1,0:T(8,128)(2,1)S(1)} %pad_maximum_fusion.refs_0_), channel_id=1, source_target_pairs={{0,16},{4,20},{8,24},{12,28},{16,0},{20,4},{24,8},{28,12},{1,17},{... | collective-permute-start | bytes 884744 | tf_op jit(solution)/shard_map/ppermute | solution.py:72
  31.5 5.6 %project.1 = (bf16[1536,768]{1,0:T(8,128)(2,1)}, bf16[1536,576]{1,0:T(8,128)(2,1)S(1)}, f32[8,768]{1,0:T(8,128)S(1)}, bf16[768,896]{1,0:T(8,128)(2,1)S(1)}, bf16[192,768]{1,0:T(8,128)(2,1)S(1)}) custom-call(s32[4]{0:T(128)S(1)} %pad_add_fusion.scalar_ref, bf16[96,896]{1,0:T(8,128)(2,1)S(1)} %concatenate.6.refs_0_, ...), custom_call_target="tpu_custom_call" | custom-call | flops 4400000 | tf_op jit(solution)/shard_map/project/pallas_call | solution.py:128
  37.1 1.9 collective-permute-start.8
  38.9 6.5 %attend_forward.2 = (bf16[192,1024]{1,0:T(8,128)(2,1)S(1)}, f32[4,8,256]{2,1,0:T(8,128)S(1)}) custom-call(s32[4]{0:T(128)S(1)} %pad_add_fusion.scalar_ref, bf16[1536,576]{1,0:T(8,128)(2,1)S(1)} %get-tuple-element.156.projected_ref.refs_0_), custom_call_target="tpu_custom_call" | custom-call | flops 1100000 | tf_op jit(solution)/shard_map/attend_forward/pallas_call | solution.py:232
  45.5 2.1 %collective-permute-start.18 = (bf16[96,1536]{1,0:T(8,128)(2,1)S(1)}, bf16[96,1536]{1,0:T(8,128)(2,1)S(1)}, u32[]{:S(2)}, u32[]{:S(2)}) collective-permute-start(bf16[96,1536]{1,0:T(8,128)(2,1)S(1)} %collective-permute-done.16.refs_4_), channel_id=1, source_target_pairs={{0,8},{4,12},{8,0},{12,4},{16,24},{20,28},{24,16},{28,20},{1,9},{5... | collective-permute-start | bytes 884744 | tf_op jit(solution)/shard_map/ppermute | solution.py:72
  47.7 1.9 collective-permute-start.20
  49.7 1.9 collective-permute-start.17
  51.6 4.8 %attend_forward.3 = (bf16[192,512]{1,0:T(8,128)(2,1)S(1)}, f32[2,8,256]{2,1,0:T(8,128)S(1)}) custom-call(s32[4]{0:T(128)S(1)} %pad_add_fusion.scalar_ref, bf16[1536,576]{1,0:T(8,128)(2,1)S(1)} %get-tuple-element.156.projected_ref.refs_0_), custom_call_target="tpu_custom_call" | custom-call | flops 1100000 | tf_op jit(solution)/shard_map/attend_forward/pallas_call | solution.py:232
  56.9 3.5 %collective-permute-done.12.refs_7_ = bf16[192,768]{1,0:T(8,128)(2,1)S(1)} collective-permute-done((bf16[192,768]{1,0:T(8,128)(2,1)S(1)}, bf16[192,768]{1,0:T(8,128)(2,1)S(1)}, u32[]{:S(2)}, u32[]{:S(2)}) %collective-permute-start.12) | collective-permute-done | bytes 294944 | tf_op jit(solution)/shard_map/ppermute | solution.py:72
  60.4 1.7 collective-permute-start.9
  62.7 3.4 %collective-permute-done.9.refs_3_ = bf16[192,512]{1,0:T(8,128)(2,1)S(1)} collective-permute-done((bf16[192,512]{1,0:T(8,128)(2,1)S(1)}, bf16[192,512]{1,0:T(8,128)(2,1)S(1)}, u32[]{:S(2)}, u32[]{:S(2)}) %collective-permute-start.9) | collective-permute-done | bytes 196640 | tf_op jit(solution)/shard_map/ppermute | solution.py:72
  68.8 4.9 %feed_forward.4 = (bf16[512,768]{1,0:T(8,128)(2,1)S(1)}, f32[8,768]{1,0:T(8,128)S(1)}, bf16[1536,768]{1,0:T(8,128)(2,1)S(1)}, bf16[1536,768]{1,0:T(8,128)(2,1)S(1)}, bf16[1536,768]{1,0:T(8,128)(2,1)S(1)}) custom-call(s32[4]{0:T(128)S(1)} %pad_add_fusion.scalar_ref, bf16[1536,768]{1,0:T(8,128)(2,1)S(1)} %copy-done, bf16[1536,768]{1,0:T(8,128)(2,1)S(1)} %copy-done.1, ...), custom_call_target="tpu_custom_call" | custom-call | flops 563200 | tf_op jit(solution)/shard_map/feed_forward/pallas_call | solution.py:430
  73.7 2.9 %feed_forward.5 = (bf16[256,768]{1,0:T(8,128)(2,1)S(1)}, f32[8,768]{1,0:T(8,128)S(1)}, bf16[1536,768]{1,0:T(8,128)(2,1)S(1)}, bf16[1536,768]{1,0:T(8,128)(2,1)S(1)}, bf16[1536,768]{1,0:T(8,128)(2,1)S(1)}) custom-call(s32[4]{0:T(128)S(1)} %pad_add_fusion.scalar_ref, ...), custom_call_target="tpu_custom_call", output_to_operand_aliasing={{2}: (15, {}), {3}: (16, {}), {4}: (17, {})} | custom-call | flops 281600 | tf_op jit(solution)/shard_map/feed_forward/pallas_call | solution.py:430
  77.2 4.7 %feed_forward.6 = (bf16[512,768]{1,0:T(8,128)(2,1)S(1)}, f32[8,768]{1,0:T(8,128)S(1)}, bf16[1536,768]{1,0:T(8,128)(2,1)S(1)}, bf16[1536,768]{1,0:T(8,128)(2,1)S(...) custom-call(s32[4]{0:T(128)S(1)} %pad_add_fusion.scalar_ref, ...), custom_call_target="tpu_custom_call", output_to_operand_aliasing={{2}: (15, {}), {3}: (16, {}), {4}: (17, {})} | custom-call | flops 563200 | tf_op jit(solution)/shard_map/feed_forward/pallas_call | solution.py:430
  83.0 1.7 collective-permute-start.28
  84.7 3.3 %feed_forward.7 = (bf16[256,768]{1,0:T(8,128)(2,1)S(1)}, f32[8,768]{1,0:T(8,128)S(1)}, bf16[1536,768]{1,0:T(8,128)(2,1)S(1)}, bf16[1536,768]{1,0:T(8,128)(2,1)S(...) custom-call(s32[4]{0:T(128)S(1)} %pad_add_fusion.scalar_ref, ...), custom_call_target="tpu_custom_call", output_to_operand_aliasing={{2}: (15, {}), {3}: (16, {}), {4}: (17, {})} | custom-call | flops 281600 | tf_op jit(solution)/shard_map/feed_forward/pallas_call | solution.py:430
  89.2 9.6 %feed_forward_weights.1 = (bf16[768,768]{1,0:T(8,128)(2,1)}, bf16[768,768]{1,0:T(8,128)(2,1)}, bf16[768,1536]{1,0:T(8,128)(2,1)}) custom-call(s32[4]{0:T(128)S(1)} %pad_add_fusion.scalar_ref, bf16[1536,768]{1,0:T(8,128)(2,1)S(1)} %get-tuple-element.149.normed_ref, bf16[1536,768]{1,0:T(8,128)(2,1)S(1)} %get-tuple-element.150.upper_ref, ...), custom_call_target="tpu_custom_call" | custom-call | flops 1100000 | tf_op jit(solution)/shard_map/feed_forward_weights/pallas_call | solution.py:505
  98.8 5.5 %all-to-all-start = ((bf16[8,96,1536]{2,1,0:T(8,128)(2,1)}), bf16[8,96,1536]{2,1,0:T(8,128)(2,1)}, u32[]{:S(2)}, u32[]{:S(2)}) async-start(bf16[8,96,1536]{2,1,0:T(8,128)(2,1)} %bitcast.9), calls=%async_computation | async-start | bytes 4718592 | tf_op jit(solution)/shard_map/all_to_all | solution.py:771
  104.3 3.8 %second_norm_backward.2.refs_6_ = bf16[512,768]{1,0:T(8,128)(2,1)S(1)} custom-call(s32[4]{0:T(128)S(1)} %pad_add_fusion.scalar_ref, bf16[512,768]{1,0:T(8,128)(2,1)} %add_convert_fusion.1.mine_ref, bf16[512,768]{1,0:T(8,128)(2,1)} %collective-permute-done.28.other_ref, f32[512,768]{1,0:T(8,128)} %get-tuple-element.161.hidden_ref.refs_0_, ...), custom_call_target="tpu_custom_call" | custom-call | flops 1100000 | tf_op jit(solution)/shard_map/second_norm_backward/pallas_call | solution.py:561
  108.7 2.5 %collective-permute-done.26.other_ref = bf16[256,768]{1,0:T(8,128)(2,1)} collective-permute-done((bf16[256,768]{1,0:T(8,128)(2,1)}, bf16[256,768]{1,0:T(8,128)(2,1)}, u32[]{:S(2)}, u32[]{:S(2)}) %collective-permute-start.26) | collective-permute-done | bytes 393248 | tf_op jit(solution)/shard_map/ppermute | solution.py:72
  111.2 2.6 %second_norm_backward.3.refs_8_ = bf16[256,768]{1,0:T(8,128)(2,1)S(1)} custom-call(s32[4]{0:T(128)S(1)} %pad_add_fusion.scalar_ref, bf16[256,768]{1,0:T(8,128)(2,1)} %add_convert_fusion.4.mine_ref, bf16[256,768]{1,0:T(8,128)(2,1)} %collective-permute-done.26.other_ref, f32[256,768]{1,0:T(8,128)} %get-tuple-element.163.hidden_ref.refs_1_, ...), custom_call_target="tpu_custom_call" | custom-call | flops 44000002048 | tf_op jit(solution)/shard_map/second_norm_backward/pallas_call | solution.py:561
  114.2 1.7 collective-permute-start.27
  116.0 18.3 %attend_backward.1 = (bf16[576,1536]{1,0:T(8,128)(2,1)S(1)}, bf16[768,192]{1,0:T(8,128)(2,1)S(1)}, bf16[1536,768]{1,0:T(8,128)(2,1)S(1)}) custom-call(s32[4]{0:T(128)S(1)} %pad_add_fusion.scalar_ref, bf16[1536,576]{1,0:T(8,128)(2,1)S(1)} %copy-done.3, bf16[192,768]{1,0:T(8,128)(2,1)S(1)} %get-tuple-element.113.refs_6_.refs_1_, ...), custom_call_target="tpu_custom_call" | custom-call | flops 8800000 | tf_op jit(solution)/shard_map/attend_backward/pallas_call | solution.py:334
  134.3 1.9 grad_normed.2
  136.4 1.9 grad_normed.3
  138.4 2.3 %projection_weights.1 = (bf16[4,96,832]{2,1,0:T(8,128)(2,1)S(1)}, bf16[4,96,832]{2,1,0:T(8,128)(2,1)S(1)}) custom-call(s32[4]{0:T(128)S(1)} %pad_add_fusion.scalar_ref, bf16[576,1536]{1,0:T(8,128)(2,1)S(1)} %get-tuple-element.164.grads_ref, bf16[1536,768]{1,0:T(8,128)(2,1)S(1)} %copy-done.6, bf16[768,192]{1,0:T(8,128)(2,1)S(1)} %get-tuple-element.169.outs_ref, ...), custom_call_target="tpu_custom_call" | custom-call | flops 1100000 | tf_op jit(solution)/shard_map/projection_weights/pallas_call | solution.py:627
  140.7 1.9 collective-permute-start.33
  143.0 1.7 collective-permute-start.35
  145.0 3.9 %layer_out.1 = (bf16[384,768]{1,0:T(8,128)(2,1)}, bf16[384,768]{1,0:T(8,128)(2,1)}, bf16[1536,768]{1,0:T(8,128)(2,1)}) custom-call(s32[4]{0:T(128)S(1)} %pad_add_fusion.scalar_ref, bf16[768,768]{1,0:T(8,128)(2,1)S(1)} %add_convert_fusion.mine_ref, bf16[768,768]{1,0:T(8,128)(2,1)S(1)} %collective-permute-done.27.other_ref, ...), custom_call_target="tpu_custom_call" | custom-call | flops 1100000 | tf_op jit(solution)/shard_map/layer_out/pallas_call | solution.py:653
  148.9 13.8 %collective-permute-done.33.other_ref = bf16[4,96,832]{2,1,0:T(8,128)(2,1)S(1)} collective-permute-done((bf16[4,96,832]{2,1,0:T(8,128)(2,1)S(1)}, bf16[4,96,832]{2,1,0:T(8,128)(2,1)S(1)}, u32[]{:S(2)}, u32[]{:S(2)}) %collective-permute-start.33) | collective-permute-done | bytes 639008 | tf_op jit(solution)/shard_map/ppermute | solution.py:72
  164.1 4.0 %collective-permute-start.36 = (bf16[96,832]{1,0:T(8,128)(2,1)}, bf16[96,832]{1,0:T(8,128)(2,1)S(1)}, u32[]{:S(2)}, u32[]{:S(2)}) collective-permute-start(bf16[96,832]{1,0:T(8,128)(2,1)} %get-tuple-element.189), channel_id=1, source_target_pairs={{0,8},{4,12},{8,0},{12,4},{16,24},{20,28},{24,16},{28,20},{1,9},{5... | collective-permute-start | bytes 479240 | tf_op jit(solution)/shard_map/ppermute | solution.py:72
  168.4 2.1 %collective-permute-start.38 = (bf16[96,832]{1,0:T(8,128)(2,1)}, bf16[96,832]{1,0:T(8,128)(2,1)}, u32[]{:S(2)}, u32[]{:S(2)}) collective-permute-start(bf16[96,832]{1,0:T(8,128)(2,1)} %get-tuple-element.191), channel_id=1, source_target_pairs={{0,24},{4,28},{8,16},{12,20},{16,8},{20,12},{24,0},{28,4},{1,25},{... | collective-permute-start | bytes 479240 | tf_op jit(solution)/shard_map/ppermute | solution.py:72
  170.4 2.5 %first_norm_backward.2 = (bf16[384,768]{1,0:T(8,128)(2,1)}, bf16[1536,768]{1,0:T(8,128)(2,1)}) custom-call(s32[4]{0:T(128)S(1)} %pad_add_fusion.scalar_ref, bf16[384,768]{1,0:T(8,128)(2,1)S(1)} %get-tuple-element.183.mine_ref, bf16[384,768]{1,0:T(8,128)(2,1)S(1)} %collective-permute-done.35.other_ref, bf16[1536,768]{1,0:T(8,128)(2,1)S(1)} %copy-done, ...), custom_call_target="tpu_custom_call" | custom-call | flops 1100000 | tf_op jit(solution)/shard_map/first_norm_backward/pallas_call | solution.py:687
  173.4 2.4 %first_norm_backward.3 = (bf16[384,768]{1,0:T(8,128)(2,1)}, bf16[1536,768]{1,0:T(8,128)(2,1)}) custom-call(s32[4]{0:T(128)S(1)} %pad_add_fusion.scalar_ref, bf16[384,768]{1,0:T(8,128)(2,1)S(1)} %get-tuple-element.181.mine_ref, bf16[384,768]{1,0:T(8,128)(2,1)S(1)} %collective-permute-done.34.other_ref, ...), custom_call_target="tpu_custom_call", output_to_operand_aliasing={{1}: (6, {})} | custom-call | flops 1100000 | tf_op jit(solution)/shard_map/first_norm_backward/pallas_call | solution.py:687
  175.8 2.8 %total.3 = (f32[96,768]{1,0:T(8,128)}, f32[96,768]{1,0:T(8,128)}) custom-call(bf16[8,96,1536]{2,1,0:T(8,128)(2,1)} %all-to-all-done.refs_0_), custom_call_target="tpu_custom_call" | custom-call | flops 1100000 | tf_op jit(solution)/shard_map/total/pallas_call | solution.py:756
  178.6 5.3 %collective-permute-done.37.refs_2_ = bf16[96,832]{1,0:T(8,128)(2,1)} collective-permute-done((bf16[96,832]{1,0:T(8,128)(2,1)}, bf16[96,832]{1,0:T(8,128)(2,1)}, u32[]{:S(2)}, u32[]{:S(2)}) %collective-permute-start.37) | collective-permute-done | bytes 159776 | tf_op jit(solution)/shard_map/ppermute | solution.py:72
  185.1 1.4 collective-permute-start.39
  186.5 1.8 total.5
  188.9 3.1 %place.1 = (bf16[1536,768]{1,0:T(8,128)(2,1)}, bf16[1536,768]{1,0:T(8,128)(2,1)}) custom-call(s32[4]{0:T(128)S(1)} %pad_add_fusion.scalar_ref, bf16[384,768]{1,0:T(8,128)(2,1)S(1)} %collective-permute-done.32.refs_0_, bf16[384,768]{1,0:T(8,128)(2,1)} %collective-permute-done.40.refs_1_, ...), custom_call_target="tpu_custom_call", output_to_operand_aliasing={{0}: (5, {}), {1}: (6, {})} | custom-call | flops 1100000 | tf_op jit(solution)/shard_map/place/pallas_call | solution.py:720
  (106 shorter events, 19.7 us)
Async XLA Ops:
  4.1 11.0 %collective-permute-start.1 = (bf16[96,896]{1,0:T(8,128)(2,1)S(1)}, bf16[96,896]{1,0:T(8,128)(2,1)S(1)}, u32[]{:S(2)}, u32[]{:S(2)}) collective-permute-start(bf16[96,896]{1,0:T(8,128)(2,1)S(1)} %concatenate.6.refs_0_), channel_id=1, source_target_pairs={{0,8},{4,12},{8,0},{12,4},{16,24},{20,28},{24,16},{28,20},{1,9},{5... | collective-permute-start | bytes 516104 | tf_op jit(solution)/shard_map/ppermute | solution.py:72
  7.2 12.1 %collective-permute-start.3 = (bf16[96,896]{1,0:T(8,128)(2,1)S(1)}, bf16[96,896]{1,0:T(8,128)(2,1)S(1)}, u32[]{:S(2)}, u32[]{:S(2)}) collective-permute-start(bf16[96,896]{1,0:T(8,128)(2,1)S(1)} %concatenate.6.refs_0_), channel_id=1, source_target_pairs={{0,16},{4,20},{8,24},{12,28},{16,0},{20,4},{24,8},{28,12},{1,17},{... | collective-permute-start | bytes 516104 | tf_op jit(solution)/shard_map/ppermute | solution.py:72
  9.8 9.5 %collective-permute-start = (bf16[96,896]{1,0:T(8,128)(2,1)S(1)}, bf16[96,896]{1,0:T(8,128)(2,1)S(1)}, u32[]{:S(2)}, u32[]{:S(2)}) collective-permute-start(bf16[96,896]{1,0:T(8,128)(2,1)S(1)} %concatenate.6.refs_0_), channel_id=1, source_target_pairs={{0,4},{4,0},{8,12},{12,8},{16,20},{20,16},{24,28},{28,24},{1,5},{5... | collective-permute-start | bytes 516104 | tf_op jit(solution)/shard_map/ppermute | solution.py:72
  15.1 5.4 %collective-permute-start.2 = (bf16[96,896]{1,0:T(8,128)(2,1)S(1)}, bf16[96,896]{1,0:T(8,128)(2,1)S(1)}, u32[]{:S(2)}, u32[]{:S(2)}) collective-permute-start(bf16[96,896]{1,0:T(8,128)(2,1)S(1)} %collective-permute-done.1.refs_2_), channel_id=1, source_target_pairs={{0,4},{4,0},{8,12},{12,8},{16,20},{20,16},{24,28},{28,24},{1,5},{5... | collective-permute-start | bytes 516104 | tf_op jit(solution)/shard_map/ppermute | solution.py:72
  16.8 7.3 %collective-permute-start.5 = (bf16[96,896]{1,0:T(8,128)(2,1)S(1)}, bf16[96,896]{1,0:T(8,128)(2,1)S(1)}, u32[]{:S(2)}, u32[]{:S(2)}) collective-permute-start(bf16[96,896]{1,0:T(8,128)(2,1)S(1)} %concatenate.6.refs_0_), channel_id=1, source_target_pairs={{0,24},{4,28},{8,16},{12,20},{16,8},{20,12},{24,0},{28,4},{1,25},{... | collective-permute-start | bytes 516104 | tf_op jit(solution)/shard_map/ppermute | solution.py:72
  20.5 5.4 %collective-permute-start.4 = (bf16[96,896]{1,0:T(8,128)(2,1)S(1)}, bf16[96,896]{1,0:T(8,128)(2,1)S(1)}, u32[]{:S(2)}, u32[]{:S(2)}) collective-permute-start(bf16[96,896]{1,0:T(8,128)(2,1)S(1)} %collective-permute-done.3.refs_4_), channel_id=1, source_target_pairs={{0,4},{4,0},{8,12},{12,8},{16,20},{20,16},{24,28},{28,24},{1,5},{5... | collective-permute-start | bytes 516104 | tf_op jit(solution)/shard_map/ppermute | solution.py:72
  23.4 22.0 %copy-start.7 = (bf16[96,1536]{1,0:T(8,128)(2,1)}, bf16[96,1536]{1,0:T(8,128)(2,1)S(1)}, u32[]{:S(2)}) copy-start(bf16[96,1536]{1,0:T(8,128)(2,1)S(1)} %pad_maximum_fusion.refs_0_) | copy-start | bytes 884740
  26.0 11.1 %collective-permute-start.7 = (bf16[96,1536]{1,0:T(8,128)(2,1)S(1)}, bf16[96,1536]{1,0:T(8,128)(2,1)}, u32[]{:S(2)}, u32[]{:S(2)}) collective-permute-start(bf16[96,1536]{1,0:T(8,128)(2,1)S(1)} %pad_maximum_fusion.refs_0_), channel_id=1, source_target_pairs={{0,8},{4,12},{8,0},{12,4},{16,24},{20,28},{24,16},{28,20},{1,9},{5... | collective-permute-start | bytes 884744 | tf_op jit(solution)/shard_map/ppermute | solution.py:72
  26.0 5.5 %collective-permute-start.6 = (bf16[96,896]{1,0:T(8,128)(2,1)S(1)}, bf16[96,896]{1,0:T(8,128)(2,1)S(1)}, u32[]{:S(2)}, u32[]{:S(2)}) collective-permute-start(bf16[96,896]{1,0:T(8,128)(2,1)S(1)} %collective-permute-done.5.refs_6_), channel_id=1, source_target_pairs={{0,4},{4,0},{8,12},{12,8},{16,20},{20,16},{24,28},{28,24},{1,5},{5... | collective-permute-start | bytes 516104 | tf_op jit(solution)/shard_map/ppermute | solution.py:72
  28.5 17.0 %collective-permute-start.16 = (bf16[96,1536]{1,0:T(8,128)(2,1)S(1)}, bf16[96,1536]{1,0:T(8,128)(2,1)S(1)}, u32[]{:S(2)}, u32[]{:S(2)}) collective-permute-start(bf16[96,1536]{1,0:T(8,128)(2,1)S(1)} %pad_maximum_fusion.refs_0_), channel_id=1, source_target_pairs={{0,16},{4,20},{8,24},{12,28},{16,0},{20,4},{24,8},{28,12},{1,17},{... | collective-permute-start | bytes 884744 | tf_op jit(solution)/shard_map/ppermute | solution.py:72
  37.1 12.7 %collective-permute-start.8 = (bf16[96,1536]{1,0:T(8,128)(2,1)}, bf16[96,1536]{1,0:T(8,128)(2,1)S(1)}, u32[]{:S(2)}, u32[]{:S(2)}) collective-permute-start(bf16[96,1536]{1,0:T(8,128)(2,1)} %collective-permute-done.7.refs_2_), channel_id=1, source_target_pairs={{0,4},{4,0},{8,12},{12,8},{16,20},{20,16},{24,28},{28,24},{1,5},{5... | collective-permute-start | bytes 884744 | tf_op jit(solution)/shard_map/ppermute | solution.py:72
  38.9 29.8 %copy-start.1 = (bf16[1536,768]{1,0:T(8,128)(2,1)S(1)}, bf16[1536,768]{1,0:T(8,128)(2,1)}, u32[]{:S(2)}) copy-start(bf16[1536,768]{1,0:T(8,128)(2,1)} %grad_ref.5) | copy-start | bytes 7077892
  45.5 23.3 %copy-start = (bf16[1536,768]{1,0:T(8,128)(2,1)S(1)}, bf16[1536,768]{1,0:T(8,128)(2,1)}, u32[]{:S(2)}) copy-start(bf16[1536,768]{1,0:T(8,128)(2,1)} %tokens_ref.7) | copy-start | bytes 7077892
  45.5 11.0 %collective-permute-start.18 = (bf16[96,1536]{1,0:T(8,128)(2,1)S(1)}, bf16[96,1536]{1,0:T(8,128)(2,1)S(1)}, u32[]{:S(2)}, u32[]{:S(2)}) collective-permute-start(bf16[96,1536]{1,0:T(8,128)(2,1)S(1)} %collective-permute-done.16.refs_4_), channel_id=1, source_target_pairs={{0,8},{4,12},{8,0},{12,4},{16,24},{20,28},{24,16},{28,20},{1,9},{5... | collective-permute-start | bytes 884744 | tf_op jit(solution)/shard_map/ppermute | solution.py:72
  47.6 9.3 %collective-permute-start.15 = (bf16[96,1536]{1,0:T(8,128)(2,1)}, bf16[96,1536]{1,0:T(8,128)(2,1)S(1)}, u32[]{:S(2)}, u32[]{:S(2)}) collective-permute-start(bf16[96,1536]{1,0:T(8,128)(2,1)} %copy-done.7), channel_id=1, source_target_pairs={{0,4},{4,0},{8,12},{12,8},{16,20},{20,16},{24,28},{28,24},{1,5},{5... | collective-permute-start | bytes 884744 | tf_op jit(solution)/shard_map/ppermute | solution.py:72
  47.7 14.4 %collective-permute-start.20 = (bf16[192,1024]{1,0:T(8,128)(2,1)S(1)}, bf16[192,1024]{1,0:T(8,128)(2,1)S(1)}, u32[]{:S(2)}, u32[]{:S(2)}) collective-permute-start(bf16[192,1024]{1,0:T(8,128)(2,1)S(1)} %get-tuple-element.110.refs_2_), channel_id=1, source_target_pairs={{0,2},{1,3},{2,0},{3,1},{4,6},{5,7},{6,4},{7,5},{8,10},{9,11},{10,... | collective-permute-start | bytes 1179656 | tf_op jit(solution)/shard_map/ppermute | solution.py:72
  49.6 10.8 %collective-permute-start.12 = (bf16[192,768]{1,0:T(8,128)(2,1)S(1)}, bf16[192,768]{1,0:T(8,128)(2,1)S(1)}, u32[]{:S(2)}, u32[]{:S(2)}) collective-permute-start(bf16[192,768]{1,0:T(8,128)(2,1)S(1)} %get-tuple-element.113.refs_6_.refs_1_), channel_id=1, source_target_pairs={{0,2},{1,3},{2,0},{3,1},{4,6},{5,7},{6,4},{7,5},{8,10},{9,11},{10,... | collective-permute-start | bytes 884744 | tf_op jit(solution)/shard_map/ppermute | solution.py:72
  49.7 12.3 %collective-permute-start.17 = (bf16[96,1536]{1,0:T(8,128)(2,1)S(1)}, bf16[96,1536]{1,0:T(8,128)(2,1)S(1)}, u32[]{:S(2)}, u32[]{:S(2)}) collective-permute-start(bf16[96,1536]{1,0:T(8,128)(2,1)S(1)} %collective-permute-done.16.refs_4_), channel_id=1, source_target_pairs={{0,4},{4,0},{8,12},{12,8},{16,20},{20,16},{24,28},{28,24},{1,5},{5... | collective-permute-start | bytes 884744 | tf_op jit(solution)/shard_map/ppermute | solution.py:72
  56.5 9.6 %collective-permute-start.19 = (bf16[96,1536]{1,0:T(8,128)(2,1)S(1)}, bf16[96,1536]{1,0:T(8,128)(2,1)S(1)}, u32[]{:S(2)}, u32[]{:S(2)}) collective-permute-start(bf16[96,1536]{1,0:T(8,128)(2,1)S(1)} %collective-permute-done.18.refs_6_), channel_id=1, source_target_pairs={{0,4},{4,0},{8,12},{12,8},{16,20},{20,16},{24,28},{28,24},{1,5},{5... | collective-permute-start | bytes 884744 | tf_op jit(solution)/shard_map/ppermute | solution.py:72
  56.9 5.7 %collective-permute-start.10 = (bf16[192,512]{1,0:T(8,128)(2,1)S(1)}, bf16[192,512]{1,0:T(8,128)(2,1)S(1)}, u32[]{:S(2)}, u32[]{:S(2)}) collective-permute-start(bf16[192,512]{1,0:T(8,128)(2,1)S(1)} %get-tuple-element.116.refs_2_.refs_3_), channel_id=1, source_target_pairs={{0,1},{1,0},{2,3},{3,2},{4,5},{5,4},{6,7},{7,6},{8,9},{9,8},{10,11... | collective-permute-start | bytes 589832 | tf_op jit(solution)/shard_map/ppermute | solution.py:72
  60.4 5.7 %collective-permute-start.9 = (bf16[192,512]{1,0:T(8,128)(2,1)S(1)}, bf16[192,512]{1,0:T(8,128)(2,1)S(1)}, u32[]{:S(2)}, u32[]{:S(2)}) collective-permute-start(bf16[192,512]{1,0:T(8,128)(2,1)S(1)} %get-tuple-element.116.refs_2_.refs_3_), channel_id=1, source_target_pairs={{0,2},{1,3},{2,0},{3,1},{4,6},{5,7},{6,4},{7,5},{8,10},{9,11},{10,... | collective-permute-start | bytes 589832 | tf_op jit(solution)/shard_map/ppermute | solution.py:72
  62.1 6.6 %collective-permute-start.21 = (bf16[192,1024]{1,0:T(8,128)(2,1)S(1)}, bf16[192,1024]{1,0:T(8,128)(2,1)S(1)}, u32[]{:S(2)}, u32[]{:S(2)}) collective-permute-start(bf16[192,1024]{1,0:T(8,128)(2,1)S(1)} %get-tuple-element.110.refs_2_), channel_id=1, source_target_pairs={{0,1},{1,0},{2,3},{3,2},{4,5},{5,4},{6,7},{7,6},{8,9},{9,8},{10,11... | collective-permute-start | bytes 1179656 | tf_op jit(solution)/shard_map/ppermute | solution.py:72
  62.1 6.7 %collective-permute-start.22 = (bf16[192,1024]{1,0:T(8,128)(2,1)S(1)}, bf16[192,1024]{1,0:T(8,128)(2,1)S(1)}, u32[]{:S(2)}, u32[]{:S(2)}) collective-permute-start(bf16[192,1024]{1,0:T(8,128)(2,1)S(1)} %collective-permute-done.20.refs_3_), channel_id=1, source_target_pairs={{0,1},{1,0},{2,3},{3,2},{4,5},{5,4},{6,7},{7,6},{8,9},{9,8},{10,11... | collective-permute-start | bytes 1179656 | tf_op jit(solution)/shard_map/ppermute | solution.py:72
  62.6 6.1 %collective-permute-start.13 = (bf16[192,768]{1,0:T(8,128)(2,1)S(1)}, bf16[192,768]{1,0:T(8,128)(2,1)S(1)}, u32[]{:S(2)}, u32[]{:S(2)}) collective-permute-start(bf16[192,768]{1,0:T(8,128)(2,1)S(1)} %get-tuple-element.113.refs_6_.refs_1_), channel_id=1, source_target_pairs={{0,1},{1,0},{2,3},{3,2},{4,5},{5,4},{6,7},{7,6},{8,9},{9,8},{10,11... | collective-permute-start | bytes 884744 | tf_op jit(solution)/shard_map/ppermute | solution.py:72
  66.1 2.6 %collective-permute-start.14 = (bf16[192,768]{1,0:T(8,128)(2,1)S(1)}, bf16[192,768]{1,0:T(8,128)(2,1)S(1)}, u32[]{:S(2)}, u32[]{:S(2)}) collective-permute-start(bf16[192,768]{1,0:T(8,128)(2,1)S(1)} %collective-permute-done.12.refs_7_), channel_id=1, source_target_pairs={{0,1},{1,0},{2,3},{3,2},{4,5},{5,4},{6,7},{7,6},{8,9},{9,8},{10,11... | collective-permute-start | bytes 884744 | tf_op jit(solution)/shard_map/ppermute | solution.py:72
  66.1 2.6 %collective-permute-start.11 = (bf16[192,512]{1,0:T(8,128)(2,1)S(1)}, bf16[192,512]{1,0:T(8,128)(2,1)S(1)}, u32[]{:S(2)}, u32[]{:S(2)}) collective-permute-start(bf16[192,512]{1,0:T(8,128)(2,1)S(1)} %collective-permute-done.9.refs_3_), channel_id=1, source_target_pairs={{0,1},{1,0},{2,3},{3,2},{4,5},{5,4},{6,7},{7,6},{8,9},{9,8},{10,11... | collective-permute-start | bytes 589832 | tf_op jit(solution)/shard_map/ppermute | solution.py:72
  73.6 8.2 %collective-permute-start.23 = (bf16[512,768]{1,0:T(8,128)(2,1)S(1)}, bf16[512,768]{1,0:T(8,128)(2,1)S(1)}, u32[]{:S(2)}, u32[]{:S(2)}) collective-permute-start(bf16[512,768]{1,0:T(8,128)(2,1)S(1)} %get-tuple-element.140), channel_id=1, source_target_pairs={{0,1},{1,0},{2,3},{3,2},{4,5},{5,4},{6,7},{7,6},{8,9},{9,8},{10,11... | collective-permute-start | bytes 2359304 | tf_op jit(solution)/shard_map/ppermute | solution.py:72
  76.7 11.3 %collective-permute-start.24 = (bf16[256,768]{1,0:T(8,128)(2,1)S(1)}, bf16[256,768]{1,0:T(8,128)(2,1)S(1)}, u32[]{:S(2)}, u32[]{:S(2)}) collective-permute-start(bf16[256,768]{1,0:T(8,128)(2,1)S(1)} %get-tuple-element.148), channel_id=1, source_target_pairs={{0,1},{1,0},{2,3},{3,2},{4,5},{5,4},{6,7},{7,6},{8,9},{9,8},{10,11... | collective-permute-start | bytes 1179656 | tf_op jit(solution)/shard_map/ppermute | solution.py:72
  83.0 21.3 %collective-permute-start.28 = (bf16[512,768]{1,0:T(8,128)(2,1)}, bf16[512,768]{1,0:T(8,128)(2,1)}, u32[]{:S(2)}, u32[]{:S(2)}) collective-permute-start(bf16[512,768]{1,0:T(8,128)(2,1)} %add_convert_fusion.1.mine_ref), channel_id=1, source_target_pairs={{0,2},{1,3},{2,0},{3,1},{4,6},{5,7},{6,4},{7,5},{8,10},{9,11},{10,... | collective-permute-start | bytes 2359304 | tf_op jit(solution)/shard_map/ppermute | solution.py:72
  88.8 22.4 %collective-permute-start.26 = (bf16[256,768]{1,0:T(8,128)(2,1)}, bf16[256,768]{1,0:T(8,128)(2,1)}, u32[]{:S(2)}, u32[]{:S(2)}) collective-permute-start(bf16[256,768]{1,0:T(8,128)(2,1)} %add_convert_fusion.4.mine_ref), channel_id=1, source_target_pairs={{0,2},{1,3},{2,0},{3,1},{4,6},{5,7},{6,4},{7,5},{8,10},{9,11},{10,... | collective-permute-start | bytes 1179656 | tf_op jit(solution)/shard_map/ppermute | solution.py:72
  98.8 77.1 %all-to-all-start = ((bf16[8,96,1536]{2,1,0:T(8,128)(2,1)}), bf16[8,96,1536]{2,1,0:T(8,128)(2,1)}, u32[]{:S(2)}, u32[]{:S(2)}) async-start(bf16[8,96,1536]{2,1,0:T(8,128)(2,1)} %bitcast.9), calls=%async_computation | async-start | bytes 4718592 | tf_op jit(solution)/shard_map/all_to_all | solution.py:771
  104.3 9.6 %collective-permute-start.25 = (bf16[768,768]{1,0:T(8,128)(2,1)}, bf16[768,768]{1,0:T(8,128)(2,1)S(1)}, u32[]{:S(2)}, u32[]{:S(2)}) collective-permute-start(bf16[768,768]{1,0:T(8,128)(2,1)} %get-tuple-element.153), channel_id=1, source_target_pairs={{0,1},{1,0},{2,3},{3,2},{4,5},{5,4},{6,7},{7,6},{8,9},{9,8},{10,11... | collective-permute-start | bytes 3538952 | tf_op jit(solution)/shard_map/ppermute | solution.py:72
  108.1 7.9 %collective-permute-start.29 = (bf16[512,768]{1,0:T(8,128)(2,1)S(1)}, bf16[512,768]{1,0:T(8,128)(2,1)S(1)}, u32[]{:S(2)}, u32[]{:S(2)}) collective-permute-start(bf16[512,768]{1,0:T(8,128)(2,1)S(1)} %second_norm_backward.2.refs_6_), channel_id=1, source_target_pairs={{0,1},{1,0},{2,3},{3,2},{4,5},{5,4},{6,7},{7,6},{8,9},{9,8},{10,11... | collective-permute-start | bytes 2359304 | tf_op jit(solution)/shard_map/ppermute | solution.py:72
  113.8 2.1 %collective-permute-start.30 = (bf16[256,768]{1,0:T(8,128)(2,1)S(1)}, bf16[256,768]{1,0:T(8,128)(2,1)S(1)}, u32[]{:S(2)}, u32[]{:S(2)}) collective-permute-start(bf16[256,768]{1,0:T(8,128)(2,1)S(1)} %second_norm_backward.3.refs_8_), channel_id=1, source_target_pairs={{0,1},{1,0},{2,3},{3,2},{4,5},{5,4},{6,7},{7,6},{8,9},{9,8},{10,11... | collective-permute-start | bytes 1179656 | tf_op jit(solution)/shard_map/ppermute | solution.py:72
  114.2 28.4 %collective-permute-start.27 = (bf16[768,768]{1,0:T(8,128)(2,1)S(1)}, bf16[768,768]{1,0:T(8,128)(2,1)S(1)}, u32[]{:S(2)}, u32[]{:S(2)}) collective-permute-start(bf16[768,768]{1,0:T(8,128)(2,1)S(1)} %add_convert_fusion.mine_ref), channel_id=1, source_target_pairs={{0,2},{1,3},{2,0},{3,1},{4,6},{5,7},{6,4},{7,5},{8,10},{9,11},{10,... | collective-permute-start | bytes 3538952 | tf_op jit(solution)/shard_map/ppermute | solution.py:72
  136.2 6.5 %collective-permute-start.31 = (bf16[768,768]{1,0:T(8,128)(2,1)S(1)}, bf16[768,768]{1,0:T(8,128)(2,1)S(1)}, u32[]{:S(2)}, u32[]{:S(2)}) collective-permute-start(bf16[768,768]{1,0:T(8,128)(2,1)S(1)} %get-tuple-element.175), channel_id=1, source_target_pairs={{0,1},{1,0},{2,3},{3,2},{4,5},{5,4},{6,7},{7,6},{8,9},{9,8},{10,11... | collective-permute-start | bytes 3538952 | tf_op jit(solution)/shard_map/ppermute | solution.py:72
  140.7 22.0 %collective-permute-start.33 = (bf16[4,96,832]{2,1,0:T(8,128)(2,1)S(1)}, bf16[4,96,832]{2,1,0:T(8,128)(2,1)S(1)}, u32[]{:S(2)}, u32[]{:S(2)}) collective-permute-start(bf16[4,96,832]{2,1,0:T(8,128)(2,1)S(1)} %get-tuple-element.173), channel_id=1, source_target_pairs={{0,4},{4,0},{8,12},{12,8},{16,20},{20,16},{24,28},{28,24},{1,5},{5... | collective-permute-start | bytes 1916936 | tf_op jit(solution)/shard_map/ppermute | solution.py:72
  143.0 27.5 %collective-permute-start.35 = (bf16[384,768]{1,0:T(8,128)(2,1)S(1)}, bf16[384,768]{1,0:T(8,128)(2,1)S(1)}, u32[]{:S(2)}, u32[]{:S(2)}) collective-permute-start(bf16[384,768]{1,0:T(8,128)(2,1)S(1)} %get-tuple-element.183.mine_ref), channel_id=1, source_target_pairs={{0,2},{1,3},{2,0},{3,1},{4,6},{5,7},{6,4},{7,5},{8,10},{9,11},{10,... | collective-permute-start | bytes 1769480 | tf_op jit(solution)/shard_map/ppermute | solution.py:72
  144.7 28.2 %collective-permute-start.34 = (bf16[384,768]{1,0:T(8,128)(2,1)S(1)}, bf16[384,768]{1,0:T(8,128)(2,1)S(1)}, u32[]{:S(2)}, u32[]{:S(2)}) collective-permute-start(bf16[384,768]{1,0:T(8,128)(2,1)S(1)} %get-tuple-element.181.mine_ref), channel_id=1, source_target_pairs={{0,2},{1,3},{2,0},{3,1},{4,6},{5,7},{6,4},{7,5},{8,10},{9,11},{10,... | collective-permute-start | bytes 1769480 | tf_op jit(solution)/shard_map/ppermute | solution.py:72
  164.1 14.5 %collective-permute-start.36 = (bf16[96,832]{1,0:T(8,128)(2,1)}, bf16[96,832]{1,0:T(8,128)(2,1)S(1)}, u32[]{:S(2)}, u32[]{:S(2)}) collective-permute-start(bf16[96,832]{1,0:T(8,128)(2,1)} %get-tuple-element.189), channel_id=1, source_target_pairs={{0,8},{4,12},{8,0},{12,4},{16,24},{20,28},{24,16},{28,20},{1,9},{5... | collective-permute-start | bytes 479240 | tf_op jit(solution)/shard_map/ppermute | solution.py:72
  168.1 15.9 %collective-permute-start.37 = (bf16[96,832]{1,0:T(8,128)(2,1)}, bf16[96,832]{1,0:T(8,128)(2,1)}, u32[]{:S(2)}, u32[]{:S(2)}) collective-permute-start(bf16[96,832]{1,0:T(8,128)(2,1)} %get-tuple-element.190), channel_id=1, source_target_pairs={{0,16},{4,20},{8,24},{12,28},{16,0},{20,4},{24,8},{28,12},{1,17},{... | collective-permute-start | bytes 479240 | tf_op jit(solution)/shard_map/ppermute | solution.py:72
  168.4 15.6 %collective-permute-start.38 = (bf16[96,832]{1,0:T(8,128)(2,1)}, bf16[96,832]{1,0:T(8,128)(2,1)}, u32[]{:S(2)}, u32[]{:S(2)}) collective-permute-start(bf16[96,832]{1,0:T(8,128)(2,1)} %get-tuple-element.191), channel_id=1, source_target_pairs={{0,24},{4,28},{8,16},{12,20},{16,8},{20,12},{24,0},{28,4},{1,25},{... | collective-permute-start | bytes 479240 | tf_op jit(solution)/shard_map/ppermute | solution.py:72
  170.4 18.4 %collective-permute-start.32 = (bf16[384,768]{1,0:T(8,128)(2,1)}, bf16[384,768]{1,0:T(8,128)(2,1)S(1)}, u32[]{:S(2)}, u32[]{:S(2)}) collective-permute-start(bf16[384,768]{1,0:T(8,128)(2,1)} %get-tuple-element.177), channel_id=1, source_target_pairs={{0,1},{1,0},{2,3},{3,2},{4,5},{5,4},{6,7},{7,6},{8,9},{9,8},{10,11... | collective-permute-start | bytes 1769480 | tf_op jit(solution)/shard_map/ppermute | solution.py:72
  172.9 16.0 %collective-permute-start.40 = (bf16[384,768]{1,0:T(8,128)(2,1)}, bf16[384,768]{1,0:T(8,128)(2,1)}, u32[]{:S(2)}, u32[]{:S(2)}) collective-permute-start(bf16[384,768]{1,0:T(8,128)(2,1)} %get-tuple-element.178), channel_id=1, source_target_pairs={{0,1},{1,0},{2,3},{3,2},{4,5},{5,4},{6,7},{7,6},{8,9},{9,8},{10,11... | collective-permute-start | bytes 1769480 | tf_op jit(solution)/shard_map/ppermute | solution.py:72
  178.6 10.3 %collective-permute-start.42 = (bf16[384,768]{1,0:T(8,128)(2,1)S(1)}, bf16[384,768]{1,0:T(8,128)(2,1)S(1)}, u32[]{:S(2)}, u32[]{:S(2)}) collective-permute-start(bf16[384,768]{1,0:T(8,128)(2,1)S(1)} %copy-done.11), channel_id=1, source_target_pairs={{0,1},{1,0},{2,3},{3,2},{4,5},{5,4},{6,7},{7,6},{8,9},{9,8},{10,11... | collective-permute-start | bytes 1769480 | tf_op jit(solution)/shard_map/ppermute | solution.py:72
  184.0 4.9 %collective-permute-start.41 = (bf16[384,768]{1,0:T(8,128)(2,1)S(1)}, bf16[384,768]{1,0:T(8,128)(2,1)S(1)}, u32[]{:S(2)}, u32[]{:S(2)}) collective-permute-start(bf16[384,768]{1,0:T(8,128)(2,1)S(1)} %copy-done.10), channel_id=1, source_target_pairs={{0,1},{1,0},{2,3},{3,2},{4,5},{5,4},{6,7},{7,6},{8,9},{9,8},{10,11... | collective-permute-start | bytes 1769480 | tf_op jit(solution)/shard_map/ppermute | solution.py:72
  185.1 3.7 %collective-permute-start.39 = (f32[16,96]{1,0:T(8,128)S(1)}, f32[16,96]{1,0:T(8,128)S(1)}, u32[]{:S(2)}, u32[]{:S(2)}) collective-permute-start(f32[16,96]{1,0:T(8,128)S(1)} %slice.38), channel_id=1, source_target_pairs={{0,2},{1,3},{2,0},{3,1},{4,6},{5,7},{6,4},{7,5},{8,10},{9,11},{10,... | collective-permute-start | bytes 18440 | tf_op jit(solution)/shard_map/ppermute | solution.py:72
  188.8 3.2 %collective-permute-start.43 = (f32[16,96]{1,0:T(8,128)S(1)}, f32[16,96]{1,0:T(8,128)S(1)}, u32[]{:S(2)}, u32[]{:S(2)}) collective-permute-start(f32[16,96]{1,0:T(8,128)S(1)} %slice_add_fusion), channel_id=1, source_target_pairs={{0,1},{1,0},{2,3},{3,2},{4,5},{5,4},{6,7},{7,6},{8,9},{9,8},{10,11... | collective-permute-start | bytes 18440 | tf_op jit(solution)/shard_map/ppermute | solution.py:72
  (9 other events, 75.7 us)

commit v5 on v4

--- a/solution.py
+++ b/solution.py
@@ -101,6 +101,31 @@
     for bits, piece in enumerate(pieces):
         at = pl.multiple_of((index ^ bits) * count, 32) if len(pieces) > 1 else 0
         scratch[pl.ds(at, count), :] = piece[...]
+
+
+def pack_kernel(query_ref, key_ref, value_ref, outs_ref, gain_ref, shift_ref, out_ref):
+    width = query_ref.shape[1]
+    out_ref[:, :width] = query_ref[...]
+    out_ref[:, width : 2 * width] = key_ref[...]
+    out_ref[:, 2 * width : 3 * width] = value_ref[...]
+    out_ref[:, 3 * width : 4 * width] = jnp.transpose(outs_ref[...].astype(WIDE)).astype(LOW)
+    rows = [gain_ref[...].astype(WIDE), shift_ref[...].astype(WIDE)]
+    rows.append(jnp.zeros((LANES - 4, gain_ref.shape[1]), WIDE))
+    out_ref[:, 4 * width :] = jnp.transpose(jnp.concatenate(rows, axis=0)).astype(LOW)
+
+
+def pack(*shards):
+    rows, width = shards[0].shape
+    return pl.pallas_call(
+        pack_kernel,
+        grid=(1,),
+        in_specs=[pl.BlockSpec(shard.shape, lambda i: (0, 0)) for shard in shards],
+        out_specs=whole(),
+        out_shape=struct((rows, 4 * width + LANES), LOW),
+        compiler_params=params(4),
+        cost_estimate=cost(1),
+        name="pack",
+    )(*(far(shard) for shard in shards))
 
 
 def project_kernel(scalar_ref, *refs, parts, width, block):
@@ -357,10 +382,10 @@
     return up * half, slope
 
 
-def add_sums(sums_ref, ahead_ref, back, scaled):
-    sums_ref[0:1, :] = ahead_ref[0:1, :] + jnp.sum(back * scaled, axis=0, keepdims=True)
-    sums_ref[1:2, :] = ahead_ref[1:2, :] + jnp.sum(back, axis=0, keepdims=True)
-    sums_ref[2:8, :] = ahead_ref[2:8, :]
+def add_sums(sums_ref, ahead_ref, back, scaled, at):
+    sums_ref[...] = ahead_ref[...]
+    sums_ref[at : at + 1, :] += jnp.sum(back * scaled, axis=0, keepdims=True)
+    sums_ref[at + 1 : at + 2, :] += jnp.sum(back, axis=0, keepdims=True)
 
 
 def feed_kernel(scalar_ref, *refs, begin, size, half, keep, given):
@@ -400,7 +425,7 @@
         upper_ref[here, part] = upper
         back = back + outer_cols(upper, up_ref[:, part])
     back_ref[...] = back.astype(LOW)
-    add_sums(sums_ref, ahead_ref, back, scaled)
+    add_sums(sums_ref, ahead_ref, back, scaled, 2)
 
 
 def feed(scalar, tokens, out_grad, mixed, outs, up, down, rows, ahead, stored, begin, size, keep):
@@ -523,23 +548,34 @@
     )(scalar, normed, upper, active, out_grad, down)
 
 
-def fold_kernel(scalar_ref, mine_ref, other_ref, *outs):
+def fold_kernel(scalar_ref, mine_ref, other_ref, *refs, given):
     place = scalar_ref[3] >> 1
+    outs = refs[given:-1] if given else refs
+    rows, cols = mine_ref.shape[1:]
+    if given:
+        refs[-1][...] = turned_sums(refs[0][...] + refs[1][...])
     for k, out in enumerate(outs):
-        out[...] = (mine_ref[place ^ k].astype(WIDE) + other_ref[place ^ k].astype(WIDE)).astype(LOW)
-
-
-def fold(scalar, mine, other):
+        shard = place ^ k
+        out[:, :cols] = (mine_ref[shard].astype(WIDE) + other_ref[shard].astype(WIDE)).astype(LOW)
+        if given:
+            at = pl.multiple_of((shard * 2 + (scalar_ref[3] & 1)) * rows, 32)
+            out[:, cols:] = refs[-1][pl.ds(at, rows), :].astype(LOW)
+
+
+def fold(scalar, mine, other, sums):
     count, rows, cols = mine.shape
-    return pl.pallas_call(
-        fold_kernel,
-        in_specs=[scalars(), whole(), whole()],
+    given = len(sums)
+    cols += LANES if given else 0
+    return pl.pallas_call(
+        functools.partial(fold_kernel, given=given),
+        in_specs=[scalars()] + [whole()] * (2 + given),
         out_specs=(whole(),) * count,
         out_shape=(struct((rows, cols), LOW),) * count,
+        scratch_shapes=[pltpu.VMEM((sums[0].shape[1], LANES), WIDE)] if given else [],
         compiler_params=params(10),
         cost_estimate=cost(1),
         name="fold",
-    )(scalar, mine, other)
+    )(scalar, mine, other, *sums)
 
 
 def second_back_kernel(scalar_ref, mine_ref, other_ref, hidden_ref, grad_ref, rows_ref, low_ref, *, begin, half):
@@ -580,7 +616,7 @@
     )
     scaled, _ = standardize(tokens_ref[...].astype(WIDE))
     back_ref[...] = back.astype(LOW)
-    add_sums(sums_ref, ahead_ref, back, scaled)
+    add_sums(sums_ref, ahead_ref, back, scaled, 0)
 
 
 def inward(scalar, grads, tokens, weights, ahead, keep):
@@ -611,28 +647,32 @@
     )(scalar, grads, tokens, weights, ahead)
 
 
-def project_back_kernel(scalar_ref, grads_ref, normed_ref, outs_ref, one_ref, two_ref, *outs, width):
-    blank = jnp.zeros((LANES - 16, one_ref.shape[1]), WIDE)
-    rows = jnp.concatenate([one_ref[...], two_ref[...], blank], axis=0)
-    rows = jnp.transpose(rows)[:, : -width % LANES].astype(LOW)
+def turned_sums(sums):
+    blank = jnp.zeros((LANES - sums.shape[0], sums.shape[1]), WIDE)
+    return jnp.transpose(jnp.concatenate([sums, blank], axis=0))
+
+
+def project_back_kernel(scalar_ref, grads_ref, normed_ref, outs_ref, *refs, given):
+    outs = refs[given:]
     grads = jnp.transpose(multiply(grads_ref[...], normed_ref[...])).astype(LOW)
-    value = jnp.concatenate([grads, rows, outs_ref[...]], axis=1)
+    value = [grads, outs_ref[...]] + [turned_sums(ref[...]).astype(LOW) for ref in refs[:given]]
+    value = jnp.concatenate(value, axis=1)
     put_shards(scalar_ref[3], outs, value, slice(0, value.shape[1]))
 
 
-def project_back(scalar, grads, normed, outs_grad, one, two, batch):
+def project_back(scalar, grads, normed, outs_grad, sums, batch):
     width = grads.shape[0]
     depth = normed.shape[1]
-    shapes = shard_shapes(batch, depth, width + -width % LANES + outs_grad.shape[1])
-    return pl.pallas_call(
-        functools.partial(project_back_kernel, width=width),
-        in_specs=[scalars()] + [whole()] * 5,
+    shapes = shard_shapes(batch, depth, width + outs_grad.shape[1] + LANES * len(sums))
+    return pl.pallas_call(
+        functools.partial(project_back_kernel, given=len(sums)),
+        in_specs=[scalars()] + [whole()] * (3 + len(sums)),
         out_specs=(whole(),) * len(shapes),
         out_shape=shapes,
         compiler_params=params(16),
         cost_estimate=cost(1),
         name="projection_weights",
-    )(scalar, grads, normed, outs_grad, one, two)
+    )(scalar, grads, normed, outs_grad, *sums)
 
 
 def finish_kernel(scalar_ref, mine_ref, other_ref, *refs, sizes, half):
@@ -764,13 +804,13 @@
     )(*parts)
 
 
-def exchange_far(scalar, shards, ahead=()):
+def exchange_far(scalar, shards, ahead=(), sums=()):
     if len(shards) == 1:
         size = lax.axis_size("batch")
         parts = shards[0].reshape(size, shards[0].shape[0] // size, shards[0].shape[1])
         return [lax.all_to_all(parts, "batch", 0, 0, tiled=True)]
-    sums = fold(scalar, after(shards[0], *ahead), shards[1])
-    return [sums[0]] + [swap(piece, "batch", 2 * k) for k, piece in enumerate(sums) if k > 0]
+    pieces = fold(scalar, after(shards[0], *ahead), shards[1], sums)
+    return [pieces[0]] + [swap(piece, "batch", 2 * k) for k, piece in enumerate(pieces) if k > 0]
 
 
 def exchange_near(shards):
@@ -792,8 +832,11 @@
     first = half // 3 * 2
     chunks = ((0, first), (first, half - first))
 
-    blank = jnp.zeros((w_query.shape[0], -(4 * width + 4) % LANES), LOW)
-    early = jnp.concatenate([w_query, w_key, w_value, w_out.T, norm_gain.T, norm_shift.T, blank], axis=1)
+    if batch == 8:
+        early = pack(w_query, w_key, w_value, w_out, norm_gain, norm_shift)
+    else:
+        blank = jnp.zeros((w_query.shape[0], -(4 * width + 4) % LANES), LOW)
+        early = jnp.concatenate([w_query, w_key, w_value, w_out.T, norm_gain.T, norm_shift.T, blank], axis=1)
     late = jnp.concatenate([w_up, w_down.T], axis=1)
     if batch == 8:
         others = gather_far(early)
@@ -863,7 +906,7 @@
         low = second_back(scalar, mine, other, hidden, out_grad, rows, begin, 40000 if grads else 1)
         grads += [low, swap(low, "tensor", 1)]
     branch_mine = (branch_keep.astype(WIDE) + beside.astype(WIDE)).astype(LOW)
-    branch_mine = after(branch_mine, halves[-1][1])
+    branch_mine = after(branch_mine, halves[0][1])
     branch_other = swap(branch_mine, "tensor", 2)
     projected = after(projected, branch_mine)
     attend_grads, outs_grad, grad_attn = attend_back(
@@ -871,12 +914,19 @@
     )
 
     there = (1 - core) * half
-    ends, ones = [], jnp.zeros((8, depth), WIDE)
+    ends = []
+    if batch == 8:
+        project_grads = exchange_near(project_back(scalar, attend_grads, normed, outs_grad, (), batch))
+        attend_grads = after(attend_grads, project_grads[0])
     for keep in (False, True):
-        back, ones = inward(scalar, attend_grads, tokens, weights, ones, keep)
+        back, twos = inward(scalar, attend_grads, tokens, weights, twos, keep)
         ends.append(back)
-    project_grads = project_back(scalar, attend_grads, normed, outs_grad, ones, twos, batch)
-    keep = after(ends[1], branch_other, *project_grads)
+    if batch == 8:
+        sums = (twos, swap(twos, "batch", 1))
+    else:
+        project_grads = project_back(scalar, attend_grads, normed, outs_grad, (twos,), batch)
+        sums = ()
+    keep = after(ends[1], branch_other)
     beside = swap(ends[0], "tensor", 1)
     tails = []
     for begin in range(0, half, STEP):
@@ -884,7 +934,7 @@
         mine = (keep[part].astype(WIDE) + beside[part].astype(WIDE)).astype(LOW)
         tails.append((mine, swap(mine, "tensor", 2)))
     *own_out, layer_out = finish(scalar, branch_mine, after(branch_other, tails[-1][0]), hiddens, count)
-    project_parts = exchange_far(scalar, exchange_near(project_grads), own_out)
+    project_parts = exchange_far(scalar, project_grads, own_out, sums)
     other_out = [swap(own, "tensor", 1) for own in own_out]
     stored, other_grads = [], []
     for number, (mine, other) in enumerate(tails):
@@ -893,26 +943,25 @@
         other_grads.append(swap(own_grad, "tensor", 1))
     feed_parts[0] = after(feed_parts[0], own_grad)
     shard_up, shard_down = total_parts(feed_parts, ((0, units), (units, 2 * units)), (False, False), 1)
-    last = 3 * width
-    final = project_parts[0].shape[-1]
+    last = 4 * width
     project_parts[0] = after(project_parts[0], shard_up)
-    (small,) = total_parts(project_parts, ((last, final - width),), (True,), 40000)
-    small = small[:16]
+    (small,) = total_parts(project_parts, ((last, last + LANES),), (True,), 40000)
+    small = small[:8]
     across = swap(small, "tensor", 2)
     project_parts[0] = after(project_parts[0], small)
     shard_query, shard_key, shard_value, shard_out = total_parts(
         project_parts,
-        ((0, width), (width, 2 * width), (2 * width, last), (final - width, final)),
+        ((0, width), (width, 2 * width), (2 * width, 3 * width), (3 * width, last)),
         (False, False, False, True),
         1,
     )
     small = small + after(across, shard_query)
     across = swap(small, "tensor", 1)
-    other_out[0] = after(other_out[0], small)
+    other_grads[0] = after(other_grads[0], small)
     layer_out, grad_input = place(scalar, other_out, other_grads, (layer_out, stored[0]))
-    small = small + after(across, layer_out)
-    shard_gain = jnp.stack([small[0], small[8]])
-    shard_shift = jnp.stack([small[1], small[9]])
+    small = small + after(across, grad_input)
+    shard_gain = jnp.stack([small[0], small[2]])
+    shard_shift = jnp.stack([small[1], small[3]])
     return (
         layer_out,
         grad_input,

time: 196 us -> 190 us (0.969)
  waiting for transfers between devices: 37 us -> 30 us
  local copies, waits for them, and re-layouts: 4.45 us -> 0.77 us
  starting transfers between devices: 52 us -> 54.3 us
    ppermute x44 -> x45, waiting for transfers between devices: 37 us -> 30 us  [swap(): return lax.ppermute(value, axis, [(i, i ^ bits) for i in range(size)])]
    unnamed x27 -> x24, local copies, waits for them, and re-layouts: 3.45 us -> 0.76 us
    ppermute x44 -> x45, starting transfers between devices: 46.5 us -> 48.6 us  [swap(): return lax.ppermute(value, axis, [(i, i ^ bits) for i in range(size)])]
    pallas_call x2 -> x3, Pallas kernels: 3.72 us -> 4.97 us  [the longest x1 2.33 us: project_back(): pl.pallas_call(functools.partial(project_back_kernel, given=len(sums)), i...]
  transfers between devices with their start and end apart: 45 -> 46, of which waited for: 11 -> 11; matrix products, arithmetic and copies ran while one was open for 2% -> 2% of each run, Pallas kernels for 46% -> 48%
where the time goes in v5:
time: 190 us; the launch traced here: 187 us
  Pallas kernels  95 us (50%)
  starting transfers between devices  54.3 us (29%)
  waiting for transfers between devices  30 us (16%)
  other arithmetic  4.86 us (3%)
    ppermute x45, starting transfers between devices, swap(): return lax.ppermute(value, axis, [(i, i ^ bits) for i in range(size)])  48.6 us
    ppermute x45, waiting for transfers between devices, swap(): return lax.ppermute(value, axis, [(i, i ^ bits) for i in range(size)])  30 us
    pallas_call x1, Pallas kernels, attend_back(): pl.pallas_call(functools.partial(attend_back_kernel, chunks=chunks, rows=...  18.3 us
    pallas_call x4, Pallas kernels, feed(): pl.pallas_call(functools.partial(feed_kernel, begin=begin, size=size, hal...  16.4 us
    pallas_call x2, Pallas kernels, attend(): pl.pallas_call(functools.partial(attend_kernel, places=places, heads=head...  11.3 us
    pallas_call x1, Pallas kernels, weigh(): pl.pallas_call(weigh_kernel, grid_spec=pltpu.PrefetchScalarGridSpec(num_s...  9.63 us
    pallas_call x2, Pallas kernels, second_back(): pl.pallas_call(functools.partial(second_back_kernel, begin=begin, half=ha...  6.38 us
    all_to_all x1, starting transfers between devices, exchange_far(): return [lax.all_to_all(parts, 'batch', 0, 0, tiled=True)]  5.61 us
  transfers between devices with their start and end apart: 46, of which 11 were waited for; matrix products, arithmetic and copies ran while one was open for 2% of the time, Pallas kernels for 48%

profile of v5, /device:TPU:0, one launch (start us, length us, event | category | flops | bytes accessed | tf_op | source)
XLA Modules:
  0.0 186.8 jit_solution(15972885647531059125)
XLA Ops:
  1.7 3.1 %collective-permute-start.1 = (bf16[96,896]{1,0:T(8,128)(2,1)S(1)}, bf16[96,896]{1,0:T(8,128)(2,1)S(1)}, u32[]{:S(2)}, u32[]{:S(2)}) collective-permute-start(bf16[96,896]{1,0:T(8,128)(2,1)S(1)} %pack.1.refs_0_), channel_id=1, source_target_pairs={{0,8},{4,12},{8,0},{12,4},{16,24},{20,28},{24,16},{28,20},{1,9},{5... | collective-permute-start | bytes 516104 | tf_op jit(solution)/shard_map/ppermute | solution.py:72
  4.8 2.6 %collective-permute-start.3 = (bf16[96,896]{1,0:T(8,128)(2,1)S(1)}, bf16[96,896]{1,0:T(8,128)(2,1)S(1)}, u32[]{:S(2)}, u32[]{:S(2)}) collective-permute-start(bf16[96,896]{1,0:T(8,128)(2,1)S(1)} %pack.1.refs_0_), channel_id=1, source_target_pairs={{0,16},{4,20},{8,24},{12,28},{16,0},{20,4},{24,8},{28,12},{1,17},{... | collective-permute-start | bytes 516104 | tf_op jit(solution)/shard_map/ppermute | solution.py:72
  8.9 3.8 %collective-permute-done.1.refs_2_ = bf16[96,896]{1,0:T(8,128)(2,1)S(1)} collective-permute-done((bf16[96,896]{1,0:T(8,128)(2,1)S(1)}, bf16[96,896]{1,0:T(8,128)(2,1)S(1)}, u32[]{:S(2)}, u32[]{:S(2)}) %collective-permute-start.1) | collective-permute-done | bytes 172064 | tf_op jit(solution)/shard_map/ppermute | solution.py:72
  12.8 1.7 collective-permute-start.2
  14.4 2.5 %collective-permute-start.5 = (bf16[96,896]{1,0:T(8,128)(2,1)S(1)}, bf16[96,896]{1,0:T(8,128)(2,1)S(1)}, u32[]{:S(2)}, u32[]{:S(2)}) collective-permute-start(bf16[96,896]{1,0:T(8,128)(2,1)S(1)} %pack.1.refs_0_), channel_id=1, source_target_pairs={{0,24},{4,28},{8,16},{12,20},{16,8},{20,12},{24,0},{28,4},{1,25},{... | collective-permute-start | bytes 516104 | tf_op jit(solution)/shard_map/ppermute | solution.py:72
  18.2 1.9 %collective-permute-start.4 = (bf16[96,896]{1,0:T(8,128)(2,1)S(1)}, bf16[96,896]{1,0:T(8,128)(2,1)S(1)}, u32[]{:S(2)}, u32[]{:S(2)}) collective-permute-start(bf16[96,896]{1,0:T(8,128)(2,1)S(1)} %collective-permute-done.3.refs_4_), channel_id=1, source_target_pairs={{0,4},{4,0},{8,12},{12,8},{16,20},{20,16},{24,28},{28,24},{1,5},{5... | collective-permute-start | bytes 516104 | tf_op jit(solution)/shard_map/ppermute | solution.py:72
  20.1 1.7 pad_maximum_fusion.refs_0_
  21.8 1.8 collective-permute-done.4.refs_5_
  23.6 1.9 %collective-permute-start.6 = (bf16[96,896]{1,0:T(8,128)(2,1)S(1)}, bf16[96,896]{1,0:T(8,128)(2,1)S(1)}, u32[]{:S(2)}, u32[]{:S(2)}) collective-permute-start(bf16[96,896]{1,0:T(8,128)(2,1)S(1)} %collective-permute-done.5.refs_6_), channel_id=1, source_target_pairs={{0,4},{4,0},{8,12},{12,8},{16,20},{20,16},{24,28},{28,24},{1,5},{5... | collective-permute-start | bytes 516104 | tf_op jit(solution)/shard_map/ppermute | solution.py:72
  26.1 2.9 %collective-permute-start.16 = (bf16[96,1536]{1,0:T(8,128)(2,1)}, bf16[96,1536]{1,0:T(8,128)(2,1)S(1)}, u32[]{:S(2)}, u32[]{:S(2)}) collective-permute-start(bf16[96,1536]{1,0:T(8,128)(2,1)} %pad_maximum_fusion.refs_0_), channel_id=1, source_target_pairs={{0,16},{4,20},{8,24},{12,28},{16,0},{20,4},{24,8},{28,12},{1,17},{... | collective-permute-start | bytes 884744 | tf_op jit(solution)/shard_map/ppermute | solution.py:72
  29.1 5.6 %project.1 = (bf16[1536,768]{1,0:T(8,128)(2,1)}, bf16[1536,576]{1,0:T(8,128)(2,1)S(1)}, f32[8,768]{1,0:T(8,128)S(1)}, bf16[768,896]{1,0:T(8,128)(2,1)S(1)}, bf16[192,768]{1,0:T(8,128)(2,1)S(1)}) custom-call(s32[4]{0:T(128)S(1)} %pad_add_fusion.scalar_ref, bf16[96,896]{1,0:T(8,128)(2,1)S(1)} %pack.1.refs_0_, ...), custom_call_target="tpu_custom_call" | custom-call | flops 4400000 | tf_op jit(solution)/shard_map/project/pallas_call | solution.py:153
  34.7 1.9 collective-permute-start.8
  37.3 6.5 %attend_forward.2 = (bf16[192,1024]{1,0:T(8,128)(2,1)S(1)}, f32[4,8,256]{2,1,0:T(8,128)S(1)}) custom-call(s32[4]{0:T(128)S(1)} %pad_add_fusion.scalar_ref, bf16[1536,576]{1,0:T(8,128)(2,1)S(1)} %get-tuple-element.157.projected_ref.refs_0_), custom_call_target="tpu_custom_call" | custom-call | flops 1100000 | tf_op jit(solution)/shard_map/attend_forward/pallas_call | solution.py:257
  43.8 2.1 %collective-permute-start.18 = (bf16[96,1536]{1,0:T(8,128)(2,1)S(1)}, bf16[96,1536]{1,0:T(8,128)(2,1)S(1)}, u32[]{:S(2)}, u32[]{:S(2)}) collective-permute-start(bf16[96,1536]{1,0:T(8,128)(2,1)S(1)} %collective-permute-done.16.refs_4_), channel_id=1, source_target_pairs={{0,8},{4,12},{8,0},{12,4},{16,24},{20,28},{24,16},{28,20},{1,9},{5... | collective-permute-start | bytes 884744 | tf_op jit(solution)/shard_map/ppermute | solution.py:72
  46.2 2.1 %collective-permute-start.20 = (bf16[192,1024]{1,0:T(8,128)(2,1)S(1)}, bf16[192,1024]{1,0:T(8,128)(2,1)S(1)}, u32[]{:S(2)}, u32[]{:S(2)}) collective-permute-start(bf16[192,1024]{1,0:T(8,128)(2,1)S(1)} %get-tuple-element.111.refs_2_), channel_id=1, source_target_pairs={{0,2},{1,3},{2,0},{3,1},{4,6},{5,7},{6,4},{7,5},{8,10},{9,11},{10,... | collective-permute-start | bytes 1179656 | tf_op jit(solution)/shard_map/ppermute | solution.py:72
  48.4 1.6 collective-permute-start.17
  50.0 4.8 %attend_forward.3 = (bf16[192,512]{1,0:T(8,128)(2,1)S(1)}, f32[2,8,256]{2,1,0:T(8,128)S(1)}) custom-call(s32[4]{0:T(128)S(1)} %pad_add_fusion.scalar_ref, bf16[1536,576]{1,0:T(8,128)(2,1)S(1)} %get-tuple-element.157.projected_ref.refs_0_), custom_call_target="tpu_custom_call" | custom-call | flops 1100000 | tf_op jit(solution)/shard_map/attend_forward/pallas_call | solution.py:257
  55.3 3.3 %collective-permute-done.12.refs_7_ = bf16[192,768]{1,0:T(8,128)(2,1)S(1)} collective-permute-done((bf16[192,768]{1,0:T(8,128)(2,1)S(1)}, bf16[192,768]{1,0:T(8,128)(2,1)S(1)}, u32[]{:S(2)}, u32[]{:S(2)}) %collective-permute-start.12) | collective-permute-done | bytes 294944 | tf_op jit(solution)/shard_map/ppermute | solution.py:72
  58.6 1.7 collective-permute-start.9
  60.9 3.4 %collective-permute-done.9.refs_3_ = bf16[192,512]{1,0:T(8,128)(2,1)S(1)} collective-permute-done((bf16[192,512]{1,0:T(8,128)(2,1)S(1)}, bf16[192,512]{1,0:T(8,128)(2,1)S(1)}, u32[]{:S(2)}, u32[]{:S(2)}) %collective-permute-start.9) | collective-permute-done | bytes 196640 | tf_op jit(solution)/shard_map/ppermute | solution.py:72
  66.2 4.9 %feed_forward.4 = (bf16[512,768]{1,0:T(8,128)(2,1)S(1)}, f32[8,768]{1,0:T(8,128)S(1)}, bf16[1536,768]{1,0:T(8,128)(2,1)S(1)}, bf16[1536,768]{1,0:T(8,128)(2,1)S(1)}, bf16[1536,768]{1,0:T(8,128)(2,1)S(1)}) custom-call(s32[4]{0:T(128)S(1)} %pad_add_fusion.scalar_ref, bf16[1536,768]{1,0:T(8,128)(2,1)S(1)} %copy-done, bf16[1536,768]{1,0:T(8,128)(2,1)S(1)} %copy-done.1, ...), custom_call_target="tpu_custom_call" | custom-call | flops 563200 | tf_op jit(solution)/shard_map/feed_forward/pallas_call | solution.py:455
  71.3 2.9 %feed_forward.5 = (bf16[256,768]{1,0:T(8,128)(2,1)S(1)}, f32[8,768]{1,0:T(8,128)S(1)}, bf16[1536,768]{1,0:T(8,128)(2,1)S(1)}, bf16[1536,768]{1,0:T(8,128)(2,1)S(1)}, bf16[1536,768]{1,0:T(8,128)(2,1)S(1)}) custom-call(s32[4]{0:T(128)S(1)} %pad_add_fusion.scalar_ref, ...), custom_call_target="tpu_custom_call", output_to_operand_aliasing={{2}: (15, {}), {3}: (16, {}), {4}: (17, {})} | custom-call | flops 281600 | tf_op jit(solution)/shard_map/feed_forward/pallas_call | solution.py:455
  74.7 4.7 %feed_forward.6 = (bf16[512,768]{1,0:T(8,128)(2,1)S(1)}, f32[8,768]{1,0:T(8,128)S(1)}, bf16[1536,768]{1,0:T(8,128)(2,1)S(1)}, bf16[1536,768]{1,0:T(8,128)(2,1)S(...) custom-call(s32[4]{0:T(128)S(1)} %pad_add_fusion.scalar_ref, ...), custom_call_target="tpu_custom_call", output_to_operand_aliasing={{2}: (15, {}), {3}: (16, {}), {4}: (17, {})} | custom-call | flops 563200 | tf_op jit(solution)/shard_map/feed_forward/pallas_call | solution.py:455
  80.4 1.7 collective-permute-start.26
  82.1 4.0 %feed_forward.7 = (bf16[256,768]{1,0:T(8,128)(2,1)S(1)}, f32[8,768]{1,0:T(8,128)S(1)}, bf16[1536,768]{1,0:T(8,128)(2,1)S(1)}, bf16[1536,768]{1,0:T(8,128)(2,1)S(...) custom-call(s32[4]{0:T(128)S(1)} %pad_add_fusion.scalar_ref, ...), custom_call_target="tpu_custom_call", output_to_operand_aliasing={{2}: (15, {}), {3}: (16, {}), {4}: (17, {})} | custom-call | flops 281600 | tf_op jit(solution)/shard_map/feed_forward/pallas_call | solution.py:455
  87.3 9.6 %feed_forward_weights.1 = (bf16[768,768]{1,0:T(8,128)(2,1)}, bf16[768,768]{1,0:T(8,128)(2,1)}, bf16[768,1536]{1,0:T(8,128)(2,1)}) custom-call(s32[4]{0:T(128)S(1)} %pad_add_fusion.scalar_ref, bf16[1536,768]{1,0:T(8,128)(2,1)S(1)} %get-tuple-element.150.normed_ref, bf16[1536,768]{1,0:T(8,128)(2,1)S(1)} %get-tuple-element.151.upper_ref, ...), custom_call_target="tpu_custom_call" | custom-call | flops 1100000 | tf_op jit(solution)/shard_map/feed_forward_weights/pallas_call | solution.py:530
  96.9 5.6 %all-to-all-start = ((bf16[8,96,1536]{2,1,0:T(8,128)(2,1)}), bf16[8,96,1536]{2,1,0:T(8,128)(2,1)}, u32[]{:S(2)}, u32[]{:S(2)}) async-start(bf16[8,96,1536]{2,1,0:T(8,128)(2,1)} %bitcast.6), calls=%async_computation | async-start | bytes 4718592 | tf_op jit(solution)/shard_map/all_to_all | solution.py:811
  102.5 3.8 %second_norm_backward.2.refs_6_ = bf16[512,768]{1,0:T(8,128)(2,1)S(1)} custom-call(s32[4]{0:T(128)S(1)} %pad_add_fusion.scalar_ref, bf16[512,768]{1,0:T(8,128)(2,1)} %add_convert_fusion.1.mine_ref, bf16[512,768]{1,0:T(8,128)(2,1)} %collective-permute-done.26.other_ref, f32[512,768]{1,0:T(8,128)} %get-tuple-element.162.hidden_ref.refs_0_, ...), custom_call_target="tpu_custom_call" | custom-call | flops 1100000 | tf_op jit(solution)/shard_map/second_norm_backward/pallas_call | solution.py:597
  106.9 1.9 collective-permute-done.29.other_ref
  108.7 2.6 %second_norm_backward.3.refs_8_ = bf16[256,768]{1,0:T(8,128)(2,1)S(1)} custom-call(s32[4]{0:T(128)S(1)} %pad_add_fusion.scalar_ref, bf16[256,768]{1,0:T(8,128)(2,1)} %add_convert_fusion.4.mine_ref, bf16[256,768]{1,0:T(8,128)(2,1)} %collective-permute-done.29.other_ref, f32[256,768]{1,0:T(8,128)} %get-tuple-element.164.hidden_ref.refs_1_, ...), custom_call_target="tpu_custom_call" | custom-call | flops 44000002048 | tf_op jit(solution)/shard_map/second_norm_backward/pallas_call | solution.py:597
  111.7 1.7 collective-permute-start.27
  113.5 18.3 %attend_backward.1 = (bf16[576,1536]{1,0:T(8,128)(2,1)S(1)}, bf16[768,192]{1,0:T(8,128)(2,1)S(1)}, bf16[1536,768]{1,0:T(8,128)(2,1)S(1)}) custom-call(s32[4]{0:T(128)S(1)} %pad_add_fusion.scalar_ref, bf16[1536,576]{1,0:T(8,128)(2,1)S(1)} %copy-done.3, bf16[192,768]{1,0:T(8,128)(2,1)S(1)} %get-tuple-element.114.refs_6_.refs_1_, ...), custom_call_target="tpu_custom_call" | custom-call | flops 8800000 | tf_op jit(solution)/shard_map/attend_backward/pallas_call | solution.py:359
  131.8 2.3 %projection_weights.1 = (bf16[4,96,768]{2,1,0:T(8,128)(2,1)S(1)}, bf16[4,96,768]{2,1,0:T(8,128)(2,1)S(1)}) custom-call(s32[4]{0:T(128)S(1)} %pad_add_fusion.scalar_ref, bf16[576,1536]{1,0:T(8,128)(2,1)S(1)} %get-tuple-element.169.grads_ref, bf16[1536,768]{1,0:T(8,128)(2,1)S(1)} %copy-done.6, bf16[768,192]{1,0:T(8,128)(2,1)S(1)} %get-tuple-element.167.outs_ref), custom_call_target="tpu_custom_call" | custom-call | flops 1100000 | tf_op jit(solution)/shard_map/projection_weights/pallas_call | solution.py:667
  134.1 1.9 %grad_normed.2 = (bf16[768,768]{1,0:T(8,128)(2,1)S(1)}, f32[8,768]{1,0:T(8,128)S(1)}) custom-call(s32[4]{0:T(128)S(1)} %pad_add_fusion.scalar_ref, bf16[576,1536]{1,0:T(8,128)(2,1)S(1)} %get-tuple-element.169.grads_ref, bf16[1536,768]{1,0:T(8,128)(2,1)S(1)} %copy-done, bf16[768,896]{1,0:T(8,128)(2,1)S(1)} %copy-done.5, f32[8,768]{1,0:T(8,128)S(1)} %get-tuple-element.171.ahead_ref), custom_call_target="tpu_custom_call" | custom-call | flops 1100000 | tf_op jit(solution)/shard_map/grad_normed/pallas_call | solution.py:630
  136.3 2.0 %collective-permute-start.36 = (bf16[4,96,768]{2,1,0:T(8,128)(2,1)S(1)}, bf16[4,96,768]{2,1,0:T(8,128)(2,1)S(1)}, u32[]{:S(2)}, u32[]{:S(2)}) collective-permute-start(bf16[4,96,768]{2,1,0:T(8,128)(2,1)S(1)} %get-tuple-element.183), channel_id=1, source_target_pairs={{0,4},{4,0},{8,12},{12,8},{16,20},{20,16},{24,28},{28,24},{1,5},{5... | collective-permute-start | bytes 1769480 | tf_op jit(solution)/shard_map/ppermute | solution.py:72
  138.3 1.9 %grad_normed.3 = (bf16[768,768]{1,0:T(8,128)(2,1)S(1)}, f32[8,768]{1,0:T(8,128)S(1)}) custom-call(s32[4]{0:T(128)S(1)} %pad_add_fusion.scalar_ref, bf16[576,1536]{1,0:T(8,128)(2,1)S(1)} %get-tuple-element.169.grads_ref, bf16[1536,768]{1,0:T(8,128)(2,1)S(1)} %copy-done, bf16[768,896]{1,0:T(8,128)(2,1)S(1)} %copy-done.5, f32[8,768]{1,0:T(8,128)S(1)} %get-tuple-element.172.ahead_ref), custom_call_target="tpu_custom_call" | custom-call | flops 1100000 | tf_op jit(solution)/shard_map/grad_normed/pallas_call | solution.py:630
  140.5 1.7 collective-permute-start.34
  142.6 1.8 collective-permute-start.37
  144.4 3.9 %layer_out.1 = (bf16[384,768]{1,0:T(8,128)(2,1)}, bf16[384,768]{1,0:T(8,128)(2,1)}, bf16[1536,768]{1,0:T(8,128)(2,1)}) custom-call(s32[4]{0:T(128)S(1)} %pad_add_fusion.scalar_ref, bf16[768,768]{1,0:T(8,128)(2,1)S(1)} %add_convert_fusion.mine_ref, bf16[768,768]{1,0:T(8,128)(2,1)S(1)} %collective-permute-done.27.other_ref, ...), custom_call_target="tpu_custom_call" | custom-call | flops 1100000 | tf_op jit(solution)/shard_map/layer_out/pallas_call | solution.py:693
  148.3 8.5 %collective-permute-done.37.refs_1_ = f32[8,768]{1,0:T(8,128)S(1)} collective-permute-done((f32[8,768]{1,0:T(8,128)S(1)}, f32[8,768]{1,0:T(8,128)S(1)}, u32[]{:S(2)}, u32[]{:S(2)}) %collective-permute-start.37) | collective-permute-done | bytes 24608 | tf_op jit(solution)/shard_map/ppermute | solution.py:72
  158.4 3.9 %collective-permute-start.39 = (bf16[96,896]{1,0:T(8,128)(2,1)}, bf16[96,896]{1,0:T(8,128)(2,1)S(1)}, u32[]{:S(2)}, u32[]{:S(2)}) collective-permute-start(bf16[96,896]{1,0:T(8,128)(2,1)} %get-tuple-element.192), channel_id=1, source_target_pairs={{0,8},{4,12},{8,0},{12,4},{16,24},{20,28},{24,16},{28,20},{1,9},{5... | collective-permute-start | bytes 516104 | tf_op jit(solution)/shard_map/ppermute | solution.py:72
  162.5 2.2 %collective-permute-start.41 = (bf16[96,896]{1,0:T(8,128)(2,1)}, bf16[96,896]{1,0:T(8,128)(2,1)}, u32[]{:S(2)}, u32[]{:S(2)}) collective-permute-start(bf16[96,896]{1,0:T(8,128)(2,1)} %get-tuple-element.194), channel_id=1, source_target_pairs={{0,24},{4,28},{8,16},{12,20},{16,8},{20,12},{24,0},{28,4},{1,25},{... | collective-permute-start | bytes 516104 | tf_op jit(solution)/shard_map/ppermute | solution.py:72
  164.7 2.5 %first_norm_backward.2 = (bf16[384,768]{1,0:T(8,128)(2,1)}, bf16[1536,768]{1,0:T(8,128)(2,1)}) custom-call(s32[4]{0:T(128)S(1)} %pad_add_fusion.scalar_ref, bf16[384,768]{1,0:T(8,128)(2,1)S(1)} %get-tuple-element.179.mine_ref, bf16[384,768]{1,0:T(8,128)(2,1)S(1)} %collective-permute-done.34.other_ref, bf16[1536,768]{1,0:T(8,128)(2,1)S(1)} %copy-done, ...), custom_call_target="tpu_custom_call" | custom-call | flops 1100000 | tf_op jit(solution)/shard_map/first_norm_backward/pallas_call | solution.py:727
  168.5 2.5 %first_norm_backward.3 = (bf16[384,768]{1,0:T(8,128)(2,1)}, bf16[1536,768]{1,0:T(8,128)(2,1)}) custom-call(s32[4]{0:T(128)S(1)} %pad_add_fusion.scalar_ref, bf16[384,768]{1,0:T(8,128)(2,1)S(1)} %get-tuple-element.186.mine_ref, bf16[384,768]{1,0:T(8,128)(2,1)S(1)} %collective-permute-done.38.other_ref, ...), custom_call_target="tpu_custom_call", output_to_operand_aliasing={{1}: (6, {})} | custom-call | flops 1100000 | tf_op jit(solution)/shard_map/first_norm_backward/pallas_call | solution.py:727
  171.0 2.8 %total.3 = (f32[96,768]{1,0:T(8,128)}, f32[96,768]{1,0:T(8,128)}) custom-call(bf16[8,96,1536]{2,1,0:T(8,128)(2,1)} %all-to-all-done.refs_0_), custom_call_target="tpu_custom_call" | custom-call | flops 1100000 | tf_op jit(solution)/shard_map/total/pallas_call | solution.py:796
  174.3 3.9 %collective-permute-done.40.refs_2_ = bf16[96,896]{1,0:T(8,128)(2,1)S(1)} collective-permute-done((bf16[96,896]{1,0:T(8,128)(2,1)}, bf16[96,896]{1,0:T(8,128)(2,1)S(1)}, u32[]{:S(2)}, u32[]{:S(2)}) %collective-permute-start.40) | collective-permute-done | bytes 172064 | tf_op jit(solution)/shard_map/ppermute | solution.py:72
  180.5 1.8 total.5
  182.9 3.1 %place.1 = (bf16[1536,768]{1,0:T(8,128)(2,1)}, bf16[1536,768]{1,0:T(8,128)(2,1)}) custom-call(s32[4]{0:T(128)S(1)} %pad_add_fusion.scalar_ref, bf16[384,768]{1,0:T(8,128)(2,1)S(1)} %collective-permute-done.32.refs_0_, bf16[384,768]{1,0:T(8,128)(2,1)} %collective-permute-done.33.refs_1_, ...), custom_call_target="tpu_custom_call", output_to_operand_aliasing={{0}: (5, {}), {1}: (6, {})} | custom-call | flops 1100000 | tf_op jit(solution)/shard_map/place/pallas_call | solution.py:760
  (104 shorter events, 20.0 us)
Async XLA Ops:
  1.7 11.0 %collective-permute-start.1 = (bf16[96,896]{1,0:T(8,128)(2,1)S(1)}, bf16[96,896]{1,0:T(8,128)(2,1)S(1)}, u32[]{:S(2)}, u32[]{:S(2)}) collective-permute-start(bf16[96,896]{1,0:T(8,128)(2,1)S(1)} %pack.1.refs_0_), channel_id=1, source_target_pairs={{0,8},{4,12},{8,0},{12,4},{16,24},{20,28},{24,16},{28,20},{1,9},{5... | collective-permute-start | bytes 516104 | tf_op jit(solution)/shard_map/ppermute | solution.py:72
  4.8 12.1 %collective-permute-start.3 = (bf16[96,896]{1,0:T(8,128)(2,1)S(1)}, bf16[96,896]{1,0:T(8,128)(2,1)S(1)}, u32[]{:S(2)}, u32[]{:S(2)}) collective-permute-start(bf16[96,896]{1,0:T(8,128)(2,1)S(1)} %pack.1.refs_0_), channel_id=1, source_target_pairs={{0,16},{4,20},{8,24},{12,28},{16,0},{20,4},{24,8},{28,12},{1,17},{... | collective-permute-start | bytes 516104 | tf_op jit(solution)/shard_map/ppermute | solution.py:72
  7.4 9.5 %collective-permute-start = (bf16[96,896]{1,0:T(8,128)(2,1)S(1)}, bf16[96,896]{1,0:T(8,128)(2,1)S(1)}, u32[]{:S(2)}, u32[]{:S(2)}) collective-permute-start(bf16[96,896]{1,0:T(8,128)(2,1)S(1)} %pack.1.refs_0_), channel_id=1, source_target_pairs={{0,4},{4,0},{8,12},{12,8},{16,20},{20,16},{24,28},{28,24},{1,5},{5... | collective-permute-start | bytes 516104 | tf_op jit(solution)/shard_map/ppermute | solution.py:72
  12.8 5.4 %collective-permute-start.2 = (bf16[96,896]{1,0:T(8,128)(2,1)S(1)}, bf16[96,896]{1,0:T(8,128)(2,1)S(1)}, u32[]{:S(2)}, u32[]{:S(2)}) collective-permute-start(bf16[96,896]{1,0:T(8,128)(2,1)S(1)} %collective-permute-done.1.refs_2_), channel_id=1, source_target_pairs={{0,4},{4,0},{8,12},{12,8},{16,20},{20,16},{24,28},{28,24},{1,5},{5... | collective-permute-start | bytes 516104 | tf_op jit(solution)/shard_map/ppermute | solution.py:72
  14.4 7.3 %collective-permute-start.5 = (bf16[96,896]{1,0:T(8,128)(2,1)S(1)}, bf16[96,896]{1,0:T(8,128)(2,1)S(1)}, u32[]{:S(2)}, u32[]{:S(2)}) collective-permute-start(bf16[96,896]{1,0:T(8,128)(2,1)S(1)} %pack.1.refs_0_), channel_id=1, source_target_pairs={{0,24},{4,28},{8,16},{12,20},{16,8},{20,12},{24,0},{28,4},{1,25},{... | collective-permute-start | bytes 516104 | tf_op jit(solution)/shard_map/ppermute | solution.py:72
  18.2 5.4 %collective-permute-start.4 = (bf16[96,896]{1,0:T(8,128)(2,1)S(1)}, bf16[96,896]{1,0:T(8,128)(2,1)S(1)}, u32[]{:S(2)}, u32[]{:S(2)}) collective-permute-start(bf16[96,896]{1,0:T(8,128)(2,1)S(1)} %collective-permute-done.3.refs_4_), channel_id=1, source_target_pairs={{0,4},{4,0},{8,12},{12,8},{16,20},{20,16},{24,28},{28,24},{1,5},{5... | collective-permute-start | bytes 516104 | tf_op jit(solution)/shard_map/ppermute | solution.py:72
  23.6 11.1 %collective-permute-start.7 = (bf16[96,1536]{1,0:T(8,128)(2,1)}, bf16[96,1536]{1,0:T(8,128)(2,1)S(1)}, u32[]{:S(2)}, u32[]{:S(2)}) collective-permute-start(bf16[96,1536]{1,0:T(8,128)(2,1)} %pad_maximum_fusion.refs_0_), channel_id=1, source_target_pairs={{0,8},{4,12},{8,0},{12,4},{16,24},{20,28},{24,16},{28,20},{1,9},{5... | collective-permute-start | bytes 884744 | tf_op jit(solution)/shard_map/ppermute | solution.py:72
  23.6 5.5 %collective-permute-start.6 = (bf16[96,896]{1,0:T(8,128)(2,1)S(1)}, bf16[96,896]{1,0:T(8,128)(2,1)S(1)}, u32[]{:S(2)}, u32[]{:S(2)}) collective-permute-start(bf16[96,896]{1,0:T(8,128)(2,1)S(1)} %collective-permute-done.5.refs_6_), channel_id=1, source_target_pairs={{0,4},{4,0},{8,12},{12,8},{16,20},{20,16},{24,28},{28,24},{1,5},{5... | collective-permute-start | bytes 516104 | tf_op jit(solution)/shard_map/ppermute | solution.py:72
  26.1 17.7 %collective-permute-start.16 = (bf16[96,1536]{1,0:T(8,128)(2,1)}, bf16[96,1536]{1,0:T(8,128)(2,1)S(1)}, u32[]{:S(2)}, u32[]{:S(2)}) collective-permute-start(bf16[96,1536]{1,0:T(8,128)(2,1)} %pad_maximum_fusion.refs_0_), channel_id=1, source_target_pairs={{0,16},{4,20},{8,24},{12,28},{16,0},{20,4},{24,8},{28,12},{1,17},{... | collective-permute-start | bytes 884744 | tf_op jit(solution)/shard_map/ppermute | solution.py:72
  34.7 13.7 %collective-permute-start.8 = (bf16[96,1536]{1,0:T(8,128)(2,1)S(1)}, bf16[96,1536]{1,0:T(8,128)(2,1)S(1)}, u32[]{:S(2)}, u32[]{:S(2)}) collective-permute-start(bf16[96,1536]{1,0:T(8,128)(2,1)S(1)} %collective-permute-done.7.refs_2_), channel_id=1, source_target_pairs={{0,4},{4,0},{8,12},{12,8},{16,20},{20,16},{24,28},{28,24},{1,5},{5... | collective-permute-start | bytes 884744 | tf_op jit(solution)/shard_map/ppermute | solution.py:72
  37.3 27.5 %copy-start.8 = (bf16[96,1536]{1,0:T(8,128)(2,1)S(1)}, bf16[96,1536]{1,0:T(8,128)(2,1)}, u32[]{:S(2)}) copy-start(bf16[96,1536]{1,0:T(8,128)(2,1)} %copy-done.7) | copy-start | bytes 884740
  37.3 28.9 %copy-start.1 = (bf16[1536,768]{1,0:T(8,128)(2,1)S(1)}, bf16[1536,768]{1,0:T(8,128)(2,1)}, u32[]{:S(2)}) copy-start(bf16[1536,768]{1,0:T(8,128)(2,1)} %grad_ref.5) | copy-start | bytes 7077892
  43.8 10.9 %collective-permute-start.18 = (bf16[96,1536]{1,0:T(8,128)(2,1)S(1)}, bf16[96,1536]{1,0:T(8,128)(2,1)S(1)}, u32[]{:S(2)}, u32[]{:S(2)}) collective-permute-start(bf16[96,1536]{1,0:T(8,128)(2,1)S(1)} %collective-permute-done.16.refs_4_), channel_id=1, source_target_pairs={{0,8},{4,12},{8,0},{12,4},{16,24},{20,28},{24,16},{28,20},{1,9},{5... | collective-permute-start | bytes 884744 | tf_op jit(solution)/shard_map/ppermute | solution.py:72
  45.9 9.4 %collective-permute-start.15 = (bf16[96,1536]{1,0:T(8,128)(2,1)}, bf16[96,1536]{1,0:T(8,128)(2,1)S(1)}, u32[]{:S(2)}, u32[]{:S(2)}) collective-permute-start(bf16[96,1536]{1,0:T(8,128)(2,1)} %pad_maximum_fusion.refs_0_), channel_id=1, source_target_pairs={{0,4},{4,0},{8,12},{12,8},{16,20},{20,16},{24,28},{28,24},{1,5},{5... | collective-permute-start | bytes 884744 | tf_op jit(solution)/shard_map/ppermute | solution.py:72
  46.2 14.0 %collective-permute-start.20 = (bf16[192,1024]{1,0:T(8,128)(2,1)S(1)}, bf16[192,1024]{1,0:T(8,128)(2,1)S(1)}, u32[]{:S(2)}, u32[]{:S(2)}) collective-permute-start(bf16[192,1024]{1,0:T(8,128)(2,1)S(1)} %get-tuple-element.111.refs_2_), channel_id=1, source_target_pairs={{0,2},{1,3},{2,0},{3,1},{4,6},{5,7},{6,4},{7,5},{8,10},{9,11},{10,... | collective-permute-start | bytes 1179656 | tf_op jit(solution)/shard_map/ppermute | solution.py:72
  48.3 10.3 %collective-permute-start.12 = (bf16[192,768]{1,0:T(8,128)(2,1)S(1)}, bf16[192,768]{1,0:T(8,128)(2,1)S(1)}, u32[]{:S(2)}, u32[]{:S(2)}) collective-permute-start(bf16[192,768]{1,0:T(8,128)(2,1)S(1)} %get-tuple-element.114.refs_6_.refs_1_), channel_id=1, source_target_pairs={{0,2},{1,3},{2,0},{3,1},{4,6},{5,7},{6,4},{7,5},{8,10},{9,11},{10,... | collective-permute-start | bytes 884744 | tf_op jit(solution)/shard_map/ppermute | solution.py:72
  48.4 11.9 %collective-permute-start.17 = (bf16[96,1536]{1,0:T(8,128)(2,1)S(1)}, bf16[96,1536]{1,0:T(8,128)(2,1)S(1)}, u32[]{:S(2)}, u32[]{:S(2)}) collective-permute-start(bf16[96,1536]{1,0:T(8,128)(2,1)S(1)} %collective-permute-done.16.refs_4_), channel_id=1, source_target_pairs={{0,4},{4,0},{8,12},{12,8},{16,20},{20,16},{24,28},{28,24},{1,5},{5... | collective-permute-start | bytes 884744 | tf_op jit(solution)/shard_map/ppermute | solution.py:72
  54.8 9.5 %collective-permute-start.19 = (bf16[96,1536]{1,0:T(8,128)(2,1)S(1)}, bf16[96,1536]{1,0:T(8,128)(2,1)S(1)}, u32[]{:S(2)}, u32[]{:S(2)}) collective-permute-start(bf16[96,1536]{1,0:T(8,128)(2,1)S(1)} %collective-permute-done.18.refs_6_), channel_id=1, source_target_pairs={{0,4},{4,0},{8,12},{12,8},{16,20},{20,16},{24,28},{28,24},{1,5},{5... | collective-permute-start | bytes 884744 | tf_op jit(solution)/shard_map/ppermute | solution.py:72
  55.3 5.5 %collective-permute-start.10 = (bf16[192,512]{1,0:T(8,128)(2,1)S(1)}, bf16[192,512]{1,0:T(8,128)(2,1)S(1)}, u32[]{:S(2)}, u32[]{:S(2)}) collective-permute-start(bf16[192,512]{1,0:T(8,128)(2,1)S(1)} %get-tuple-element.117.refs_2_.refs_3_), channel_id=1, source_target_pairs={{0,1},{1,0},{2,3},{3,2},{4,5},{5,4},{6,7},{7,6},{8,9},{9,8},{10,11... | collective-permute-start | bytes 589832 | tf_op jit(solution)/shard_map/ppermute | solution.py:72
  58.6 5.7 %collective-permute-start.9 = (bf16[192,512]{1,0:T(8,128)(2,1)S(1)}, bf16[192,512]{1,0:T(8,128)(2,1)S(1)}, u32[]{:S(2)}, u32[]{:S(2)}) collective-permute-start(bf16[192,512]{1,0:T(8,128)(2,1)S(1)} %get-tuple-element.117.refs_2_.refs_3_), channel_id=1, source_target_pairs={{0,2},{1,3},{2,0},{3,1},{4,6},{5,7},{6,4},{7,5},{8,10},{9,11},{10,... | collective-permute-start | bytes 589832 | tf_op jit(solution)/shard_map/ppermute | solution.py:72
  60.3 5.9 %collective-permute-start.21 = (bf16[192,1024]{1,0:T(8,128)(2,1)S(1)}, bf16[192,1024]{1,0:T(8,128)(2,1)S(1)}, u32[]{:S(2)}, u32[]{:S(2)}) collective-permute-start(bf16[192,1024]{1,0:T(8,128)(2,1)S(1)} %get-tuple-element.111.refs_2_), channel_id=1, source_target_pairs={{0,1},{1,0},{2,3},{3,2},{4,5},{5,4},{6,7},{7,6},{8,9},{9,8},{10,11... | collective-permute-start | bytes 1179656 | tf_op jit(solution)/shard_map/ppermute | solution.py:72
  60.3 5.9 %collective-permute-start.22 = (bf16[192,1024]{1,0:T(8,128)(2,1)S(1)}, bf16[192,1024]{1,0:T(8,128)(2,1)S(1)}, u32[]{:S(2)}, u32[]{:S(2)}) collective-permute-start(bf16[192,1024]{1,0:T(8,128)(2,1)S(1)} %collective-permute-done.20.refs_3_), channel_id=1, source_target_pairs={{0,1},{1,0},{2,3},{3,2},{4,5},{5,4},{6,7},{7,6},{8,9},{9,8},{10,11... | collective-permute-start | bytes 1179656 | tf_op jit(solution)/shard_map/ppermute | solution.py:72
  60.8 5.4 %collective-permute-start.13 = (bf16[192,768]{1,0:T(8,128)(2,1)S(1)}, bf16[192,768]{1,0:T(8,128)(2,1)S(1)}, u32[]{:S(2)}, u32[]{:S(2)}) collective-permute-start(bf16[192,768]{1,0:T(8,128)(2,1)S(1)} %get-tuple-element.114.refs_6_.refs_1_), channel_id=1, source_target_pairs={{0,1},{1,0},{2,3},{3,2},{4,5},{5,4},{6,7},{7,6},{8,9},{9,8},{10,11... | collective-permute-start | bytes 884744 | tf_op jit(solution)/shard_map/ppermute | solution.py:72
  64.3 1.9 %collective-permute-start.14 = (bf16[192,768]{1,0:T(8,128)(2,1)S(1)}, bf16[192,768]{1,0:T(8,128)(2,1)S(1)}, u32[]{:S(2)}, u32[]{:S(2)}) collective-permute-start(bf16[192,768]{1,0:T(8,128)(2,1)S(1)} %collective-permute-done.12.refs_7_), channel_id=1, source_target_pairs={{0,1},{1,0},{2,3},{3,2},{4,5},{5,4},{6,7},{7,6},{8,9},{9,8},{10,11... | collective-permute-start | bytes 884744 | tf_op jit(solution)/shard_map/ppermute | solution.py:72
  64.3 1.9 collective-permute-start.11
  71.1 8.2 %collective-permute-start.23 = (bf16[512,768]{1,0:T(8,128)(2,1)S(1)}, bf16[512,768]{1,0:T(8,128)(2,1)S(1)}, u32[]{:S(2)}, u32[]{:S(2)}) collective-permute-start(bf16[512,768]{1,0:T(8,128)(2,1)S(1)} %get-tuple-element.141), channel_id=1, source_target_pairs={{0,1},{1,0},{2,3},{3,2},{4,5},{5,4},{6,7},{7,6},{8,9},{9,8},{10,11... | collective-permute-start | bytes 2359304 | tf_op jit(solution)/shard_map/ppermute | solution.py:72
  74.2 11.8 %collective-permute-start.24 = (bf16[256,768]{1,0:T(8,128)(2,1)S(1)}, bf16[256,768]{1,0:T(8,128)(2,1)S(1)}, u32[]{:S(2)}, u32[]{:S(2)}) collective-permute-start(bf16[256,768]{1,0:T(8,128)(2,1)S(1)} %get-tuple-element.149), channel_id=1, source_target_pairs={{0,1},{1,0},{2,3},{3,2},{4,5},{5,4},{6,7},{7,6},{8,9},{9,8},{10,11... | collective-permute-start | bytes 1179656 | tf_op jit(solution)/shard_map/ppermute | solution.py:72
  80.4 22.1 %collective-permute-start.26 = (bf16[512,768]{1,0:T(8,128)(2,1)}, bf16[512,768]{1,0:T(8,128)(2,1)}, u32[]{:S(2)}, u32[]{:S(2)}) collective-permute-start(bf16[512,768]{1,0:T(8,128)(2,1)} %add_convert_fusion.1.mine_ref), channel_id=1, source_target_pairs={{0,2},{1,3},{2,0},{3,1},{4,6},{5,7},{6,4},{7,5},{8,10},{9,11},{10,... | collective-permute-start | bytes 2359304 | tf_op jit(solution)/shard_map/ppermute | solution.py:72
  86.9 21.8 %collective-permute-start.29 = (bf16[256,768]{1,0:T(8,128)(2,1)}, bf16[256,768]{1,0:T(8,128)(2,1)}, u32[]{:S(2)}, u32[]{:S(2)}) collective-permute-start(bf16[256,768]{1,0:T(8,128)(2,1)} %add_convert_fusion.4.mine_ref), channel_id=1, source_target_pairs={{0,2},{1,3},{2,0},{3,1},{4,6},{5,7},{6,4},{7,5},{8,10},{9,11},{10,... | collective-permute-start | bytes 1179656 | tf_op jit(solution)/shard_map/ppermute | solution.py:72
  96.9 74.1 %all-to-all-start = ((bf16[8,96,1536]{2,1,0:T(8,128)(2,1)}), bf16[8,96,1536]{2,1,0:T(8,128)(2,1)}, u32[]{:S(2)}, u32[]{:S(2)}) async-start(bf16[8,96,1536]{2,1,0:T(8,128)(2,1)} %bitcast.6), calls=%async_computation | async-start | bytes 4718592 | tf_op jit(solution)/shard_map/all_to_all | solution.py:811
  102.5 8.9 %collective-permute-start.25 = (bf16[768,768]{1,0:T(8,128)(2,1)}, bf16[768,768]{1,0:T(8,128)(2,1)S(1)}, u32[]{:S(2)}, u32[]{:S(2)}) collective-permute-start(bf16[768,768]{1,0:T(8,128)(2,1)} %get-tuple-element.154), channel_id=1, source_target_pairs={{0,1},{1,0},{2,3},{3,2},{4,5},{5,4},{6,7},{7,6},{8,9},{9,8},{10,11... | collective-permute-start | bytes 3538952 | tf_op jit(solution)/shard_map/ppermute | solution.py:72
  106.3 7.2 %collective-permute-start.28 = (bf16[512,768]{1,0:T(8,128)(2,1)S(1)}, bf16[512,768]{1,0:T(8,128)(2,1)S(1)}, u32[]{:S(2)}, u32[]{:S(2)}) collective-permute-start(bf16[512,768]{1,0:T(8,128)(2,1)S(1)} %second_norm_backward.2.refs_6_), channel_id=1, source_target_pairs={{0,1},{1,0},{2,3},{3,2},{4,5},{5,4},{6,7},{7,6},{8,9},{9,8},{10,11... | collective-permute-start | bytes 2359304 | tf_op jit(solution)/shard_map/ppermute | solution.py:72
  111.3 2.1 %collective-permute-start.30 = (bf16[256,768]{1,0:T(8,128)(2,1)S(1)}, bf16[256,768]{1,0:T(8,128)(2,1)S(1)}, u32[]{:S(2)}, u32[]{:S(2)}) collective-permute-start(bf16[256,768]{1,0:T(8,128)(2,1)S(1)} %second_norm_backward.3.refs_8_), channel_id=1, source_target_pairs={{0,1},{1,0},{2,3},{3,2},{4,5},{5,4},{6,7},{7,6},{8,9},{9,8},{10,11... | collective-permute-start | bytes 1179656 | tf_op jit(solution)/shard_map/ppermute | solution.py:72
  111.7 28.5 %collective-permute-start.27 = (bf16[768,768]{1,0:T(8,128)(2,1)S(1)}, bf16[768,768]{1,0:T(8,128)(2,1)S(1)}, u32[]{:S(2)}, u32[]{:S(2)}) collective-permute-start(bf16[768,768]{1,0:T(8,128)(2,1)S(1)} %add_convert_fusion.mine_ref), channel_id=1, source_target_pairs={{0,2},{1,3},{2,0},{3,1},{4,6},{5,7},{6,4},{7,5},{8,10},{9,11},{10,... | collective-permute-start | bytes 3538952 | tf_op jit(solution)/shard_map/ppermute | solution.py:72
  136.1 4.2 %collective-permute-start.31 = (bf16[768,768]{1,0:T(8,128)(2,1)S(1)}, bf16[768,768]{1,0:T(8,128)(2,1)S(1)}, u32[]{:S(2)}, u32[]{:S(2)}) collective-permute-start(bf16[768,768]{1,0:T(8,128)(2,1)S(1)} %get-tuple-element.175), channel_id=1, source_target_pairs={{0,1},{1,0},{2,3},{3,2},{4,5},{5,4},{6,7},{7,6},{8,9},{9,8},{10,11... | collective-permute-start | bytes 3538952 | tf_op jit(solution)/shard_map/ppermute | solution.py:72
  136.3 20.5 %collective-permute-start.36 = (bf16[4,96,768]{2,1,0:T(8,128)(2,1)S(1)}, bf16[4,96,768]{2,1,0:T(8,128)(2,1)S(1)}, u32[]{:S(2)}, u32[]{:S(2)}) collective-permute-start(bf16[4,96,768]{2,1,0:T(8,128)(2,1)S(1)} %get-tuple-element.183), channel_id=1, source_target_pairs={{0,4},{4,0},{8,12},{12,8},{16,20},{20,16},{24,28},{28,24},{1,5},{5... | collective-permute-start | bytes 1769480 | tf_op jit(solution)/shard_map/ppermute | solution.py:72
  140.5 24.2 %collective-permute-start.34 = (bf16[384,768]{1,0:T(8,128)(2,1)S(1)}, bf16[384,768]{1,0:T(8,128)(2,1)S(1)}, u32[]{:S(2)}, u32[]{:S(2)}) collective-permute-start(bf16[384,768]{1,0:T(8,128)(2,1)S(1)} %get-tuple-element.179.mine_ref), channel_id=1, source_target_pairs={{0,2},{1,3},{2,0},{3,1},{4,6},{5,7},{6,4},{7,5},{8,10},{9,11},{10,... | collective-permute-start | bytes 1769480 | tf_op jit(solution)/shard_map/ppermute | solution.py:72
  142.2 26.3 %collective-permute-start.38 = (bf16[384,768]{1,0:T(8,128)(2,1)S(1)}, bf16[384,768]{1,0:T(8,128)(2,1)S(1)}, u32[]{:S(2)}, u32[]{:S(2)}) collective-permute-start(bf16[384,768]{1,0:T(8,128)(2,1)S(1)} %get-tuple-element.186.mine_ref), channel_id=1, source_target_pairs={{0,2},{1,3},{2,0},{3,1},{4,6},{5,7},{6,4},{7,5},{8,10},{9,11},{10,... | collective-permute-start | bytes 1769480 | tf_op jit(solution)/shard_map/ppermute | solution.py:72
  142.6 14.2 %collective-permute-start.37 = (f32[8,768]{1,0:T(8,128)S(1)}, f32[8,768]{1,0:T(8,128)S(1)}, u32[]{:S(2)}, u32[]{:S(2)}) collective-permute-start(f32[8,768]{1,0:T(8,128)S(1)} %get-tuple-element.184.refs_0_), channel_id=1, source_target_pairs={{0,4},{4,0},{8,12},{12,8},{16,20},{20,16},{24,28},{28,24},{1,5},{5... | collective-permute-start | bytes 73736 | tf_op jit(solution)/shard_map/ppermute | solution.py:72
  158.4 15.3 %collective-permute-start.39 = (bf16[96,896]{1,0:T(8,128)(2,1)}, bf16[96,896]{1,0:T(8,128)(2,1)S(1)}, u32[]{:S(2)}, u32[]{:S(2)}) collective-permute-start(bf16[96,896]{1,0:T(8,128)(2,1)} %get-tuple-element.192), channel_id=1, source_target_pairs={{0,8},{4,12},{8,0},{12,4},{16,24},{20,28},{24,16},{28,20},{1,9},{5... | collective-permute-start | bytes 516104 | tf_op jit(solution)/shard_map/ppermute | solution.py:72
  162.3 15.8 %collective-permute-start.40 = (bf16[96,896]{1,0:T(8,128)(2,1)}, bf16[96,896]{1,0:T(8,128)(2,1)S(1)}, u32[]{:S(2)}, u32[]{:S(2)}) collective-permute-start(bf16[96,896]{1,0:T(8,128)(2,1)} %get-tuple-element.193), channel_id=1, source_target_pairs={{0,16},{4,20},{8,24},{12,28},{16,0},{20,4},{24,8},{28,12},{1,17},{... | collective-permute-start | bytes 516104 | tf_op jit(solution)/shard_map/ppermute | solution.py:72
  162.5 15.6 %collective-permute-start.41 = (bf16[96,896]{1,0:T(8,128)(2,1)}, bf16[96,896]{1,0:T(8,128)(2,1)}, u32[]{:S(2)}, u32[]{:S(2)}) collective-permute-start(bf16[96,896]{1,0:T(8,128)(2,1)} %get-tuple-element.194), channel_id=1, source_target_pairs={{0,24},{4,28},{8,16},{12,20},{16,8},{20,12},{24,0},{28,4},{1,25},{... | collective-permute-start | bytes 516104 | tf_op jit(solution)/shard_map/ppermute | solution.py:72
  164.7 18.1 %collective-permute-start.32 = (bf16[384,768]{1,0:T(8,128)(2,1)}, bf16[384,768]{1,0:T(8,128)(2,1)S(1)}, u32[]{:S(2)}, u32[]{:S(2)}) collective-permute-start(bf16[384,768]{1,0:T(8,128)(2,1)} %get-tuple-element.177), channel_id=1, source_target_pairs={{0,1},{1,0},{2,3},{3,2},{4,5},{5,4},{6,7},{7,6},{8,9},{9,8},{10,11... | collective-permute-start | bytes 1769480 | tf_op jit(solution)/shard_map/ppermute | solution.py:72
  168.5 14.3 %collective-permute-start.33 = (bf16[384,768]{1,0:T(8,128)(2,1)}, bf16[384,768]{1,0:T(8,128)(2,1)}, u32[]{:S(2)}, u32[]{:S(2)}) collective-permute-start(bf16[384,768]{1,0:T(8,128)(2,1)} %get-tuple-element.178), channel_id=1, source_target_pairs={{0,1},{1,0},{2,3},{3,2},{4,5},{5,4},{6,7},{7,6},{8,9},{9,8},{10,11... | collective-permute-start | bytes 1769480 | tf_op jit(solution)/shard_map/ppermute | solution.py:72
  173.7 9.1 %collective-permute-start.43 = (bf16[384,768]{1,0:T(8,128)(2,1)S(1)}, bf16[384,768]{1,0:T(8,128)(2,1)S(1)}, u32[]{:S(2)}, u32[]{:S(2)}) collective-permute-start(bf16[384,768]{1,0:T(8,128)(2,1)S(1)} %copy-done.10), channel_id=1, source_target_pairs={{0,1},{1,0},{2,3},{3,2},{4,5},{5,4},{6,7},{7,6},{8,9},{9,8},{10,11... | collective-permute-start | bytes 1769480 | tf_op jit(solution)/shard_map/ppermute | solution.py:72
  178.1 4.7 %collective-permute-start.35 = (bf16[384,768]{1,0:T(8,128)(2,1)S(1)}, bf16[384,768]{1,0:T(8,128)(2,1)S(1)}, u32[]{:S(2)}, u32[]{:S(2)}) collective-permute-start(bf16[384,768]{1,0:T(8,128)(2,1)S(1)} %copy-done.11), channel_id=1, source_target_pairs={{0,1},{1,0},{2,3},{3,2},{4,5},{5,4},{6,7},{7,6},{8,9},{9,8},{10,11... | collective-permute-start | bytes 1769480 | tf_op jit(solution)/shard_map/ppermute | solution.py:72
  179.2 3.7 %collective-permute-start.42 = (f32[8,96]{1,0:T(8,128)S(1)}, f32[8,96]{1,0:T(8,128)S(1)}, u32[]{:S(2)}, u32[]{:S(2)}) collective-permute-start(f32[8,96]{1,0:T(8,128)S(1)} %slice.38), channel_id=1, source_target_pairs={{0,2},{1,3},{2,0},{3,1},{4,6},{5,7},{6,4},{7,5},{8,10},{9,11},{10,... | collective-permute-start | bytes 9224 | tf_op jit(solution)/shard_map/ppermute | solution.py:72
  182.8 3.2 %collective-permute-start.44 = (f32[8,96]{1,0:T(8,128)S(1)}, f32[8,96]{1,0:T(8,128)S(1)}, u32[]{:S(2)}, u32[]{:S(2)}) collective-permute-start(f32[8,96]{1,0:T(8,128)S(1)} %slice_add_fusion), channel_id=1, source_target_pairs={{0,1},{1,0},{2,3},{3,2},{4,5},{5,4},{6,7},{7,6},{8,9},{9,8},{10,11... | collective-permute-start | bytes 9224 | tf_op jit(solution)/shard_map/ppermute | solution.py:72
  (10 other events, 98.7 us)

commit v6 on v5

--- a/solution.py
+++ b/solution.py
@@ -315,35 +315,31 @@
             cols = slice(h * HD, (h + 1) * HD)
             k = projected_ref[here, width + h * HD : width + (h + 1) * HD]
             v = projected_ref[here, 2 * width + h * HD : 2 * width + (h + 1) * HD]
-            dk = jnp.zeros((BLOCK, HD), WIDE)
-            dv = jnp.zeros((BLOCK, HD), WIDE)
-            for part in (here, later):
-                span = part.stop - part.start
-                if span == 0:
-                    continue
-                q = projected_ref[part, cols]
-                g = grad_mixed[part, cols]
-                scores = outer_cols(k, q)
-                grad_weights = outer_cols(v, g)
-                reach = jnp.abs(scores) * factor - logs[h : h + 1, part]
-                if part is here:
-                    key = lax.broadcasted_iota(jnp.int32, (BLOCK, span), 0) + j * BLOCK
-                    row = lax.broadcasted_iota(jnp.int32, (1, span), 1) + j * BLOCK
-                    reach = jnp.where(key <= jnp.minimum(row, length - 1), reach, FAR)
-                elif (j + 1) * BLOCK > sure:
-                    key = lax.broadcasted_iota(jnp.int32, (BLOCK, 1), 0) + j * BLOCK
-                    reach = jnp.where(key < length, reach, FAR)
-                sign = sign_of(scores)
-                weights = jnp.exp2(reach)
-                signed = sign.astype(WIDE)
-                raw = (weights * (grad_weights - signed * delta[h : h + 1, part])).astype(LOW) * (sign * sign)
-                dv = dv + multiply(weights.astype(LOW) * sign, g)
-                dk = dk + multiply(raw, q)
-                more = inner_rows(k, raw)
-                if j == 0:
-                    dq_turned[cols, part] = more
-                else:
-                    dq_turned[cols, part] += more
+            part = slice(j * BLOCK, rows)
+            q = projected_ref[part, cols]
+            g = grad_mixed[part, cols]
+            scores = outer_cols(k, q)
+            grad_weights = outer_cols(v, g)
+            reach = jnp.abs(scores) * factor - logs[h : h + 1, part]
+            key = lax.broadcasted_iota(jnp.int32, (BLOCK, 1), 0) + j * BLOCK
+            row = lax.broadcasted_iota(jnp.int32, (1, BLOCK), 1) + j * BLOCK
+            near = jnp.where(key <= jnp.minimum(row, length - 1), reach[:, :BLOCK], FAR)
+            if part.stop > (j + 1) * BLOCK:
+                past = reach[:, BLOCK:]
+                if (j + 1) * BLOCK > sure:
+                    past = jnp.where(key < length, past, FAR)
+                near = jnp.concatenate([near, past], axis=1)
+            sign = sign_of(scores)
+            weights = jnp.exp2(near)
+            signed = sign.astype(WIDE)
+            raw = (weights * (grad_weights - signed * delta[h : h + 1, part])).astype(LOW) * (sign * sign)
+            dv = multiply(weights.astype(LOW) * sign, g)
+            dk = multiply(raw, q)
+            more = inner_rows(k, raw)
+            if j == 0:
+                dq_turned[cols, part] = more
+            else:
+                dq_turned[cols, part] += more
             dks.append(dk * scaling)
             dvs.append(dv)
         grads_ref[:width, here] = (dq_turned[:, here] * scaling).astype(LOW)
@@ -450,7 +446,7 @@
         struct((count, depth), LOW),
         struct((count, units), LOW),
         struct((count, units), LOW),
-        stored_far((size, depth), WIDE),
+        (struct if begin else stored_far)((size, depth), WIDE),
     )[: 6 if keep else 5]
     return pl.pallas_call(
         functools.partial(feed_kernel, begin=begin, size=size, half=half, keep=keep, given=len(stored)),
@@ -599,14 +595,14 @@
         grid_spec=pltpu.PrefetchScalarGridSpec(
             num_scalar_prefetch=1,
             grid=(1,),
-            in_specs=[whole()] * 2 + [pl.BlockSpec((size, depth), lambda i, scalar_ref: (0, 0)), placed, whole()],
+            in_specs=[whole()] * 3 + [placed, whole()],
             out_specs=whole(),
         ),
         out_shape=struct((size, depth), LOW),
         compiler_params=params(14),
         cost_estimate=cost(guess),
         name="second_norm_backward",
-    )(scalar, mine, other, far(hidden), far(out_grad), rows)
+    )(scalar, mine, other, hidden if begin else far(hidden), far(out_grad), rows)
 
 
 def inward_kernel(scalar_ref, grads_ref, tokens_ref, weights_ref, ahead_ref, back_ref, sums_ref):

time: 190 us -> 189 us (level)
  Pallas kernels: 95 us -> 93 us
  transfers between devices with their start and end apart: 46 -> 46, of which waited for: 11 -> 12; matrix products, arithmetic and copies ran while one was open for 2% -> 2% of each run, Pallas kernels for 48% -> 47%
where the time goes in v6:
time: 189 us; the launch traced here: 186 us
  Pallas kernels  93 us (49%)
  starting transfers between devices  54.3 us (29%)
  waiting for transfers between devices  29.8 us (16%)
  other arithmetic  4.86 us (3%)
    ppermute x45, starting transfers between devices, swap(): return lax.ppermute(value, axis, [(i, i ^ bits) for i in range(size)])  48.7 us
    ppermute x45, waiting for transfers between devices, swap(): return lax.ppermute(value, axis, [(i, i ^ bits) for i in range(size)])  29.8 us
    pallas_call x1, Pallas kernels, attend_back(): pl.pallas_call(functools.partial(attend_back_kernel, chunks=chunks, rows=...  17.2 us
    pallas_call x4, Pallas kernels, feed(): pl.pallas_call(functools.partial(feed_kernel, begin=begin, size=size, hal...  15.8 us
    pallas_call x2, Pallas kernels, attend(): pl.pallas_call(functools.partial(attend_kernel, places=places, heads=head...  11.3 us
    pallas_call x1, Pallas kernels, weigh(): pl.pallas_call(weigh_kernel, grid_spec=pltpu.PrefetchScalarGridSpec(num_s...  9.61 us
    pallas_call x2, Pallas kernels, second_back(): pl.pallas_call(functools.partial(second_back_kernel, begin=begin, half=ha...  6.15 us
    all_to_all x1, starting transfers between devices, exchange_far(): return [lax.all_to_all(parts, 'batch', 0, 0, tiled=True)]  5.61 us
  transfers between devices with their start and end apart: 46, of which 12 were waited for; matrix products, arithmetic and copies ran while one was open for 2% of the time, Pallas kernels for 47%

profile of v6, /device:TPU:0, one launch (start us, length us, event | category | flops | bytes accessed | tf_op | source)
XLA Modules:
  0.0 185.5 jit_solution(12358721247343398686)
XLA Ops:
  1.7 3.1 %collective-permute-start.1 = (bf16[96,896]{1,0:T(8,128)(2,1)S(1)}, bf16[96,896]{1,0:T(8,128)(2,1)S(1)}, u32[]{:S(2)}, u32[]{:S(2)}) collective-permute-start(bf16[96,896]{1,0:T(8,128)(2,1)S(1)} %pack.1.refs_0_), channel_id=1, source_target_pairs={{0,8},{4,12},{8,0},{12,4},{16,24},{20,28},{24,16},{28,20},{1,9},{5... | collective-permute-start | bytes 516104 | tf_op jit(solution)/shard_map/ppermute | solution.py:72
  4.8 2.6 %collective-permute-start.3 = (bf16[96,896]{1,0:T(8,128)(2,1)S(1)}, bf16[96,896]{1,0:T(8,128)(2,1)S(1)}, u32[]{:S(2)}, u32[]{:S(2)}) collective-permute-start(bf16[96,896]{1,0:T(8,128)(2,1)S(1)} %pack.1.refs_0_), channel_id=1, source_target_pairs={{0,16},{4,20},{8,24},{12,28},{16,0},{20,4},{24,8},{28,12},{1,17},{... | collective-permute-start | bytes 516104 | tf_op jit(solution)/shard_map/ppermute | solution.py:72
  8.9 3.8 %collective-permute-done.1.refs_2_ = bf16[96,896]{1,0:T(8,128)(2,1)S(1)} collective-permute-done((bf16[96,896]{1,0:T(8,128)(2,1)S(1)}, bf16[96,896]{1,0:T(8,128)(2,1)S(1)}, u32[]{:S(2)}, u32[]{:S(2)}) %collective-permute-start.1) | collective-permute-done | bytes 172064 | tf_op jit(solution)/shard_map/ppermute | solution.py:72
  12.8 1.7 collective-permute-start.2
  14.4 2.5 %collective-permute-start.5 = (bf16[96,896]{1,0:T(8,128)(2,1)S(1)}, bf16[96,896]{1,0:T(8,128)(2,1)S(1)}, u32[]{:S(2)}, u32[]{:S(2)}) collective-permute-start(bf16[96,896]{1,0:T(8,128)(2,1)S(1)} %pack.1.refs_0_), channel_id=1, source_target_pairs={{0,24},{4,28},{8,16},{12,20},{16,8},{20,12},{24,0},{28,4},{1,25},{... | collective-permute-start | bytes 516104 | tf_op jit(solution)/shard_map/ppermute | solution.py:72
  18.2 1.9 %collective-permute-start.4 = (bf16[96,896]{1,0:T(8,128)(2,1)S(1)}, bf16[96,896]{1,0:T(8,128)(2,1)S(1)}, u32[]{:S(2)}, u32[]{:S(2)}) collective-permute-start(bf16[96,896]{1,0:T(8,128)(2,1)S(1)} %collective-permute-done.3.refs_4_), channel_id=1, source_target_pairs={{0,4},{4,0},{8,12},{12,8},{16,20},{20,16},{24,28},{28,24},{1,5},{5... | collective-permute-start | bytes 516104 | tf_op jit(solution)/shard_map/ppermute | solution.py:72
  20.1 1.7 pad_maximum_fusion.refs_0_
  21.8 1.8 collective-permute-done.4.refs_5_
  23.6 1.9 %collective-permute-start.6 = (bf16[96,896]{1,0:T(8,128)(2,1)S(1)}, bf16[96,896]{1,0:T(8,128)(2,1)S(1)}, u32[]{:S(2)}, u32[]{:S(2)}) collective-permute-start(bf16[96,896]{1,0:T(8,128)(2,1)S(1)} %collective-permute-done.5.refs_6_), channel_id=1, source_target_pairs={{0,4},{4,0},{8,12},{12,8},{16,20},{20,16},{24,28},{28,24},{1,5},{5... | collective-permute-start | bytes 516104 | tf_op jit(solution)/shard_map/ppermute | solution.py:72
  26.1 2.9 %collective-permute-start.16 = (bf16[96,1536]{1,0:T(8,128)(2,1)}, bf16[96,1536]{1,0:T(8,128)(2,1)S(1)}, u32[]{:S(2)}, u32[]{:S(2)}) collective-permute-start(bf16[96,1536]{1,0:T(8,128)(2,1)} %pad_maximum_fusion.refs_0_), channel_id=1, source_target_pairs={{0,16},{4,20},{8,24},{12,28},{16,0},{20,4},{24,8},{28,12},{1,17},{... | collective-permute-start | bytes 884744 | tf_op jit(solution)/shard_map/ppermute | solution.py:72
  29.1 5.6 %project.1 = (bf16[1536,768]{1,0:T(8,128)(2,1)}, bf16[1536,576]{1,0:T(8,128)(2,1)S(1)}, f32[8,768]{1,0:T(8,128)S(1)}, bf16[768,896]{1,0:T(8,128)(2,1)S(1)}, bf16[192,768]{1,0:T(8,128)(2,1)S(1)}) custom-call(s32[4]{0:T(128)S(1)} %pad_add_fusion.scalar_ref, bf16[96,896]{1,0:T(8,128)(2,1)S(1)} %pack.1.refs_0_, ...), custom_call_target="tpu_custom_call" | custom-call | flops 4400000 | tf_op jit(solution)/shard_map/project/pallas_call | solution.py:153
  34.7 1.9 %collective-permute-start.8 = (bf16[96,1536]{1,0:T(8,128)(2,1)S(1)}, bf16[96,1536]{1,0:T(8,128)(2,1)S(1)}, u32[]{:S(2)}, u32[]{:S(2)}) collective-permute-start(bf16[96,1536]{1,0:T(8,128)(2,1)S(1)} %collective-permute-done.7.refs_2_), channel_id=1, source_target_pairs={{0,4},{4,0},{8,12},{12,8},{16,20},{20,16},{24,28},{28,24},{1,5},{5... | collective-permute-start | bytes 884744 | tf_op jit(solution)/shard_map/ppermute | solution.py:72
  37.3 6.5 %attend_forward.2 = (bf16[192,1024]{1,0:T(8,128)(2,1)S(1)}, f32[4,8,256]{2,1,0:T(8,128)S(1)}) custom-call(s32[4]{0:T(128)S(1)} %pad_add_fusion.scalar_ref, bf16[1536,576]{1,0:T(8,128)(2,1)S(1)} %get-tuple-element.157.projected_ref.refs_0_), custom_call_target="tpu_custom_call" | custom-call | flops 1100000 | tf_op jit(solution)/shard_map/attend_forward/pallas_call | solution.py:257
  43.8 2.1 %collective-permute-start.18 = (bf16[96,1536]{1,0:T(8,128)(2,1)S(1)}, bf16[96,1536]{1,0:T(8,128)(2,1)S(1)}, u32[]{:S(2)}, u32[]{:S(2)}) collective-permute-start(bf16[96,1536]{1,0:T(8,128)(2,1)S(1)} %collective-permute-done.16.refs_4_), channel_id=1, source_target_pairs={{0,8},{4,12},{8,0},{12,4},{16,24},{20,28},{24,16},{28,20},{1,9},{5... | collective-permute-start | bytes 884744 | tf_op jit(solution)/shard_map/ppermute | solution.py:72
  46.2 2.1 %collective-permute-start.20 = (bf16[192,1024]{1,0:T(8,128)(2,1)S(1)}, bf16[192,1024]{1,0:T(8,128)(2,1)S(1)}, u32[]{:S(2)}, u32[]{:S(2)}) collective-permute-start(bf16[192,1024]{1,0:T(8,128)(2,1)S(1)} %get-tuple-element.111.refs_2_), channel_id=1, source_target_pairs={{0,2},{1,3},{2,0},{3,1},{4,6},{5,7},{6,4},{7,5},{8,10},{9,11},{10,... | collective-permute-start | bytes 1179656 | tf_op jit(solution)/shard_map/ppermute | solution.py:72
  50.0 4.8 %attend_forward.3 = (bf16[192,512]{1,0:T(8,128)(2,1)S(1)}, f32[2,8,256]{2,1,0:T(8,128)S(1)}) custom-call(s32[4]{0:T(128)S(1)} %pad_add_fusion.scalar_ref, bf16[1536,576]{1,0:T(8,128)(2,1)S(1)} %get-tuple-element.157.projected_ref.refs_0_), custom_call_target="tpu_custom_call" | custom-call | flops 1100000 | tf_op jit(solution)/shard_map/attend_forward/pallas_call | solution.py:257
  55.3 3.3 %collective-permute-done.12.refs_7_ = bf16[192,768]{1,0:T(8,128)(2,1)S(1)} collective-permute-done((bf16[192,768]{1,0:T(8,128)(2,1)S(1)}, bf16[192,768]{1,0:T(8,128)(2,1)S(1)}, u32[]{:S(2)}, u32[]{:S(2)}) %collective-permute-start.12) | collective-permute-done | bytes 294944 | tf_op jit(solution)/shard_map/ppermute | solution.py:72
  58.6 1.7 collective-permute-start.9
  60.9 3.4 %collective-permute-done.9.refs_3_ = bf16[192,512]{1,0:T(8,128)(2,1)S(1)} collective-permute-done((bf16[192,512]{1,0:T(8,128)(2,1)S(1)}, bf16[192,512]{1,0:T(8,128)(2,1)S(1)}, u32[]{:S(2)}, u32[]{:S(2)}) %collective-permute-start.9) | collective-permute-done | bytes 196640 | tf_op jit(solution)/shard_map/ppermute | solution.py:72
  66.2 4.9 %feed_forward.4 = (bf16[512,768]{1,0:T(8,128)(2,1)S(1)}, f32[8,768]{1,0:T(8,128)S(1)}, bf16[1536,768]{1,0:T(8,128)(2,1)S(1)}, bf16[1536,768]{1,0:T(8,128)(2,1)S(1)}, bf16[1536,768]{1,0:T(8,128)(2,1)S(1)}) custom-call(s32[4]{0:T(128)S(1)} %pad_add_fusion.scalar_ref, bf16[1536,768]{1,0:T(8,128)(2,1)S(1)} %copy-done, bf16[1536,768]{1,0:T(8,128)(2,1)S(1)} %copy-done.1, ...), custom_call_target="tpu_custom_call" | custom-call | flops 563200 | tf_op jit(solution)/shard_map/feed_forward/pallas_call | solution.py:451
  71.3 2.9 %feed_forward.5 = (bf16[256,768]{1,0:T(8,128)(2,1)S(1)}, f32[8,768]{1,0:T(8,128)S(1)}, bf16[1536,768]{1,0:T(8,128)(2,1)S(1)}, bf16[1536,768]{1,0:T(8,128)(2,1)S(1)}, bf16[1536,768]{1,0:T(8,128)(2,1)S(1)}) custom-call(s32[4]{0:T(128)S(1)} %pad_add_fusion.scalar_ref, ...), custom_call_target="tpu_custom_call", output_to_operand_aliasing={{2}: (15, {}), {3}: (16, {}), {4}: (17, {})} | custom-call | flops 281600 | tf_op jit(solution)/shard_map/feed_forward/pallas_call | solution.py:451
  74.7 4.7 %feed_forward.6 = (bf16[512,768]{1,0:T(8,128)(2,1)S(1)}, f32[8,768]{1,0:T(8,128)S(1)}, bf16[1536,768]{1,0:T(8,128)(2,1)S(1)}, bf16[1536,768]{1,0:T(8,128)(2,1)S(...) custom-call(s32[4]{0:T(128)S(1)} %pad_add_fusion.scalar_ref, ...), custom_call_target="tpu_custom_call", output_to_operand_aliasing={{2}: (15, {}), {3}: (16, {}), {4}: (17, {})} | custom-call | flops 563200 | tf_op jit(solution)/shard_map/feed_forward/pallas_call | solution.py:451
  80.4 1.7 collective-permute-start.26
  82.1 3.3 %feed_forward.7 = (bf16[256,768]{1,0:T(8,128)(2,1)S(1)}, f32[8,768]{1,0:T(8,128)S(1)}, bf16[1536,768]{1,0:T(8,128)(2,1)S(1)}, bf16[1536,768]{1,0:T(8,128)(2,1)S(...) custom-call(s32[4]{0:T(128)S(1)} %pad_add_fusion.scalar_ref, ...), custom_call_target="tpu_custom_call", output_to_operand_aliasing={{2}: (15, {}), {3}: (16, {}), {4}: (17, {})} | custom-call | flops 281600 | tf_op jit(solution)/shard_map/feed_forward/pallas_call | solution.py:451
  87.5 9.6 %feed_forward_weights.1 = (bf16[768,768]{1,0:T(8,128)(2,1)}, bf16[768,768]{1,0:T(8,128)(2,1)}, bf16[768,1536]{1,0:T(8,128)(2,1)}) custom-call(s32[4]{0:T(128)S(1)} %pad_add_fusion.scalar_ref, bf16[1536,768]{1,0:T(8,128)(2,1)S(1)} %get-tuple-element.150.normed_ref, bf16[1536,768]{1,0:T(8,128)(2,1)S(1)} %get-tuple-element.151.upper_ref, ...), custom_call_target="tpu_custom_call" | custom-call | flops 1100000 | tf_op jit(solution)/shard_map/feed_forward_weights/pallas_call | solution.py:526
  97.1 5.6 %all-to-all-start = ((bf16[8,96,1536]{2,1,0:T(8,128)(2,1)}), bf16[8,96,1536]{2,1,0:T(8,128)(2,1)}, u32[]{:S(2)}, u32[]{:S(2)}) async-start(bf16[8,96,1536]{2,1,0:T(8,128)(2,1)} %bitcast.6), calls=%async_computation | async-start | bytes 4718592 | tf_op jit(solution)/shard_map/all_to_all | solution.py:807
  102.7 3.8 %second_norm_backward.2.refs_6_ = bf16[512,768]{1,0:T(8,128)(2,1)S(1)} custom-call(s32[4]{0:T(128)S(1)} %pad_add_fusion.scalar_ref, bf16[512,768]{1,0:T(8,128)(2,1)} %add_convert_fusion.1.mine_ref, bf16[512,768]{1,0:T(8,128)(2,1)} %collective-permute-done.26.other_ref, f32[512,768]{1,0:T(8,128)} %get-tuple-element.162.hidden_ref.refs_0_, ...), custom_call_target="tpu_custom_call" | custom-call | flops 1100000 | tf_op jit(solution)/shard_map/second_norm_backward/pallas_call | solution.py:593
  107.1 1.7 collective-permute-done.29.other_ref
  108.7 2.4 %second_norm_backward.3.refs_8_ = bf16[256,768]{1,0:T(8,128)(2,1)S(1)} custom-call(s32[4]{0:T(128)S(1)} %pad_add_fusion.scalar_ref, bf16[256,768]{1,0:T(8,128)(2,1)} %add_convert_fusion.4.mine_ref, bf16[256,768]{1,0:T(8,128)(2,1)} %collective-permute-done.29.other_ref, f32[256,768]{1,0:T(8,128)S(1)} %copy-done.8, bf16[1536,768]{1,0:T(8,128)(2,1)} %grad_ref.5, ...), custom_call_target="tpu_custom_call" | custom-call | flops 44000002048 | tf_op jit(solution)/shard_map/second_norm_backward/pallas_call | solution.py:593
  111.5 1.7 collective-permute-start.27
  113.3 17.2 %attend_backward.1 = (bf16[576,1536]{1,0:T(8,128)(2,1)S(1)}, bf16[768,192]{1,0:T(8,128)(2,1)S(1)}, bf16[1536,768]{1,0:T(8,128)(2,1)S(1)}) custom-call(s32[4]{0:T(128)S(1)} %pad_add_fusion.scalar_ref, bf16[1536,576]{1,0:T(8,128)(2,1)S(1)} %copy-done.3, bf16[192,768]{1,0:T(8,128)(2,1)S(1)} %get-tuple-element.114.refs_6_.refs_1_, ...), custom_call_target="tpu_custom_call" | custom-call | flops 8800000 | tf_op jit(solution)/shard_map/attend_backward/pallas_call | solution.py:355
  130.5 2.3 %projection_weights.1 = (bf16[4,96,768]{2,1,0:T(8,128)(2,1)S(1)}, bf16[4,96,768]{2,1,0:T(8,128)(2,1)S(1)}) custom-call(s32[4]{0:T(128)S(1)} %pad_add_fusion.scalar_ref, bf16[576,1536]{1,0:T(8,128)(2,1)S(1)} %get-tuple-element.169.grads_ref, bf16[1536,768]{1,0:T(8,128)(2,1)S(1)} %copy-done.6, bf16[768,192]{1,0:T(8,128)(2,1)S(1)} %get-tuple-element.167.outs_ref), custom_call_target="tpu_custom_call" | custom-call | flops 1100000 | tf_op jit(solution)/shard_map/projection_weights/pallas_call | solution.py:663
  132.8 1.9 %grad_normed.2 = (bf16[768,768]{1,0:T(8,128)(2,1)S(1)}, f32[8,768]{1,0:T(8,128)S(1)}) custom-call(s32[4]{0:T(128)S(1)} %pad_add_fusion.scalar_ref, bf16[576,1536]{1,0:T(8,128)(2,1)S(1)} %get-tuple-element.169.grads_ref, bf16[1536,768]{1,0:T(8,128)(2,1)S(1)} %copy-done, bf16[768,896]{1,0:T(8,128)(2,1)S(1)} %copy-done.5, f32[8,768]{1,0:T(8,128)S(1)} %get-tuple-element.171.ahead_ref), custom_call_target="tpu_custom_call" | custom-call | flops 1100000 | tf_op jit(solution)/shard_map/grad_normed/pallas_call | solution.py:626
  135.0 2.0 %collective-permute-start.36 = (bf16[4,96,768]{2,1,0:T(8,128)(2,1)S(1)}, bf16[4,96,768]{2,1,0:T(8,128)(2,1)S(1)}, u32[]{:S(2)}, u32[]{:S(2)}) collective-permute-start(bf16[4,96,768]{2,1,0:T(8,128)(2,1)S(1)} %get-tuple-element.183), channel_id=1, source_target_pairs={{0,4},{4,0},{8,12},{12,8},{16,20},{20,16},{24,28},{28,24},{1,5},{5... | collective-permute-start | bytes 1769480 | tf_op jit(solution)/shard_map/ppermute | solution.py:72
  137.0 1.9 %grad_normed.3 = (bf16[768,768]{1,0:T(8,128)(2,1)S(1)}, f32[8,768]{1,0:T(8,128)S(1)}) custom-call(s32[4]{0:T(128)S(1)} %pad_add_fusion.scalar_ref, bf16[576,1536]{1,0:T(8,128)(2,1)S(1)} %get-tuple-element.169.grads_ref, bf16[1536,768]{1,0:T(8,128)(2,1)S(1)} %copy-done, bf16[768,896]{1,0:T(8,128)(2,1)S(1)} %copy-done.5, f32[8,768]{1,0:T(8,128)S(1)} %get-tuple-element.172.ahead_ref), custom_call_target="tpu_custom_call" | custom-call | flops 1100000 | tf_op jit(solution)/shard_map/grad_normed/pallas_call | solution.py:626
  140.2 1.7 collective-permute-start.34
  142.3 1.9 %collective-permute-start.37 = (f32[8,768]{1,0:T(8,128)S(1)}, f32[8,768]{1,0:T(8,128)S(1)}, u32[]{:S(2)}, u32[]{:S(2)}) collective-permute-start(f32[8,768]{1,0:T(8,128)S(1)} %get-tuple-element.184.refs_0_), channel_id=1, source_target_pairs={{0,4},{4,0},{8,12},{12,8},{16,20},{20,16},{24,28},{28,24},{1,5},{5... | collective-permute-start | bytes 73736 | tf_op jit(solution)/shard_map/ppermute | solution.py:72
  144.2 3.9 %layer_out.1 = (bf16[384,768]{1,0:T(8,128)(2,1)}, bf16[384,768]{1,0:T(8,128)(2,1)}, bf16[1536,768]{1,0:T(8,128)(2,1)}) custom-call(s32[4]{0:T(128)S(1)} %pad_add_fusion.scalar_ref, bf16[768,768]{1,0:T(8,128)(2,1)S(1)} %add_convert_fusion.mine_ref, bf16[768,768]{1,0:T(8,128)(2,1)S(1)} %collective-permute-done.27.other_ref, ...), custom_call_target="tpu_custom_call" | custom-call | flops 1100000 | tf_op jit(solution)/shard_map/layer_out/pallas_call | solution.py:689
  148.1 7.5 %collective-permute-done.37.refs_1_ = f32[8,768]{1,0:T(8,128)S(1)} collective-permute-done((f32[8,768]{1,0:T(8,128)S(1)}, f32[8,768]{1,0:T(8,128)S(1)}, u32[]{:S(2)}, u32[]{:S(2)}) %collective-permute-start.37) | collective-permute-done | bytes 24608 | tf_op jit(solution)/shard_map/ppermute | solution.py:72
  157.1 3.9 %collective-permute-start.39 = (bf16[96,896]{1,0:T(8,128)(2,1)}, bf16[96,896]{1,0:T(8,128)(2,1)S(1)}, u32[]{:S(2)}, u32[]{:S(2)}) collective-permute-start(bf16[96,896]{1,0:T(8,128)(2,1)} %get-tuple-element.192), channel_id=1, source_target_pairs={{0,8},{4,12},{8,0},{12,4},{16,24},{20,28},{24,16},{28,20},{1,9},{5... | collective-permute-start | bytes 516104 | tf_op jit(solution)/shard_map/ppermute | solution.py:72
  161.5 1.9 %collective-permute-start.41 = (bf16[96,896]{1,0:T(8,128)(2,1)}, bf16[96,896]{1,0:T(8,128)(2,1)}, u32[]{:S(2)}, u32[]{:S(2)}) collective-permute-start(bf16[96,896]{1,0:T(8,128)(2,1)} %get-tuple-element.194), channel_id=1, source_target_pairs={{0,24},{4,28},{8,16},{12,20},{16,8},{20,12},{24,0},{28,4},{1,25},{... | collective-permute-start | bytes 516104 | tf_op jit(solution)/shard_map/ppermute | solution.py:72
  163.4 2.5 %first_norm_backward.2 = (bf16[384,768]{1,0:T(8,128)(2,1)}, bf16[1536,768]{1,0:T(8,128)(2,1)}) custom-call(s32[4]{0:T(128)S(1)} %pad_add_fusion.scalar_ref, bf16[384,768]{1,0:T(8,128)(2,1)S(1)} %get-tuple-element.179.mine_ref, bf16[384,768]{1,0:T(8,128)(2,1)S(1)} %collective-permute-done.34.other_ref, bf16[1536,768]{1,0:T(8,128)(2,1)S(1)} %copy-done, ...), custom_call_target="tpu_custom_call" | custom-call | flops 1100000 | tf_op jit(solution)/shard_map/first_norm_backward/pallas_call | solution.py:723
  165.9 2.1 %collective-permute-done.38.other_ref = bf16[384,768]{1,0:T(8,128)(2,1)S(1)} collective-permute-done((bf16[384,768]{1,0:T(8,128)(2,1)S(1)}, bf16[384,768]{1,0:T(8,128)(2,1)S(1)}, u32[]{:S(2)}, u32[]{:S(2)}) %collective-permute-start.38) | collective-permute-done | bytes 589856 | tf_op jit(solution)/shard_map/ppermute | solution.py:72
  168.0 2.5 %first_norm_backward.3 = (bf16[384,768]{1,0:T(8,128)(2,1)}, bf16[1536,768]{1,0:T(8,128)(2,1)}) custom-call(s32[4]{0:T(128)S(1)} %pad_add_fusion.scalar_ref, bf16[384,768]{1,0:T(8,128)(2,1)S(1)} %get-tuple-element.186.mine_ref, bf16[384,768]{1,0:T(8,128)(2,1)S(1)} %collective-permute-done.38.other_ref, ...), custom_call_target="tpu_custom_call", output_to_operand_aliasing={{1}: (6, {})} | custom-call | flops 1100000 | tf_op jit(solution)/shard_map/first_norm_backward/pallas_call | solution.py:723
  170.4 2.8 %total.3 = (f32[96,768]{1,0:T(8,128)}, f32[96,768]{1,0:T(8,128)}) custom-call(bf16[8,96,1536]{2,1,0:T(8,128)(2,1)} %all-to-all-done.refs_0_), custom_call_target="tpu_custom_call" | custom-call | flops 1100000 | tf_op jit(solution)/shard_map/total/pallas_call | solution.py:792
  173.7 3.1 %collective-permute-done.40.refs_2_ = bf16[96,896]{1,0:T(8,128)(2,1)S(1)} collective-permute-done((bf16[96,896]{1,0:T(8,128)(2,1)}, bf16[96,896]{1,0:T(8,128)(2,1)S(1)}, u32[]{:S(2)}, u32[]{:S(2)}) %collective-permute-start.40) | collective-permute-done | bytes 172064 | tf_op jit(solution)/shard_map/ppermute | solution.py:72
  179.2 1.8 total.5
  181.6 3.1 %place.1 = (bf16[1536,768]{1,0:T(8,128)(2,1)}, bf16[1536,768]{1,0:T(8,128)(2,1)}) custom-call(s32[4]{0:T(128)S(1)} %pad_add_fusion.scalar_ref, bf16[384,768]{1,0:T(8,128)(2,1)S(1)} %collective-permute-done.32.refs_0_, bf16[384,768]{1,0:T(8,128)(2,1)} %collective-permute-done.33.refs_1_, ...), custom_call_target="tpu_custom_call", output_to_operand_aliasing={{0}: (5, {}), {1}: (6, {})} | custom-call | flops 1100000 | tf_op jit(solution)/shard_map/place/pallas_call | solution.py:756
  (108 shorter events, 22.3 us)
Async XLA Ops:
  1.7 11.0 %collective-permute-start.1 = (bf16[96,896]{1,0:T(8,128)(2,1)S(1)}, bf16[96,896]{1,0:T(8,128)(2,1)S(1)}, u32[]{:S(2)}, u32[]{:S(2)}) collective-permute-start(bf16[96,896]{1,0:T(8,128)(2,1)S(1)} %pack.1.refs_0_), channel_id=1, source_target_pairs={{0,8},{4,12},{8,0},{12,4},{16,24},{20,28},{24,16},{28,20},{1,9},{5... | collective-permute-start | bytes 516104 | tf_op jit(solution)/shard_map/ppermute | solution.py:72
  4.8 12.1 %collective-permute-start.3 = (bf16[96,896]{1,0:T(8,128)(2,1)S(1)}, bf16[96,896]{1,0:T(8,128)(2,1)S(1)}, u32[]{:S(2)}, u32[]{:S(2)}) collective-permute-start(bf16[96,896]{1,0:T(8,128)(2,1)S(1)} %pack.1.refs_0_), channel_id=1, source_target_pairs={{0,16},{4,20},{8,24},{12,28},{16,0},{20,4},{24,8},{28,12},{1,17},{... | collective-permute-start | bytes 516104 | tf_op jit(solution)/shard_map/ppermute | solution.py:72
  7.4 9.5 %collective-permute-start = (bf16[96,896]{1,0:T(8,128)(2,1)S(1)}, bf16[96,896]{1,0:T(8,128)(2,1)S(1)}, u32[]{:S(2)}, u32[]{:S(2)}) collective-permute-start(bf16[96,896]{1,0:T(8,128)(2,1)S(1)} %pack.1.refs_0_), channel_id=1, source_target_pairs={{0,4},{4,0},{8,12},{12,8},{16,20},{20,16},{24,28},{28,24},{1,5},{5... | collective-permute-start | bytes 516104 | tf_op jit(solution)/shard_map/ppermute | solution.py:72
  12.8 5.4 %collective-permute-start.2 = (bf16[96,896]{1,0:T(8,128)(2,1)S(1)}, bf16[96,896]{1,0:T(8,128)(2,1)S(1)}, u32[]{:S(2)}, u32[]{:S(2)}) collective-permute-start(bf16[96,896]{1,0:T(8,128)(2,1)S(1)} %collective-permute-done.1.refs_2_), channel_id=1, source_target_pairs={{0,4},{4,0},{8,12},{12,8},{16,20},{20,16},{24,28},{28,24},{1,5},{5... | collective-permute-start | bytes 516104 | tf_op jit(solution)/shard_map/ppermute | solution.py:72
  14.4 7.3 %collective-permute-start.5 = (bf16[96,896]{1,0:T(8,128)(2,1)S(1)}, bf16[96,896]{1,0:T(8,128)(2,1)S(1)}, u32[]{:S(2)}, u32[]{:S(2)}) collective-permute-start(bf16[96,896]{1,0:T(8,128)(2,1)S(1)} %pack.1.refs_0_), channel_id=1, source_target_pairs={{0,24},{4,28},{8,16},{12,20},{16,8},{20,12},{24,0},{28,4},{1,25},{... | collective-permute-start | bytes 516104 | tf_op jit(solution)/shard_map/ppermute | solution.py:72
  18.2 5.4 %collective-permute-start.4 = (bf16[96,896]{1,0:T(8,128)(2,1)S(1)}, bf16[96,896]{1,0:T(8,128)(2,1)S(1)}, u32[]{:S(2)}, u32[]{:S(2)}) collective-permute-start(bf16[96,896]{1,0:T(8,128)(2,1)S(1)} %collective-permute-done.3.refs_4_), channel_id=1, source_target_pairs={{0,4},{4,0},{8,12},{12,8},{16,20},{20,16},{24,28},{28,24},{1,5},{5... | collective-permute-start | bytes 516104 | tf_op jit(solution)/shard_map/ppermute | solution.py:72
  23.6 11.1 %collective-permute-start.7 = (bf16[96,1536]{1,0:T(8,128)(2,1)}, bf16[96,1536]{1,0:T(8,128)(2,1)S(1)}, u32[]{:S(2)}, u32[]{:S(2)}) collective-permute-start(bf16[96,1536]{1,0:T(8,128)(2,1)} %pad_maximum_fusion.refs_0_), channel_id=1, source_target_pairs={{0,8},{4,12},{8,0},{12,4},{16,24},{20,28},{24,16},{28,20},{1,9},{5... | collective-permute-start | bytes 884744 | tf_op jit(solution)/shard_map/ppermute | solution.py:72
  23.6 5.5 %collective-permute-start.6 = (bf16[96,896]{1,0:T(8,128)(2,1)S(1)}, bf16[96,896]{1,0:T(8,128)(2,1)S(1)}, u32[]{:S(2)}, u32[]{:S(2)}) collective-permute-start(bf16[96,896]{1,0:T(8,128)(2,1)S(1)} %collective-permute-done.5.refs_6_), channel_id=1, source_target_pairs={{0,4},{4,0},{8,12},{12,8},{16,20},{20,16},{24,28},{28,24},{1,5},{5... | collective-permute-start | bytes 516104 | tf_op jit(solution)/shard_map/ppermute | solution.py:72
  26.1 17.7 %collective-permute-start.16 = (bf16[96,1536]{1,0:T(8,128)(2,1)}, bf16[96,1536]{1,0:T(8,128)(2,1)S(1)}, u32[]{:S(2)}, u32[]{:S(2)}) collective-permute-start(bf16[96,1536]{1,0:T(8,128)(2,1)} %pad_maximum_fusion.refs_0_), channel_id=1, source_target_pairs={{0,16},{4,20},{8,24},{12,28},{16,0},{20,4},{24,8},{28,12},{1,17},{... | collective-permute-start | bytes 884744 | tf_op jit(solution)/shard_map/ppermute | solution.py:72
  34.7 13.7 %collective-permute-start.8 = (bf16[96,1536]{1,0:T(8,128)(2,1)S(1)}, bf16[96,1536]{1,0:T(8,128)(2,1)S(1)}, u32[]{:S(2)}, u32[]{:S(2)}) collective-permute-start(bf16[96,1536]{1,0:T(8,128)(2,1)S(1)} %collective-permute-done.7.refs_2_), channel_id=1, source_target_pairs={{0,4},{4,0},{8,12},{12,8},{16,20},{20,16},{24,28},{28,24},{1,5},{5... | collective-permute-start | bytes 884744 | tf_op jit(solution)/shard_map/ppermute | solution.py:72
  37.3 27.5 %copy-start.10 = (bf16[96,1536]{1,0:T(8,128)(2,1)S(1)}, bf16[96,1536]{1,0:T(8,128)(2,1)}, u32[]{:S(2)}) copy-start(bf16[96,1536]{1,0:T(8,128)(2,1)} %copy-done.9) | copy-start | bytes 884740
  37.3 28.9 %copy-start.1 = (bf16[1536,768]{1,0:T(8,128)(2,1)S(1)}, bf16[1536,768]{1,0:T(8,128)(2,1)}, u32[]{:S(2)}) copy-start(bf16[1536,768]{1,0:T(8,128)(2,1)} %grad_ref.5) | copy-start | bytes 7077892
  43.8 10.9 %collective-permute-start.18 = (bf16[96,1536]{1,0:T(8,128)(2,1)S(1)}, bf16[96,1536]{1,0:T(8,128)(2,1)S(1)}, u32[]{:S(2)}, u32[]{:S(2)}) collective-permute-start(bf16[96,1536]{1,0:T(8,128)(2,1)S(1)} %collective-permute-done.16.refs_4_), channel_id=1, source_target_pairs={{0,8},{4,12},{8,0},{12,4},{16,24},{20,28},{24,16},{28,20},{1,9},{5... | collective-permute-start | bytes 884744 | tf_op jit(solution)/shard_map/ppermute | solution.py:72
  45.9 9.4 %collective-permute-start.15 = (bf16[96,1536]{1,0:T(8,128)(2,1)}, bf16[96,1536]{1,0:T(8,128)(2,1)S(1)}, u32[]{:S(2)}, u32[]{:S(2)}) collective-permute-start(bf16[96,1536]{1,0:T(8,128)(2,1)} %pad_maximum_fusion.refs_0_), channel_id=1, source_target_pairs={{0,4},{4,0},{8,12},{12,8},{16,20},{20,16},{24,28},{28,24},{1,5},{5... | collective-permute-start | bytes 884744 | tf_op jit(solution)/shard_map/ppermute | solution.py:72
  46.2 14.0 %collective-permute-start.20 = (bf16[192,1024]{1,0:T(8,128)(2,1)S(1)}, bf16[192,1024]{1,0:T(8,128)(2,1)S(1)}, u32[]{:S(2)}, u32[]{:S(2)}) collective-permute-start(bf16[192,1024]{1,0:T(8,128)(2,1)S(1)} %get-tuple-element.111.refs_2_), channel_id=1, source_target_pairs={{0,2},{1,3},{2,0},{3,1},{4,6},{5,7},{6,4},{7,5},{8,10},{9,11},{10,... | collective-permute-start | bytes 1179656 | tf_op jit(solution)/shard_map/ppermute | solution.py:72
  48.3 10.3 %collective-permute-start.12 = (bf16[192,768]{1,0:T(8,128)(2,1)S(1)}, bf16[192,768]{1,0:T(8,128)(2,1)S(1)}, u32[]{:S(2)}, u32[]{:S(2)}) collective-permute-start(bf16[192,768]{1,0:T(8,128)(2,1)S(1)} %get-tuple-element.114.refs_6_.refs_1_), channel_id=1, source_target_pairs={{0,2},{1,3},{2,0},{3,1},{4,6},{5,7},{6,4},{7,5},{8,10},{9,11},{10,... | collective-permute-start | bytes 884744 | tf_op jit(solution)/shard_map/ppermute | solution.py:72
  48.4 11.9 %collective-permute-start.17 = (bf16[96,1536]{1,0:T(8,128)(2,1)S(1)}, bf16[96,1536]{1,0:T(8,128)(2,1)S(1)}, u32[]{:S(2)}, u32[]{:S(2)}) collective-permute-start(bf16[96,1536]{1,0:T(8,128)(2,1)S(1)} %collective-permute-done.16.refs_4_), channel_id=1, source_target_pairs={{0,4},{4,0},{8,12},{12,8},{16,20},{20,16},{24,28},{28,24},{1,5},{5... | collective-permute-start | bytes 884744 | tf_op jit(solution)/shard_map/ppermute | solution.py:72
  54.8 9.5 %collective-permute-start.19 = (bf16[96,1536]{1,0:T(8,128)(2,1)S(1)}, bf16[96,1536]{1,0:T(8,128)(2,1)S(1)}, u32[]{:S(2)}, u32[]{:S(2)}) collective-permute-start(bf16[96,1536]{1,0:T(8,128)(2,1)S(1)} %collective-permute-done.18.refs_6_), channel_id=1, source_target_pairs={{0,4},{4,0},{8,12},{12,8},{16,20},{20,16},{24,28},{28,24},{1,5},{5... | collective-permute-start | bytes 884744 | tf_op jit(solution)/shard_map/ppermute | solution.py:72
  55.3 5.5 %collective-permute-start.10 = (bf16[192,512]{1,0:T(8,128)(2,1)S(1)}, bf16[192,512]{1,0:T(8,128)(2,1)S(1)}, u32[]{:S(2)}, u32[]{:S(2)}) collective-permute-start(bf16[192,512]{1,0:T(8,128)(2,1)S(1)} %get-tuple-element.117.refs_2_.refs_3_), channel_id=1, source_target_pairs={{0,1},{1,0},{2,3},{3,2},{4,5},{5,4},{6,7},{7,6},{8,9},{9,8},{10,11... | collective-permute-start | bytes 589832 | tf_op jit(solution)/shard_map/ppermute | solution.py:72
  58.6 5.7 %collective-permute-start.9 = (bf16[192,512]{1,0:T(8,128)(2,1)S(1)}, bf16[192,512]{1,0:T(8,128)(2,1)S(1)}, u32[]{:S(2)}, u32[]{:S(2)}) collective-permute-start(bf16[192,512]{1,0:T(8,128)(2,1)S(1)} %get-tuple-element.117.refs_2_.refs_3_), channel_id=1, source_target_pairs={{0,2},{1,3},{2,0},{3,1},{4,6},{5,7},{6,4},{7,5},{8,10},{9,11},{10,... | collective-permute-start | bytes 589832 | tf_op jit(solution)/shard_map/ppermute | solution.py:72
  60.3 5.9 %collective-permute-start.21 = (bf16[192,1024]{1,0:T(8,128)(2,1)S(1)}, bf16[192,1024]{1,0:T(8,128)(2,1)S(1)}, u32[]{:S(2)}, u32[]{:S(2)}) collective-permute-start(bf16[192,1024]{1,0:T(8,128)(2,1)S(1)} %get-tuple-element.111.refs_2_), channel_id=1, source_target_pairs={{0,1},{1,0},{2,3},{3,2},{4,5},{5,4},{6,7},{7,6},{8,9},{9,8},{10,11... | collective-permute-start | bytes 1179656 | tf_op jit(solution)/shard_map/ppermute | solution.py:72
  60.3 5.9 %collective-permute-start.22 = (bf16[192,1024]{1,0:T(8,128)(2,1)S(1)}, bf16[192,1024]{1,0:T(8,128)(2,1)S(1)}, u32[]{:S(2)}, u32[]{:S(2)}) collective-permute-start(bf16[192,1024]{1,0:T(8,128)(2,1)S(1)} %collective-permute-done.20.refs_3_), channel_id=1, source_target_pairs={{0,1},{1,0},{2,3},{3,2},{4,5},{5,4},{6,7},{7,6},{8,9},{9,8},{10,11... | collective-permute-start | bytes 1179656 | tf_op jit(solution)/shard_map/ppermute | solution.py:72
  60.8 5.4 %collective-permute-start.13 = (bf16[192,768]{1,0:T(8,128)(2,1)S(1)}, bf16[192,768]{1,0:T(8,128)(2,1)S(1)}, u32[]{:S(2)}, u32[]{:S(2)}) collective-permute-start(bf16[192,768]{1,0:T(8,128)(2,1)S(1)} %get-tuple-element.114.refs_6_.refs_1_), channel_id=1, source_target_pairs={{0,1},{1,0},{2,3},{3,2},{4,5},{5,4},{6,7},{7,6},{8,9},{9,8},{10,11... | collective-permute-start | bytes 884744 | tf_op jit(solution)/shard_map/ppermute | solution.py:72
  64.3 1.9 %collective-permute-start.14 = (bf16[192,768]{1,0:T(8,128)(2,1)S(1)}, bf16[192,768]{1,0:T(8,128)(2,1)S(1)}, u32[]{:S(2)}, u32[]{:S(2)}) collective-permute-start(bf16[192,768]{1,0:T(8,128)(2,1)S(1)} %collective-permute-done.12.refs_7_), channel_id=1, source_target_pairs={{0,1},{1,0},{2,3},{3,2},{4,5},{5,4},{6,7},{7,6},{8,9},{9,8},{10,11... | collective-permute-start | bytes 884744 | tf_op jit(solution)/shard_map/ppermute | solution.py:72
  64.3 1.9 %collective-permute-start.11 = (bf16[192,512]{1,0:T(8,128)(2,1)S(1)}, bf16[192,512]{1,0:T(8,128)(2,1)S(1)}, u32[]{:S(2)}, u32[]{:S(2)}) collective-permute-start(bf16[192,512]{1,0:T(8,128)(2,1)S(1)} %collective-permute-done.9.refs_3_), channel_id=1, source_target_pairs={{0,1},{1,0},{2,3},{3,2},{4,5},{5,4},{6,7},{7,6},{8,9},{9,8},{10,11... | collective-permute-start | bytes 589832 | tf_op jit(solution)/shard_map/ppermute | solution.py:72
  71.1 8.2 %collective-permute-start.23 = (bf16[512,768]{1,0:T(8,128)(2,1)S(1)}, bf16[512,768]{1,0:T(8,128)(2,1)S(1)}, u32[]{:S(2)}, u32[]{:S(2)}) collective-permute-start(bf16[512,768]{1,0:T(8,128)(2,1)S(1)} %get-tuple-element.141), channel_id=1, source_target_pairs={{0,1},{1,0},{2,3},{3,2},{4,5},{5,4},{6,7},{7,6},{8,9},{9,8},{10,11... | collective-permute-start | bytes 2359304 | tf_op jit(solution)/shard_map/ppermute | solution.py:72
  74.2 12.1 %collective-permute-start.24 = (bf16[256,768]{1,0:T(8,128)(2,1)S(1)}, bf16[256,768]{1,0:T(8,128)(2,1)S(1)}, u32[]{:S(2)}, u32[]{:S(2)}) collective-permute-start(bf16[256,768]{1,0:T(8,128)(2,1)S(1)} %get-tuple-element.149), channel_id=1, source_target_pairs={{0,1},{1,0},{2,3},{3,2},{4,5},{5,4},{6,7},{7,6},{8,9},{9,8},{10,11... | collective-permute-start | bytes 1179656 | tf_op jit(solution)/shard_map/ppermute | solution.py:72
  80.4 22.3 %collective-permute-start.26 = (bf16[512,768]{1,0:T(8,128)(2,1)}, bf16[512,768]{1,0:T(8,128)(2,1)}, u32[]{:S(2)}, u32[]{:S(2)}) collective-permute-start(bf16[512,768]{1,0:T(8,128)(2,1)} %add_convert_fusion.1.mine_ref), channel_id=1, source_target_pairs={{0,2},{1,3},{2,0},{3,1},{4,6},{5,7},{6,4},{7,5},{8,10},{9,11},{10,... | collective-permute-start | bytes 2359304 | tf_op jit(solution)/shard_map/ppermute | solution.py:72
  87.1 21.6 %collective-permute-start.29 = (bf16[256,768]{1,0:T(8,128)(2,1)}, bf16[256,768]{1,0:T(8,128)(2,1)}, u32[]{:S(2)}, u32[]{:S(2)}) collective-permute-start(bf16[256,768]{1,0:T(8,128)(2,1)} %add_convert_fusion.4.mine_ref), channel_id=1, source_target_pairs={{0,2},{1,3},{2,0},{3,1},{4,6},{5,7},{6,4},{7,5},{8,10},{9,11},{10,... | collective-permute-start | bytes 1179656 | tf_op jit(solution)/shard_map/ppermute | solution.py:72
  97.1 73.3 %all-to-all-start = ((bf16[8,96,1536]{2,1,0:T(8,128)(2,1)}), bf16[8,96,1536]{2,1,0:T(8,128)(2,1)}, u32[]{:S(2)}, u32[]{:S(2)}) async-start(bf16[8,96,1536]{2,1,0:T(8,128)(2,1)} %bitcast.6), calls=%async_computation | async-start | bytes 4718592 | tf_op jit(solution)/shard_map/all_to_all | solution.py:807
  102.7 8.5 %collective-permute-start.25 = (bf16[768,768]{1,0:T(8,128)(2,1)}, bf16[768,768]{1,0:T(8,128)(2,1)S(1)}, u32[]{:S(2)}, u32[]{:S(2)}) collective-permute-start(bf16[768,768]{1,0:T(8,128)(2,1)} %get-tuple-element.154), channel_id=1, source_target_pairs={{0,1},{1,0},{2,3},{3,2},{4,5},{5,4},{6,7},{7,6},{8,9},{9,8},{10,11... | collective-permute-start | bytes 3538952 | tf_op jit(solution)/shard_map/ppermute | solution.py:72
  106.5 6.7 %collective-permute-start.28 = (bf16[512,768]{1,0:T(8,128)(2,1)S(1)}, bf16[512,768]{1,0:T(8,128)(2,1)S(1)}, u32[]{:S(2)}, u32[]{:S(2)}) collective-permute-start(bf16[512,768]{1,0:T(8,128)(2,1)S(1)} %second_norm_backward.2.refs_6_), channel_id=1, source_target_pairs={{0,1},{1,0},{2,3},{3,2},{4,5},{5,4},{6,7},{7,6},{8,9},{9,8},{10,11... | collective-permute-start | bytes 2359304 | tf_op jit(solution)/shard_map/ppermute | solution.py:72
  111.1 2.1 %collective-permute-start.30 = (bf16[256,768]{1,0:T(8,128)(2,1)S(1)}, bf16[256,768]{1,0:T(8,128)(2,1)S(1)}, u32[]{:S(2)}, u32[]{:S(2)}) collective-permute-start(bf16[256,768]{1,0:T(8,128)(2,1)S(1)} %second_norm_backward.3.refs_8_), channel_id=1, source_target_pairs={{0,1},{1,0},{2,3},{3,2},{4,5},{5,4},{6,7},{7,6},{8,9},{9,8},{10,11... | collective-permute-start | bytes 1179656 | tf_op jit(solution)/shard_map/ppermute | solution.py:72
  111.5 28.4 %collective-permute-start.27 = (bf16[768,768]{1,0:T(8,128)(2,1)S(1)}, bf16[768,768]{1,0:T(8,128)(2,1)S(1)}, u32[]{:S(2)}, u32[]{:S(2)}) collective-permute-start(bf16[768,768]{1,0:T(8,128)(2,1)S(1)} %add_convert_fusion.mine_ref), channel_id=1, source_target_pairs={{0,2},{1,3},{2,0},{3,1},{4,6},{5,7},{6,4},{7,5},{8,10},{9,11},{10,... | collective-permute-start | bytes 3538952 | tf_op jit(solution)/shard_map/ppermute | solution.py:72
  134.8 5.2 %collective-permute-start.31 = (bf16[768,768]{1,0:T(8,128)(2,1)S(1)}, bf16[768,768]{1,0:T(8,128)(2,1)S(1)}, u32[]{:S(2)}, u32[]{:S(2)}) collective-permute-start(bf16[768,768]{1,0:T(8,128)(2,1)S(1)} %get-tuple-element.175), channel_id=1, source_target_pairs={{0,1},{1,0},{2,3},{3,2},{4,5},{5,4},{6,7},{7,6},{8,9},{9,8},{10,11... | collective-permute-start | bytes 3538952 | tf_op jit(solution)/shard_map/ppermute | solution.py:72
  135.0 20.5 %collective-permute-start.36 = (bf16[4,96,768]{2,1,0:T(8,128)(2,1)S(1)}, bf16[4,96,768]{2,1,0:T(8,128)(2,1)S(1)}, u32[]{:S(2)}, u32[]{:S(2)}) collective-permute-start(bf16[4,96,768]{2,1,0:T(8,128)(2,1)S(1)} %get-tuple-element.183), channel_id=1, source_target_pairs={{0,4},{4,0},{8,12},{12,8},{16,20},{20,16},{24,28},{28,24},{1,5},{5... | collective-permute-start | bytes 1769480 | tf_op jit(solution)/shard_map/ppermute | solution.py:72
  140.2 23.2 %collective-permute-start.34 = (bf16[384,768]{1,0:T(8,128)(2,1)S(1)}, bf16[384,768]{1,0:T(8,128)(2,1)S(1)}, u32[]{:S(2)}, u32[]{:S(2)}) collective-permute-start(bf16[384,768]{1,0:T(8,128)(2,1)S(1)} %get-tuple-element.179.mine_ref), channel_id=1, source_target_pairs={{0,2},{1,3},{2,0},{3,1},{4,6},{5,7},{6,4},{7,5},{8,10},{9,11},{10,... | collective-permute-start | bytes 1769480 | tf_op jit(solution)/shard_map/ppermute | solution.py:72
  141.9 26.0 %collective-permute-start.38 = (bf16[384,768]{1,0:T(8,128)(2,1)S(1)}, bf16[384,768]{1,0:T(8,128)(2,1)S(1)}, u32[]{:S(2)}, u32[]{:S(2)}) collective-permute-start(bf16[384,768]{1,0:T(8,128)(2,1)S(1)} %get-tuple-element.186.mine_ref), channel_id=1, source_target_pairs={{0,2},{1,3},{2,0},{3,1},{4,6},{5,7},{6,4},{7,5},{8,10},{9,11},{10,... | collective-permute-start | bytes 1769480 | tf_op jit(solution)/shard_map/ppermute | solution.py:72
  142.3 13.2 %collective-permute-start.37 = (f32[8,768]{1,0:T(8,128)S(1)}, f32[8,768]{1,0:T(8,128)S(1)}, u32[]{:S(2)}, u32[]{:S(2)}) collective-permute-start(f32[8,768]{1,0:T(8,128)S(1)} %get-tuple-element.184.refs_0_), channel_id=1, source_target_pairs={{0,4},{4,0},{8,12},{12,8},{16,20},{20,16},{24,28},{28,24},{1,5},{5... | collective-permute-start | bytes 73736 | tf_op jit(solution)/shard_map/ppermute | solution.py:72
  157.1 16.1 %collective-permute-start.39 = (bf16[96,896]{1,0:T(8,128)(2,1)}, bf16[96,896]{1,0:T(8,128)(2,1)S(1)}, u32[]{:S(2)}, u32[]{:S(2)}) collective-permute-start(bf16[96,896]{1,0:T(8,128)(2,1)} %get-tuple-element.192), channel_id=1, source_target_pairs={{0,8},{4,12},{8,0},{12,4},{16,24},{20,28},{24,16},{28,20},{1,9},{5... | collective-permute-start | bytes 516104 | tf_op jit(solution)/shard_map/ppermute | solution.py:72
  161.0 15.8 %collective-permute-start.40 = (bf16[96,896]{1,0:T(8,128)(2,1)}, bf16[96,896]{1,0:T(8,128)(2,1)S(1)}, u32[]{:S(2)}, u32[]{:S(2)}) collective-permute-start(bf16[96,896]{1,0:T(8,128)(2,1)} %get-tuple-element.193), channel_id=1, source_target_pairs={{0,16},{4,20},{8,24},{12,28},{16,0},{20,4},{24,8},{28,12},{1,17},{... | collective-permute-start | bytes 516104 | tf_op jit(solution)/shard_map/ppermute | solution.py:72
  161.5 15.4 %collective-permute-start.41 = (bf16[96,896]{1,0:T(8,128)(2,1)}, bf16[96,896]{1,0:T(8,128)(2,1)}, u32[]{:S(2)}, u32[]{:S(2)}) collective-permute-start(bf16[96,896]{1,0:T(8,128)(2,1)} %get-tuple-element.194), channel_id=1, source_target_pairs={{0,24},{4,28},{8,16},{12,20},{16,8},{20,12},{24,0},{28,4},{1,25},{... | collective-permute-start | bytes 516104 | tf_op jit(solution)/shard_map/ppermute | solution.py:72
  163.4 18.1 %collective-permute-start.32 = (bf16[384,768]{1,0:T(8,128)(2,1)}, bf16[384,768]{1,0:T(8,128)(2,1)S(1)}, u32[]{:S(2)}, u32[]{:S(2)}) collective-permute-start(bf16[384,768]{1,0:T(8,128)(2,1)} %get-tuple-element.177), channel_id=1, source_target_pairs={{0,1},{1,0},{2,3},{3,2},{4,5},{5,4},{6,7},{7,6},{8,9},{9,8},{10,11... | collective-permute-start | bytes 1769480 | tf_op jit(solution)/shard_map/ppermute | solution.py:72
  168.0 13.6 %collective-permute-start.33 = (bf16[384,768]{1,0:T(8,128)(2,1)}, bf16[384,768]{1,0:T(8,128)(2,1)}, u32[]{:S(2)}, u32[]{:S(2)}) collective-permute-start(bf16[384,768]{1,0:T(8,128)(2,1)} %get-tuple-element.178), channel_id=1, source_target_pairs={{0,1},{1,0},{2,3},{3,2},{4,5},{5,4},{6,7},{7,6},{8,9},{9,8},{10,11... | collective-permute-start | bytes 1769480 | tf_op jit(solution)/shard_map/ppermute | solution.py:72
  173.2 8.4 %collective-permute-start.43 = (bf16[384,768]{1,0:T(8,128)(2,1)S(1)}, bf16[384,768]{1,0:T(8,128)(2,1)S(1)}, u32[]{:S(2)}, u32[]{:S(2)}) collective-permute-start(bf16[384,768]{1,0:T(8,128)(2,1)S(1)} %copy-done.12), channel_id=1, source_target_pairs={{0,1},{1,0},{2,3},{3,2},{4,5},{5,4},{6,7},{7,6},{8,9},{9,8},{10,11... | collective-permute-start | bytes 1769480 | tf_op jit(solution)/shard_map/ppermute | solution.py:72
  176.8 4.7 %collective-permute-start.35 = (bf16[384,768]{1,0:T(8,128)(2,1)S(1)}, bf16[384,768]{1,0:T(8,128)(2,1)S(1)}, u32[]{:S(2)}, u32[]{:S(2)}) collective-permute-start(bf16[384,768]{1,0:T(8,128)(2,1)S(1)} %copy-done.13), channel_id=1, source_target_pairs={{0,1},{1,0},{2,3},{3,2},{4,5},{5,4},{6,7},{7,6},{8,9},{9,8},{10,11... | collective-permute-start | bytes 1769480 | tf_op jit(solution)/shard_map/ppermute | solution.py:72
  177.9 3.7 %collective-permute-start.42 = (f32[8,96]{1,0:T(8,128)S(1)}, f32[8,96]{1,0:T(8,128)S(1)}, u32[]{:S(2)}, u32[]{:S(2)}) collective-permute-start(f32[8,96]{1,0:T(8,128)S(1)} %slice.38), channel_id=1, source_target_pairs={{0,2},{1,3},{2,0},{3,1},{4,6},{5,7},{6,4},{7,5},{8,10},{9,11},{10,... | collective-permute-start | bytes 9224 | tf_op jit(solution)/shard_map/ppermute | solution.py:72
  181.5 3.2 %collective-permute-start.44 = (f32[8,96]{1,0:T(8,128)S(1)}, f32[8,96]{1,0:T(8,128)S(1)}, u32[]{:S(2)}, u32[]{:S(2)}) collective-permute-start(f32[8,96]{1,0:T(8,128)S(1)} %slice_add_fusion), channel_id=1, source_target_pairs={{0,1},{1,0},{2,3},{3,2},{4,5},{5,4},{6,7},{7,6},{8,9},{9,8},{10,11... | collective-permute-start | bytes 9224 | tf_op jit(solution)/shard_map/ppermute | solution.py:72
  (12 other events, 103.5 us)

commit v7 on v6

--- a/solution.py
+++ b/solution.py
@@ -222,25 +222,21 @@
         def split(value, h):
             return value[h * BLOCK : (h + 1) * BLOCK]
 
-        near = each(lambda h: outer_cols(projected_ref[here, column(0, h)], projected_ref[here, column(1, h)]))
-        near_size = jnp.where(jnp.concatenate([allowed] * heads, axis=0), jnp.abs(near) * factor, FAR)
-        top = jnp.max(near_size, axis=1, keepdims=True)
+        until = slice(0, row0 + BLOCK)
+        scores = each(lambda h: outer_cols(projected_ref[here, column(0, h)], projected_ref[until, column(1, h)]))
+        reach = jnp.abs(scores) * factor
+        near = jnp.where(jnp.concatenate([allowed] * heads, axis=0), reach[:, row0:], FAR)
         if row0 > 0:
-            past = each(lambda h: outer_cols(projected_ref[here, column(0, h)], projected_ref[:row0, column(1, h)]))
-            past_size = jnp.abs(past) * factor
+            past = reach[:, :row0]
             if row0 > sure:
                 past_key = lax.broadcasted_iota(jnp.int32, (1, row0), 1)
-                past_size = jnp.where(past_key < length, past_size, FAR)
-            top = jnp.maximum(top, jnp.max(past_size, axis=1, keepdims=True))
-            past_prob = jnp.exp2(past_size - top)
-            past_signed = past_prob.astype(LOW) * sign_of(past)
-        near_prob = jnp.exp2(near_size - top)
-        near_signed = near_prob.astype(LOW) * sign_of(near)
-        total = jnp.sum(near_prob, axis=1, keepdims=True)
-        mixed = each(lambda h: multiply(split(near_signed, h), projected_ref[here, column(2, h)]))
-        if row0 > 0:
-            total = total + jnp.sum(past_prob, axis=1, keepdims=True)
-            mixed = mixed + each(lambda h: multiply(split(past_signed, h), projected_ref[:row0, column(2, h)]))
+                past = jnp.where(past_key < length, past, FAR)
+            near = jnp.concatenate([past, near], axis=1)
+        top = jnp.max(near, axis=1, keepdims=True)
+        prob = jnp.exp2(near - top)
+        signed = prob.astype(LOW) * sign_of(scores)
+        total = jnp.sum(prob, axis=1, keepdims=True)
+        mixed = each(lambda h: multiply(split(signed, h), projected_ref[until, column(2, h)]))
         mixed = (mixed / total).astype(LOW)
         logs = top + jnp.log2(total)
         outs = [split(mixed, h) for h in range(heads)]

time: 189 us -> 189 us (level)
  transfers between devices with their start and end apart: 46 -> 46, of which waited for: 12 -> 13; matrix products, arithmetic and copies ran while one was open for 2% -> 2% of each run, Pallas kernels for 47% -> 47%
where the time goes in v7:
time: 189 us; the launch traced here: 185 us
  Pallas kernels  92.8 us (49%)
  starting transfers between devices  54.4 us (29%)
  waiting for transfers between devices  29.8 us (16%)
  other arithmetic  4.86 us (3%)
    ppermute x45, starting transfers between devices, swap(): return lax.ppermute(value, axis, [(i, i ^ bits) for i in range(size)])  48.7 us
    ppermute x45, waiting for transfers between devices, swap(): return lax.ppermute(value, axis, [(i, i ^ bits) for i in range(size)])  29.8 us
    pallas_call x1, Pallas kernels, attend_back(): pl.pallas_call(functools.partial(attend_back_kernel, chunks=chunks, rows=...  17.2 us
    pallas_call x4, Pallas kernels, feed(): pl.pallas_call(functools.partial(feed_kernel, begin=begin, size=size, hal...  15.8 us
    pallas_call x2, Pallas kernels, attend(): pl.pallas_call(functools.partial(attend_kernel, places=places, heads=head...  11.1 us
    pallas_call x1, Pallas kernels, weigh(): pl.pallas_call(weigh_kernel, grid_spec=pltpu.PrefetchScalarGridSpec(num_s...  9.61 us
    pallas_call x2, Pallas kernels, second_back(): pl.pallas_call(functools.partial(second_back_kernel, begin=begin, half=ha...  6.15 us
    all_to_all x1, starting transfers between devices, exchange_far(): return [lax.all_to_all(parts, 'batch', 0, 0, tiled=True)]  5.63 us
  transfers between devices with their start and end apart: 46, of which 13 were waited for; matrix products, arithmetic and copies ran while one was open for 2% of the time, Pallas kernels for 47%

profile of v7, /device:TPU:0, one launch (start us, length us, event | category | flops | bytes accessed | tf_op | source)
XLA Modules:
  0.0 185.4 jit_solution(153979577941929998)
XLA Ops:
  1.7 3.1 %collective-permute-start.1 = (bf16[96,896]{1,0:T(8,128)(2,1)S(1)}, bf16[96,896]{1,0:T(8,128)(2,1)S(1)}, u32[]{:S(2)}, u32[]{:S(2)}) collective-permute-start(bf16[96,896]{1,0:T(8,128)(2,1)S(1)} %pack.1.refs_0_), channel_id=1, source_target_pairs={{0,8},{4,12},{8,0},{12,4},{16,24},{20,28},{24,16},{28,20},{1,9},{5... | collective-permute-start | bytes 516104 | tf_op jit(solution)/shard_map/ppermute | solution.py:72
  4.8 2.6 %collective-permute-start.3 = (bf16[96,896]{1,0:T(8,128)(2,1)S(1)}, bf16[96,896]{1,0:T(8,128)(2,1)S(1)}, u32[]{:S(2)}, u32[]{:S(2)}) collective-permute-start(bf16[96,896]{1,0:T(8,128)(2,1)S(1)} %pack.1.refs_0_), channel_id=1, source_target_pairs={{0,16},{4,20},{8,24},{12,28},{16,0},{20,4},{24,8},{28,12},{1,17},{... | collective-permute-start | bytes 516104 | tf_op jit(solution)/shard_map/ppermute | solution.py:72
  8.9 3.8 %collective-permute-done.1.refs_2_ = bf16[96,896]{1,0:T(8,128)(2,1)S(1)} collective-permute-done((bf16[96,896]{1,0:T(8,128)(2,1)S(1)}, bf16[96,896]{1,0:T(8,128)(2,1)S(1)}, u32[]{:S(2)}, u32[]{:S(2)}) %collective-permute-start.1) | collective-permute-done | bytes 172064 | tf_op jit(solution)/shard_map/ppermute | solution.py:72
  12.8 1.7 collective-permute-start.2
  14.4 2.5 %collective-permute-start.5 = (bf16[96,896]{1,0:T(8,128)(2,1)S(1)}, bf16[96,896]{1,0:T(8,128)(2,1)S(1)}, u32[]{:S(2)}, u32[]{:S(2)}) collective-permute-start(bf16[96,896]{1,0:T(8,128)(2,1)S(1)} %pack.1.refs_0_), channel_id=1, source_target_pairs={{0,24},{4,28},{8,16},{12,20},{16,8},{20,12},{24,0},{28,4},{1,25},{... | collective-permute-start | bytes 516104 | tf_op jit(solution)/shard_map/ppermute | solution.py:72
  18.2 1.9 %collective-permute-start.4 = (bf16[96,896]{1,0:T(8,128)(2,1)S(1)}, bf16[96,896]{1,0:T(8,128)(2,1)S(1)}, u32[]{:S(2)}, u32[]{:S(2)}) collective-permute-start(bf16[96,896]{1,0:T(8,128)(2,1)S(1)} %collective-permute-done.3.refs_4_), channel_id=1, source_target_pairs={{0,4},{4,0},{8,12},{12,8},{16,20},{20,16},{24,28},{28,24},{1,5},{5... | collective-permute-start | bytes 516104 | tf_op jit(solution)/shard_map/ppermute | solution.py:72
  20.1 1.7 pad_maximum_fusion.refs_0_
  21.8 1.8 collective-permute-done.4.refs_5_
  23.6 1.9 %collective-permute-start.6 = (bf16[96,896]{1,0:T(8,128)(2,1)S(1)}, bf16[96,896]{1,0:T(8,128)(2,1)S(1)}, u32[]{:S(2)}, u32[]{:S(2)}) collective-permute-start(bf16[96,896]{1,0:T(8,128)(2,1)S(1)} %collective-permute-done.5.refs_6_), channel_id=1, source_target_pairs={{0,4},{4,0},{8,12},{12,8},{16,20},{20,16},{24,28},{28,24},{1,5},{5... | collective-permute-start | bytes 516104 | tf_op jit(solution)/shard_map/ppermute | solution.py:72
  26.1 2.9 %collective-permute-start.16 = (bf16[96,1536]{1,0:T(8,128)(2,1)}, bf16[96,1536]{1,0:T(8,128)(2,1)S(1)}, u32[]{:S(2)}, u32[]{:S(2)}) collective-permute-start(bf16[96,1536]{1,0:T(8,128)(2,1)} %pad_maximum_fusion.refs_0_), channel_id=1, source_target_pairs={{0,16},{4,20},{8,24},{12,28},{16,0},{20,4},{24,8},{28,12},{1,17},{... | collective-permute-start | bytes 884744 | tf_op jit(solution)/shard_map/ppermute | solution.py:72
  29.1 5.6 %project.1 = (bf16[1536,768]{1,0:T(8,128)(2,1)}, bf16[1536,576]{1,0:T(8,128)(2,1)S(1)}, f32[8,768]{1,0:T(8,128)S(1)}, bf16[768,896]{1,0:T(8,128)(2,1)S(1)}, bf16[192,768]{1,0:T(8,128)(2,1)S(1)}) custom-call(s32[4]{0:T(128)S(1)} %pad_add_fusion.scalar_ref, bf16[96,896]{1,0:T(8,128)(2,1)S(1)} %pack.1.refs_0_, ...), custom_call_target="tpu_custom_call" | custom-call | flops 4400000 | tf_op jit(solution)/shard_map/project/pallas_call | solution.py:153
  34.7 1.9 %collective-permute-start.8 = (bf16[96,1536]{1,0:T(8,128)(2,1)S(1)}, bf16[96,1536]{1,0:T(8,128)(2,1)S(1)}, u32[]{:S(2)}, u32[]{:S(2)}) collective-permute-start(bf16[96,1536]{1,0:T(8,128)(2,1)S(1)} %collective-permute-done.7.refs_2_), channel_id=1, source_target_pairs={{0,4},{4,0},{8,12},{12,8},{16,20},{20,16},{24,28},{28,24},{1,5},{5... | collective-permute-start | bytes 884744 | tf_op jit(solution)/shard_map/ppermute | solution.py:72
  37.3 6.4 %attend_forward.2 = (bf16[192,1024]{1,0:T(8,128)(2,1)S(1)}, f32[4,8,256]{2,1,0:T(8,128)S(1)}) custom-call(s32[4]{0:T(128)S(1)} %pad_add_fusion.scalar_ref, bf16[1536,576]{1,0:T(8,128)(2,1)S(1)} %get-tuple-element.157.projected_ref.refs_0_), custom_call_target="tpu_custom_call" | custom-call | flops 1100000 | tf_op jit(solution)/shard_map/attend_forward/pallas_call | solution.py:253
  43.7 2.1 %collective-permute-start.18 = (bf16[96,1536]{1,0:T(8,128)(2,1)S(1)}, bf16[96,1536]{1,0:T(8,128)(2,1)S(1)}, u32[]{:S(2)}, u32[]{:S(2)}) collective-permute-start(bf16[96,1536]{1,0:T(8,128)(2,1)S(1)} %collective-permute-done.16.refs_4_), channel_id=1, source_target_pairs={{0,8},{4,12},{8,0},{12,4},{16,24},{20,28},{24,16},{28,20},{1,9},{5... | collective-permute-start | bytes 884744 | tf_op jit(solution)/shard_map/ppermute | solution.py:72
  46.1 2.1 %collective-permute-start.20 = (bf16[192,1024]{1,0:T(8,128)(2,1)S(1)}, bf16[192,1024]{1,0:T(8,128)(2,1)S(1)}, u32[]{:S(2)}, u32[]{:S(2)}) collective-permute-start(bf16[192,1024]{1,0:T(8,128)(2,1)S(1)} %get-tuple-element.111.refs_2_), channel_id=1, source_target_pairs={{0,2},{1,3},{2,0},{3,1},{4,6},{5,7},{6,4},{7,5},{8,10},{9,11},{10,... | collective-permute-start | bytes 1179656 | tf_op jit(solution)/shard_map/ppermute | solution.py:72
  49.8 4.7 %attend_forward.3 = (bf16[192,512]{1,0:T(8,128)(2,1)S(1)}, f32[2,8,256]{2,1,0:T(8,128)S(1)}) custom-call(s32[4]{0:T(128)S(1)} %pad_add_fusion.scalar_ref, bf16[1536,576]{1,0:T(8,128)(2,1)S(1)} %get-tuple-element.157.projected_ref.refs_0_), custom_call_target="tpu_custom_call" | custom-call | flops 1100000 | tf_op jit(solution)/shard_map/attend_forward/pallas_call | solution.py:253
  55.1 3.3 %collective-permute-done.12.refs_7_ = bf16[192,768]{1,0:T(8,128)(2,1)S(1)} collective-permute-done((bf16[192,768]{1,0:T(8,128)(2,1)S(1)}, bf16[192,768]{1,0:T(8,128)(2,1)S(1)}, u32[]{:S(2)}, u32[]{:S(2)}) %collective-permute-start.12) | collective-permute-done | bytes 294944 | tf_op jit(solution)/shard_map/ppermute | solution.py:72
  58.5 1.7 collective-permute-start.9
  60.7 3.4 %collective-permute-done.9.refs_3_ = bf16[192,512]{1,0:T(8,128)(2,1)S(1)} collective-permute-done((bf16[192,512]{1,0:T(8,128)(2,1)S(1)}, bf16[192,512]{1,0:T(8,128)(2,1)S(1)}, u32[]{:S(2)}, u32[]{:S(2)}) %collective-permute-start.9) | collective-permute-done | bytes 196640 | tf_op jit(solution)/shard_map/ppermute | solution.py:72
  66.1 4.9 %feed_forward.4 = (bf16[512,768]{1,0:T(8,128)(2,1)S(1)}, f32[8,768]{1,0:T(8,128)S(1)}, bf16[1536,768]{1,0:T(8,128)(2,1)S(1)}, bf16[1536,768]{1,0:T(8,128)(2,1)S(1)}, bf16[1536,768]{1,0:T(8,128)(2,1)S(1)}) custom-call(s32[4]{0:T(128)S(1)} %pad_add_fusion.scalar_ref, bf16[1536,768]{1,0:T(8,128)(2,1)S(1)} %copy-done, bf16[1536,768]{1,0:T(8,128)(2,1)S(1)} %copy-done.1, ...), custom_call_target="tpu_custom_call" | custom-call | flops 563200 | tf_op jit(solution)/shard_map/feed_forward/pallas_call | solution.py:447
  71.1 2.9 %feed_forward.5 = (bf16[256,768]{1,0:T(8,128)(2,1)S(1)}, f32[8,768]{1,0:T(8,128)S(1)}, bf16[1536,768]{1,0:T(8,128)(2,1)S(1)}, bf16[1536,768]{1,0:T(8,128)(2,1)S(1)}, bf16[1536,768]{1,0:T(8,128)(2,1)S(1)}) custom-call(s32[4]{0:T(128)S(1)} %pad_add_fusion.scalar_ref, ...), custom_call_target="tpu_custom_call", output_to_operand_aliasing={{2}: (15, {}), {3}: (16, {}), {4}: (17, {})} | custom-call | flops 281600 | tf_op jit(solution)/shard_map/feed_forward/pallas_call | solution.py:447
  74.5 4.7 %feed_forward.6 = (bf16[512,768]{1,0:T(8,128)(2,1)S(1)}, f32[8,768]{1,0:T(8,128)S(1)}, bf16[1536,768]{1,0:T(8,128)(2,1)S(1)}, bf16[1536,768]{1,0:T(8,128)(2,1)S(...) custom-call(s32[4]{0:T(128)S(1)} %pad_add_fusion.scalar_ref, ...), custom_call_target="tpu_custom_call", output_to_operand_aliasing={{2}: (15, {}), {3}: (16, {}), {4}: (17, {})} | custom-call | flops 563200 | tf_op jit(solution)/shard_map/feed_forward/pallas_call | solution.py:447
  80.2 1.7 collective-permute-start.26
  81.9 3.3 %feed_forward.7 = (bf16[256,768]{1,0:T(8,128)(2,1)S(1)}, f32[8,768]{1,0:T(8,128)S(1)}, bf16[1536,768]{1,0:T(8,128)(2,1)S(1)}, bf16[1536,768]{1,0:T(8,128)(2,1)S(...) custom-call(s32[4]{0:T(128)S(1)} %pad_add_fusion.scalar_ref, ...), custom_call_target="tpu_custom_call", output_to_operand_aliasing={{2}: (15, {}), {3}: (16, {}), {4}: (17, {})} | custom-call | flops 281600 | tf_op jit(solution)/shard_map/feed_forward/pallas_call | solution.py:447
  87.3 9.6 %feed_forward_weights.1 = (bf16[768,768]{1,0:T(8,128)(2,1)}, bf16[768,768]{1,0:T(8,128)(2,1)}, bf16[768,1536]{1,0:T(8,128)(2,1)}) custom-call(s32[4]{0:T(128)S(1)} %pad_add_fusion.scalar_ref, bf16[1536,768]{1,0:T(8,128)(2,1)S(1)} %get-tuple-element.150.normed_ref, bf16[1536,768]{1,0:T(8,128)(2,1)S(1)} %get-tuple-element.151.upper_ref, ...), custom_call_target="tpu_custom_call" | custom-call | flops 1100000 | tf_op jit(solution)/shard_map/feed_forward_weights/pallas_call | solution.py:522
  96.9 5.6 %all-to-all-start = ((bf16[8,96,1536]{2,1,0:T(8,128)(2,1)}), bf16[8,96,1536]{2,1,0:T(8,128)(2,1)}, u32[]{:S(2)}, u32[]{:S(2)}) async-start(bf16[8,96,1536]{2,1,0:T(8,128)(2,1)} %bitcast.6), calls=%async_computation | async-start | bytes 4718592 | tf_op jit(solution)/shard_map/all_to_all | solution.py:803
  102.6 3.8 %second_norm_backward.2.refs_6_ = bf16[512,768]{1,0:T(8,128)(2,1)S(1)} custom-call(s32[4]{0:T(128)S(1)} %pad_add_fusion.scalar_ref, bf16[512,768]{1,0:T(8,128)(2,1)} %add_convert_fusion.1.mine_ref, bf16[512,768]{1,0:T(8,128)(2,1)} %collective-permute-done.26.other_ref, f32[512,768]{1,0:T(8,128)} %get-tuple-element.162.hidden_ref.refs_0_, ...), custom_call_target="tpu_custom_call" | custom-call | flops 1100000 | tf_op jit(solution)/shard_map/second_norm_backward/pallas_call | solution.py:589
  106.9 1.6 collective-permute-done.29.other_ref
  108.6 2.4 %second_norm_backward.3.refs_8_ = bf16[256,768]{1,0:T(8,128)(2,1)S(1)} custom-call(s32[4]{0:T(128)S(1)} %pad_add_fusion.scalar_ref, bf16[256,768]{1,0:T(8,128)(2,1)} %add_convert_fusion.4.mine_ref, bf16[256,768]{1,0:T(8,128)(2,1)} %collective-permute-done.29.other_ref, f32[256,768]{1,0:T(8,128)S(1)} %copy-done.8, bf16[1536,768]{1,0:T(8,128)(2,1)} %grad_ref.5, ...), custom_call_target="tpu_custom_call" | custom-call | flops 44000002048 | tf_op jit(solution)/shard_map/second_norm_backward/pallas_call | solution.py:589
  111.4 1.7 collective-permute-start.27
  113.1 17.2 %attend_backward.1 = (bf16[576,1536]{1,0:T(8,128)(2,1)S(1)}, bf16[768,192]{1,0:T(8,128)(2,1)S(1)}, bf16[1536,768]{1,0:T(8,128)(2,1)S(1)}) custom-call(s32[4]{0:T(128)S(1)} %pad_add_fusion.scalar_ref, bf16[1536,576]{1,0:T(8,128)(2,1)S(1)} %copy-done.3, bf16[192,768]{1,0:T(8,128)(2,1)S(1)} %get-tuple-element.114.refs_6_.refs_1_, ...), custom_call_target="tpu_custom_call" | custom-call | flops 8800000 | tf_op jit(solution)/shard_map/attend_backward/pallas_call | solution.py:351
  130.3 2.3 %projection_weights.1 = (bf16[4,96,768]{2,1,0:T(8,128)(2,1)S(1)}, bf16[4,96,768]{2,1,0:T(8,128)(2,1)S(1)}) custom-call(s32[4]{0:T(128)S(1)} %pad_add_fusion.scalar_ref, bf16[576,1536]{1,0:T(8,128)(2,1)S(1)} %get-tuple-element.169.grads_ref, bf16[1536,768]{1,0:T(8,128)(2,1)S(1)} %copy-done.6, bf16[768,192]{1,0:T(8,128)(2,1)S(1)} %get-tuple-element.167.outs_ref), custom_call_target="tpu_custom_call" | custom-call | flops 1100000 | tf_op jit(solution)/shard_map/projection_weights/pallas_call | solution.py:659
  132.7 1.9 %grad_normed.2 = (bf16[768,768]{1,0:T(8,128)(2,1)S(1)}, f32[8,768]{1,0:T(8,128)S(1)}) custom-call(s32[4]{0:T(128)S(1)} %pad_add_fusion.scalar_ref, bf16[576,1536]{1,0:T(8,128)(2,1)S(1)} %get-tuple-element.169.grads_ref, bf16[1536,768]{1,0:T(8,128)(2,1)S(1)} %copy-done, bf16[768,896]{1,0:T(8,128)(2,1)S(1)} %copy-done.5, f32[8,768]{1,0:T(8,128)S(1)} %get-tuple-element.171.ahead_ref), custom_call_target="tpu_custom_call" | custom-call | flops 1100000 | tf_op jit(solution)/shard_map/grad_normed/pallas_call | solution.py:622
  134.9 2.0 %collective-permute-start.36 = (bf16[4,96,768]{2,1,0:T(8,128)(2,1)S(1)}, bf16[4,96,768]{2,1,0:T(8,128)(2,1)S(1)}, u32[]{:S(2)}, u32[]{:S(2)}) collective-permute-start(bf16[4,96,768]{2,1,0:T(8,128)(2,1)S(1)} %get-tuple-element.183), channel_id=1, source_target_pairs={{0,4},{4,0},{8,12},{12,8},{16,20},{20,16},{24,28},{28,24},{1,5},{5... | collective-permute-start | bytes 1769480 | tf_op jit(solution)/shard_map/ppermute | solution.py:72
  136.9 1.9 %grad_normed.3 = (bf16[768,768]{1,0:T(8,128)(2,1)S(1)}, f32[8,768]{1,0:T(8,128)S(1)}) custom-call(s32[4]{0:T(128)S(1)} %pad_add_fusion.scalar_ref, bf16[576,1536]{1,0:T(8,128)(2,1)S(1)} %get-tuple-element.169.grads_ref, bf16[1536,768]{1,0:T(8,128)(2,1)S(1)} %copy-done, bf16[768,896]{1,0:T(8,128)(2,1)S(1)} %copy-done.5, f32[8,768]{1,0:T(8,128)S(1)} %get-tuple-element.172.ahead_ref), custom_call_target="tpu_custom_call" | custom-call | flops 1100000 | tf_op jit(solution)/shard_map/grad_normed/pallas_call | solution.py:622
  140.1 1.7 collective-permute-start.34
  142.1 1.9 %collective-permute-start.37 = (f32[8,768]{1,0:T(8,128)S(1)}, f32[8,768]{1,0:T(8,128)S(1)}, u32[]{:S(2)}, u32[]{:S(2)}) collective-permute-start(f32[8,768]{1,0:T(8,128)S(1)} %get-tuple-element.184.refs_0_), channel_id=1, source_target_pairs={{0,4},{4,0},{8,12},{12,8},{16,20},{20,16},{24,28},{28,24},{1,5},{5... | collective-permute-start | bytes 73736 | tf_op jit(solution)/shard_map/ppermute | solution.py:72
  144.1 3.9 %layer_out.1 = (bf16[384,768]{1,0:T(8,128)(2,1)}, bf16[384,768]{1,0:T(8,128)(2,1)}, bf16[1536,768]{1,0:T(8,128)(2,1)}) custom-call(s32[4]{0:T(128)S(1)} %pad_add_fusion.scalar_ref, bf16[768,768]{1,0:T(8,128)(2,1)S(1)} %add_convert_fusion.mine_ref, bf16[768,768]{1,0:T(8,128)(2,1)S(1)} %collective-permute-done.27.other_ref, ...), custom_call_target="tpu_custom_call" | custom-call | flops 1100000 | tf_op jit(solution)/shard_map/layer_out/pallas_call | solution.py:685
  148.0 7.5 %collective-permute-done.37.refs_1_ = f32[8,768]{1,0:T(8,128)S(1)} collective-permute-done((f32[8,768]{1,0:T(8,128)S(1)}, f32[8,768]{1,0:T(8,128)S(1)}, u32[]{:S(2)}, u32[]{:S(2)}) %collective-permute-start.37) | collective-permute-done | bytes 24608 | tf_op jit(solution)/shard_map/ppermute | solution.py:72
  157.0 3.9 %collective-permute-start.39 = (bf16[96,896]{1,0:T(8,128)(2,1)}, bf16[96,896]{1,0:T(8,128)(2,1)S(1)}, u32[]{:S(2)}, u32[]{:S(2)}) collective-permute-start(bf16[96,896]{1,0:T(8,128)(2,1)} %get-tuple-element.192), channel_id=1, source_target_pairs={{0,8},{4,12},{8,0},{12,4},{16,24},{20,28},{24,16},{28,20},{1,9},{5... | collective-permute-start | bytes 516104 | tf_op jit(solution)/shard_map/ppermute | solution.py:72
  161.4 1.9 %collective-permute-start.41 = (bf16[96,896]{1,0:T(8,128)(2,1)}, bf16[96,896]{1,0:T(8,128)(2,1)}, u32[]{:S(2)}, u32[]{:S(2)}) collective-permute-start(bf16[96,896]{1,0:T(8,128)(2,1)} %get-tuple-element.194), channel_id=1, source_target_pairs={{0,24},{4,28},{8,16},{12,20},{16,8},{20,12},{24,0},{28,4},{1,25},{... | collective-permute-start | bytes 516104 | tf_op jit(solution)/shard_map/ppermute | solution.py:72
  163.3 2.5 %first_norm_backward.2 = (bf16[384,768]{1,0:T(8,128)(2,1)}, bf16[1536,768]{1,0:T(8,128)(2,1)}) custom-call(s32[4]{0:T(128)S(1)} %pad_add_fusion.scalar_ref, bf16[384,768]{1,0:T(8,128)(2,1)S(1)} %get-tuple-element.179.mine_ref, bf16[384,768]{1,0:T(8,128)(2,1)S(1)} %collective-permute-done.34.other_ref, bf16[1536,768]{1,0:T(8,128)(2,1)S(1)} %copy-done, ...), custom_call_target="tpu_custom_call" | custom-call | flops 1100000 | tf_op jit(solution)/shard_map/first_norm_backward/pallas_call | solution.py:719
  165.7 2.1 %collective-permute-done.38.other_ref = bf16[384,768]{1,0:T(8,128)(2,1)S(1)} collective-permute-done((bf16[384,768]{1,0:T(8,128)(2,1)S(1)}, bf16[384,768]{1,0:T(8,128)(2,1)S(1)}, u32[]{:S(2)}, u32[]{:S(2)}) %collective-permute-start.38) | collective-permute-done | bytes 589856 | tf_op jit(solution)/shard_map/ppermute | solution.py:72
  167.8 2.5 %first_norm_backward.3 = (bf16[384,768]{1,0:T(8,128)(2,1)}, bf16[1536,768]{1,0:T(8,128)(2,1)}) custom-call(s32[4]{0:T(128)S(1)} %pad_add_fusion.scalar_ref, bf16[384,768]{1,0:T(8,128)(2,1)S(1)} %get-tuple-element.186.mine_ref, bf16[384,768]{1,0:T(8,128)(2,1)S(1)} %collective-permute-done.38.other_ref, ...), custom_call_target="tpu_custom_call", output_to_operand_aliasing={{1}: (6, {})} | custom-call | flops 1100000 | tf_op jit(solution)/shard_map/first_norm_backward/pallas_call | solution.py:719
  170.3 2.8 %total.3 = (f32[96,768]{1,0:T(8,128)}, f32[96,768]{1,0:T(8,128)}) custom-call(bf16[8,96,1536]{2,1,0:T(8,128)(2,1)} %all-to-all-done.refs_0_), custom_call_target="tpu_custom_call" | custom-call | flops 1100000 | tf_op jit(solution)/shard_map/total/pallas_call | solution.py:788
  173.5 3.1 %collective-permute-done.40.refs_2_ = bf16[96,896]{1,0:T(8,128)(2,1)S(1)} collective-permute-done((bf16[96,896]{1,0:T(8,128)(2,1)}, bf16[96,896]{1,0:T(8,128)(2,1)S(1)}, u32[]{:S(2)}, u32[]{:S(2)}) %collective-permute-start.40) | collective-permute-done | bytes 172064 | tf_op jit(solution)/shard_map/ppermute | solution.py:72
  179.1 1.8 total.5
  181.4 3.1 %place.1 = (bf16[1536,768]{1,0:T(8,128)(2,1)}, bf16[1536,768]{1,0:T(8,128)(2,1)}) custom-call(s32[4]{0:T(128)S(1)} %pad_add_fusion.scalar_ref, bf16[384,768]{1,0:T(8,128)(2,1)S(1)} %collective-permute-done.32.refs_0_, bf16[384,768]{1,0:T(8,128)(2,1)} %collective-permute-done.33.refs_1_, ...), custom_call_target="tpu_custom_call", output_to_operand_aliasing={{0}: (5, {}), {1}: (6, {})} | custom-call | flops 1100000 | tf_op jit(solution)/shard_map/place/pallas_call | solution.py:752
  (108 shorter events, 22.4 us)
Async XLA Ops:
  1.7 11.0 %collective-permute-start.1 = (bf16[96,896]{1,0:T(8,128)(2,1)S(1)}, bf16[96,896]{1,0:T(8,128)(2,1)S(1)}, u32[]{:S(2)}, u32[]{:S(2)}) collective-permute-start(bf16[96,896]{1,0:T(8,128)(2,1)S(1)} %pack.1.refs_0_), channel_id=1, source_target_pairs={{0,8},{4,12},{8,0},{12,4},{16,24},{20,28},{24,16},{28,20},{1,9},{5... | collective-permute-start | bytes 516104 | tf_op jit(solution)/shard_map/ppermute | solution.py:72
  4.8 12.1 %collective-permute-start.3 = (bf16[96,896]{1,0:T(8,128)(2,1)S(1)}, bf16[96,896]{1,0:T(8,128)(2,1)S(1)}, u32[]{:S(2)}, u32[]{:S(2)}) collective-permute-start(bf16[96,896]{1,0:T(8,128)(2,1)S(1)} %pack.1.refs_0_), channel_id=1, source_target_pairs={{0,16},{4,20},{8,24},{12,28},{16,0},{20,4},{24,8},{28,12},{1,17},{... | collective-permute-start | bytes 516104 | tf_op jit(solution)/shard_map/ppermute | solution.py:72
  7.4 9.5 %collective-permute-start = (bf16[96,896]{1,0:T(8,128)(2,1)S(1)}, bf16[96,896]{1,0:T(8,128)(2,1)S(1)}, u32[]{:S(2)}, u32[]{:S(2)}) collective-permute-start(bf16[96,896]{1,0:T(8,128)(2,1)S(1)} %pack.1.refs_0_), channel_id=1, source_target_pairs={{0,4},{4,0},{8,12},{12,8},{16,20},{20,16},{24,28},{28,24},{1,5},{5... | collective-permute-start | bytes 516104 | tf_op jit(solution)/shard_map/ppermute | solution.py:72
  12.8 5.4 %collective-permute-start.2 = (bf16[96,896]{1,0:T(8,128)(2,1)S(1)}, bf16[96,896]{1,0:T(8,128)(2,1)S(1)}, u32[]{:S(2)}, u32[]{:S(2)}) collective-permute-start(bf16[96,896]{1,0:T(8,128)(2,1)S(1)} %collective-permute-done.1.refs_2_), channel_id=1, source_target_pairs={{0,4},{4,0},{8,12},{12,8},{16,20},{20,16},{24,28},{28,24},{1,5},{5... | collective-permute-start | bytes 516104 | tf_op jit(solution)/shard_map/ppermute | solution.py:72
  14.4 7.3 %collective-permute-start.5 = (bf16[96,896]{1,0:T(8,128)(2,1)S(1)}, bf16[96,896]{1,0:T(8,128)(2,1)S(1)}, u32[]{:S(2)}, u32[]{:S(2)}) collective-permute-start(bf16[96,896]{1,0:T(8,128)(2,1)S(1)} %pack.1.refs_0_), channel_id=1, source_target_pairs={{0,24},{4,28},{8,16},{12,20},{16,8},{20,12},{24,0},{28,4},{1,25},{... | collective-permute-start | bytes 516104 | tf_op jit(solution)/shard_map/ppermute | solution.py:72
  18.2 5.4 %collective-permute-start.4 = (bf16[96,896]{1,0:T(8,128)(2,1)S(1)}, bf16[96,896]{1,0:T(8,128)(2,1)S(1)}, u32[]{:S(2)}, u32[]{:S(2)}) collective-permute-start(bf16[96,896]{1,0:T(8,128)(2,1)S(1)} %collective-permute-done.3.refs_4_), channel_id=1, source_target_pairs={{0,4},{4,0},{8,12},{12,8},{16,20},{20,16},{24,28},{28,24},{1,5},{5... | collective-permute-start | bytes 516104 | tf_op jit(solution)/shard_map/ppermute | solution.py:72
  23.6 11.1 %collective-permute-start.7 = (bf16[96,1536]{1,0:T(8,128)(2,1)}, bf16[96,1536]{1,0:T(8,128)(2,1)S(1)}, u32[]{:S(2)}, u32[]{:S(2)}) collective-permute-start(bf16[96,1536]{1,0:T(8,128)(2,1)} %pad_maximum_fusion.refs_0_), channel_id=1, source_target_pairs={{0,8},{4,12},{8,0},{12,4},{16,24},{20,28},{24,16},{28,20},{1,9},{5... | collective-permute-start | bytes 884744 | tf_op jit(solution)/shard_map/ppermute | solution.py:72
  23.6 5.5 %collective-permute-start.6 = (bf16[96,896]{1,0:T(8,128)(2,1)S(1)}, bf16[96,896]{1,0:T(8,128)(2,1)S(1)}, u32[]{:S(2)}, u32[]{:S(2)}) collective-permute-start(bf16[96,896]{1,0:T(8,128)(2,1)S(1)} %collective-permute-done.5.refs_6_), channel_id=1, source_target_pairs={{0,4},{4,0},{8,12},{12,8},{16,20},{20,16},{24,28},{28,24},{1,5},{5... | collective-permute-start | bytes 516104 | tf_op jit(solution)/shard_map/ppermute | solution.py:72
  26.1 17.5 %collective-permute-start.16 = (bf16[96,1536]{1,0:T(8,128)(2,1)}, bf16[96,1536]{1,0:T(8,128)(2,1)S(1)}, u32[]{:S(2)}, u32[]{:S(2)}) collective-permute-start(bf16[96,1536]{1,0:T(8,128)(2,1)} %pad_maximum_fusion.refs_0_), channel_id=1, source_target_pairs={{0,16},{4,20},{8,24},{12,28},{16,0},{20,4},{24,8},{28,12},{1,17},{... | collective-permute-start | bytes 884744 | tf_op jit(solution)/shard_map/ppermute | solution.py:72
  34.7 13.5 %collective-permute-start.8 = (bf16[96,1536]{1,0:T(8,128)(2,1)S(1)}, bf16[96,1536]{1,0:T(8,128)(2,1)S(1)}, u32[]{:S(2)}, u32[]{:S(2)}) collective-permute-start(bf16[96,1536]{1,0:T(8,128)(2,1)S(1)} %collective-permute-done.7.refs_2_), channel_id=1, source_target_pairs={{0,4},{4,0},{8,12},{12,8},{16,20},{20,16},{24,28},{28,24},{1,5},{5... | collective-permute-start | bytes 884744 | tf_op jit(solution)/shard_map/ppermute | solution.py:72
  37.3 27.4 %copy-start.10 = (bf16[96,1536]{1,0:T(8,128)(2,1)S(1)}, bf16[96,1536]{1,0:T(8,128)(2,1)}, u32[]{:S(2)}) copy-start(bf16[96,1536]{1,0:T(8,128)(2,1)} %copy-done.9) | copy-start | bytes 884740
  37.3 28.7 %copy-start.1 = (bf16[1536,768]{1,0:T(8,128)(2,1)S(1)}, bf16[1536,768]{1,0:T(8,128)(2,1)}, u32[]{:S(2)}) copy-start(bf16[1536,768]{1,0:T(8,128)(2,1)} %grad_ref.5) | copy-start | bytes 7077892
  43.7 10.9 %collective-permute-start.18 = (bf16[96,1536]{1,0:T(8,128)(2,1)S(1)}, bf16[96,1536]{1,0:T(8,128)(2,1)S(1)}, u32[]{:S(2)}, u32[]{:S(2)}) collective-permute-start(bf16[96,1536]{1,0:T(8,128)(2,1)S(1)} %collective-permute-done.16.refs_4_), channel_id=1, source_target_pairs={{0,8},{4,12},{8,0},{12,4},{16,24},{20,28},{24,16},{28,20},{1,9},{5... | collective-permute-start | bytes 884744 | tf_op jit(solution)/shard_map/ppermute | solution.py:72
  45.8 9.4 %collective-permute-start.15 = (bf16[96,1536]{1,0:T(8,128)(2,1)}, bf16[96,1536]{1,0:T(8,128)(2,1)S(1)}, u32[]{:S(2)}, u32[]{:S(2)}) collective-permute-start(bf16[96,1536]{1,0:T(8,128)(2,1)} %pad_maximum_fusion.refs_0_), channel_id=1, source_target_pairs={{0,4},{4,0},{8,12},{12,8},{16,20},{20,16},{24,28},{28,24},{1,5},{5... | collective-permute-start | bytes 884744 | tf_op jit(solution)/shard_map/ppermute | solution.py:72
  46.1 14.1 %collective-permute-start.20 = (bf16[192,1024]{1,0:T(8,128)(2,1)S(1)}, bf16[192,1024]{1,0:T(8,128)(2,1)S(1)}, u32[]{:S(2)}, u32[]{:S(2)}) collective-permute-start(bf16[192,1024]{1,0:T(8,128)(2,1)S(1)} %get-tuple-element.111.refs_2_), channel_id=1, source_target_pairs={{0,2},{1,3},{2,0},{3,1},{4,6},{5,7},{6,4},{7,5},{8,10},{9,11},{10,... | collective-permute-start | bytes 1179656 | tf_op jit(solution)/shard_map/ppermute | solution.py:72
  48.2 10.3 %collective-permute-start.12 = (bf16[192,768]{1,0:T(8,128)(2,1)S(1)}, bf16[192,768]{1,0:T(8,128)(2,1)S(1)}, u32[]{:S(2)}, u32[]{:S(2)}) collective-permute-start(bf16[192,768]{1,0:T(8,128)(2,1)S(1)} %get-tuple-element.114.refs_6_.refs_1_), channel_id=1, source_target_pairs={{0,2},{1,3},{2,0},{3,1},{4,6},{5,7},{6,4},{7,5},{8,10},{9,11},{10,... | collective-permute-start | bytes 884744 | tf_op jit(solution)/shard_map/ppermute | solution.py:72
  48.2 11.9 %collective-permute-start.17 = (bf16[96,1536]{1,0:T(8,128)(2,1)S(1)}, bf16[96,1536]{1,0:T(8,128)(2,1)S(1)}, u32[]{:S(2)}, u32[]{:S(2)}) collective-permute-start(bf16[96,1536]{1,0:T(8,128)(2,1)S(1)} %collective-permute-done.16.refs_4_), channel_id=1, source_target_pairs={{0,4},{4,0},{8,12},{12,8},{16,20},{20,16},{24,28},{28,24},{1,5},{5... | collective-permute-start | bytes 884744 | tf_op jit(solution)/shard_map/ppermute | solution.py:72
  54.6 9.6 %collective-permute-start.19 = (bf16[96,1536]{1,0:T(8,128)(2,1)S(1)}, bf16[96,1536]{1,0:T(8,128)(2,1)S(1)}, u32[]{:S(2)}, u32[]{:S(2)}) collective-permute-start(bf16[96,1536]{1,0:T(8,128)(2,1)S(1)} %collective-permute-done.18.refs_6_), channel_id=1, source_target_pairs={{0,4},{4,0},{8,12},{12,8},{16,20},{20,16},{24,28},{28,24},{1,5},{5... | collective-permute-start | bytes 884744 | tf_op jit(solution)/shard_map/ppermute | solution.py:72
  55.1 5.5 %collective-permute-start.10 = (bf16[192,512]{1,0:T(8,128)(2,1)S(1)}, bf16[192,512]{1,0:T(8,128)(2,1)S(1)}, u32[]{:S(2)}, u32[]{:S(2)}) collective-permute-start(bf16[192,512]{1,0:T(8,128)(2,1)S(1)} %get-tuple-element.117.refs_2_.refs_3_), channel_id=1, source_target_pairs={{0,1},{1,0},{2,3},{3,2},{4,5},{5,4},{6,7},{7,6},{8,9},{9,8},{10,11... | collective-permute-start | bytes 589832 | tf_op jit(solution)/shard_map/ppermute | solution.py:72
  58.5 5.7 %collective-permute-start.9 = (bf16[192,512]{1,0:T(8,128)(2,1)S(1)}, bf16[192,512]{1,0:T(8,128)(2,1)S(1)}, u32[]{:S(2)}, u32[]{:S(2)}) collective-permute-start(bf16[192,512]{1,0:T(8,128)(2,1)S(1)} %get-tuple-element.117.refs_2_.refs_3_), channel_id=1, source_target_pairs={{0,2},{1,3},{2,0},{3,1},{4,6},{5,7},{6,4},{7,5},{8,10},{9,11},{10,... | collective-permute-start | bytes 589832 | tf_op jit(solution)/shard_map/ppermute | solution.py:72
  60.1 5.9 %collective-permute-start.21 = (bf16[192,1024]{1,0:T(8,128)(2,1)S(1)}, bf16[192,1024]{1,0:T(8,128)(2,1)S(1)}, u32[]{:S(2)}, u32[]{:S(2)}) collective-permute-start(bf16[192,1024]{1,0:T(8,128)(2,1)S(1)} %get-tuple-element.111.refs_2_), channel_id=1, source_target_pairs={{0,1},{1,0},{2,3},{3,2},{4,5},{5,4},{6,7},{7,6},{8,9},{9,8},{10,11... | collective-permute-start | bytes 1179656 | tf_op jit(solution)/shard_map/ppermute | solution.py:72
  60.1 5.9 %collective-permute-start.22 = (bf16[192,1024]{1,0:T(8,128)(2,1)S(1)}, bf16[192,1024]{1,0:T(8,128)(2,1)S(1)}, u32[]{:S(2)}, u32[]{:S(2)}) collective-permute-start(bf16[192,1024]{1,0:T(8,128)(2,1)S(1)} %collective-permute-done.20.refs_3_), channel_id=1, source_target_pairs={{0,1},{1,0},{2,3},{3,2},{4,5},{5,4},{6,7},{7,6},{8,9},{9,8},{10,11... | collective-permute-start | bytes 1179656 | tf_op jit(solution)/shard_map/ppermute | solution.py:72
  60.7 5.3 %collective-permute-start.13 = (bf16[192,768]{1,0:T(8,128)(2,1)S(1)}, bf16[192,768]{1,0:T(8,128)(2,1)S(1)}, u32[]{:S(2)}, u32[]{:S(2)}) collective-permute-start(bf16[192,768]{1,0:T(8,128)(2,1)S(1)} %get-tuple-element.114.refs_6_.refs_1_), channel_id=1, source_target_pairs={{0,1},{1,0},{2,3},{3,2},{4,5},{5,4},{6,7},{7,6},{8,9},{9,8},{10,11... | collective-permute-start | bytes 884744 | tf_op jit(solution)/shard_map/ppermute | solution.py:72
  64.1 1.9 %collective-permute-start.14 = (bf16[192,768]{1,0:T(8,128)(2,1)S(1)}, bf16[192,768]{1,0:T(8,128)(2,1)S(1)}, u32[]{:S(2)}, u32[]{:S(2)}) collective-permute-start(bf16[192,768]{1,0:T(8,128)(2,1)S(1)} %collective-permute-done.12.refs_7_), channel_id=1, source_target_pairs={{0,1},{1,0},{2,3},{3,2},{4,5},{5,4},{6,7},{7,6},{8,9},{9,8},{10,11... | collective-permute-start | bytes 884744 | tf_op jit(solution)/shard_map/ppermute | solution.py:72
  64.1 1.9 %collective-permute-start.11 = (bf16[192,512]{1,0:T(8,128)(2,1)S(1)}, bf16[192,512]{1,0:T(8,128)(2,1)S(1)}, u32[]{:S(2)}, u32[]{:S(2)}) collective-permute-start(bf16[192,512]{1,0:T(8,128)(2,1)S(1)} %collective-permute-done.9.refs_3_), channel_id=1, source_target_pairs={{0,1},{1,0},{2,3},{3,2},{4,5},{5,4},{6,7},{7,6},{8,9},{9,8},{10,11... | collective-permute-start | bytes 589832 | tf_op jit(solution)/shard_map/ppermute | solution.py:72
  70.9 8.2 %collective-permute-start.23 = (bf16[512,768]{1,0:T(8,128)(2,1)S(1)}, bf16[512,768]{1,0:T(8,128)(2,1)S(1)}, u32[]{:S(2)}, u32[]{:S(2)}) collective-permute-start(bf16[512,768]{1,0:T(8,128)(2,1)S(1)} %get-tuple-element.141), channel_id=1, source_target_pairs={{0,1},{1,0},{2,3},{3,2},{4,5},{5,4},{6,7},{7,6},{8,9},{9,8},{10,11... | collective-permute-start | bytes 2359304 | tf_op jit(solution)/shard_map/ppermute | solution.py:72
  74.0 12.1 %collective-permute-start.24 = (bf16[256,768]{1,0:T(8,128)(2,1)S(1)}, bf16[256,768]{1,0:T(8,128)(2,1)S(1)}, u32[]{:S(2)}, u32[]{:S(2)}) collective-permute-start(bf16[256,768]{1,0:T(8,128)(2,1)S(1)} %get-tuple-element.149), channel_id=1, source_target_pairs={{0,1},{1,0},{2,3},{3,2},{4,5},{5,4},{6,7},{7,6},{8,9},{9,8},{10,11... | collective-permute-start | bytes 1179656 | tf_op jit(solution)/shard_map/ppermute | solution.py:72
  80.2 22.3 %collective-permute-start.26 = (bf16[512,768]{1,0:T(8,128)(2,1)}, bf16[512,768]{1,0:T(8,128)(2,1)}, u32[]{:S(2)}, u32[]{:S(2)}) collective-permute-start(bf16[512,768]{1,0:T(8,128)(2,1)} %add_convert_fusion.1.mine_ref), channel_id=1, source_target_pairs={{0,2},{1,3},{2,0},{3,1},{4,6},{5,7},{6,4},{7,5},{8,10},{9,11},{10,... | collective-permute-start | bytes 2359304 | tf_op jit(solution)/shard_map/ppermute | solution.py:72
  86.9 21.6 %collective-permute-start.29 = (bf16[256,768]{1,0:T(8,128)(2,1)}, bf16[256,768]{1,0:T(8,128)(2,1)}, u32[]{:S(2)}, u32[]{:S(2)}) collective-permute-start(bf16[256,768]{1,0:T(8,128)(2,1)} %add_convert_fusion.4.mine_ref), channel_id=1, source_target_pairs={{0,2},{1,3},{2,0},{3,1},{4,6},{5,7},{6,4},{7,5},{8,10},{9,11},{10,... | collective-permute-start | bytes 1179656 | tf_op jit(solution)/shard_map/ppermute | solution.py:72
  96.9 73.3 %all-to-all-start = ((bf16[8,96,1536]{2,1,0:T(8,128)(2,1)}), bf16[8,96,1536]{2,1,0:T(8,128)(2,1)}, u32[]{:S(2)}, u32[]{:S(2)}) async-start(bf16[8,96,1536]{2,1,0:T(8,128)(2,1)} %bitcast.6), calls=%async_computation | async-start | bytes 4718592 | tf_op jit(solution)/shard_map/all_to_all | solution.py:803
  102.6 8.5 %collective-permute-start.25 = (bf16[768,768]{1,0:T(8,128)(2,1)}, bf16[768,768]{1,0:T(8,128)(2,1)S(1)}, u32[]{:S(2)}, u32[]{:S(2)}) collective-permute-start(bf16[768,768]{1,0:T(8,128)(2,1)} %get-tuple-element.154), channel_id=1, source_target_pairs={{0,1},{1,0},{2,3},{3,2},{4,5},{5,4},{6,7},{7,6},{8,9},{9,8},{10,11... | collective-permute-start | bytes 3538952 | tf_op jit(solution)/shard_map/ppermute | solution.py:72
  106.4 6.7 %collective-permute-start.28 = (bf16[512,768]{1,0:T(8,128)(2,1)S(1)}, bf16[512,768]{1,0:T(8,128)(2,1)S(1)}, u32[]{:S(2)}, u32[]{:S(2)}) collective-permute-start(bf16[512,768]{1,0:T(8,128)(2,1)S(1)} %second_norm_backward.2.refs_6_), channel_id=1, source_target_pairs={{0,1},{1,0},{2,3},{3,2},{4,5},{5,4},{6,7},{7,6},{8,9},{9,8},{10,11... | collective-permute-start | bytes 2359304 | tf_op jit(solution)/shard_map/ppermute | solution.py:72
  111.0 2.1 %collective-permute-start.30 = (bf16[256,768]{1,0:T(8,128)(2,1)S(1)}, bf16[256,768]{1,0:T(8,128)(2,1)S(1)}, u32[]{:S(2)}, u32[]{:S(2)}) collective-permute-start(bf16[256,768]{1,0:T(8,128)(2,1)S(1)} %second_norm_backward.3.refs_8_), channel_id=1, source_target_pairs={{0,1},{1,0},{2,3},{3,2},{4,5},{5,4},{6,7},{7,6},{8,9},{9,8},{10,11... | collective-permute-start | bytes 1179656 | tf_op jit(solution)/shard_map/ppermute | solution.py:72
  111.4 28.4 %collective-permute-start.27 = (bf16[768,768]{1,0:T(8,128)(2,1)S(1)}, bf16[768,768]{1,0:T(8,128)(2,1)S(1)}, u32[]{:S(2)}, u32[]{:S(2)}) collective-permute-start(bf16[768,768]{1,0:T(8,128)(2,1)S(1)} %add_convert_fusion.mine_ref), channel_id=1, source_target_pairs={{0,2},{1,3},{2,0},{3,1},{4,6},{5,7},{6,4},{7,5},{8,10},{9,11},{10,... | collective-permute-start | bytes 3538952 | tf_op jit(solution)/shard_map/ppermute | solution.py:72
  134.6 5.2 %collective-permute-start.31 = (bf16[768,768]{1,0:T(8,128)(2,1)S(1)}, bf16[768,768]{1,0:T(8,128)(2,1)S(1)}, u32[]{:S(2)}, u32[]{:S(2)}) collective-permute-start(bf16[768,768]{1,0:T(8,128)(2,1)S(1)} %get-tuple-element.175), channel_id=1, source_target_pairs={{0,1},{1,0},{2,3},{3,2},{4,5},{5,4},{6,7},{7,6},{8,9},{9,8},{10,11... | collective-permute-start | bytes 3538952 | tf_op jit(solution)/shard_map/ppermute | solution.py:72
  134.9 20.6 %collective-permute-start.36 = (bf16[4,96,768]{2,1,0:T(8,128)(2,1)S(1)}, bf16[4,96,768]{2,1,0:T(8,128)(2,1)S(1)}, u32[]{:S(2)}, u32[]{:S(2)}) collective-permute-start(bf16[4,96,768]{2,1,0:T(8,128)(2,1)S(1)} %get-tuple-element.183), channel_id=1, source_target_pairs={{0,4},{4,0},{8,12},{12,8},{16,20},{20,16},{24,28},{28,24},{1,5},{5... | collective-permute-start | bytes 1769480 | tf_op jit(solution)/shard_map/ppermute | solution.py:72
  140.1 23.2 %collective-permute-start.34 = (bf16[384,768]{1,0:T(8,128)(2,1)S(1)}, bf16[384,768]{1,0:T(8,128)(2,1)S(1)}, u32[]{:S(2)}, u32[]{:S(2)}) collective-permute-start(bf16[384,768]{1,0:T(8,128)(2,1)S(1)} %get-tuple-element.179.mine_ref), channel_id=1, source_target_pairs={{0,2},{1,3},{2,0},{3,1},{4,6},{5,7},{6,4},{7,5},{8,10},{9,11},{10,... | collective-permute-start | bytes 1769480 | tf_op jit(solution)/shard_map/ppermute | solution.py:72
  141.8 26.0 %collective-permute-start.38 = (bf16[384,768]{1,0:T(8,128)(2,1)S(1)}, bf16[384,768]{1,0:T(8,128)(2,1)S(1)}, u32[]{:S(2)}, u32[]{:S(2)}) collective-permute-start(bf16[384,768]{1,0:T(8,128)(2,1)S(1)} %get-tuple-element.186.mine_ref), channel_id=1, source_target_pairs={{0,2},{1,3},{2,0},{3,1},{4,6},{5,7},{6,4},{7,5},{8,10},{9,11},{10,... | collective-permute-start | bytes 1769480 | tf_op jit(solution)/shard_map/ppermute | solution.py:72
  142.1 13.3 %collective-permute-start.37 = (f32[8,768]{1,0:T(8,128)S(1)}, f32[8,768]{1,0:T(8,128)S(1)}, u32[]{:S(2)}, u32[]{:S(2)}) collective-permute-start(f32[8,768]{1,0:T(8,128)S(1)} %get-tuple-element.184.refs_0_), channel_id=1, source_target_pairs={{0,4},{4,0},{8,12},{12,8},{16,20},{20,16},{24,28},{28,24},{1,5},{5... | collective-permute-start | bytes 73736 | tf_op jit(solution)/shard_map/ppermute | solution.py:72
  157.0 16.0 %collective-permute-start.39 = (bf16[96,896]{1,0:T(8,128)(2,1)}, bf16[96,896]{1,0:T(8,128)(2,1)S(1)}, u32[]{:S(2)}, u32[]{:S(2)}) collective-permute-start(bf16[96,896]{1,0:T(8,128)(2,1)} %get-tuple-element.192), channel_id=1, source_target_pairs={{0,8},{4,12},{8,0},{12,4},{16,24},{20,28},{24,16},{28,20},{1,9},{5... | collective-permute-start | bytes 516104 | tf_op jit(solution)/shard_map/ppermute | solution.py:72
  160.9 15.8 %collective-permute-start.40 = (bf16[96,896]{1,0:T(8,128)(2,1)}, bf16[96,896]{1,0:T(8,128)(2,1)S(1)}, u32[]{:S(2)}, u32[]{:S(2)}) collective-permute-start(bf16[96,896]{1,0:T(8,128)(2,1)} %get-tuple-element.193), channel_id=1, source_target_pairs={{0,16},{4,20},{8,24},{12,28},{16,0},{20,4},{24,8},{28,12},{1,17},{... | collective-permute-start | bytes 516104 | tf_op jit(solution)/shard_map/ppermute | solution.py:72
  161.4 15.3 %collective-permute-start.41 = (bf16[96,896]{1,0:T(8,128)(2,1)}, bf16[96,896]{1,0:T(8,128)(2,1)}, u32[]{:S(2)}, u32[]{:S(2)}) collective-permute-start(bf16[96,896]{1,0:T(8,128)(2,1)} %get-tuple-element.194), channel_id=1, source_target_pairs={{0,24},{4,28},{8,16},{12,20},{16,8},{20,12},{24,0},{28,4},{1,25},{... | collective-permute-start | bytes 516104 | tf_op jit(solution)/shard_map/ppermute | solution.py:72
  163.2 18.1 %collective-permute-start.32 = (bf16[384,768]{1,0:T(8,128)(2,1)}, bf16[384,768]{1,0:T(8,128)(2,1)S(1)}, u32[]{:S(2)}, u32[]{:S(2)}) collective-permute-start(bf16[384,768]{1,0:T(8,128)(2,1)} %get-tuple-element.177), channel_id=1, source_target_pairs={{0,1},{1,0},{2,3},{3,2},{4,5},{5,4},{6,7},{7,6},{8,9},{9,8},{10,11... | collective-permute-start | bytes 1769480 | tf_op jit(solution)/shard_map/ppermute | solution.py:72
  167.8 13.6 %collective-permute-start.33 = (bf16[384,768]{1,0:T(8,128)(2,1)}, bf16[384,768]{1,0:T(8,128)(2,1)}, u32[]{:S(2)}, u32[]{:S(2)}) collective-permute-start(bf16[384,768]{1,0:T(8,128)(2,1)} %get-tuple-element.178), channel_id=1, source_target_pairs={{0,1},{1,0},{2,3},{3,2},{4,5},{5,4},{6,7},{7,6},{8,9},{9,8},{10,11... | collective-permute-start | bytes 1769480 | tf_op jit(solution)/shard_map/ppermute | solution.py:72
  173.0 8.4 %collective-permute-start.43 = (bf16[384,768]{1,0:T(8,128)(2,1)S(1)}, bf16[384,768]{1,0:T(8,128)(2,1)S(1)}, u32[]{:S(2)}, u32[]{:S(2)}) collective-permute-start(bf16[384,768]{1,0:T(8,128)(2,1)S(1)} %copy-done.12), channel_id=1, source_target_pairs={{0,1},{1,0},{2,3},{3,2},{4,5},{5,4},{6,7},{7,6},{8,9},{9,8},{10,11... | collective-permute-start | bytes 1769480 | tf_op jit(solution)/shard_map/ppermute | solution.py:72
  176.7 4.7 %collective-permute-start.35 = (bf16[384,768]{1,0:T(8,128)(2,1)S(1)}, bf16[384,768]{1,0:T(8,128)(2,1)S(1)}, u32[]{:S(2)}, u32[]{:S(2)}) collective-permute-start(bf16[384,768]{1,0:T(8,128)(2,1)S(1)} %copy-done.13), channel_id=1, source_target_pairs={{0,1},{1,0},{2,3},{3,2},{4,5},{5,4},{6,7},{7,6},{8,9},{9,8},{10,11... | collective-permute-start | bytes 1769480 | tf_op jit(solution)/shard_map/ppermute | solution.py:72
  177.7 3.7 %collective-permute-start.42 = (f32[8,96]{1,0:T(8,128)S(1)}, f32[8,96]{1,0:T(8,128)S(1)}, u32[]{:S(2)}, u32[]{:S(2)}) collective-permute-start(f32[8,96]{1,0:T(8,128)S(1)} %slice.38), channel_id=1, source_target_pairs={{0,2},{1,3},{2,0},{3,1},{4,6},{5,7},{6,4},{7,5},{8,10},{9,11},{10,... | collective-permute-start | bytes 9224 | tf_op jit(solution)/shard_map/ppermute | solution.py:72
  181.4 3.2 %collective-permute-start.44 = (f32[8,96]{1,0:T(8,128)S(1)}, f32[8,96]{1,0:T(8,128)S(1)}, u32[]{:S(2)}, u32[]{:S(2)}) collective-permute-start(f32[8,96]{1,0:T(8,128)S(1)} %slice_add_fusion), channel_id=1, source_target_pairs={{0,1},{1,0},{2,3},{3,2},{4,5},{5,4},{6,7},{7,6},{8,9},{9,8},{10,11... | collective-permute-start | bytes 9224 | tf_op jit(solution)/shard_map/ppermute | solution.py:72
  (12 other events, 103.1 us)
